TPU v7x, 32 devices: a whole 2x2x4 slice. The times are simulated.
32 devices in a mesh: frame: 16 (over z, y, core), state: 2 (over x).
Axes of the slice: x: 2, y: 2, z: 4, core: 2. Of those that a mesh axis runs over, the one named last changes fastest.
Arguments:
- object_slices: float32 [2, 2, 4096, 512], P(None, None, 'frame'), may hold values from -4 to 4
- probe: float32 [2, 2, 256, 256], P('state'), may hold values from -4 to 4
- amplitude: float32 [16, 256, 256], P('frame'), may hold values from 0.5 to 4
- positions: int32 [16, 2], P('frame'), may hold values from 0 to 256, as said below
- propagator: float32 [256, 256], replicated, may hold values from -3.140625 to 3.140625
Outputs:
- gradient: float32 [2, 2, 4096, 512], P(None, None, ('frame', 'state'))
Inputs may be any that keep to these rules, and one draw needn't show every extreme that they name: positions[f, 0] is the row offset of frame f's patch within the rows owned by its owner f, from 0 to 255; positions[f, 1] is its column offset, from 0 to 256.
All inputs are finite; a program needn't handle non-finite values.
Results may differ from a plain program's by a relative error of at most 0.0001.
Values sent between devices are 32-bit elements; how exact they have to be, the bound alone decides.
No kernel may reach another device: no remote copies, remote signals or barrier semaphores. Data moves between devices by JAX's collectives and lax.ppermute only.
A program may use at most 64 MiB of HBM per device.

v0:
```python
import functools
import math

import jax
import jax.numpy as jnp
import numpy as np
from jax import lax
from jax.experimental import pallas as pl
from jax.experimental.pallas import tpu as pltpu
from jax.sharding import PartitionSpec as P

F32 = jnp.float32
BF16 = jnp.bfloat16
VMEM = pl.BlockSpec(memory_space=pltpu.VMEM)
SMEM = pl.BlockSpec(memory_space=pltpu.SMEM)
LIMIT = 24 * 1024 * 1024


def shifted(value, axis, by):
    count = lax.axis_size(axis)
    return lax.ppermute(value, axis, [(i, (i + by) % count) for i in range(count)])


def call(body, outs, ins, scratch=(), flops=0, moved=0):
    return pl.pallas_call(
        body,
        out_shape=[jax.ShapeDtypeStruct(shape, F32) for shape in outs],
        in_specs=ins,
        out_specs=[VMEM] * len(outs),
        scratch_shapes=list(scratch),
        compiler_params=pltpu.CompilerParams(vmem_limit_bytes=LIMIT),
        cost_estimate=pl.CostEstimate(flops=flops, bytes_accessed=moved, transcendentals=0),
    )


def tables(length):
    half = length // 2
    n = np.arange(half)[:, None]
    forms = []
    for parity in (0, 1):
        k = 2 * np.arange(half)[None, :] + parity
        angle = -2.0 * math.pi * ((n * k) % length) / length
        re, im = np.cos(angle) / math.sqrt(length), np.sin(angle) / math.sqrt(length)
        right = np.block([[re, im], [-im, re]])
        forms += [right, right.T]
    stack = np.stack(forms).astype(np.float64)
    top = stack.astype(BF16)
    rest = (stack - top.astype(np.float64)).astype(BF16)
    return jnp.asarray(np.stack([top, rest]))


def halves(value):
    top = value.astype(BF16)
    return top, (value - top.astype(F32)).astype(BF16)


def dot(a, b):
    return lax.dot_general(a, b, (((1,), (0,)), ((), ())), preferred_element_type=F32)


def times_table(value, tab, which):
    top, rest = halves(value)
    return dot(top, tab[0, which]) + (dot(rest, tab[0, which]) + dot(top, tab[1, which]))


def table_times(value, tab, which):
    top, rest = halves(value)
    return dot(tab[0, which], top) + (dot(tab[0, which], rest) + dot(tab[1, which], top))


def columns_forward(re, im, tab):
    h = re.shape[1] // 2
    r0, r1, i0, i1 = re[:, :h], re[:, h:], im[:, :h], im[:, h:]
    even = times_table(jnp.concatenate([r0 + r1, i0 + i1], 1), tab, 0)
    odd = times_table(jnp.concatenate([r0 - r1, i0 - i1], 1), tab, 2)
    return (
        jnp.concatenate([even[:, :h], odd[:, :h]], 1),
        jnp.concatenate([even[:, h:], odd[:, h:]], 1),
    )


def columns_inverse(re, im, tab):
    h = re.shape[1] // 2
    even = times_table(jnp.concatenate([re[:, :h], im[:, :h]], 1), tab, 1)
    odd = times_table(jnp.concatenate([re[:, h:], im[:, h:]], 1), tab, 3)
    total, gap = even + odd, even - odd
    return (
        jnp.concatenate([total[:, :h], gap[:, :h]], 1),
        jnp.concatenate([total[:, h:], gap[:, h:]], 1),
    )


def rows_forward(re, im, tab):
    h = re.shape[0] // 2
    r0, r1, i0, i1 = re[:h], re[h:], im[:h], im[h:]
    even = table_times(jnp.concatenate([r0 + r1, i0 + i1], 0), tab, 1)
    odd = table_times(jnp.concatenate([r0 - r1, i0 - i1], 0), tab, 3)
    return (
        jnp.concatenate([even[:h], odd[:h]], 0),
        jnp.concatenate([even[h:], odd[h:]], 0),
    )


def rows_inverse(re, im, tab):
    h = re.shape[0] // 2
    even = table_times(jnp.concatenate([re[:h], im[:h]], 0), tab, 0)
    odd = table_times(jnp.concatenate([re[h:], im[h:]], 0), tab, 2)
    total, gap = even + odd, even - odd
    return (
        jnp.concatenate([total[:h], gap[:h]], 0),
        jnp.concatenate([total[h:], gap[h:]], 0),
    )


def forward(re, im, tab):
    return rows_forward(*columns_forward(re, im, tab), tab)


def inverse(re, im, tab):
    return columns_inverse(*rows_inverse(re, im, tab), tab)


def thirds(value):
    top = value.astype(BF16)
    left = value - top.astype(F32)
    mid = left.astype(BF16)
    return top, mid, (left - mid.astype(F32)).astype(BF16)


def by_parity(value):
    size = value.shape[0]
    h = size // 2
    picks = []
    for along in (0, 1):
        place = lax.broadcasted_iota(jnp.int32, (size, size), along)
        source = lax.broadcasted_iota(jnp.int32, (size, size), 1 - along)
        wanted = jnp.where(place < h, 2 * place, 2 * (place - h) + 1)
        picks.append(jnp.where(source == wanted, 1.0, 0.0).astype(BF16))
    top, mid, low = thirds(value)
    value = (dot(picks[0], top) + dot(picks[0], mid)) + dot(picks[0], low)
    top, mid, low = thirds(value)
    return (dot(top, picks[1]) + dot(mid, picks[1])) + dot(low, picks[1])


def prepare_body(prop_ref, amp_ref, wave_re, wave_im, amp_out):
    phase = by_parity(prop_ref[...])
    wave_re[...] = jnp.cos(phase)
    wave_im[...] = jnp.sin(phase)
    amp_out[...] = by_parity(amp_ref[0])


def turn_body(pos_ref, probe_ref, out_ref):
    size = probe_ref.shape[-1]
    row, col = pos_ref[0, 0], lax.rem(pos_ref[0, 1], size)
    for m in range(probe_ref.shape[0]):
        for c in range(2):
            out_ref[m, c] = pltpu.roll(pltpu.roll(probe_ref[m, c], row, 0), col, 1)


def patch_of(own_ref, halo_ref, row, col):
    size = halo_ref.shape[-1]
    r = lax.broadcasted_iota(jnp.int32, (size, size), 0)
    c = lax.broadcasted_iota(jnp.int32, (size, size), 1)
    parts = []
    for part in range(2):
        own = jnp.where(c < col, own_ref[0, part, :, size:], own_ref[0, part, :, :size])
        parts.append(jnp.where(r < row, halo_ref[part], own))
    return parts


def inner_body(kept, count, pos_ref, own_ref, halo_ref, probe_ref, kr_ref, ki_ref, tab, *refs):
    before = refs[:-2]
    out_ref, patch = refs[-2:]
    for ref in before:
        out_ref[:kept] = ref[...]
    re, im = patch_of(own_ref, halo_ref, pos_ref[0, 0], pos_ref[0, 1])
    patch[0] = re
    patch[1] = im

    def state(m, carry):
        pr, pi = probe_ref[m, 0], probe_ref[m, 1]
        ar, ai = patch[0], patch[1]
        wr, wi = forward(pr * ar - pi * ai, pr * ai + pi * ar, tab)
        kr, ki = kr_ref[...], ki_ref[...]
        ir, ii = inverse(kr * wr - ki * wi, kr * wi + ki * wr, tab)
        out_ref[kept + m, 0] = ir
        out_ref[kept + m, 1] = ii
        return carry

    lax.fori_loop(0, count, state, 0)


def middle_body(rows, pos_ref, own_ref, halo_ref, inner_ref, amp_ref, tab, term_ref, chi_ref, patch, far, power):
    states = inner_ref.shape[0]
    re, im = patch_of(own_ref, halo_ref, pos_ref[0, 0], pos_ref[0, 1])
    patch[0] = re
    patch[1] = im
    power[...] = jnp.zeros_like(power)

    def outward(m, carry):
        br, bi = patch[0], patch[1]
        ir, ii = inner_ref[m, 0], inner_ref[m, 1]
        fr, fi = forward(br * ir - bi * ii, br * ii + bi * ir, tab)
        far[m, 0] = fr
        far[m, 1] = fi
        power[...] += fr * fr + fi * fi
        return carry

    lax.fori_loop(0, states, outward, 0)
    power[...] = 1.0 - amp_ref[...] / jnp.sqrt(power[...] + 1.0)
    term_ref[...] = jnp.zeros_like(term_ref)
    start = pl.multiple_of(pos_ref[0, 2] * rows, rows)

    def homeward(m, carry):
        factor = power[...]
        kr, ki = inverse(factor * far[m, 0], factor * far[m, 1], tab)
        far[m, 0] = kr
        far[m, 1] = ki
        br, bi = patch[0], patch[1]
        chi_ref[m, 0] = br * kr + bi * ki
        chi_ref[m, 1] = br * ki - bi * kr
        take = pl.ds(start, rows)
        ir, ii = inner_ref[m, 0, take], inner_ref[m, 1, take]
        kr, ki = far[m, 0, take], far[m, 1, take]
        term_ref[0] += ir * kr + ii * ki
        term_ref[1] += ir * ki - ii * kr
        return carry

    lax.fori_loop(0, states, homeward, 0)


def last_body(rows, pos_ref, chi_ref, first_ref, rest_ref, kr_ref, ki_ref, tab, term_ref, front):
    term_ref[...] = jnp.zeros_like(term_ref)
    start = pl.multiple_of(pos_ref[0, 2] * rows, rows)
    take = pl.ds(start, rows)

    def state(m, carry):
        wr, wi = forward(chi_ref[m, 0], chi_ref[m, 1], tab)
        kr, ki = kr_ref[...], ki_ref[...]
        ur, ui = rows_inverse(kr * wr + ki * wi, kr * wi - ki * wr, tab)
        front[0] = ur
        front[1] = ui
        fr, fi = columns_inverse(front[0, take], front[1, take], tab)
        own = m == 0
        at = jnp.maximum(m - 1, 0)
        pr = jnp.where(own, first_ref[0, 0, take], rest_ref[at, 0, take])
        pi = jnp.where(own, first_ref[0, 1, take], rest_ref[at, 1, take])
        term_ref[0] += pr * fr + pi * fi
        term_ref[1] += pr * fi - pi * fr
        return carry

    lax.fori_loop(0, chi_ref.shape[0], state, 0)


def gather_body(rows, pos_ref, zero_ref, zero_in, one_ref, one_in, out_ref):
    size = zero_ref.shape[-1]
    start = pos_ref[0, 2] * rows
    r = lax.broadcasted_iota(jnp.int32, (rows, size), 0) + start
    c = lax.broadcasted_iota(jnp.int32, (rows, size), 1)
    here, there = r >= pos_ref[0, 0], r < pos_ref[0, 3]
    here_right, there_right = c < pos_ref[0, 1], c < pos_ref[0, 4]
    for s, (own, came) in enumerate(((zero_ref, zero_in), (one_ref, one_in))):
        for part in range(2):
            mine = jnp.where(here, own[part], 0.0)
            theirs = jnp.where(there, came[part], 0.0)
            out_ref[s, part, :, :size] = jnp.where(here_right, 0.0, mine) + jnp.where(there_right, 0.0, theirs)
            out_ref[s, part, :, size:] = jnp.where(here_right, mine, 0.0) + jnp.where(there_right, theirs, 0.0)


def on_device(object_slices, probe, amplitude, positions, propagator):
    states = lax.axis_size("state")
    size = amplitude.shape[1]
    rows = object_slices.shape[2] // states
    assert object_slices.shape[2:] == (size, 2 * size) and positions.shape[0] == 1
    before = shifted(positions, "frame", 1)
    others = [shifted(probe, "state", by) for by in range(1, states)]
    rest = others[0] if states == 2 else jnp.concatenate(others, 0)
    tab = tables(size)
    flops = 24 * size**3
    share = states - 1

    column = lax.broadcasted_iota(jnp.int32, (2, size, size), 2)
    halos = []
    for s in range(2):
        picked = jnp.where(column < before[0, 1], object_slices[s, :, :, size:], object_slices[s, :, :, :size])
        halos.append(shifted(picked, "frame", -1))
    index = lax.axis_index("state").astype(jnp.int32)
    where = jnp.concatenate([positions, index[None, None], before], 1)

    grid = (size, size)
    kr, ki, amp = call(prepare_body, [grid] * 3, [VMEM] * 2, flops=2 * size**3, moved=20 * size**2)(propagator, amplitude)
    (first,) = call(turn_body, [probe.shape], [SMEM, VMEM], moved=16 * size**2)(positions, probe)
    (rest,) = call(turn_body, [rest.shape], [SMEM, VMEM], moved=16 * size**2 * share)(positions, rest)

    def inner(kept, count, at, turned, *given):
        (result,) = call(
            functools.partial(inner_body, kept, count),
            [(kept + count, 2) + grid],
            [SMEM, VMEM, VMEM, VMEM, VMEM, VMEM, VMEM] + [VMEM] * len(given),
            [pltpu.VMEM((2,) + grid, F32)],
            flops=2 * flops * count,
            moved=16 * size**2 * count,
        )(where, object_slices[0:1], halos[0], turned, kr, ki, tab, *given)
        return result

    waves = inner(0, 1, 0, first)
    waves = inner(1, share, 1, rest, waves)
    term_one, chi = call(
        functools.partial(middle_body, rows),
        [(2, rows, size), (states, 2) + grid],
        [SMEM] + [VMEM] * 5,
        [pltpu.VMEM((2,) + grid, F32), pltpu.VMEM((states, 2) + grid, F32), pltpu.VMEM(grid, F32)],
        flops=2 * flops * states,
        moved=32 * size**2 * states,
    )(where, object_slices[1:2], halos[1], waves, amp, tab)
    came_one = shifted(term_one, "frame", 1)
    (term_zero,) = call(
        functools.partial(last_body, rows),
        [(2, rows, size)],
        [SMEM] + [VMEM] * 6,
        [pltpu.VMEM((2,) + grid, F32)],
        flops=2 * flops * states,
        moved=16 * size**2 * states,
    )(where, chi, first, rest, kr, ki, tab)
    came_zero = shifted(term_zero, "frame", 1)
    (gradient,) = call(
        functools.partial(gather_body, rows),
        [(2, 2, rows, 2 * size)],
        [SMEM] + [VMEM] * 4,
        moved=64 * rows * size,
    )(where, term_zero, came_zero, term_one, came_one)
    return gradient


def solution(mesh):
    return jax.shard_map(
        on_device,
        mesh=mesh,
        in_specs=(
            P(None, None, "frame", None),
            P("state", None, None, None),
            P("frame", None, None),
            P("frame", None),
            P(),
        ),
        out_specs=P(None, None, ("frame", "state"), None),
        check_vma=False,
    )
```

profile of v0, /device:TPU:0, one launch (start us, length us, event | category | flops | bytes accessed | tf_op | source)
XLA Modules:
  0.0 43.2 jit_solution(11800942172043233610)
XLA Ops:
  0.0 0.5 %collective-permute-start = (s32[1,2]{1,0:T(1,128)}, s32[1,2]{1,0:T(1,128)S(1)}, u32[]{:S(2)}, u32[]{:S(2)}) collective-permute-start(s32[1,2]{1,0:T(1,128)} %pos_ref.3), channel_id=1, source_target_pairs={{0,2},{2,4},{4,6},{6,8},{8,10},{10,12},{12,14},{14,16},{16,18},{18... | collective-permute-start | bytes 32 | tf_op jit(solution)/shard_map/ppermute | solution.py:21
  0.5 2.5 %collective-permute-start.3 = (f32[1,2,256,256]{3,2,1,0:T(8,128)}, f32[1,2,256,256]{3,2,1,0:T(8,128)S(1)}, u32[]{:S(2)}, u32[]{:S(2)}) collective-permute-start(f32[1,2,256,256]{3,2,1,0:T(8,128)} %probe_ref.1), channel_id=1, source_target_pairs={{0,1},{1,0},{2,3},{3,2},{4,5},{5,4},{6,7},{7,6},{8,9},{9,8},{10,11... | collective-permute-start | bytes 1572872 | tf_op jit(solution)/shard_map/ppermute | solution.py:21
  3.0 3.9 %collective-permute-done = s32[1,2]{1,0:T(1,128)S(1)} collective-permute-done((s32[1,2]{1,0:T(1,128)}, s32[1,2]{1,0:T(1,128)S(1)}, u32[]{:S(2)}, u32[]{:S(2)}) %collective-permute-start) | collective-permute-done | bytes 40 | tf_op jit(solution)/shard_map/ppermute | solution.py:21
  6.9 0.6 %slice.24 = s32[1,1]{1,0:T(1,128)} slice(s32[1,2]{1,0:T(1,128)S(1)} %collective-permute-done), slice={[0:1], [1:2]} | slice | bytes 8 | tf_op jit(solution)/shard_map/slice | solution.py:285
  7.5 0.6 %iota_compare_fusion = pred[256]{0:T(512)(128)(4,1)S(1)} fusion(s32[]{:T(128)} %bitcast.1), kind=kLoop, calls=%fused_computation.2 | loop fusion | flops 256 | bytes 260 | tf_op jit(solution)/shard_map/lt | solution.py:285
  8.2 0.0 copy-start.2
  8.2 0.0 copy-start.3
  8.2 1.7 %bitcast_select_fusion = (f32[2,256,256]{2,1,0:T(8,128)S(1)}, f32[2,256,256]{2,1,0:T(8,128)S(1)}) fusion(f32[2,2,256,512]{3,2,1,0:T(8,128)} %param.6, pred[256]{0:T(512)(128)(4,1)S(1)} %iota_compare_fusion), kind=kLoop, calls=%fused_computation | loop fusion | flops 262144 | bytes 3145984 | tf_op jit(solution)/shard_map/jit(_where)/select_n | solution.py:285
  9.9 0.3 collective-permute-start.2
  10.2 0.0 copy-done.4
  10.2 0.0 copy-done.1
  10.2 0.8 %shard_map.66.probe_ref.first_ref = f32[1,2,256,256]{3,2,1,0:T(8,128)S(1)} custom-call(s32[1,2]{1,0:T(1,128)S(1)} %copy-done.4, f32[1,2,256,256]{3,2,1,0:T(8,128)S(1)} %copy-done.1), custom_call_target="tpu_custom_call" | custom-call | bytes 1048576 | tf_op jit(solution)/shard_map/pallas_call | solution.py:292
  10.9 0.0 copy-done.2
  11.0 0.0 copy-done.3
  11.0 1.6 %shard_map.65 = (f32[256,256]{1,0:T(8,128)S(1)}, f32[256,256]{1,0:T(8,128)S(1)}, f32[256,256]{1,0:T(8,128)S(1)}) custom-call(f32[256,256]{1,0:T(8,128)S(1)} %copy-done.2, f32[1,256,256]{2,1,0:T(8,128)S(1)} %copy-done.3), custom_call_target="tpu_custom_call" | custom-call | flops 33554432 | bytes 1310720 | tf_op jit(solution)/shard_map/pallas_call | solution.py:291
  12.6 0.0 copy-start
  12.6 2.2 %collective-permute-start.1 = (f32[2,256,256]{2,1,0:T(8,128)S(1)}, f32[2,256,256]{2,1,0:T(8,128)S(1)}, u32[]{:S(2)}, u32[]{:S(2)}) collective-permute-start(f32[2,256,256]{2,1,0:T(8,128)S(1)} %get-tuple-element.16), channel_id=1, source_target_pairs={{0,30},{2,0},{4,2},{6,4},{8,6},{10,8},{12,10},{14,12},{16,14},{18,... | collective-permute-start | bytes 1572872 | tf_op jit(solution)/shard_map/ppermute | solution.py:21
  14.8 1.7 %fusion = (f32[1,2,256,512]{3,2,1,0:T(8,128)S(1)}, f32[1,2,256,512]{3,2,1,0:T(8,128)S(1)}) fusion(f32[2,2,256,512]{3,2,1,0:T(8,128)} %param.6), kind=kLoop, calls=%fused_computation.4 | loop fusion | bytes 4194304 | tf_op jit(solution)/shard_map/slice | solution.py:303
  16.6 0.1 pad_add_fusion.pos_ref
  16.6 0.0 collective-permute-done.3.probe_ref
  16.6 0.8 %shard_map.64.probe_ref.rest_ref = f32[1,2,256,256]{3,2,1,0:T(8,128)S(1)} custom-call(s32[1,2]{1,0:T(1,128)S(1)} %copy-done.4, f32[1,2,256,256]{3,2,1,0:T(8,128)S(1)} %collective-permute-done.3.probe_ref), custom_call_target="tpu_custom_call" | custom-call | bytes 1048576 | tf_op jit(solution)/shard_map/pallas_call | solution.py:293
  17.4 0.0 collective-permute-done.2.halo_ref
  17.4 2.1 %shard_map.67.refs_0_ = f32[1,2,256,256]{3,2,1,0:T(8,128)S(1)} custom-call(s32[1,5]{1,0:T(1,128)S(1)} %pad_add_fusion.pos_ref, f32[1,2,256,512]{3,2,1,0:T(8,128)S(1)} %get-tuple-element.17.own_ref, f32[2,256,256]{2,1,0:T(8,128)S(1)} %collective-permute-done.2.halo_ref, f32[1,2,256,256]{3,2,1,0:T(8,128)S(1)} %shard_map.66.probe_ref.first_ref, ...), custom_call_target="tpu_custom_call" | custom-call | flops 805306368 | bytes 1048576 | tf_op jit(solution)/shard_map/pallas_call | solution.py:296
  19.6 2.1 %shard_map.68.inner_ref = f32[2,2,256,256]{3,2,1,0:T(8,128)S(1)} custom-call(s32[1,5]{1,0:T(1,128)S(1)} %pad_add_fusion.pos_ref, f32[1,2,256,512]{3,2,1,0:T(8,128)S(1)} %get-tuple-element.17.own_ref, f32[2,256,256]{2,1,0:T(8,128)S(1)} %collective-permute-done.2.halo_ref, f32[1,2,256,256]{3,2,1,0:T(8,128)S(1)} %shard_map.64.probe_ref.rest_ref, ...), custom_call_target="tpu_custom_call" | custom-call | flops 805306368 | bytes 1048576 | tf_op jit(solution)/shard_map/pallas_call | solution.py:296
  21.7 0.8 %collective-permute-done.1.halo_ref = f32[2,256,256]{2,1,0:T(8,128)S(1)} collective-permute-done((f32[2,256,256]{2,1,0:T(8,128)S(1)}, f32[2,256,256]{2,1,0:T(8,128)S(1)}, u32[]{:S(2)}, u32[]{:S(2)}) %collective-permute-start.1) | collective-permute-done | bytes 524320 | tf_op jit(solution)/shard_map/ppermute | solution.py:21
  22.5 4.0 %shard_map.69 = (f32[2,128,256]{2,1,0:T(8,128)S(1)}, f32[2,2,256,256]{3,2,1,0:T(8,128)S(1)}) custom-call(s32[1,5]{1,0:T(1,128)S(1)} %pad_add_fusion.pos_ref, f32[1,2,256,512]{3,2,1,0:T(8,128)S(1)} %get-tuple-element.18.own_ref, f32[2,256,256]{2,1,0:T(8,128)S(1)} %collective-permute-done.1.halo_ref, f32[2,2,256,256]{3,2,1,0:T(8,128)S(1)} %shard_map.68.inner_ref, ...), custom_call_target="tpu_custom_call" | custom-call | flops 1610612736 | bytes 4194304 | tf_op jit(solution)/shard_map/pallas_call | solution.py:308
  26.5 3.5 %shard_map.70.zero_ref = f32[2,128,256]{2,1,0:T(8,128)S(1)} custom-call(s32[1,5]{1,0:T(1,128)S(1)} %pad_add_fusion.pos_ref, f32[2,2,256,256]{3,2,1,0:T(8,128)S(1)} %get-tuple-element.13.chi_ref, f32[1,2,256,256]{3,2,1,0:T(8,128)S(1)} %shard_map.66.probe_ref.first_ref, f32[1,2,256,256]{3,2,1,0:T(8,128)S(1)} %shard_map.64.probe_ref.rest_ref, ...), custom_call_target="tpu_custom_call" | custom-call | flops 1610612736 | bytes 2097152 | tf_op jit(solution)/shard_map/pallas_call | solution.py:317
  30.0 0.1 collective-permute-start.4
  30.1 0.2 collective-permute-start.5
  30.3 8.5 %collective-permute-done.4.zero_in = f32[2,128,256]{2,1,0:T(8,128)S(1)} collective-permute-done((f32[2,128,256]{2,1,0:T(8,128)S(1)}, f32[2,128,256]{2,1,0:T(8,128)S(1)}, u32[]{:S(2)}, u32[]{:S(2)}) %collective-permute-start.4) | collective-permute-done | bytes 262176 | tf_op jit(solution)/shard_map/ppermute | solution.py:21
  38.7 2.8 %collective-permute-done.5.one_in = f32[2,128,256]{2,1,0:T(8,128)S(1)} collective-permute-done((f32[2,128,256]{2,1,0:T(8,128)S(1)}, f32[2,128,256]{2,1,0:T(8,128)S(1)}, u32[]{:S(2)}, u32[]{:S(2)}) %collective-permute-start.5) | collective-permute-done | bytes 262176 | tf_op jit(solution)/shard_map/ppermute | solution.py:21
  41.5 1.7 %shard_map.71 = f32[2,2,128,512]{3,2,1,0:T(8,128)} custom-call(s32[1,5]{1,0:T(1,128)S(1)} %pad_add_fusion.pos_ref, f32[2,128,256]{2,1,0:T(8,128)S(1)} %shard_map.70.zero_ref, f32[2,128,256]{2,1,0:T(8,128)S(1)} %collective-permute-done.4.zero_in, f32[2,128,256]{2,1,0:T(8,128)S(1)} %get-tuple-element.14.one_ref, f32[2,128,256]{2,1,0:T(8,128)S(1)} %collective-permute-done.5.one_in), custom_call_target="tpu_custom_call" | custom-call | bytes 2097152 | tf_op jit(solution)/shard_map/pallas_call | solution.py:326
  (3 shorter events, 0.0 us)
Async XLA Ops:
  0.0 10.2 %copy-start.4 = (s32[1,2]{1,0:T(1,128)S(1)}, s32[1,2]{1,0:T(1,128)}, u32[]{:S(2)}) copy-start(s32[1,2]{1,0:T(1,128)} %pos_ref.3) | copy-start | bytes 28
  0.0 10.2 %copy-start.1 = (f32[1,2,256,256]{3,2,1,0:T(8,128)S(1)}, f32[1,2,256,256]{3,2,1,0:T(8,128)}, u32[]{:S(2)}) copy-start(f32[1,2,256,256]{3,2,1,0:T(8,128)} %probe_ref.1) | copy-start | bytes 1572868
  0.0 6.9 %collective-permute-start = (s32[1,2]{1,0:T(1,128)}, s32[1,2]{1,0:T(1,128)S(1)}, u32[]{:S(2)}, u32[]{:S(2)}) collective-permute-start(s32[1,2]{1,0:T(1,128)} %pos_ref.3), channel_id=1, source_target_pairs={{0,2},{2,4},{4,6},{6,8},{8,10},{10,12},{12,14},{14,16},{16,18},{18... | collective-permute-start | bytes 32 | tf_op jit(solution)/shard_map/ppermute | solution.py:21
  0.5 16.1 %collective-permute-start.3 = (f32[1,2,256,256]{3,2,1,0:T(8,128)}, f32[1,2,256,256]{3,2,1,0:T(8,128)S(1)}, u32[]{:S(2)}, u32[]{:S(2)}) collective-permute-start(f32[1,2,256,256]{3,2,1,0:T(8,128)} %probe_ref.1), channel_id=1, source_target_pairs={{0,1},{1,0},{2,3},{3,2},{4,5},{5,4},{6,7},{7,6},{8,9},{9,8},{10,11... | collective-permute-start | bytes 1572872 | tf_op jit(solution)/shard_map/ppermute | solution.py:21
  8.2 2.8 %copy-start.2 = (f32[256,256]{1,0:T(8,128)S(1)}, f32[256,256]{1,0:T(8,128)}, u32[]{:S(2)}) copy-start(f32[256,256]{1,0:T(8,128)} %prop_ref.1) | copy-start | bytes 786436
  8.2 2.8 %copy-start.3 = (f32[1,256,256]{2,1,0:T(8,128)S(1)}, f32[1,256,256]{2,1,0:T(8,128)}, u32[]{:S(2)}) copy-start(f32[1,256,256]{2,1,0:T(8,128)} %amp_ref.1) | copy-start | bytes 786436
  9.9 7.5 %collective-permute-start.2 = (f32[2,256,256]{2,1,0:T(8,128)S(1)}, f32[2,256,256]{2,1,0:T(8,128)S(1)}, u32[]{:S(2)}, u32[]{:S(2)}) collective-permute-start(f32[2,256,256]{2,1,0:T(8,128)S(1)} %get-tuple-element.15), channel_id=1, source_target_pairs={{0,30},{2,0},{4,2},{6,4},{8,6},{10,8},{12,10},{14,12},{16,14},{18,... | collective-permute-start | bytes 1572872 | tf_op jit(solution)/shard_map/ppermute | solution.py:21
  12.6 4.8 %copy-start = (bf16[2,4,256,256]{3,2,1,0:T(8,128)(2,1)S(1)}, bf16[2,4,256,256]{3,2,1,0:T(8,128)(2,1)}, u32[]{:S(2)}) copy-start(bf16[2,4,256,256]{3,2,1,0:T(8,128)(2,1)} %constant.6.clone.tab) | copy-start | bytes 3145732
  12.6 9.9 %collective-permute-start.1 = (f32[2,256,256]{2,1,0:T(8,128)S(1)}, f32[2,256,256]{2,1,0:T(8,128)S(1)}, u32[]{:S(2)}, u32[]{:S(2)}) collective-permute-start(f32[2,256,256]{2,1,0:T(8,128)S(1)} %get-tuple-element.16), channel_id=1, source_target_pairs={{0,30},{2,0},{4,2},{6,4},{8,6},{10,8},{12,10},{14,12},{16,14},{18,... | collective-permute-start | bytes 1572872 | tf_op jit(solution)/shard_map/ppermute | solution.py:21
  30.0 8.7 %collective-permute-start.4 = (f32[2,128,256]{2,1,0:T(8,128)S(1)}, f32[2,128,256]{2,1,0:T(8,128)S(1)}, u32[]{:S(2)}, u32[]{:S(2)}) collective-permute-start(f32[2,128,256]{2,1,0:T(8,128)S(1)} %shard_map.70.zero_ref), channel_id=1, source_target_pairs={{0,2},{2,4},{4,6},{6,8},{8,10},{10,12},{12,14},{14,16},{16,18},{18... | collective-permute-start | bytes 786440 | tf_op jit(solution)/shard_map/ppermute | solution.py:21
  30.1 11.5 %collective-permute-start.5 = (f32[2,128,256]{2,1,0:T(8,128)S(1)}, f32[2,128,256]{2,1,0:T(8,128)S(1)}, u32[]{:S(2)}, u32[]{:S(2)}) collective-permute-start(f32[2,128,256]{2,1,0:T(8,128)S(1)} %get-tuple-element.14.one_ref), channel_id=1, source_target_pairs={{0,2},{2,4},{4,6},{6,8},{8,10},{10,12},{12,14},{14,16},{16,18},{18... | collective-permute-start | bytes 786440 | tf_op jit(solution)/shard_map/ppermute | solution.py:21
where the time goes:
time: 43.4 us; the launch traced here: 43.2 us
  Pallas kernels  16.6 us (38%)
  waiting for transfers between devices  15.9 us (37%)
  starting transfers between devices  5.74 us (13%)
  other arithmetic  2.43 us (6%)
  local copies, waits for them, and re-layouts  2.34 us (5%)
    ppermute x6, waiting for transfers between devices, shifted(): lax.ppermute(value, axis, [(i, (i + by) % count) for i in range(count)])  15.9 us
    ppermute x6, starting transfers between devices, shifted(): lax.ppermute(value, axis, [(i, (i + by) % count) for i in range(count)])  5.74 us
    pallas_call x2, Pallas kernels, inner(): call(functools.partial(inner_body, kept, count), [(kept + count, 2) + gri...  4.25 us
    pallas_call x1, Pallas kernels, on_device(): call(functools.partial(middle_body, rows), [(2, rows, size), (states, 2)...  4.05 us
    pallas_call x1, Pallas kernels, on_device(): call(functools.partial(last_body, rows), [(2, rows, size)], [SMEM] + [VME...  3.46 us
    slice x1, local copies, waits for them, and re-layouts, inner(): object_slices[0:1]  1.73 us
    select_n x1, other arithmetic, on_device(): jnp.where(column < before[0, 1], object_slices[s, :, :, size:], object_sl...  1.71 us
    pallas_call x1, Pallas kernels, on_device(): call(functools.partial(gather_body, rows), [(2, 2, rows, 2 * size)], [SME...  1.68 us
  transfers between devices with their start and end apart: 6, of which 4 were waited for; matrix products, arithmetic and copies ran while one was open for 11% of the time, Pallas kernels for 17%

commit v1 on v0

v1 whole, which is shorter than its diff:
```python
import functools
import math

import jax
import jax.numpy as jnp
import numpy as np
from jax import lax
from jax.experimental import pallas as pl
from jax.experimental.pallas import tpu as pltpu
from jax.sharding import PartitionSpec as P


F32 = jnp.float32
BF16 = jnp.bfloat16
VMEM = pl.BlockSpec(memory_space=pltpu.VMEM)
SMEM = pl.BlockSpec(memory_space=pltpu.SMEM)
LIMIT = 24 * 1024 * 1024


def shifted(value, axis, by):
    count = lax.axis_size(axis)
    return lax.ppermute(value, axis, [(i, (i + by) % count) for i in range(count)])


def call(body, outs, ins, scratch=(), flops=0, moved=0):
    return pl.pallas_call(
        body,
        out_shape=[jax.ShapeDtypeStruct(shape, F32) for shape in outs],
        in_specs=ins,
        out_specs=[VMEM] * len(outs),
        scratch_shapes=list(scratch),
        compiler_params=pltpu.CompilerParams(vmem_limit_bytes=LIMIT),
        cost_estimate=pl.CostEstimate(flops=flops, bytes_accessed=moved, transcendentals=0),
    )


def tables(length):
    half = length // 2
    n = np.arange(half)[:, None]
    forms = []
    for parity in (0, 1):
        k = 2 * np.arange(half)[None, :] + parity
        angle = -2.0 * math.pi * ((n * k) % length) / length
        re, im = np.cos(angle) / math.sqrt(length), np.sin(angle) / math.sqrt(length)
        right = np.block([[re, im], [-im, re]])
        forms += [right, right.T]
    stack = np.stack(forms).astype(np.float64)
    top = stack.astype(BF16)
    rest = (stack - top.astype(np.float64)).astype(BF16)
    return jnp.asarray(np.stack([top, rest]))


def halves(value):
    top = value.astype(BF16)
    return top, (value - top.astype(F32)).astype(BF16)


def dot(a, b):
    return lax.dot_general(a, b, (((1,), (0,)), ((), ())), preferred_element_type=F32)


def times_table(value, tab, which):
    top, rest = halves(value)
    return dot(top, tab[0, which]) + (dot(rest, tab[0, which]) + dot(top, tab[1, which]))


def table_times(value, tab, which):
    top, rest = halves(value)
    return dot(tab[0, which], top) + (dot(tab[0, which], rest) + dot(tab[1, which], top))


def columns_forward(re, im, tab):
    h = re.shape[1] // 2
    r0, r1, i0, i1 = re[:, :h], re[:, h:], im[:, :h], im[:, h:]
    even = times_table(jnp.concatenate([r0 + r1, i0 + i1], 1), tab, 0)
    odd = times_table(jnp.concatenate([r0 - r1, i0 - i1], 1), tab, 2)
    return (
        jnp.concatenate([even[:, :h], odd[:, :h]], 1),
        jnp.concatenate([even[:, h:], odd[:, h:]], 1),
    )


def columns_inverse(re, im, tab):
    h = re.shape[1] // 2
    even = times_table(jnp.concatenate([re[:, :h], im[:, :h]], 1), tab, 1)
    odd = times_table(jnp.concatenate([re[:, h:], im[:, h:]], 1), tab, 3)
    total, gap = even + odd, even - odd
    return (
        jnp.concatenate([total[:, :h], gap[:, :h]], 1),
        jnp.concatenate([total[:, h:], gap[:, h:]], 1),
    )


def rows_forward(re, im, tab):
    h = re.shape[0] // 2
    r0, r1, i0, i1 = re[:h], re[h:], im[:h], im[h:]
    even = table_times(jnp.concatenate([r0 + r1, i0 + i1], 0), tab, 1)
    odd = table_times(jnp.concatenate([r0 - r1, i0 - i1], 0), tab, 3)
    return (
        jnp.concatenate([even[:h], odd[:h]], 0),
        jnp.concatenate([even[h:], odd[h:]], 0),
    )


def rows_inverse(re, im, tab):
    h = re.shape[0] // 2
    even = table_times(jnp.concatenate([re[:h], im[:h]], 0), tab, 0)
    odd = table_times(jnp.concatenate([re[h:], im[h:]], 0), tab, 2)
    total, gap = even + odd, even - odd
    return (
        jnp.concatenate([total[:h], gap[:h]], 0),
        jnp.concatenate([total[h:], gap[h:]], 0),
    )


def forward(waves, tab):
    waves = [columns_forward(*wave, tab) for wave in waves]
    return [rows_forward(*wave, tab) for wave in waves]


def inverse(waves, tab):
    waves = [rows_inverse(*wave, tab) for wave in waves]
    return [columns_inverse(*wave, tab) for wave in waves]


def times(a, b):
    return a[0] * b[0] - a[1] * b[1], a[0] * b[1] + a[1] * b[0]


def times_conj(a, b):
    return a[0] * b[0] + a[1] * b[1], a[0] * b[1] - a[1] * b[0]


def in_groups(states, body):
    group = 2 if states % 2 == 0 else 1
    if states == group:
        body([m for m in range(group)])
        return

    def step(g, carry):
        body([g * group + m for m in range(group)])
        return carry

    lax.fori_loop(0, states // group, step, 0)


def thirds(value):
    top = value.astype(BF16)
    left = value - top.astype(F32)
    mid = left.astype(BF16)
    return top, mid, (left - mid.astype(F32)).astype(BF16)


def by_parity(value):
    size = value.shape[0]
    h = size // 2
    picks = []
    for along in (0, 1):
        place = lax.broadcasted_iota(jnp.int32, (size, size), along)
        source = lax.broadcasted_iota(jnp.int32, (size, size), 1 - along)
        wanted = jnp.where(place < h, 2 * place, 2 * (place - h) + 1)
        picks.append(jnp.where(source == wanted, 1.0, 0.0).astype(BF16))
    top, mid, low = thirds(value)
    value = (dot(picks[0], top) + dot(picks[0], mid)) + dot(picks[0], low)
    top, mid, low = thirds(value)
    return (dot(top, picks[1]) + dot(mid, picks[1])) + dot(low, picks[1])


def prepare_body(prop_ref, amp_ref, wave_re, wave_im, amp_out):
    phase = by_parity(prop_ref[...])
    wave_re[...] = jnp.cos(phase)
    wave_im[...] = jnp.sin(phase)
    amp_out[...] = by_parity(amp_ref[0])


def turn_body(pos_ref, probe_ref, out_ref):
    size = probe_ref.shape[-1]
    row, col = pos_ref[0, 0], lax.rem(pos_ref[0, 1], size)
    for m in range(probe_ref.shape[0]):
        for c in range(2):
            out_ref[m, c] = pltpu.roll(pltpu.roll(probe_ref[m, c], row, 0), col, 1)


def wrapped(ref, s, part, col):
    size = ref.shape[-2]
    c = lax.broadcasted_iota(jnp.int32, (size, size), 1)
    return jnp.where(c < col, ref[s, part, :, size:], ref[s, part, :, :size])


def send_body(before_ref, object_ref, zero_ref, one_ref):
    for s, out in enumerate((zero_ref, one_ref)):
        for part in range(2):
            out[part] = wrapped(object_ref, s, part, before_ref[0, 1])


def patch_of(s, object_ref, halo_ref, pos_ref):
    size = halo_ref.shape[-1]
    r = lax.broadcasted_iota(jnp.int32, (size, size), 0)
    return [
        jnp.where(r < pos_ref[0, 0], halo_ref[part], wrapped(object_ref, s, part, pos_ref[0, 1]))
        for part in range(2)
    ]


def pair(ref, *at):
    return ref[(*at, 0)], ref[(*at, 1)]


def inner_body(pos_ref, object_ref, halo_ref, first_ref, rest_ref, kr_ref, ki_ref, tab, out_ref, patch, probes):
    states = out_ref.shape[0]
    patch[0], patch[1] = patch_of(0, object_ref, halo_ref, pos_ref)
    probes[:1] = first_ref[...]
    probes[1:] = rest_ref[...]

    def body(group):
        waves = forward([times(pair(probes, m), pair(patch)) for m in group], tab)
        waves = inverse([times((kr_ref[...], ki_ref[...]), wave) for wave in waves], tab)
        for m, wave in zip(group, waves):
            out_ref[m, 0], out_ref[m, 1] = wave

    in_groups(states, body)


def middle_body(rows, pos_ref, object_ref, halo_ref, inner_ref, amp_ref, tab, term_ref, chi_ref, patch, far, power):
    states = inner_ref.shape[0]
    patch[0], patch[1] = patch_of(1, object_ref, halo_ref, pos_ref)
    power[...] = jnp.zeros_like(power)

    def outward(group):
        waves = forward([times(pair(patch), pair(inner_ref, m)) for m in group], tab)
        total = power[...]
        for m, wave in zip(group, waves):
            far[m, 0], far[m, 1] = wave
            total += wave[0] * wave[0] + wave[1] * wave[1]
        power[...] = total

    in_groups(states, outward)
    power[...] = 1.0 - amp_ref[...] / jnp.sqrt(power[...] + 1.0)
    term_ref[...] = jnp.zeros_like(term_ref)
    take = pl.ds(pl.multiple_of(pos_ref[0, 2] * rows, rows), rows)

    def homeward(group):
        waves = inverse([(power[...] * far[m, 0], power[...] * far[m, 1]) for m in group], tab)
        for m, wave in zip(group, waves):
            far[m, 0], far[m, 1] = wave
            chi_ref[m, 0], chi_ref[m, 1] = times_conj(pair(patch), wave)
        for m in group:
            part = times_conj(
                (inner_ref[m, 0, take], inner_ref[m, 1, take]), (far[m, 0, take], far[m, 1, take])
            )
            term_ref[0] += part[0]
            term_ref[1] += part[1]

    in_groups(states, homeward)


def last_body(rows, pos_ref, chi_ref, first_ref, rest_ref, kr_ref, ki_ref, tab, term_ref, front, probes):
    states = chi_ref.shape[0]
    take = pl.ds(pl.multiple_of(pos_ref[0, 2] * rows, rows), rows)
    term_ref[...] = jnp.zeros_like(term_ref)
    probes[:1] = first_ref[:, :, take]
    probes[1:] = rest_ref[:, :, take]

    def body(group):
        waves = forward([pair(chi_ref, m) for m in group], tab)
        waves = [rows_inverse(*times_conj((kr_ref[...], ki_ref[...]), wave), tab) for wave in waves]
        for m, wave in zip(group, waves):
            front[m, 0], front[m, 1] = wave
        for m in group:
            wave = columns_inverse(front[m, 0, take], front[m, 1, take], tab)
            part = times_conj(pair(probes, m), wave)
            term_ref[0] += part[0]
            term_ref[1] += part[1]

    in_groups(states, body)


def gather_body(slice_id, rows, pos_ref, own_ref, came_ref, *refs):
    out_ref, held, sem = refs[-3:]
    size = own_ref.shape[-1]
    start = pos_ref[0, 2] * rows
    r = lax.broadcasted_iota(jnp.int32, (rows, size), 0) + start
    c = lax.broadcasted_iota(jnp.int32, (rows, size), 1)
    here, there = r >= pos_ref[0, 0], r < pos_ref[0, 3]
    here_right, there_right = c < pos_ref[0, 1], c < pos_ref[0, 4]
    copies = []
    for part in range(2):
        mine = jnp.where(here, own_ref[part], 0.0)
        theirs = jnp.where(there, came_ref[part], 0.0)
        held[part, :, :size] = jnp.where(here_right, 0.0, mine) + jnp.where(there_right, 0.0, theirs)
        held[part, :, size:] = jnp.where(here_right, mine, 0.0) + jnp.where(there_right, theirs, 0.0)
        copies.append(pltpu.make_async_copy(held.at[part], out_ref.at[slice_id, part], sem.at[part]))
        copies[-1].start()
    for copy in copies:
        copy.wait()


def gather(slice_id, rows, size, where, own, came, *given):
    return pl.pallas_call(
        functools.partial(gather_body, slice_id, rows),
        out_shape=jax.ShapeDtypeStruct((2, 2, rows, 2 * size), F32),
        in_specs=[SMEM, VMEM, VMEM] + [pl.BlockSpec(memory_space=pl.ANY)] * len(given),
        out_specs=pl.BlockSpec(memory_space=pl.ANY),
        scratch_shapes=[pltpu.VMEM((2, rows, 2 * size), F32), pltpu.SemaphoreType.DMA((2,))],
        input_output_aliases={3: 0} if given else {},
        compiler_params=pltpu.CompilerParams(vmem_limit_bytes=LIMIT),
        cost_estimate=pl.CostEstimate(flops=0, bytes_accessed=32 * rows * size, transcendentals=0),
    )(where, own, came, *given)


def on_device(object_slices, probe, amplitude, positions, propagator):
    states = lax.axis_size("state")
    size = amplitude.shape[1]
    rows = object_slices.shape[2] // states
    assert object_slices.shape[2:] == (size, 2 * size) and positions.shape[0] == 1
    return gradient_of(object_slices, probe, amplitude, positions, propagator, states, size, rows)


def gradient_of(object_slices, probe, amplitude, positions, propagator, states, size, rows):
    grid = (size, size)
    unit = size * size
    flops = 24 * size**3
    tab = tables(size)
    before = shifted(positions, "frame", 1)
    others = [shifted(probe, "state", by) for by in range(1, states)]
    kr, ki, amp = call(prepare_body, [grid] * 3, [VMEM] * 2, flops=2 * size**3, moved=20 * unit)(propagator, amplitude)
    (first,) = call(turn_body, [probe.shape], [SMEM, VMEM], moved=16 * unit)(positions, probe)
    before, kr, ki, amp, first = lax.optimization_barrier((before, kr, ki, amp, first))
    index = lax.axis_index("state").astype(jnp.int32)
    where = jnp.concatenate([positions, index[None, None], before], 1)

    picked = call(send_body, [(2,) + grid] * 2, [SMEM, VMEM], moved=16 * unit)(before, object_slices)
    halo_zero = shifted(picked[0], "frame", -1)
    halo_one = shifted(picked[1], "frame", -1)
    rest = others[0] if states == 2 else jnp.concatenate(others, 0)
    (rest,) = call(turn_body, [rest.shape], [SMEM, VMEM], moved=16 * unit * (states - 1))(positions, rest)

    (waves,) = call(
        inner_body,
        [(states, 2) + grid],
        [SMEM] + [VMEM] * 7,
        [pltpu.VMEM((2,) + grid, F32), pltpu.VMEM((states, 2) + grid, F32)],
        flops=2 * flops * states,
        moved=16 * unit * states,
    )(where, object_slices, halo_zero, first, rest, kr, ki, tab)
    term_one, chi = call(
        functools.partial(middle_body, rows),
        [(2, rows, size), (states, 2) + grid],
        [SMEM] + [VMEM] * 5,
        [pltpu.VMEM((2,) + grid, F32), pltpu.VMEM((states, 2) + grid, F32), pltpu.VMEM(grid, F32)],
        flops=2 * flops * states,
        moved=32 * unit * states,
    )(where, object_slices, halo_one, waves, amp, tab)
    came_one = shifted(term_one, "frame", 1)
    (term_zero,) = call(
        functools.partial(last_body, rows),
        [(2, rows, size)],
        [SMEM] + [VMEM] * 6,
        [pltpu.VMEM((states, 2) + grid, F32), pltpu.VMEM((states, 2, rows, size), F32)],
        flops=2 * flops * states,
        moved=16 * unit * states,
    )(where, chi, first, rest, kr, ki, tab)
    came_zero = shifted(term_zero, "frame", 1)
    gradient = gather(1, rows, size, where, term_one, came_one)
    return gather(0, rows, size, where, term_zero, came_zero, gradient)


def solution(mesh):
    return jax.shard_map(
        on_device,
        mesh=mesh,
        in_specs=(
            P(None, None, "frame", None),
            P("state", None, None, None),
            P("frame", None, None),
            P("frame", None),
            P(),
        ),
        out_specs=P(None, None, ("frame", "state"), None),
        check_vma=False,
    )
```

time: 43.4 us -> 46.7 us (1.076)
  local copies, waits for them, and re-layouts: 2.34 us -> 8.21 us
  waiting for transfers between devices: 15.9 us -> 13.3 us
  other arithmetic: 2.43 us -> 0.07 us
  starting transfers between devices: 5.74 us -> 7.76 us
    unnamed x10 -> x28, local copies, waits for them, and re-layouts: 0.03 us -> 8.21 us
    ppermute x6, waiting for transfers between devices: 15.9 us -> 13.3 us  [shifted(): lax.ppermute(value, axis, [(i, (i + by) % count) for i in range(count)])]
    slice x2 -> x0, local copies, waits for them, and re-layouts: 2.31 us -> none  [the longest x1 1.73 us: inner(): object_slices[0:1]]
    ppermute x6, starting transfers between devices: 5.74 us -> 7.76 us  [shifted(): lax.ppermute(value, axis, [(i, (i + by) % count) for i in range(count)])]
    select_n x1 -> x0, other arithmetic: 1.71 us -> none  [on_device(): jnp.where(column < before[0, 1], object_slices[s, :, :, size:], object_sl...]
    lt x1 -> x0, other arithmetic: 0.65 us -> none  [on_device(): column < before[0, 1]]
    pallas_call x8 -> x9, Pallas kernels: 16.6 us -> 16.8 us  [the longest x1 3.48 us: gradient_of(): call(functools.partial(middle_body, rows), [(2, rows, size), (states, 2)...]
  transfers between devices with their start and end apart: 6 -> 6, of which waited for: 4 -> 4; matrix products, arithmetic and copies ran while one was open for 11% -> 0% of each run, Pallas kernels for 17% -> 26%
where the time goes in v1:
time: 46.7 us; the launch traced here: 46.2 us
  Pallas kernels  16.8 us (36%)
  waiting for transfers between devices  13.3 us (28%)
  local copies, waits for them, and re-layouts  8.21 us (18%)
  starting transfers between devices  7.76 us (17%)
    ppermute x6, waiting for transfers between devices, shifted(): lax.ppermute(value, axis, [(i, (i + by) % count) for i in range(count)])  13.3 us
    unnamed x28, local copies, waits for them, and re-layouts  8.21 us
    ppermute x6, starting transfers between devices, shifted(): lax.ppermute(value, axis, [(i, (i + by) % count) for i in range(count)])  7.76 us
    pallas_call x1, Pallas kernels, gradient_of(): call(functools.partial(middle_body, rows), [(2, rows, size), (states, 2)...  3.48 us
    pallas_call x2, Pallas kernels, gather(): pl.pallas_call(functools.partial(gather_body, slice_id, rows), out_shape=...  2.79 us
    pallas_call x1, Pallas kernels, gradient_of(): call(inner_body, [(states, 2) + grid], [SMEM] + [VMEM] * 7, [pltpu.VMEM((...  2.74 us
    pallas_call x1, Pallas kernels, gradient_of(): call(functools.partial(last_body, rows), [(2, rows, size)], [SMEM] + [VME...  2.48 us
    pallas_call x1, Pallas kernels, gradient_of(): call(prepare_body, [grid] * 3, [VMEM] * 2, flops=2 * size ** 3, moved=20...  1.63 us
  transfers between devices with their start and end apart: 6, of which 4 were waited for; matrix products, arithmetic and copies ran while one was open for 0% of the time, Pallas kernels for 26%

profile of v1, /device:TPU:0, one launch (start us, length us, event | category | flops | bytes accessed | tf_op | source)
XLA Modules:
  0.0 46.2 jit_solution(14852798602866445891)
XLA Ops:
  0.0 0.5 %collective-permute-start = (s32[1,2]{1,0:T(1,128)}, s32[1,2]{1,0:T(1,128)S(1)}, u32[]{:S(2)}, u32[]{:S(2)}) collective-permute-start(s32[1,2]{1,0:T(1,128)} %pos_ref.3), channel_id=1, source_target_pairs={{0,2},{2,4},{4,6},{6,8},{8,10},{10,12},{12,14},{14,16},{16,18},{18... | collective-permute-start | bytes 32 | tf_op jit(solution)/shard_map/ppermute | solution.py:22
  0.5 2.5 %collective-permute-start.3 = (f32[1,2,256,256]{3,2,1,0:T(8,128)}, f32[1,2,256,256]{3,2,1,0:T(8,128)}, u32[]{:S(2)}, u32[]{:S(2)}) collective-permute-start(f32[1,2,256,256]{3,2,1,0:T(8,128)} %probe_ref.1), channel_id=1, source_target_pairs={{0,1},{1,0},{2,3},{3,2},{4,5},{5,4},{6,7},{7,6},{8,9},{9,8},{10,11... | collective-permute-start | bytes 1572872 | tf_op jit(solution)/shard_map/ppermute | solution.py:22
  3.0 1.1 %copy-done.4 = f32[1,2,256,256]{3,2,1,0:T(8,128)S(1)} copy-done((f32[1,2,256,256]{3,2,1,0:T(8,128)S(1)}, f32[1,2,256,256]{3,2,1,0:T(8,128)}, u32[]{:S(2)}) %copy-start.4) | copy-done | bytes 524312
  4.0 0.7 %copy-done.10 = s32[1,2]{1,0:T(1,128)S(1)} copy-done((s32[1,2]{1,0:T(1,128)S(1)}, s32[1,2]{1,0:T(1,128)}, u32[]{:S(2)}) %copy-start.10) | copy-done | bytes 32
  4.7 0.8 %shard_map.65.first_ref = f32[1,2,256,256]{3,2,1,0:T(8,128)S(1)} custom-call(s32[1,2]{1,0:T(1,128)S(1)} %copy-done.10, f32[1,2,256,256]{3,2,1,0:T(8,128)S(1)} %copy-done.4), custom_call_target="tpu_custom_call" | custom-call | bytes 1048576 | tf_op jit(solution)/shard_map/pallas_call | solution.py:327
  5.5 0.0 copy-start.8
  5.5 0.9 %copy-done.8 = f32[256,256]{1,0:T(8,128)S(1)} copy-done((f32[256,256]{1,0:T(8,128)S(1)}, f32[256,256]{1,0:T(8,128)}, u32[]{:S(2)}) %copy-start.8) | copy-done | bytes 262168
  6.4 0.9 %copy-done.9 = f32[1,256,256]{2,1,0:T(8,128)S(1)} copy-done((f32[1,256,256]{2,1,0:T(8,128)S(1)}, f32[1,256,256]{2,1,0:T(8,128)}, u32[]{:S(2)}) %copy-start.9) | copy-done | bytes 262168
  7.4 1.6 %shard_map.64 = (f32[256,256]{1,0:T(8,128)S(1)}, f32[256,256]{1,0:T(8,128)S(1)}, f32[256,256]{1,0:T(8,128)S(1)}) custom-call(f32[256,256]{1,0:T(8,128)S(1)} %copy-done.8, f32[1,256,256]{2,1,0:T(8,128)S(1)} %copy-done.9), custom_call_target="tpu_custom_call" | custom-call | flops 33554432 | bytes 1310720 | tf_op jit(solution)/shard_map/pallas_call | solution.py:326
  9.0 0.7 %copy-done.5 = f32[256,256]{1,0:T(8,128)} copy-done((f32[256,256]{1,0:T(8,128)}, f32[256,256]{1,0:T(8,128)S(1)}, u32[]{:S(2)}) %copy-start.5) | copy-done | bytes 262168
  9.7 0.0 collective-permute-done.before_ref
  9.7 1.7 %copy-done = f32[2,2,256,512]{3,2,1,0:T(8,128)S(1)} copy-done((f32[2,2,256,512]{3,2,1,0:T(8,128)S(1)}, f32[2,2,256,512]{3,2,1,0:T(8,128)}, u32[]{:S(2)}) %copy-start) | copy-done | bytes 2097176
  11.4 1.6 %shard_map.66 = (f32[2,256,256]{2,1,0:T(8,128)}, f32[2,256,256]{2,1,0:T(8,128)}) custom-call(s32[1,2]{1,0:T(1,128)S(1)} %collective-permute-done.before_ref, f32[2,2,256,512]{3,2,1,0:T(8,128)S(1)} %copy-done), custom_call_target="tpu_custom_call" | custom-call | bytes 1048576 | tf_op jit(solution)/shard_map/pallas_call | solution.py:332
  13.0 4.2 %collective-permute-start.2 = (f32[2,256,256]{2,1,0:T(8,128)}, f32[2,256,256]{2,1,0:T(8,128)S(1)}, u32[]{:S(2)}, u32[]{:S(2)}) collective-permute-start(f32[2,256,256]{2,1,0:T(8,128)} %get-tuple-element.22), channel_id=1, source_target_pairs={{0,30},{2,0},{4,2},{6,4},{8,6},{10,8},{12,10},{14,12},{16,14},{18,... | collective-permute-start | bytes 1572872 | tf_op jit(solution)/shard_map/ppermute | solution.py:22
  17.2 0.5 %collective-permute-start.1 = (f32[2,256,256]{2,1,0:T(8,128)}, f32[2,256,256]{2,1,0:T(8,128)}, u32[]{:S(2)}, u32[]{:S(2)}) collective-permute-start(f32[2,256,256]{2,1,0:T(8,128)} %get-tuple-element.21), channel_id=1, source_target_pairs={{0,30},{2,0},{4,2},{6,4},{8,6},{10,8},{12,10},{14,12},{16,14},{18,... | collective-permute-start | bytes 1572872 | tf_op jit(solution)/shard_map/ppermute | solution.py:22
  17.7 0.1 pad_add_fusion.pos_ref
  17.8 0.0 collective-permute-done.3.probe_ref
  17.8 1.3 %shard_map.67.rest_ref = f32[1,2,256,256]{3,2,1,0:T(8,128)S(1)} custom-call(s32[1,2]{1,0:T(1,128)S(1)} %copy-done.11, f32[1,2,256,256]{3,2,1,0:T(8,128)} %collective-permute-done.3.probe_ref), custom_call_target="tpu_custom_call" | custom-call | bytes 1048576 | tf_op jit(solution)/shard_map/pallas_call | solution.py:336
  19.1 5.1 %collective-permute-done.2.halo_ref = f32[2,256,256]{2,1,0:T(8,128)S(1)} collective-permute-done((f32[2,256,256]{2,1,0:T(8,128)}, f32[2,256,256]{2,1,0:T(8,128)S(1)}, u32[]{:S(2)}, u32[]{:S(2)}) %collective-permute-start.2) | collective-permute-done | bytes 524320 | tf_op jit(solution)/shard_map/ppermute | solution.py:22
  24.2 1.2 %copy-done.2 = bf16[2,4,256,256]{3,2,1,0:T(8,128)(2,1)S(1)} copy-done((bf16[2,4,256,256]{3,2,1,0:T(8,128)(2,1)S(1)}, bf16[2,4,256,256]{3,2,1,0:T(8,128)(2,1)}, u32[]{:S(2)}) %copy-start.2) | copy-done | bytes 1048600
  25.4 0.9 %copy-done.6 = f32[256,256]{1,0:T(8,128)S(1)} copy-done((f32[256,256]{1,0:T(8,128)S(1)}, f32[256,256]{1,0:T(8,128)}, u32[]{:S(2)}) %copy-start.6) | copy-done | bytes 262168
  26.4 2.7 %shard_map.68.inner_ref = f32[2,2,256,256]{3,2,1,0:T(8,128)S(1)} custom-call(s32[1,5]{1,0:T(1,128)S(1)} %pad_add_fusion.pos_ref, f32[2,2,256,512]{3,2,1,0:T(8,128)S(1)} %copy-done.1, f32[2,256,256]{2,1,0:T(8,128)S(1)} %collective-permute-done.2.halo_ref, f32[1,2,256,256]{3,2,1,0:T(8,128)S(1)} %shard_map.65.first_ref, ...), custom_call_target="tpu_custom_call" | custom-call | flops 1610612736 | bytes 2097152 | tf_op jit(solution)/shard_map/pallas_call | solution.py:338
  29.2 0.7 %collective-permute-done.1.halo_ref = f32[2,256,256]{2,1,0:T(8,128)} collective-permute-done((f32[2,256,256]{2,1,0:T(8,128)}, f32[2,256,256]{2,1,0:T(8,128)}, u32[]{:S(2)}, u32[]{:S(2)}) %collective-permute-start.1) | collective-permute-done | bytes 524320 | tf_op jit(solution)/shard_map/ppermute | solution.py:22
  29.8 0.0 copy-done.13
  29.8 3.5 %shard_map.69 = (f32[2,128,256]{2,1,0:T(8,128)S(1)}, f32[2,2,256,256]{3,2,1,0:T(8,128)S(1)}) custom-call(s32[1,5]{1,0:T(1,128)S(1)} %pad_add_fusion.pos_ref, f32[2,2,256,512]{3,2,1,0:T(8,128)S(1)} %copy-done.1, f32[2,256,256]{2,1,0:T(8,128)} %collective-permute-done.1.halo_ref, f32[2,2,256,256]{3,2,1,0:T(8,128)S(1)} %shard_map.68.inner_ref, ...), custom_call_target="tpu_custom_call" | custom-call | flops 1610612736 | bytes 4194304 | tf_op jit(solution)/shard_map/pallas_call | solution.py:346
  33.3 0.1 collective-permute-start.5
  33.4 2.5 %shard_map.70.own_ref = f32[2,128,256]{2,1,0:T(8,128)S(1)} custom-call(s32[1,5]{1,0:T(1,128)S(1)} %pad_add_fusion.pos_ref, f32[2,2,256,256]{3,2,1,0:T(8,128)S(1)} %get-tuple-element.27.chi_ref, f32[1,2,256,256]{3,2,1,0:T(8,128)S(1)} %shard_map.65.first_ref, f32[1,2,256,256]{3,2,1,0:T(8,128)S(1)} %shard_map.67.rest_ref, ...), custom_call_target="tpu_custom_call" | custom-call | flops 1610612736 | bytes 2097152 | tf_op jit(solution)/shard_map/pallas_call | solution.py:355
  35.9 0.1 collective-permute-start.4
  36.0 6.1 %collective-permute-done.5.came_ref = f32[2,128,256]{2,1,0:T(8,128)S(1)} collective-permute-done((f32[2,128,256]{2,1,0:T(8,128)S(1)}, f32[2,128,256]{2,1,0:T(8,128)S(1)}, u32[]{:S(2)}, u32[]{:S(2)}) %collective-permute-start.5) | collective-permute-done | bytes 262176 | tf_op jit(solution)/shard_map/ppermute | solution.py:22
  42.0 1.4 %shard_map.71.refs_0_ = f32[2,2,128,512]{3,2,1,0:T(8,128)} custom-call(s32[1,5]{1,0:T(1,128)S(1)} %pad_add_fusion.pos_ref, f32[2,128,256]{2,1,0:T(8,128)S(1)} %get-tuple-element.28.own_ref, f32[2,128,256]{2,1,0:T(8,128)S(1)} %collective-permute-done.5.came_ref), custom_call_target="tpu_custom_call" | custom-call | bytes 1048576 | tf_op jit(solution)/shard_map/pallas_call | solution.py:299
  43.4 1.4 %collective-permute-done.4.came_ref = f32[2,128,256]{2,1,0:T(8,128)S(1)} collective-permute-done((f32[2,128,256]{2,1,0:T(8,128)S(1)}, f32[2,128,256]{2,1,0:T(8,128)S(1)}, u32[]{:S(2)}, u32[]{:S(2)}) %collective-permute-start.4) | collective-permute-done | bytes 262176 | tf_op jit(solution)/shard_map/ppermute | solution.py:22
  44.8 1.4 %shard_map.72 = f32[2,2,128,512]{3,2,1,0:T(8,128)} custom-call(s32[1,5]{1,0:T(1,128)S(1)} %pad_add_fusion.pos_ref, f32[2,128,256]{2,1,0:T(8,128)S(1)} %shard_map.70.own_ref, f32[2,128,256]{2,1,0:T(8,128)S(1)} %collective-permute-done.4.came_ref, f32[2,2,128,512]{3,2,1,0:T(8,128)} %shard_map.71.refs_0_), custom_call_target="tpu_custom_call", output_to_operand_aliasing={{}: (3, {})} | custom-call | bytes 1048576 | tf_op jit(solution)/shard_map/pallas_call | solution.py:299
  (18 shorter events, 0.0 us)
Async XLA Ops:
  0.0 9.7 %collective-permute-start = (s32[1,2]{1,0:T(1,128)}, s32[1,2]{1,0:T(1,128)S(1)}, u32[]{:S(2)}, u32[]{:S(2)}) collective-permute-start(s32[1,2]{1,0:T(1,128)} %pos_ref.3), channel_id=1, source_target_pairs={{0,2},{2,4},{4,6},{6,8},{8,10},{10,12},{12,14},{14,16},{16,18},{18... | collective-permute-start | bytes 32 | tf_op jit(solution)/shard_map/ppermute | solution.py:22
  0.5 17.3 %collective-permute-start.3 = (f32[1,2,256,256]{3,2,1,0:T(8,128)}, f32[1,2,256,256]{3,2,1,0:T(8,128)}, u32[]{:S(2)}, u32[]{:S(2)}) collective-permute-start(f32[1,2,256,256]{3,2,1,0:T(8,128)} %probe_ref.1), channel_id=1, source_target_pairs={{0,1},{1,0},{2,3},{3,2},{4,5},{5,4},{6,7},{7,6},{8,9},{9,8},{10,11... | collective-permute-start | bytes 1572872 | tf_op jit(solution)/shard_map/ppermute | solution.py:22
  3.0 1.1 %copy-start.4 = (f32[1,2,256,256]{3,2,1,0:T(8,128)S(1)}, f32[1,2,256,256]{3,2,1,0:T(8,128)}, u32[]{:S(2)}) copy-start(f32[1,2,256,256]{3,2,1,0:T(8,128)} %probe_ref.1) | copy-start | bytes 1572868
  4.0 0.7 %copy-start.10 = (s32[1,2]{1,0:T(1,128)S(1)}, s32[1,2]{1,0:T(1,128)}, u32[]{:S(2)}) copy-start(s32[1,2]{1,0:T(1,128)} %pos_ref.3) | copy-start | bytes 28
  4.7 13.0 %copy-start.11 = (s32[1,2]{1,0:T(1,128)S(1)}, s32[1,2]{1,0:T(1,128)}, u32[]{:S(2)}) copy-start(s32[1,2]{1,0:T(1,128)} %pos_ref.3) | copy-start | bytes 28
  5.5 1.0 %copy-start.8 = (f32[256,256]{1,0:T(8,128)S(1)}, f32[256,256]{1,0:T(8,128)}, u32[]{:S(2)}) copy-start(f32[256,256]{1,0:T(8,128)} %prop_ref.1) | copy-start | bytes 786436
  6.4 0.9 %copy-start.9 = (f32[1,256,256]{2,1,0:T(8,128)S(1)}, f32[1,256,256]{2,1,0:T(8,128)}, u32[]{:S(2)}) copy-start(f32[1,256,256]{2,1,0:T(8,128)} %amp_ref.1) | copy-start | bytes 786436
  9.0 0.7 %copy-start.5 = (f32[256,256]{1,0:T(8,128)}, f32[256,256]{1,0:T(8,128)S(1)}, u32[]{:S(2)}) copy-start(f32[256,256]{1,0:T(8,128)S(1)} %get-tuple-element.25.ki_ref) | copy-start | bytes 786436
  9.7 3.3 %copy-start.12 = (f32[256,256]{1,0:T(8,128)}, f32[256,256]{1,0:T(8,128)S(1)}, u32[]{:S(2)}) copy-start(f32[256,256]{1,0:T(8,128)S(1)} %get-tuple-element.26.amp_ref) | copy-start | bytes 786436
  9.7 1.7 %copy-start = (f32[2,2,256,512]{3,2,1,0:T(8,128)S(1)}, f32[2,2,256,512]{3,2,1,0:T(8,128)}, u32[]{:S(2)}) copy-start(f32[2,2,256,512]{3,2,1,0:T(8,128)} %object_ref.5) | copy-start | bytes 6291460
  11.4 12.8 %copy-start.1 = (f32[2,2,256,512]{3,2,1,0:T(8,128)S(1)}, f32[2,2,256,512]{3,2,1,0:T(8,128)}, u32[]{:S(2)}) copy-start(f32[2,2,256,512]{3,2,1,0:T(8,128)} %object_ref.5) | copy-start | bytes 6291460
  13.0 11.2 %collective-permute-start.2 = (f32[2,256,256]{2,1,0:T(8,128)}, f32[2,256,256]{2,1,0:T(8,128)S(1)}, u32[]{:S(2)}, u32[]{:S(2)}) collective-permute-start(f32[2,256,256]{2,1,0:T(8,128)} %get-tuple-element.22), channel_id=1, source_target_pairs={{0,30},{2,0},{4,2},{6,4},{8,6},{10,8},{12,10},{14,12},{16,14},{18,... | collective-permute-start | bytes 1572872 | tf_op jit(solution)/shard_map/ppermute | solution.py:22
  17.2 12.6 %collective-permute-start.1 = (f32[2,256,256]{2,1,0:T(8,128)}, f32[2,256,256]{2,1,0:T(8,128)}, u32[]{:S(2)}, u32[]{:S(2)}) collective-permute-start(f32[2,256,256]{2,1,0:T(8,128)} %get-tuple-element.21), channel_id=1, source_target_pairs={{0,30},{2,0},{4,2},{6,4},{8,6},{10,8},{12,10},{14,12},{16,14},{18,... | collective-permute-start | bytes 1572872 | tf_op jit(solution)/shard_map/ppermute | solution.py:22
  24.2 1.2 %copy-start.2 = (bf16[2,4,256,256]{3,2,1,0:T(8,128)(2,1)S(1)}, bf16[2,4,256,256]{3,2,1,0:T(8,128)(2,1)}, u32[]{:S(2)}) copy-start(bf16[2,4,256,256]{3,2,1,0:T(8,128)(2,1)} %constant.6.clone.tab) | copy-start | bytes 3145732
  25.4 0.9 %copy-start.6 = (f32[256,256]{1,0:T(8,128)S(1)}, f32[256,256]{1,0:T(8,128)}, u32[]{:S(2)}) copy-start(f32[256,256]{1,0:T(8,128)} %copy-done.5) | copy-start | bytes 786436
  26.4 3.4 %copy-start.3 = (bf16[2,4,256,256]{3,2,1,0:T(8,128)(2,1)S(1)}, bf16[2,4,256,256]{3,2,1,0:T(8,128)(2,1)}, u32[]{:S(2)}) copy-start(bf16[2,4,256,256]{3,2,1,0:T(8,128)(2,1)} %constant.6.clone.tab) | copy-start | bytes 3145732
  26.4 3.4 %copy-start.13 = (f32[256,256]{1,0:T(8,128)S(1)}, f32[256,256]{1,0:T(8,128)}, u32[]{:S(2)}) copy-start(f32[256,256]{1,0:T(8,128)} %copy-done.12) | copy-start | bytes 786436
  29.1 4.3 %copy-start.7 = (f32[256,256]{1,0:T(8,128)S(1)}, f32[256,256]{1,0:T(8,128)}, u32[]{:S(2)}) copy-start(f32[256,256]{1,0:T(8,128)} %copy-done.5) | copy-start | bytes 786436
  33.3 8.7 %collective-permute-start.5 = (f32[2,128,256]{2,1,0:T(8,128)S(1)}, f32[2,128,256]{2,1,0:T(8,128)S(1)}, u32[]{:S(2)}, u32[]{:S(2)}) collective-permute-start(f32[2,128,256]{2,1,0:T(8,128)S(1)} %get-tuple-element.28.own_ref), channel_id=1, source_target_pairs={{0,2},{2,4},{4,6},{6,8},{8,10},{10,12},{12,14},{14,16},{16,18},{18... | collective-permute-start | bytes 786440 | tf_op jit(solution)/shard_map/ppermute | solution.py:22
  35.9 9.0 %collective-permute-start.4 = (f32[2,128,256]{2,1,0:T(8,128)S(1)}, f32[2,128,256]{2,1,0:T(8,128)S(1)}, u32[]{:S(2)}, u32[]{:S(2)}) collective-permute-start(f32[2,128,256]{2,1,0:T(8,128)S(1)} %shard_map.70.own_ref), channel_id=1, source_target_pairs={{0,2},{2,4},{4,6},{6,8},{8,10},{10,12},{12,14},{14,16},{16,18},{18... | collective-permute-start | bytes 786440 | tf_op jit(solution)/shard_map/ppermute | solution.py:22

commit v2 on v1

--- a/solution.py
+++ b/solution.py
@@ -13,6 +13,7 @@
 F32 = jnp.float32
 BF16 = jnp.bfloat16
 VMEM = pl.BlockSpec(memory_space=pltpu.VMEM)
+HBM = pl.BlockSpec(memory_space=pltpu.MemorySpace.HBM)
 SMEM = pl.BlockSpec(memory_space=pltpu.SMEM)
 LIMIT = 24 * 1024 * 1024
 
@@ -20,6 +21,10 @@
 def shifted(value, axis, by):
     count = lax.axis_size(axis)
     return lax.ppermute(value, axis, [(i, (i + by) % count) for i in range(count)])
+
+
+def in_hbm(value):
+    return pltpu.with_memory_space_constraint(value, pltpu.MemorySpace.HBM)
 
 
 def call(body, outs, ins, scratch=(), flops=0, moved=0):
@@ -166,38 +171,68 @@
     return (dot(top, picks[1]) + dot(mid, picks[1])) + dot(low, picks[1])
 
 
-def prepare_body(prop_ref, amp_ref, wave_re, wave_im, amp_out):
-    phase = by_parity(prop_ref[...])
+def turned(value, row, col):
+    return pltpu.roll(pltpu.roll(value, row, 0), col, 1)
+
+
+def prepare_body(
+    pos_hbm, probe_hbm, prop_hbm, amp_hbm, object_hbm, tab_hbm,
+    wave_re, wave_im, amp_out, first_out, object_out, tab_out, pos_out,
+    pos, probe, prop, amp, sem,
+):
+    moves = (
+        (pos_hbm, pos), (probe_hbm, probe), (prop_hbm, prop), (amp_hbm, amp),
+        (pos_hbm, pos_out), (object_hbm, object_out), (tab_hbm, tab_out),
+    )
+    copies = [pltpu.make_async_copy(src, dst, sem.at[i]) for i, (src, dst) in enumerate(moves)]
+    for copy in copies:
+        copy.start()
+    copies[0].wait()
+    copies[1].wait()
+    size = prop.shape[0]
+    row, col = pos[0, 0], lax.rem(pos[0, 1], size)
+    for c in range(2):
+        first_out[0, c] = turned(probe[0, c], row, col)
+    copies[2].wait()
+    phase = by_parity(prop[...])
     wave_re[...] = jnp.cos(phase)
     wave_im[...] = jnp.sin(phase)
-    amp_out[...] = by_parity(amp_ref[0])
-
-
-def turn_body(pos_ref, probe_ref, out_ref):
+    copies[3].wait()
+    amp_out[...] = by_parity(amp[0])
+    for copy in copies[4:]:
+        copy.wait()
+
+
+def turn_body(pos_ref, first_ref, probe_ref, out_ref):
     size = probe_ref.shape[-1]
     row, col = pos_ref[0, 0], lax.rem(pos_ref[0, 1], size)
+    out_ref[:1] = first_ref[...]
     for m in range(probe_ref.shape[0]):
         for c in range(2):
-            out_ref[m, c] = pltpu.roll(pltpu.roll(probe_ref[m, c], row, 0), col, 1)
-
-
-def wrapped(ref, s, part, col):
+            out_ref[1 + m, c] = turned(probe_ref[m, c], row, col)
+
+
+def spread(ref, which, shape):
+    return jnp.broadcast_to(ref[0:1, which : which + 1], shape)
+
+
+def wrapped(ref, s, part, col_ref):
     size = ref.shape[-2]
     c = lax.broadcasted_iota(jnp.int32, (size, size), 1)
-    return jnp.where(c < col, ref[s, part, :, size:], ref[s, part, :, :size])
+    return jnp.where(c < spread(col_ref, 1, c.shape), ref[s, part, :, size:], ref[s, part, :, :size])
 
 
 def send_body(before_ref, object_ref, zero_ref, one_ref):
     for s, out in enumerate((zero_ref, one_ref)):
         for part in range(2):
-            out[part] = wrapped(object_ref, s, part, before_ref[0, 1])
+            out[part] = wrapped(object_ref, s, part, before_ref)
 
 
 def patch_of(s, object_ref, halo_ref, pos_ref):
     size = halo_ref.shape[-1]
     r = lax.broadcasted_iota(jnp.int32, (size, size), 0)
     return [
-        jnp.where(r < pos_ref[0, 0], halo_ref[part], wrapped(object_ref, s, part, pos_ref[0, 1]))
+        jnp.where(r < spread(pos_ref, 0, r.shape), halo_ref[part], wrapped(object_ref, s, part, pos_ref))
         for part in range(2)
     ]
 
@@ -206,14 +241,12 @@
     return ref[(*at, 0)], ref[(*at, 1)]
 
 
-def inner_body(pos_ref, object_ref, halo_ref, first_ref, rest_ref, kr_ref, ki_ref, tab, out_ref, patch, probes):
+def inner_body(pos_ref, object_ref, halo_ref, probe_ref, kr_ref, ki_ref, tab, out_ref, patch):
     states = out_ref.shape[0]
     patch[0], patch[1] = patch_of(0, object_ref, halo_ref, pos_ref)
-    probes[:1] = first_ref[...]
-    probes[1:] = rest_ref[...]
 
     def body(group):
-        waves = forward([times(pair(probes, m), pair(patch)) for m in group], tab)
+        waves = forward([times(pair(probe_ref, m), pair(patch)) for m in group], tab)
         waves = inverse([times((kr_ref[...], ki_ref[...]), wave) for wave in waves], tab)
         for m, wave in zip(group, waves):
             out_ref[m, 0], out_ref[m, 1] = wave
@@ -237,7 +270,7 @@
     in_groups(states, outward)
     power[...] = 1.0 - amp_ref[...] / jnp.sqrt(power[...] + 1.0)
     term_ref[...] = jnp.zeros_like(term_ref)
-    take = pl.ds(pl.multiple_of(pos_ref[0, 2] * rows, rows), rows)
+    take = pl.ds(pl.multiple_of(lax.axis_index("state") * rows, rows), rows)
 
     def homeward(group):
         waves = inverse([(power[...] * far[m, 0], power[...] * far[m, 1]) for m in group], tab)
@@ -254,12 +287,10 @@
     in_groups(states, homeward)
 
 
-def last_body(rows, pos_ref, chi_ref, first_ref, rest_ref, kr_ref, ki_ref, tab, term_ref, front, probes):
+def last_body(rows, chi_ref, probe_ref, kr_ref, ki_ref, tab, term_ref, front):
     states = chi_ref.shape[0]
-    take = pl.ds(pl.multiple_of(pos_ref[0, 2] * rows, rows), rows)
+    take = pl.ds(pl.multiple_of(lax.axis_index("state") * rows, rows), rows)
     term_ref[...] = jnp.zeros_like(term_ref)
-    probes[:1] = first_ref[:, :, take]
-    probes[1:] = rest_ref[:, :, take]
 
     def body(group):
         waves = forward([pair(chi_ref, m) for m in group], tab)
@@ -268,21 +299,21 @@
             front[m, 0], front[m, 1] = wave
         for m in group:
             wave = columns_inverse(front[m, 0, take], front[m, 1, take], tab)
-            part = times_conj(pair(probes, m), wave)
+            part = times_conj((probe_ref[m, 0, take], probe_ref[m, 1, take]), wave)
             term_ref[0] += part[0]
             term_ref[1] += part[1]
 
     in_groups(states, body)
 
 
-def gather_body(slice_id, rows, pos_ref, own_ref, came_ref, *refs):
+def gather_body(slice_id, rows, pos_ref, before_ref, own_ref, came_ref, *refs):
     out_ref, held, sem = refs[-3:]
     size = own_ref.shape[-1]
-    start = pos_ref[0, 2] * rows
+    start = lax.axis_index("state") * rows
     r = lax.broadcasted_iota(jnp.int32, (rows, size), 0) + start
     c = lax.broadcasted_iota(jnp.int32, (rows, size), 1)
-    here, there = r >= pos_ref[0, 0], r < pos_ref[0, 3]
-    here_right, there_right = c < pos_ref[0, 1], c < pos_ref[0, 4]
+    here, there = r >= spread(pos_ref, 0, r.shape), r < spread(before_ref, 0, r.shape)
+    here_right, there_right = c < spread(pos_ref, 1, c.shape), c < spread(before_ref, 1, c.shape)
     copies = []
     for part in range(2):
         mine = jnp.where(here, own_ref[part], 0.0)
@@ -295,17 +326,17 @@
         copy.wait()
 
 
-def gather(slice_id, rows, size, where, own, came, *given):
+def gather(slice_id, rows, size, pos, before, own, came, *given):
     return pl.pallas_call(
         functools.partial(gather_body, slice_id, rows),
         out_shape=jax.ShapeDtypeStruct((2, 2, rows, 2 * size), F32),
-        in_specs=[SMEM, VMEM, VMEM] + [pl.BlockSpec(memory_space=pl.ANY)] * len(given),
+        in_specs=[VMEM] * 4 + [pl.BlockSpec(memory_space=pl.ANY)] * len(given),
         out_specs=pl.BlockSpec(memory_space=pl.ANY),
         scratch_shapes=[pltpu.VMEM((2, rows, 2 * size), F32), pltpu.SemaphoreType.DMA((2,))],
-        input_output_aliases={3: 0} if given else {},
+        input_output_aliases={4: 0} if given else {},
         compiler_params=pltpu.CompilerParams(vmem_limit_bytes=LIMIT),
         cost_estimate=pl.CostEstimate(flops=0, bytes_accessed=32 * rows * size, transcendentals=0),
-    )(where, own, came, *given)
+    )(pos, before, own, came, *given)
 
 
 def on_device(object_slices, probe, amplitude, positions, propagator):
@@ -323,46 +354,58 @@
     tab = tables(size)
     before = shifted(positions, "frame", 1)
     others = [shifted(probe, "state", by) for by in range(1, states)]
-    kr, ki, amp = call(prepare_body, [grid] * 3, [VMEM] * 2, flops=2 * size**3, moved=20 * unit)(propagator, amplitude)
-    (first,) = call(turn_body, [probe.shape], [SMEM, VMEM], moved=16 * unit)(positions, probe)
-    before, kr, ki, amp, first = lax.optimization_barrier((before, kr, ki, amp, first))
-    index = lax.axis_index("state").astype(jnp.int32)
-    where = jnp.concatenate([positions, index[None, None], before], 1)
-
-    picked = call(send_body, [(2,) + grid] * 2, [SMEM, VMEM], moved=16 * unit)(before, object_slices)
+    kr, ki, amp, first, held, tab, pos = pl.pallas_call(
+        prepare_body,
+        out_shape=[jax.ShapeDtypeStruct(grid, F32)] * 3
+        + [jax.ShapeDtypeStruct(x.shape, x.dtype) for x in (probe, object_slices, tab, positions)],
+        in_specs=[HBM] * 6,
+        out_specs=[VMEM] * 7,
+        scratch_shapes=[
+            pltpu.SMEM(positions.shape, jnp.int32),
+            pltpu.VMEM(probe.shape, F32),
+            pltpu.VMEM(grid, F32),
+            pltpu.VMEM(amplitude.shape, F32),
+            pltpu.SemaphoreType.DMA((7,)),
+        ],
+        compiler_params=pltpu.CompilerParams(vmem_limit_bytes=LIMIT),
+        cost_estimate=pl.CostEstimate(flops=2 * size**3, bytes_accessed=60 * unit, transcendentals=0),
+    )(*(in_hbm(x) for x in (positions, probe, propagator, amplitude, object_slices, tab)))
+    picked = call(send_body, [(2,) + grid] * 2, [VMEM, VMEM], moved=16 * unit)(before, held)
     halo_zero = shifted(picked[0], "frame", -1)
     halo_one = shifted(picked[1], "frame", -1)
     rest = others[0] if states == 2 else jnp.concatenate(others, 0)
-    (rest,) = call(turn_body, [rest.shape], [SMEM, VMEM], moved=16 * unit * (states - 1))(positions, rest)
+    (probes,) = call(turn_body, [(states, 2) + grid], [SMEM, VMEM, VMEM], moved=16 * unit * (states - 1))(
+        pos, first, rest
+    )
 
     (waves,) = call(
         inner_body,
         [(states, 2) + grid],
-        [SMEM] + [VMEM] * 7,
-        [pltpu.VMEM((2,) + grid, F32), pltpu.VMEM((states, 2) + grid, F32)],
+        [VMEM] * 7,
+        [pltpu.VMEM((2,) + grid, F32)],
         flops=2 * flops * states,
         moved=16 * unit * states,
-    )(where, object_slices, halo_zero, first, rest, kr, ki, tab)
+    )(pos, held, halo_zero, probes, kr, ki, tab)
     term_one, chi = call(
         functools.partial(middle_body, rows),
         [(2, rows, size), (states, 2) + grid],
-        [SMEM] + [VMEM] * 5,
+        [VMEM] * 6,
         [pltpu.VMEM((2,) + grid, F32), pltpu.VMEM((states, 2) + grid, F32), pltpu.VMEM(grid, F32)],
         flops=2 * flops * states,
         moved=32 * unit * states,
-    )(where, object_slices, halo_one, waves, amp, tab)
+    )(pos, held, halo_one, waves, amp, tab)
     came_one = shifted(term_one, "frame", 1)
     (term_zero,) = call(
         functools.partial(last_body, rows),
         [(2, rows, size)],
-        [SMEM] + [VMEM] * 6,
-        [pltpu.VMEM((states, 2) + grid, F32), pltpu.VMEM((states, 2, rows, size), F32)],
+        [VMEM] * 5,
+        [pltpu.VMEM((states, 2) + grid, F32)],
         flops=2 * flops * states,
         moved=16 * unit * states,
-    )(where, chi, first, rest, kr, ki, tab)
+    )(chi, probes, kr, ki, tab)
     came_zero = shifted(term_zero, "frame", 1)
-    gradient = gather(1, rows, size, where, term_one, came_one)
-    return gather(0, rows, size, where, term_zero, came_zero, gradient)
+    gradient = gather(1, rows, size, pos, before, term_one, came_one)
+    return gather(0, rows, size, pos, before, term_zero, came_zero, gradient)
 
 
 def solution(mesh):

time: 46.7 us -> 38.3 us (0.82)
  local copies, waits for them, and re-layouts: 8.21 us -> 0 us
  waiting for transfers between devices: 13.3 us -> 17.8 us
  Pallas kernels: 16.8 us -> 12.8 us
    unnamed x28 -> x0, local copies, waits for them, and re-layouts: 8.21 us -> none
    ppermute x6, waiting for transfers between devices: 13.3 us -> 17.8 us  [shifted(): lax.ppermute(value, axis, [(i, (i + by) % count) for i in range(count)])]
    pallas_call x6 -> x5, Pallas kernels: 10.5 us -> 8.49 us  [the longest x1 3.48 us: gradient_of(): pl.pallas_call(prepare_body, out_shape=[jax.ShapeDtypeStruct(grid, F32)]...]
    pallas_call x1, Pallas kernels: 3.48 us -> 2.51 us  [gradient_of(): call(functools.partial(middle_body, rows), [(2, rows, size), (states, 2)...]
    pallas_call x2, Pallas kernels: 2.79 us -> 1.85 us  [gather(): pl.pallas_call(functools.partial(gather_body, slice_id, rows), out_shape=...]
  transfers between devices with their start and end apart: 6 -> 6, of which waited for: 4 -> 6; matrix products, arithmetic and copies ran while one was open for 0% -> 0% of each run, Pallas kernels for 26% -> 25%
where the time goes in v2:
time: 38.3 us; the launch traced here: 38.1 us
  waiting for transfers between devices  17.8 us (46%)
  Pallas kernels  12.8 us (33%)
  starting transfers between devices  7.42 us (19%)
    ppermute x6, waiting for transfers between devices, shifted(): lax.ppermute(value, axis, [(i, (i + by) % count) for i in range(count)])  17.8 us
    ppermute x6, starting transfers between devices, shifted(): lax.ppermute(value, axis, [(i, (i + by) % count) for i in range(count)])  7.42 us
    pallas_call x1, Pallas kernels, gradient_of(): pl.pallas_call(prepare_body, out_shape=[jax.ShapeDtypeStruct(grid, F32)]...  3.48 us
    pallas_call x1, Pallas kernels, gradient_of(): call(functools.partial(middle_body, rows), [(2, rows, size), (states, 2)...  2.51 us
    pallas_call x1, Pallas kernels, gradient_of(): call(inner_body, [(states, 2) + grid], [VMEM] * 7, [pltpu.VMEM((2,) + gri...  2.18 us
    pallas_call x1, Pallas kernels, gradient_of(): call(functools.partial(last_body, rows), [(2, rows, size)], [VMEM] * 5, [...  1.89 us
    pallas_call x2, Pallas kernels, gather(): pl.pallas_call(functools.partial(gather_body, slice_id, rows), out_shape=...  1.85 us
    pallas_call x1, Pallas kernels, gradient_of(): call(turn_body, [(states, 2) + grid], [SMEM, VMEM, VMEM], moved=16 * unit...  0.77 us
  transfers between devices with their start and end apart: 6, of which 6 were waited for; matrix products, arithmetic and copies ran while one was open for 0% of the time, Pallas kernels for 25%

profile of v2, /device:TPU:0, one launch (start us, length us, event | category | flops | bytes accessed | tf_op | source)
XLA Modules:
  0.0 38.1 jit_solution(4499391607502811383)
XLA Ops:
  0.0 0.5 %collective-permute-start = (s32[1,2]{1,0:T(1,128)}, s32[1,2]{1,0:T(1,128)S(1)}, u32[]{:S(2)}, u32[]{:S(2)}) collective-permute-start(s32[1,2]{1,0:T(1,128)} %pos_hbm.1), channel_id=1, source_target_pairs={{0,2},{2,4},{4,6},{6,8},{8,10},{10,12},{12,14},{14,16},{16,18},{18... | collective-permute-start | bytes 32 | tf_op jit(solution)/shard_map/ppermute | solution.py:23
  0.5 2.5 %collective-permute-start.3 = (f32[1,2,256,256]{3,2,1,0:T(8,128)}, f32[1,2,256,256]{3,2,1,0:T(8,128)S(1)}, u32[]{:S(2)}, u32[]{:S(2)}) collective-permute-start(f32[1,2,256,256]{3,2,1,0:T(8,128)} %probe_hbm.1), channel_id=1, source_target_pairs={{0,1},{1,0},{2,3},{3,2},{4,5},{5,4},{6,7},{7,6},{8,9},{9,8},{10,11... | collective-permute-start | bytes 1572872 | tf_op jit(solution)/shard_map/ppermute | solution.py:23
  3.0 3.5 %shard_map.64 = (f32[256,256]{1,0:T(8,128)S(1)}, f32[256,256]{1,0:T(8,128)S(1)}, f32[256,256]{1,0:T(8,128)S(1)}, f32[1,2,256,256]{3,2,1,0:T(8,128)S(1)}, f32[2,2...) custom-call(s32[1,2]{1,0:T(1,128)} %pos_hbm.1, f32[1,2,256,256]{3,2,1,0:T(8,128)} %probe_hbm.1, ...), custom_call_target="tpu_custom_call" | custom-call | flops 33554432 | bytes 3932160 | tf_op jit(solution)/shard_map/pallas_call | solution.py:357
  6.5 0.4 %collective-permute-done.before_ref = s32[1,2]{1,0:T(1,128)S(1)} collective-permute-done((s32[1,2]{1,0:T(1,128)}, s32[1,2]{1,0:T(1,128)S(1)}, u32[]{:S(2)}, u32[]{:S(2)}) %collective-permute-start) | collective-permute-done | bytes 40 | tf_op jit(solution)/shard_map/ppermute | solution.py:23
  6.9 0.2 shard_map.65
  7.0 3.8 %collective-permute-start.2 = (f32[2,256,256]{2,1,0:T(8,128)S(1)}, f32[2,256,256]{2,1,0:T(8,128)S(1)}, u32[]{:S(2)}, u32[]{:S(2)}) collective-permute-start(f32[2,256,256]{2,1,0:T(8,128)S(1)} %get-tuple-element.19), channel_id=1, source_target_pairs={{0,30},{2,0},{4,2},{6,4},{8,6},{10,8},{12,10},{14,12},{16,14},{18,... | collective-permute-start | bytes 1572872 | tf_op jit(solution)/shard_map/ppermute | solution.py:23
  10.9 0.5 %collective-permute-start.1 = (f32[2,256,256]{2,1,0:T(8,128)S(1)}, f32[2,256,256]{2,1,0:T(8,128)S(1)}, u32[]{:S(2)}, u32[]{:S(2)}) collective-permute-start(f32[2,256,256]{2,1,0:T(8,128)S(1)} %get-tuple-element.18), channel_id=1, source_target_pairs={{0,30},{2,0},{4,2},{6,4},{8,6},{10,8},{12,10},{14,12},{16,14},{18,... | collective-permute-start | bytes 1572872 | tf_op jit(solution)/shard_map/ppermute | solution.py:23
  11.4 3.6 %collective-permute-done.3.probe_ref = f32[1,2,256,256]{3,2,1,0:T(8,128)S(1)} collective-permute-done((f32[1,2,256,256]{3,2,1,0:T(8,128)}, f32[1,2,256,256]{3,2,1,0:T(8,128)S(1)}, u32[]{:S(2)}, u32[]{:S(2)}) %collective-permute-start.3) | collective-permute-done | bytes 524320 | tf_op jit(solution)/shard_map/ppermute | solution.py:23
  14.9 0.8 %shard_map.66.probe_ref = f32[2,2,256,256]{3,2,1,0:T(8,128)S(1)} custom-call(s32[1,2]{1,0:T(1,128)S(1)} %get-tuple-element.16.pos_ref, f32[1,2,256,256]{3,2,1,0:T(8,128)S(1)} %get-tuple-element.20.first_ref, f32[1,2,256,256]{3,2,1,0:T(8,128)S(1)} %collective-permute-done.3.probe_ref), custom_call_target="tpu_custom_call" | custom-call | bytes 1048576 | tf_op jit(solution)/shard_map/pallas_call | solution.py:377
  15.7 1.8 %collective-permute-done.2.halo_ref = f32[2,256,256]{2,1,0:T(8,128)S(1)} collective-permute-done((f32[2,256,256]{2,1,0:T(8,128)S(1)}, f32[2,256,256]{2,1,0:T(8,128)S(1)}, u32[]{:S(2)}, u32[]{:S(2)}) %collective-permute-start.2) | collective-permute-done | bytes 524320 | tf_op jit(solution)/shard_map/ppermute | solution.py:23
  17.6 2.2 %shard_map.67.inner_ref = f32[2,2,256,256]{3,2,1,0:T(8,128)S(1)} custom-call(s32[1,2]{1,0:T(1,128)S(1)} %get-tuple-element.16.pos_ref, f32[2,2,256,512]{3,2,1,0:T(8,128)S(1)} %get-tuple-element.17.object_ref, f32[2,256,256]{2,1,0:T(8,128)S(1)} %collective-permute-done.2.halo_ref, f32[2,2,256,256]{3,2,1,0:T(8,128)S(1)} %shard_map.66.probe_ref, ...), custom_call_target="tpu_custom_call" | custom-call | flops 1610612736 | bytes 2097152 | tf_op jit(solution)/shard_map/pallas_call | solution.py:381
  19.7 3.4 %collective-permute-done.1.halo_ref = f32[2,256,256]{2,1,0:T(8,128)S(1)} collective-permute-done((f32[2,256,256]{2,1,0:T(8,128)S(1)}, f32[2,256,256]{2,1,0:T(8,128)S(1)}, u32[]{:S(2)}, u32[]{:S(2)}) %collective-permute-start.1) | collective-permute-done | bytes 524320 | tf_op jit(solution)/shard_map/ppermute | solution.py:23
  23.2 2.5 %shard_map.68 = (f32[2,128,256]{2,1,0:T(8,128)S(1)}, f32[2,2,256,256]{3,2,1,0:T(8,128)S(1)}) custom-call(s32[1,2]{1,0:T(1,128)S(1)} %get-tuple-element.16.pos_ref, f32[2,2,256,512]{3,2,1,0:T(8,128)S(1)} %get-tuple-element.17.object_ref, f32[2,256,256]{2,1,0:T(8,128)S(1)} %collective-permute-done.1.halo_ref, f32[2,2,256,256]{3,2,1,0:T(8,128)S(1)} %shard_map.67.inner_ref, ...), custom_call_target="tpu_custom_call" | custom-call | flops 1610612736 | bytes 4194304 | tf_op jit(solution)/shard_map/pallas_call | solution.py:389
  25.7 0.1 collective-permute-start.5
  25.8 1.9 %shard_map.69.own_ref = f32[2,128,256]{2,1,0:T(8,128)S(1)} custom-call(f32[2,2,256,256]{3,2,1,0:T(8,128)S(1)} %get-tuple-element.25.chi_ref, f32[2,2,256,256]{3,2,1,0:T(8,128)S(1)} %shard_map.66.probe_ref, f32[256,256]{1,0:T(8,128)S(1)} %get-tuple-element.21.kr_ref, f32[256,256]{1,0:T(8,128)S(1)} %get-tuple-element.22.ki_ref, ...), custom_call_target="tpu_custom_call" | custom-call | flops 1610612736 | bytes 2097152 | tf_op jit(solution)/shard_map/pallas_call | solution.py:398
  27.7 0.1 collective-permute-start.4
  27.7 6.7 %collective-permute-done.5.came_ref = f32[2,128,256]{2,1,0:T(8,128)S(1)} collective-permute-done((f32[2,128,256]{2,1,0:T(8,128)S(1)}, f32[2,128,256]{2,1,0:T(8,128)S(1)}, u32[]{:S(2)}, u32[]{:S(2)}) %collective-permute-start.5) | collective-permute-done | bytes 262176 | tf_op jit(solution)/shard_map/ppermute | solution.py:23
  34.4 0.9 %shard_map.70.refs_0_ = f32[2,2,128,512]{3,2,1,0:T(8,128)} custom-call(s32[1,2]{1,0:T(1,128)S(1)} %get-tuple-element.16.pos_ref, s32[1,2]{1,0:T(1,128)S(1)} %collective-permute-done.before_ref, f32[2,128,256]{2,1,0:T(8,128)S(1)} %get-tuple-element.26.own_ref, f32[2,128,256]{2,1,0:T(8,128)S(1)} %collective-permute-done.5.came_ref), custom_call_target="tpu_custom_call" | custom-call | bytes 1048576 | tf_op jit(solution)/shard_map/pallas_call | solution.py:330
  35.3 1.9 %collective-permute-done.4.came_ref = f32[2,128,256]{2,1,0:T(8,128)S(1)} collective-permute-done((f32[2,128,256]{2,1,0:T(8,128)S(1)}, f32[2,128,256]{2,1,0:T(8,128)S(1)}, u32[]{:S(2)}, u32[]{:S(2)}) %collective-permute-start.4) | collective-permute-done | bytes 262176 | tf_op jit(solution)/shard_map/ppermute | solution.py:23
  37.2 0.9 %shard_map.71 = f32[2,2,128,512]{3,2,1,0:T(8,128)} custom-call(s32[1,2]{1,0:T(1,128)S(1)} %get-tuple-element.16.pos_ref, s32[1,2]{1,0:T(1,128)S(1)} %collective-permute-done.before_ref, f32[2,128,256]{2,1,0:T(8,128)S(1)} %shard_map.69.own_ref, f32[2,128,256]{2,1,0:T(8,128)S(1)} %collective-permute-done.4.came_ref, ...), custom_call_target="tpu_custom_call", output_to_operand_aliasing={{}: (4, {})} | custom-call | bytes 1048576 | tf_op jit(solution)/shard_map/pallas_call | solution.py:330
Async XLA Ops:
  0.0 6.9 %collective-permute-start = (s32[1,2]{1,0:T(1,128)}, s32[1,2]{1,0:T(1,128)S(1)}, u32[]{:S(2)}, u32[]{:S(2)}) collective-permute-start(s32[1,2]{1,0:T(1,128)} %pos_hbm.1), channel_id=1, source_target_pairs={{0,2},{2,4},{4,6},{6,8},{8,10},{10,12},{12,14},{14,16},{16,18},{18... | collective-permute-start | bytes 32 | tf_op jit(solution)/shard_map/ppermute | solution.py:23
  0.5 14.4 %collective-permute-start.3 = (f32[1,2,256,256]{3,2,1,0:T(8,128)}, f32[1,2,256,256]{3,2,1,0:T(8,128)S(1)}, u32[]{:S(2)}, u32[]{:S(2)}) collective-permute-start(f32[1,2,256,256]{3,2,1,0:T(8,128)} %probe_hbm.1), channel_id=1, source_target_pairs={{0,1},{1,0},{2,3},{3,2},{4,5},{5,4},{6,7},{7,6},{8,9},{9,8},{10,11... | collective-permute-start | bytes 1572872 | tf_op jit(solution)/shard_map/ppermute | solution.py:23
  7.0 10.5 %collective-permute-start.2 = (f32[2,256,256]{2,1,0:T(8,128)S(1)}, f32[2,256,256]{2,1,0:T(8,128)S(1)}, u32[]{:S(2)}, u32[]{:S(2)}) collective-permute-start(f32[2,256,256]{2,1,0:T(8,128)S(1)} %get-tuple-element.19), channel_id=1, source_target_pairs={{0,30},{2,0},{4,2},{6,4},{8,6},{10,8},{12,10},{14,12},{16,14},{18,... | collective-permute-start | bytes 1572872 | tf_op jit(solution)/shard_map/ppermute | solution.py:23
  10.9 12.3 %collective-permute-start.1 = (f32[2,256,256]{2,1,0:T(8,128)S(1)}, f32[2,256,256]{2,1,0:T(8,128)S(1)}, u32[]{:S(2)}, u32[]{:S(2)}) collective-permute-start(f32[2,256,256]{2,1,0:T(8,128)S(1)} %get-tuple-element.18), channel_id=1, source_target_pairs={{0,30},{2,0},{4,2},{6,4},{8,6},{10,8},{12,10},{14,12},{16,14},{18,... | collective-permute-start | bytes 1572872 | tf_op jit(solution)/shard_map/ppermute | solution.py:23
  25.7 8.7 %collective-permute-start.5 = (f32[2,128,256]{2,1,0:T(8,128)S(1)}, f32[2,128,256]{2,1,0:T(8,128)S(1)}, u32[]{:S(2)}, u32[]{:S(2)}) collective-permute-start(f32[2,128,256]{2,1,0:T(8,128)S(1)} %get-tuple-element.26.own_ref), channel_id=1, source_target_pairs={{0,2},{2,4},{4,6},{6,8},{8,10},{10,12},{12,14},{14,16},{16,18},{18... | collective-permute-start | bytes 786440 | tf_op jit(solution)/shard_map/ppermute | solution.py:23
  27.7 9.6 %collective-permute-start.4 = (f32[2,128,256]{2,1,0:T(8,128)S(1)}, f32[2,128,256]{2,1,0:T(8,128)S(1)}, u32[]{:S(2)}, u32[]{:S(2)}) collective-permute-start(f32[2,128,256]{2,1,0:T(8,128)S(1)} %shard_map.69.own_ref), channel_id=1, source_target_pairs={{0,2},{2,4},{4,6},{6,8},{8,10},{10,12},{12,14},{14,16},{16,18},{18... | collective-permute-start | bytes 786440 | tf_op jit(solution)/shard_map/ppermute | solution.py:23

commit v3 on v2

--- a/solution.py
+++ b/solution.py
@@ -175,18 +175,28 @@
     return pltpu.roll(pltpu.roll(value, row, 0), col, 1)
 
 
-def prepare_body(
-    pos_hbm, probe_hbm, prop_hbm, amp_hbm, object_hbm, tab_hbm,
-    wave_re, wave_im, amp_out, first_out, object_out, tab_out, pos_out,
-    pos, probe, prop, amp, sem,
-):
-    moves = (
-        (pos_hbm, pos), (probe_hbm, probe), (prop_hbm, prop), (amp_hbm, amp),
-        (pos_hbm, pos_out), (object_hbm, object_out), (tab_hbm, tab_out),
-    )
+def run_copies(moves, sem):
     copies = [pltpu.make_async_copy(src, dst, sem.at[i]) for i, (src, dst) in enumerate(moves)]
     for copy in copies:
         copy.start()
+    return copies
+
+
+def load_body(pos_hbm, probe_hbm, object_hbm, pos_out, plane_out, object_out, sem):
+    plane = lax.rem(lax.axis_index("frame"), 2)
+    moves = ((probe_hbm.at[0, plane], plane_out), (pos_hbm, pos_out), (object_hbm, object_out))
+    for copy in run_copies(moves, sem):
+        copy.wait()
+
+
+def prepare_body(
+    pos_hbm, probe_hbm, prop_hbm, amp_hbm, tab_hbm,
+    wave_re, wave_im, amp_out, first_out, tab_out,
+    pos, probe, prop, amp, sem,
+):
+    copies = run_copies(
+        ((pos_hbm, pos), (probe_hbm, probe), (prop_hbm, prop), (amp_hbm, amp), (tab_hbm, tab_out)), sem
+    )
     copies[0].wait()
     copies[1].wait()
     size = prop.shape[0]
@@ -199,17 +209,18 @@
     wave_im[...] = jnp.sin(phase)
     copies[3].wait()
     amp_out[...] = by_parity(amp[0])
-    for copy in copies[4:]:
-        copy.wait()
-
-
-def turn_body(pos_ref, first_ref, probe_ref, out_ref):
-    size = probe_ref.shape[-1]
+    copies[4].wait()
+
+
+def turn_body(pos_ref, first_ref, *refs):
+    out_ref = refs[-1]
+    size = out_ref.shape[-1]
     row, col = pos_ref[0, 0], lax.rem(pos_ref[0, 1], size)
+    swap = lax.rem(lax.axis_index("frame"), 2) == 1
     out_ref[:1] = first_ref[...]
-    for m in range(probe_ref.shape[0]):
-        for c in range(2):
-            out_ref[1 + m, c] = turned(probe_ref[m, c], row, col)
+    for m, (came, given) in enumerate(zip(refs[:-1:2], refs[1:-1:2])):
+        for c, planes in enumerate(((came, given), (given, came))):
+            out_ref[1 + m, c] = turned(jnp.where(swap, planes[1][...], planes[0][...]), row, col)
 
 
 def spread(ref, which, shape):
@@ -344,6 +355,7 @@
     size = amplitude.shape[1]
     rows = object_slices.shape[2] // states
     assert object_slices.shape[2:] == (size, 2 * size) and positions.shape[0] == 1
+    assert lax.axis_size("frame") % 2 == 0
     return gradient_of(object_slices, probe, amplitude, positions, propagator, states, size, rows)
 
 
@@ -353,30 +365,49 @@
     flops = 24 * size**3
     tab = tables(size)
     before = shifted(positions, "frame", 1)
-    others = [shifted(probe, "state", by) for by in range(1, states)]
-    kr, ki, amp, first, held, tab, pos = pl.pallas_call(
+    given = [in_hbm(x) for x in (positions, probe, object_slices)]
+    pos, plane, held = pl.pallas_call(
+        load_body,
+        out_shape=[
+            jax.ShapeDtypeStruct(positions.shape, jnp.int32),
+            jax.ShapeDtypeStruct(grid, F32),
+            jax.ShapeDtypeStruct(object_slices.shape, F32),
+        ],
+        in_specs=[HBM] * 3,
+        out_specs=[VMEM] * 3,
+        scratch_shapes=[pltpu.SemaphoreType.DMA((3,))],
+        compiler_params=pltpu.CompilerParams(vmem_limit_bytes=LIMIT),
+        cost_estimate=pl.CostEstimate(flops=0, bytes_accessed=40 * unit, transcendentals=0),
+    )(*given)
+    planes = []
+    for by in range(1, states):
+        planes.append(shifted(plane, "state", by))
+    picked = call(send_body, [(2,) + grid] * 2, [VMEM, VMEM], moved=16 * unit)(before, held)
+    halo_zero = shifted(picked[0], "frame", -1)
+    halo_one = shifted(picked[1], "frame", -1)
+    kr, ki, amp, first, tab = pl.pallas_call(
         prepare_body,
         out_shape=[jax.ShapeDtypeStruct(grid, F32)] * 3
-        + [jax.ShapeDtypeStruct(x.shape, x.dtype) for x in (probe, object_slices, tab, positions)],
-        in_specs=[HBM] * 6,
-        out_specs=[VMEM] * 7,
+        + [jax.ShapeDtypeStruct(x.shape, x.dtype) for x in (probe, tab)],
+        in_specs=[HBM] * 5,
+        out_specs=[VMEM] * 5,
         scratch_shapes=[
             pltpu.SMEM(positions.shape, jnp.int32),
             pltpu.VMEM(probe.shape, F32),
             pltpu.VMEM(grid, F32),
             pltpu.VMEM(amplitude.shape, F32),
-            pltpu.SemaphoreType.DMA((7,)),
+            pltpu.SemaphoreType.DMA((5,)),
         ],
         compiler_params=pltpu.CompilerParams(vmem_limit_bytes=LIMIT),
         cost_estimate=pl.CostEstimate(flops=2 * size**3, bytes_accessed=60 * unit, transcendentals=0),
-    )(*(in_hbm(x) for x in (positions, probe, propagator, amplitude, object_slices, tab)))
-    picked = call(send_body, [(2,) + grid] * 2, [VMEM, VMEM], moved=16 * unit)(before, held)
-    halo_zero = shifted(picked[0], "frame", -1)
-    halo_one = shifted(picked[1], "frame", -1)
-    rest = others[0] if states == 2 else jnp.concatenate(others, 0)
-    (probes,) = call(turn_body, [(states, 2) + grid], [SMEM, VMEM, VMEM], moved=16 * unit * (states - 1))(
-        pos, first, rest
-    )
+    )(*given[:2], *(in_hbm(x) for x in (propagator, amplitude, tab)))
+    frames = lax.axis_size("frame")
+    pairs = []
+    for came in planes:
+        pairs += [came, lax.ppermute(came, "frame", [(i, i ^ 1) for i in range(frames)])]
+    (probes,) = call(
+        turn_body, [(states, 2) + grid], [SMEM] + [VMEM] * (1 + len(pairs)), moved=16 * unit * (states - 1)
+    )(pos, first, *pairs)
 
     (waves,) = call(
         inner_body,

time: 38.3 us -> 36.6 us (0.956)
  waiting for transfers between devices: 17.8 us -> 15 us
  Pallas kernels: 12.8 us -> 14.5 us
  starting transfers between devices: 7.42 us -> 6.74 us
    ppermute x6, waiting for transfers between devices: 17.8 us -> 15 us  [shifted(): lax.ppermute(value, axis, [(i, (i + by) % count) for i in range(count)])]
    pallas_call x1 -> x2, Pallas kernels: 0.77 us -> 2.54 us  [the longest x1 1.73 us: gradient_of(): pl.pallas_call(load_body, out_shape=[jax.ShapeDtypeStruct(positions.shape...]
    ppermute x6, starting transfers between devices: 7.42 us -> 5.8 us  [shifted(): lax.ppermute(value, axis, [(i, (i + by) % count) for i in range(count)])]
    ppermute x0 -> x1, starting transfers between devices: none -> 0.95 us  [gradient_of(): lax.ppermute(came, 'frame', [(i, i ^ 1) for i in range(frames)])]
  transfers between devices with their start and end apart: 6 -> 7, of which waited for: 6 -> 5; matrix products, arithmetic and copies ran while one was open for 0% -> 0% of each run, Pallas kernels for 25% -> 31%
where the time goes in v3:
time: 36.6 us; the launch traced here: 36.4 us
  waiting for transfers between devices  15 us (41%)
  Pallas kernels  14.5 us (40%)
  starting transfers between devices  6.74 us (18%)
    ppermute x6, waiting for transfers between devices, shifted(): lax.ppermute(value, axis, [(i, (i + by) % count) for i in range(count)])  15 us
    ppermute x6, starting transfers between devices, shifted(): lax.ppermute(value, axis, [(i, (i + by) % count) for i in range(count)])  5.8 us
    pallas_call x1, Pallas kernels, gradient_of(): pl.pallas_call(prepare_body, out_shape=[jax.ShapeDtypeStruct(grid, F32)]...  3.42 us
    pallas_call x1, Pallas kernels, gradient_of(): call(functools.partial(middle_body, rows), [(2, rows, size), (states, 2)...  2.49 us
    pallas_call x1, Pallas kernels, gradient_of(): call(inner_body, [(states, 2) + grid], [VMEM] * 7, [pltpu.VMEM((2,) + gri...  2.2 us
    pallas_call x1, Pallas kernels, gradient_of(): call(functools.partial(last_body, rows), [(2, rows, size)], [VMEM] * 5, [...  1.88 us
    pallas_call x2, Pallas kernels, gather(): pl.pallas_call(functools.partial(gather_body, slice_id, rows), out_shape=...  1.85 us
    pallas_call x1, Pallas kernels, gradient_of(): pl.pallas_call(load_body, out_shape=[jax.ShapeDtypeStruct(positions.shape...  1.73 us
  transfers between devices with their start and end apart: 7, of which 5 were waited for; matrix products, arithmetic and copies ran while one was open for 0% of the time, Pallas kernels for 31%

profile of v3, /device:TPU:0, one launch (start us, length us, event | category | flops | bytes accessed | tf_op | source)
XLA Modules:
  0.0 36.4 jit_solution(3687085433836957145)
XLA Ops:
  0.0 0.5 %collective-permute-start = (s32[1,2]{1,0:T(1,128)}, s32[1,2]{1,0:T(1,128)S(1)}, u32[]{:S(2)}, u32[]{:S(2)}) collective-permute-start(s32[1,2]{1,0:T(1,128)} %pos_hbm.3), channel_id=1, source_target_pairs={{0,2},{2,4},{4,6},{6,8},{8,10},{10,12},{12,14},{14,16},{16,18},{18... | collective-permute-start | bytes 32 | tf_op jit(solution)/shard_map/ppermute | solution.py:23
  0.5 1.7 %shard_map.64 = (s32[1,2]{1,0:T(1,128)S(1)}, f32[256,256]{1,0:T(8,128)S(1)}, f32[2,2,256,512]{3,2,1,0:T(8,128)S(1)}) custom-call(s32[1,2]{1,0:T(1,128)} %pos_hbm.3, f32[1,2,256,256]{3,2,1,0:T(8,128)} %probe_hbm.3, f32[2,2,256,512]{3,2,1,0:T(8,128)} %object_hbm.1), custom_call_target="tpu_custom_call" | custom-call | bytes 2621440 | tf_op jit(solution)/shard_map/pallas_call | solution.py:369
  2.2 2.5 %collective-permute-start.3 = (f32[256,256]{1,0:T(8,128)S(1)}, f32[256,256]{1,0:T(8,128)S(1)}, u32[]{:S(2)}, u32[]{:S(2)}) collective-permute-start(f32[256,256]{1,0:T(8,128)S(1)} %get-tuple-element.22), channel_id=1, source_target_pairs={{0,1},{1,0},{2,3},{3,2},{4,5},{5,4},{6,7},{7,6},{8,9},{9,8},{10,11... | collective-permute-start | bytes 786440 | tf_op jit(solution)/shard_map/ppermute | solution.py:23
  4.8 2.1 %collective-permute-done.before_ref = s32[1,2]{1,0:T(1,128)S(1)} collective-permute-done((s32[1,2]{1,0:T(1,128)}, s32[1,2]{1,0:T(1,128)S(1)}, u32[]{:S(2)}, u32[]{:S(2)}) %collective-permute-start) | collective-permute-done | bytes 40 | tf_op jit(solution)/shard_map/ppermute | solution.py:23
  6.9 0.2 shard_map.65
  7.0 2.1 %collective-permute-start.2 = (f32[2,256,256]{2,1,0:T(8,128)S(1)}, f32[2,256,256]{2,1,0:T(8,128)S(1)}, u32[]{:S(2)}, u32[]{:S(2)}) collective-permute-start(f32[2,256,256]{2,1,0:T(8,128)S(1)} %get-tuple-element.20), channel_id=1, source_target_pairs={{0,30},{2,0},{4,2},{6,4},{8,6},{10,8},{12,10},{14,12},{16,14},{18,... | collective-permute-start | bytes 1572872 | tf_op jit(solution)/shard_map/ppermute | solution.py:23
  9.2 0.5 %collective-permute-start.1 = (f32[2,256,256]{2,1,0:T(8,128)S(1)}, f32[2,256,256]{2,1,0:T(8,128)S(1)}, u32[]{:S(2)}, u32[]{:S(2)}) collective-permute-start(f32[2,256,256]{2,1,0:T(8,128)S(1)} %get-tuple-element.19), channel_id=1, source_target_pairs={{0,30},{2,0},{4,2},{6,4},{8,6},{10,8},{12,10},{14,12},{16,14},{18,... | collective-permute-start | bytes 1572872 | tf_op jit(solution)/shard_map/ppermute | solution.py:23
  9.7 1.1 %collective-permute-done.3.refs_0_ = f32[256,256]{1,0:T(8,128)S(1)} collective-permute-done((f32[256,256]{1,0:T(8,128)S(1)}, f32[256,256]{1,0:T(8,128)S(1)}, u32[]{:S(2)}, u32[]{:S(2)}) %collective-permute-start.3) | collective-permute-done | bytes 262176 | tf_op jit(solution)/shard_map/ppermute | solution.py:23
  10.8 0.9 %collective-permute-start.4 = (f32[256,256]{1,0:T(8,128)S(1)}, f32[256,256]{1,0:T(8,128)S(1)}, u32[]{:S(2)}, u32[]{:S(2)}) collective-permute-start(f32[256,256]{1,0:T(8,128)S(1)} %collective-permute-done.3.refs_0_), channel_id=1, source_target_pairs={{0,2},{2,0},{4,6},{6,4},{8,10},{10,8},{12,14},{14,12},{16,18},{18,... | collective-permute-start | bytes 786440 | tf_op jit(solution)/shard_map/ppermute | solution.py:407
  11.8 3.4 %shard_map.66 = (f32[256,256]{1,0:T(8,128)S(1)}, f32[256,256]{1,0:T(8,128)S(1)}, f32[256,256]{1,0:T(8,128)S(1)}, f32[1,2,256,256]{3,2,1,0:T(8,128)S(1)}, bf16[2,4,256,256]{3,2,1,0:T(8,128)(2,1)S(1)}) custom-call(s32[1,2]{1,0:T(1,128)} %pos_hbm.3, f32[1,2,256,256]{3,2,1,0:T(8,128)} %probe_hbm.3, f32[256,256]{1,0:T(8,128)} %prop_hbm.1, ...), custom_call_target="tpu_custom_call" | custom-call | flops 33554432 | bytes 3932160 | tf_op jit(solution)/shard_map/pallas_call | solution.py:388
  15.2 0.0 collective-permute-done.4.refs_1_
  15.2 0.8 %shard_map.67.probe_ref = f32[2,2,256,256]{3,2,1,0:T(8,128)S(1)} custom-call(s32[1,2]{1,0:T(1,128)S(1)} %get-tuple-element.17.pos_ref, f32[1,2,256,256]{3,2,1,0:T(8,128)S(1)} %get-tuple-element.21.first_ref, f32[256,256]{1,0:T(8,128)S(1)} %collective-permute-done.3.refs_0_, f32[256,256]{1,0:T(8,128)S(1)} %collective-permute-done.4.refs_1_), custom_call_target="tpu_custom_call" | custom-call | bytes 1048576 | tf_op jit(solution)/shard_map/pallas_call | solution.py:408
  16.0 0.0 collective-permute-done.2.halo_ref
  16.0 2.2 %shard_map.68.inner_ref = f32[2,2,256,256]{3,2,1,0:T(8,128)S(1)} custom-call(s32[1,2]{1,0:T(1,128)S(1)} %get-tuple-element.17.pos_ref, f32[2,2,256,512]{3,2,1,0:T(8,128)S(1)} %get-tuple-element.18.object_ref, f32[2,256,256]{2,1,0:T(8,128)S(1)} %collective-permute-done.2.halo_ref, f32[2,2,256,256]{3,2,1,0:T(8,128)S(1)} %shard_map.67.probe_ref, ...), custom_call_target="tpu_custom_call" | custom-call | flops 1610612736 | bytes 2097152 | tf_op jit(solution)/shard_map/pallas_call | solution.py:412
  18.2 3.2 %collective-permute-done.1.halo_ref = f32[2,256,256]{2,1,0:T(8,128)S(1)} collective-permute-done((f32[2,256,256]{2,1,0:T(8,128)S(1)}, f32[2,256,256]{2,1,0:T(8,128)S(1)}, u32[]{:S(2)}, u32[]{:S(2)}) %collective-permute-start.1) | collective-permute-done | bytes 524320 | tf_op jit(solution)/shard_map/ppermute | solution.py:23
  21.5 2.5 %shard_map.69 = (f32[2,128,256]{2,1,0:T(8,128)S(1)}, f32[2,2,256,256]{3,2,1,0:T(8,128)S(1)}) custom-call(s32[1,2]{1,0:T(1,128)S(1)} %get-tuple-element.17.pos_ref, f32[2,2,256,512]{3,2,1,0:T(8,128)S(1)} %get-tuple-element.18.object_ref, f32[2,256,256]{2,1,0:T(8,128)S(1)} %collective-permute-done.1.halo_ref, f32[2,2,256,256]{3,2,1,0:T(8,128)S(1)} %shard_map.68.inner_ref, ...), custom_call_target="tpu_custom_call" | custom-call | flops 1610612736 | bytes 4194304 | tf_op jit(solution)/shard_map/pallas_call | solution.py:420
  24.0 0.1 collective-permute-start.6
  24.0 1.9 %shard_map.70.own_ref = f32[2,128,256]{2,1,0:T(8,128)S(1)} custom-call(f32[2,2,256,256]{3,2,1,0:T(8,128)S(1)} %get-tuple-element.27.chi_ref, f32[2,2,256,256]{3,2,1,0:T(8,128)S(1)} %shard_map.67.probe_ref, f32[256,256]{1,0:T(8,128)S(1)} %get-tuple-element.23.kr_ref, f32[256,256]{1,0:T(8,128)S(1)} %get-tuple-element.24.ki_ref, ...), custom_call_target="tpu_custom_call" | custom-call | flops 1610612736 | bytes 2097152 | tf_op jit(solution)/shard_map/pallas_call | solution.py:429
  25.9 0.1 collective-permute-start.5
  26.0 6.7 %collective-permute-done.6.came_ref = f32[2,128,256]{2,1,0:T(8,128)S(1)} collective-permute-done((f32[2,128,256]{2,1,0:T(8,128)S(1)}, f32[2,128,256]{2,1,0:T(8,128)S(1)}, u32[]{:S(2)}, u32[]{:S(2)}) %collective-permute-start.6) | collective-permute-done | bytes 262176 | tf_op jit(solution)/shard_map/ppermute | solution.py:23
  32.7 0.9 %shard_map.71.refs_0_ = f32[2,2,128,512]{3,2,1,0:T(8,128)} custom-call(s32[1,2]{1,0:T(1,128)S(1)} %get-tuple-element.17.pos_ref, s32[1,2]{1,0:T(1,128)S(1)} %collective-permute-done.before_ref, f32[2,128,256]{2,1,0:T(8,128)S(1)} %get-tuple-element.28.own_ref, f32[2,128,256]{2,1,0:T(8,128)S(1)} %collective-permute-done.6.came_ref), custom_call_target="tpu_custom_call" | custom-call | bytes 1048576 | tf_op jit(solution)/shard_map/pallas_call | solution.py:341
  33.6 1.9 %collective-permute-done.5.came_ref = f32[2,128,256]{2,1,0:T(8,128)S(1)} collective-permute-done((f32[2,128,256]{2,1,0:T(8,128)S(1)}, f32[2,128,256]{2,1,0:T(8,128)S(1)}, u32[]{:S(2)}, u32[]{:S(2)}) %collective-permute-start.5) | collective-permute-done | bytes 262176 | tf_op jit(solution)/shard_map/ppermute | solution.py:23
  35.5 0.9 %shard_map.72 = f32[2,2,128,512]{3,2,1,0:T(8,128)} custom-call(s32[1,2]{1,0:T(1,128)S(1)} %get-tuple-element.17.pos_ref, s32[1,2]{1,0:T(1,128)S(1)} %collective-permute-done.before_ref, f32[2,128,256]{2,1,0:T(8,128)S(1)} %shard_map.70.own_ref, f32[2,128,256]{2,1,0:T(8,128)S(1)} %collective-permute-done.5.came_ref, ...), custom_call_target="tpu_custom_call", output_to_operand_aliasing={{}: (4, {})} | custom-call | bytes 1048576 | tf_op jit(solution)/shard_map/pallas_call | solution.py:341
Async XLA Ops:
  0.0 6.9 %collective-permute-start = (s32[1,2]{1,0:T(1,128)}, s32[1,2]{1,0:T(1,128)S(1)}, u32[]{:S(2)}, u32[]{:S(2)}) collective-permute-start(s32[1,2]{1,0:T(1,128)} %pos_hbm.3), channel_id=1, source_target_pairs={{0,2},{2,4},{4,6},{6,8},{8,10},{10,12},{12,14},{14,16},{16,18},{18... | collective-permute-start | bytes 32 | tf_op jit(solution)/shard_map/ppermute | solution.py:23
  2.2 8.6 %collective-permute-start.3 = (f32[256,256]{1,0:T(8,128)S(1)}, f32[256,256]{1,0:T(8,128)S(1)}, u32[]{:S(2)}, u32[]{:S(2)}) collective-permute-start(f32[256,256]{1,0:T(8,128)S(1)} %get-tuple-element.22), channel_id=1, source_target_pairs={{0,1},{1,0},{2,3},{3,2},{4,5},{5,4},{6,7},{7,6},{8,9},{9,8},{10,11... | collective-permute-start | bytes 786440 | tf_op jit(solution)/shard_map/ppermute | solution.py:23
  7.0 9.0 %collective-permute-start.2 = (f32[2,256,256]{2,1,0:T(8,128)S(1)}, f32[2,256,256]{2,1,0:T(8,128)S(1)}, u32[]{:S(2)}, u32[]{:S(2)}) collective-permute-start(f32[2,256,256]{2,1,0:T(8,128)S(1)} %get-tuple-element.20), channel_id=1, source_target_pairs={{0,30},{2,0},{4,2},{6,4},{8,6},{10,8},{12,10},{14,12},{16,14},{18,... | collective-permute-start | bytes 1572872 | tf_op jit(solution)/shard_map/ppermute | solution.py:23
  9.2 12.3 %collective-permute-start.1 = (f32[2,256,256]{2,1,0:T(8,128)S(1)}, f32[2,256,256]{2,1,0:T(8,128)S(1)}, u32[]{:S(2)}, u32[]{:S(2)}) collective-permute-start(f32[2,256,256]{2,1,0:T(8,128)S(1)} %get-tuple-element.19), channel_id=1, source_target_pairs={{0,30},{2,0},{4,2},{6,4},{8,6},{10,8},{12,10},{14,12},{16,14},{18,... | collective-permute-start | bytes 1572872 | tf_op jit(solution)/shard_map/ppermute | solution.py:23
  10.8 4.4 %collective-permute-start.4 = (f32[256,256]{1,0:T(8,128)S(1)}, f32[256,256]{1,0:T(8,128)S(1)}, u32[]{:S(2)}, u32[]{:S(2)}) collective-permute-start(f32[256,256]{1,0:T(8,128)S(1)} %collective-permute-done.3.refs_0_), channel_id=1, source_target_pairs={{0,2},{2,0},{4,6},{6,4},{8,10},{10,8},{12,14},{14,12},{16,18},{18,... | collective-permute-start | bytes 786440 | tf_op jit(solution)/shard_map/ppermute | solution.py:407
  24.0 8.7 %collective-permute-start.6 = (f32[2,128,256]{2,1,0:T(8,128)S(1)}, f32[2,128,256]{2,1,0:T(8,128)S(1)}, u32[]{:S(2)}, u32[]{:S(2)}) collective-permute-start(f32[2,128,256]{2,1,0:T(8,128)S(1)} %get-tuple-element.28.own_ref), channel_id=1, source_target_pairs={{0,2},{2,4},{4,6},{6,8},{8,10},{10,12},{12,14},{14,16},{16,18},{18... | collective-permute-start | bytes 786440 | tf_op jit(solution)/shard_map/ppermute | solution.py:23
  25.9 9.6 %collective-permute-start.5 = (f32[2,128,256]{2,1,0:T(8,128)S(1)}, f32[2,128,256]{2,1,0:T(8,128)S(1)}, u32[]{:S(2)}, u32[]{:S(2)}) collective-permute-start(f32[2,128,256]{2,1,0:T(8,128)S(1)} %shard_map.70.own_ref), channel_id=1, source_target_pairs={{0,2},{2,4},{4,6},{6,8},{8,10},{10,12},{12,14},{14,16},{16,18},{18... | collective-permute-start | bytes 786440 | tf_op jit(solution)/shard_map/ppermute | solution.py:23

commit v4 on v3

--- a/solution.py
+++ b/solution.py
@@ -184,7 +184,13 @@
 
 def load_body(pos_hbm, probe_hbm, object_hbm, pos_out, plane_out, object_out, sem):
     plane = lax.rem(lax.axis_index("frame"), 2)
-    moves = ((probe_hbm.at[0, plane], plane_out), (pos_hbm, pos_out), (object_hbm, object_out))
+    half = object_hbm.shape[2] // 2
+    moves = [(pos_hbm, pos_out)]
+    for s in range(2):
+        for part in range(2):
+            for at in (pl.ds(0, half), pl.ds(half, half)):
+                moves.append((object_hbm.at[s, part, at], object_out.at[s, part, at]))
+    moves.append((probe_hbm.at[0, plane], plane_out))
     for copy in run_copies(moves, sem):
         copy.wait()
 
@@ -375,16 +381,16 @@
         ],
         in_specs=[HBM] * 3,
         out_specs=[VMEM] * 3,
-        scratch_shapes=[pltpu.SemaphoreType.DMA((3,))],
+        scratch_shapes=[pltpu.SemaphoreType.DMA((10,))],
         compiler_params=pltpu.CompilerParams(vmem_limit_bytes=LIMIT),
         cost_estimate=pl.CostEstimate(flops=0, bytes_accessed=40 * unit, transcendentals=0),
     )(*given)
+    picked = call(send_body, [(2,) + grid] * 2, [VMEM, VMEM], moved=16 * unit)(before, held)
+    halo_zero = shifted(picked[0], "frame", -1)
+    halo_one = shifted(picked[1], "frame", -1)
     planes = []
     for by in range(1, states):
         planes.append(shifted(plane, "state", by))
-    picked = call(send_body, [(2,) + grid] * 2, [VMEM, VMEM], moved=16 * unit)(before, held)
-    halo_zero = shifted(picked[0], "frame", -1)
-    halo_one = shifted(picked[1], "frame", -1)
     kr, ki, amp, first, tab = pl.pallas_call(
         prepare_body,
         out_shape=[jax.ShapeDtypeStruct(grid, F32)] * 3

time: 36.6 us -> 36.5 us (level)
  transfers between devices with their start and end apart: 7 -> 7, of which waited for: 5 -> 5; matrix products, arithmetic and copies ran while one was open for 0% -> 0% of each run, Pallas kernels for 31% -> 30%
where the time goes in v4:
time: 36.5 us; the launch traced here: 36.4 us
  waiting for transfers between devices  15.1 us (41%)
  Pallas kernels  14.5 us (40%)
  starting transfers between devices  6.69 us (18%)
    ppermute x6, waiting for transfers between devices, shifted(): lax.ppermute(value, axis, [(i, (i + by) % count) for i in range(count)])  15.1 us
    ppermute x6, starting transfers between devices, shifted(): lax.ppermute(value, axis, [(i, (i + by) % count) for i in range(count)])  5.75 us
    pallas_call x1, Pallas kernels, gradient_of(): pl.pallas_call(prepare_body, out_shape=[jax.ShapeDtypeStruct(grid, F32)]...  3.42 us
    pallas_call x1, Pallas kernels, gradient_of(): call(functools.partial(middle_body, rows), [(2, rows, size), (states, 2)...  2.49 us
    pallas_call x1, Pallas kernels, gradient_of(): call(inner_body, [(states, 2) + grid], [VMEM] * 7, [pltpu.VMEM((2,) + gri...  2.2 us
    pallas_call x1, Pallas kernels, gradient_of(): call(functools.partial(last_body, rows), [(2, rows, size)], [VMEM] * 5, [...  1.89 us
    pallas_call x2, Pallas kernels, gather(): pl.pallas_call(functools.partial(gather_body, slice_id, rows), out_shape=...  1.85 us
    pallas_call x1, Pallas kernels, gradient_of(): pl.pallas_call(load_body, out_shape=[jax.ShapeDtypeStruct(positions.shape...  1.68 us
  transfers between devices with their start and end apart: 7, of which 5 were waited for; matrix products, arithmetic and copies ran while one was open for 0% of the time, Pallas kernels for 30%

profile of v4, /device:TPU:0, one launch (start us, length us, event | category | flops | bytes accessed | tf_op | source)
XLA Modules:
  0.0 36.4 jit_solution(3937197577121529598)
XLA Ops:
  0.0 0.5 %collective-permute-start = (s32[1,2]{1,0:T(1,128)}, s32[1,2]{1,0:T(1,128)S(1)}, u32[]{:S(2)}, u32[]{:S(2)}) collective-permute-start(s32[1,2]{1,0:T(1,128)} %pos_hbm.3), channel_id=1, source_target_pairs={{0,2},{2,4},{4,6},{6,8},{8,10},{10,12},{12,14},{14,16},{16,18},{18... | collective-permute-start | bytes 32 | tf_op jit(solution)/shard_map/ppermute | solution.py:23
  0.5 1.7 %shard_map.64 = (s32[1,2]{1,0:T(1,128)S(1)}, f32[256,256]{1,0:T(8,128)S(1)}, f32[2,2,256,512]{3,2,1,0:T(8,128)S(1)}) custom-call(s32[1,2]{1,0:T(1,128)} %pos_hbm.3, f32[1,2,256,256]{3,2,1,0:T(8,128)} %probe_hbm.3, f32[2,2,256,512]{3,2,1,0:T(8,128)} %object_hbm.1), custom_call_target="tpu_custom_call" | custom-call | bytes 2621440 | tf_op jit(solution)/shard_map/pallas_call | solution.py:375
  2.2 2.5 %collective-permute-start.3 = (f32[256,256]{1,0:T(8,128)S(1)}, f32[256,256]{1,0:T(8,128)S(1)}, u32[]{:S(2)}, u32[]{:S(2)}) collective-permute-start(f32[256,256]{1,0:T(8,128)S(1)} %get-tuple-element.22), channel_id=1, source_target_pairs={{0,1},{1,0},{2,3},{3,2},{4,5},{5,4},{6,7},{7,6},{8,9},{9,8},{10,11... | collective-permute-start | bytes 786440 | tf_op jit(solution)/shard_map/ppermute | solution.py:23
  4.7 2.1 %collective-permute-done.before_ref = s32[1,2]{1,0:T(1,128)S(1)} collective-permute-done((s32[1,2]{1,0:T(1,128)}, s32[1,2]{1,0:T(1,128)S(1)}, u32[]{:S(2)}, u32[]{:S(2)}) %collective-permute-start) | collective-permute-done | bytes 40 | tf_op jit(solution)/shard_map/ppermute | solution.py:23
  6.9 0.2 shard_map.65
  7.0 2.1 %collective-permute-start.2 = (f32[2,256,256]{2,1,0:T(8,128)S(1)}, f32[2,256,256]{2,1,0:T(8,128)S(1)}, u32[]{:S(2)}, u32[]{:S(2)}) collective-permute-start(f32[2,256,256]{2,1,0:T(8,128)S(1)} %get-tuple-element.20), channel_id=1, source_target_pairs={{0,30},{2,0},{4,2},{6,4},{8,6},{10,8},{12,10},{14,12},{16,14},{18,... | collective-permute-start | bytes 1572872 | tf_op jit(solution)/shard_map/ppermute | solution.py:23
  9.1 0.5 %collective-permute-start.1 = (f32[2,256,256]{2,1,0:T(8,128)S(1)}, f32[2,256,256]{2,1,0:T(8,128)S(1)}, u32[]{:S(2)}, u32[]{:S(2)}) collective-permute-start(f32[2,256,256]{2,1,0:T(8,128)S(1)} %get-tuple-element.19), channel_id=1, source_target_pairs={{0,30},{2,0},{4,2},{6,4},{8,6},{10,8},{12,10},{14,12},{16,14},{18,... | collective-permute-start | bytes 1572872 | tf_op jit(solution)/shard_map/ppermute | solution.py:23
  9.6 1.1 %collective-permute-done.3.refs_0_ = f32[256,256]{1,0:T(8,128)S(1)} collective-permute-done((f32[256,256]{1,0:T(8,128)S(1)}, f32[256,256]{1,0:T(8,128)S(1)}, u32[]{:S(2)}, u32[]{:S(2)}) %collective-permute-start.3) | collective-permute-done | bytes 262176 | tf_op jit(solution)/shard_map/ppermute | solution.py:23
  10.8 0.9 %collective-permute-start.4 = (f32[256,256]{1,0:T(8,128)S(1)}, f32[256,256]{1,0:T(8,128)S(1)}, u32[]{:S(2)}, u32[]{:S(2)}) collective-permute-start(f32[256,256]{1,0:T(8,128)S(1)} %collective-permute-done.3.refs_0_), channel_id=1, source_target_pairs={{0,2},{2,0},{4,6},{6,4},{8,10},{10,8},{12,14},{14,12},{16,18},{18,... | collective-permute-start | bytes 786440 | tf_op jit(solution)/shard_map/ppermute | solution.py:413
  11.7 3.4 %shard_map.66 = (f32[256,256]{1,0:T(8,128)S(1)}, f32[256,256]{1,0:T(8,128)S(1)}, f32[256,256]{1,0:T(8,128)S(1)}, f32[1,2,256,256]{3,2,1,0:T(8,128)S(1)}, bf16[2,4,256,256]{3,2,1,0:T(8,128)(2,1)S(1)}) custom-call(s32[1,2]{1,0:T(1,128)} %pos_hbm.3, f32[1,2,256,256]{3,2,1,0:T(8,128)} %probe_hbm.3, f32[256,256]{1,0:T(8,128)} %prop_hbm.1, ...), custom_call_target="tpu_custom_call" | custom-call | flops 33554432 | bytes 3932160 | tf_op jit(solution)/shard_map/pallas_call | solution.py:394
  15.1 0.0 collective-permute-done.4.refs_1_
  15.1 0.8 %shard_map.67.probe_ref = f32[2,2,256,256]{3,2,1,0:T(8,128)S(1)} custom-call(s32[1,2]{1,0:T(1,128)S(1)} %get-tuple-element.17.pos_ref, f32[1,2,256,256]{3,2,1,0:T(8,128)S(1)} %get-tuple-element.21.first_ref, f32[256,256]{1,0:T(8,128)S(1)} %collective-permute-done.3.refs_0_, f32[256,256]{1,0:T(8,128)S(1)} %collective-permute-done.4.refs_1_), custom_call_target="tpu_custom_call" | custom-call | bytes 1048576 | tf_op jit(solution)/shard_map/pallas_call | solution.py:414
  16.0 0.0 collective-permute-done.2.halo_ref
  16.0 2.2 %shard_map.68.inner_ref = f32[2,2,256,256]{3,2,1,0:T(8,128)S(1)} custom-call(s32[1,2]{1,0:T(1,128)S(1)} %get-tuple-element.17.pos_ref, f32[2,2,256,512]{3,2,1,0:T(8,128)S(1)} %get-tuple-element.18.object_ref, f32[2,256,256]{2,1,0:T(8,128)S(1)} %collective-permute-done.2.halo_ref, f32[2,2,256,256]{3,2,1,0:T(8,128)S(1)} %shard_map.67.probe_ref, ...), custom_call_target="tpu_custom_call" | custom-call | flops 1610612736 | bytes 2097152 | tf_op jit(solution)/shard_map/pallas_call | solution.py:418
  18.2 3.2 %collective-permute-done.1.halo_ref = f32[2,256,256]{2,1,0:T(8,128)S(1)} collective-permute-done((f32[2,256,256]{2,1,0:T(8,128)S(1)}, f32[2,256,256]{2,1,0:T(8,128)S(1)}, u32[]{:S(2)}, u32[]{:S(2)}) %collective-permute-start.1) | collective-permute-done | bytes 524320 | tf_op jit(solution)/shard_map/ppermute | solution.py:23
  21.4 2.5 %shard_map.69 = (f32[2,128,256]{2,1,0:T(8,128)S(1)}, f32[2,2,256,256]{3,2,1,0:T(8,128)S(1)}) custom-call(s32[1,2]{1,0:T(1,128)S(1)} %get-tuple-element.17.pos_ref, f32[2,2,256,512]{3,2,1,0:T(8,128)S(1)} %get-tuple-element.18.object_ref, f32[2,256,256]{2,1,0:T(8,128)S(1)} %collective-permute-done.1.halo_ref, f32[2,2,256,256]{3,2,1,0:T(8,128)S(1)} %shard_map.68.inner_ref, ...), custom_call_target="tpu_custom_call" | custom-call | flops 1610612736 | bytes 4194304 | tf_op jit(solution)/shard_map/pallas_call | solution.py:426
  23.9 0.1 collective-permute-start.6
  24.0 1.9 %shard_map.70.own_ref = f32[2,128,256]{2,1,0:T(8,128)S(1)} custom-call(f32[2,2,256,256]{3,2,1,0:T(8,128)S(1)} %get-tuple-element.27.chi_ref, f32[2,2,256,256]{3,2,1,0:T(8,128)S(1)} %shard_map.67.probe_ref, f32[256,256]{1,0:T(8,128)S(1)} %get-tuple-element.23.kr_ref, f32[256,256]{1,0:T(8,128)S(1)} %get-tuple-element.24.ki_ref, ...), custom_call_target="tpu_custom_call" | custom-call | flops 1610612736 | bytes 2097152 | tf_op jit(solution)/shard_map/pallas_call | solution.py:435
  25.9 0.1 collective-permute-start.5
  25.9 6.7 %collective-permute-done.6.came_ref = f32[2,128,256]{2,1,0:T(8,128)S(1)} collective-permute-done((f32[2,128,256]{2,1,0:T(8,128)S(1)}, f32[2,128,256]{2,1,0:T(8,128)S(1)}, u32[]{:S(2)}, u32[]{:S(2)}) %collective-permute-start.6) | collective-permute-done | bytes 262176 | tf_op jit(solution)/shard_map/ppermute | solution.py:23
  32.6 0.9 %shard_map.71.refs_0_ = f32[2,2,128,512]{3,2,1,0:T(8,128)} custom-call(s32[1,2]{1,0:T(1,128)S(1)} %get-tuple-element.17.pos_ref, s32[1,2]{1,0:T(1,128)S(1)} %collective-permute-done.before_ref, f32[2,128,256]{2,1,0:T(8,128)S(1)} %get-tuple-element.28.own_ref, f32[2,128,256]{2,1,0:T(8,128)S(1)} %collective-permute-done.6.came_ref), custom_call_target="tpu_custom_call" | custom-call | bytes 1048576 | tf_op jit(solution)/shard_map/pallas_call | solution.py:347
  33.6 1.9 %collective-permute-done.5.came_ref = f32[2,128,256]{2,1,0:T(8,128)S(1)} collective-permute-done((f32[2,128,256]{2,1,0:T(8,128)S(1)}, f32[2,128,256]{2,1,0:T(8,128)S(1)}, u32[]{:S(2)}, u32[]{:S(2)}) %collective-permute-start.5) | collective-permute-done | bytes 262176 | tf_op jit(solution)/shard_map/ppermute | solution.py:23
  35.4 0.9 %shard_map.72 = f32[2,2,128,512]{3,2,1,0:T(8,128)} custom-call(s32[1,2]{1,0:T(1,128)S(1)} %get-tuple-element.17.pos_ref, s32[1,2]{1,0:T(1,128)S(1)} %collective-permute-done.before_ref, f32[2,128,256]{2,1,0:T(8,128)S(1)} %shard_map.70.own_ref, f32[2,128,256]{2,1,0:T(8,128)S(1)} %collective-permute-done.5.came_ref, ...), custom_call_target="tpu_custom_call", output_to_operand_aliasing={{}: (4, {})} | custom-call | bytes 1048576 | tf_op jit(solution)/shard_map/pallas_call | solution.py:347
Async XLA Ops:
  0.0 6.9 %collective-permute-start = (s32[1,2]{1,0:T(1,128)}, s32[1,2]{1,0:T(1,128)S(1)}, u32[]{:S(2)}, u32[]{:S(2)}) collective-permute-start(s32[1,2]{1,0:T(1,128)} %pos_hbm.3), channel_id=1, source_target_pairs={{0,2},{2,4},{4,6},{6,8},{8,10},{10,12},{12,14},{14,16},{16,18},{18... | collective-permute-start | bytes 32 | tf_op jit(solution)/shard_map/ppermute | solution.py:23
  2.2 8.6 %collective-permute-start.3 = (f32[256,256]{1,0:T(8,128)S(1)}, f32[256,256]{1,0:T(8,128)S(1)}, u32[]{:S(2)}, u32[]{:S(2)}) collective-permute-start(f32[256,256]{1,0:T(8,128)S(1)} %get-tuple-element.22), channel_id=1, source_target_pairs={{0,1},{1,0},{2,3},{3,2},{4,5},{5,4},{6,7},{7,6},{8,9},{9,8},{10,11... | collective-permute-start | bytes 786440 | tf_op jit(solution)/shard_map/ppermute | solution.py:23
  7.0 8.9 %collective-permute-start.2 = (f32[2,256,256]{2,1,0:T(8,128)S(1)}, f32[2,256,256]{2,1,0:T(8,128)S(1)}, u32[]{:S(2)}, u32[]{:S(2)}) collective-permute-start(f32[2,256,256]{2,1,0:T(8,128)S(1)} %get-tuple-element.20), channel_id=1, source_target_pairs={{0,30},{2,0},{4,2},{6,4},{8,6},{10,8},{12,10},{14,12},{16,14},{18,... | collective-permute-start | bytes 1572872 | tf_op jit(solution)/shard_map/ppermute | solution.py:23
  9.1 12.3 %collective-permute-start.1 = (f32[2,256,256]{2,1,0:T(8,128)S(1)}, f32[2,256,256]{2,1,0:T(8,128)S(1)}, u32[]{:S(2)}, u32[]{:S(2)}) collective-permute-start(f32[2,256,256]{2,1,0:T(8,128)S(1)} %get-tuple-element.19), channel_id=1, source_target_pairs={{0,30},{2,0},{4,2},{6,4},{8,6},{10,8},{12,10},{14,12},{16,14},{18,... | collective-permute-start | bytes 1572872 | tf_op jit(solution)/shard_map/ppermute | solution.py:23
  10.8 4.4 %collective-permute-start.4 = (f32[256,256]{1,0:T(8,128)S(1)}, f32[256,256]{1,0:T(8,128)S(1)}, u32[]{:S(2)}, u32[]{:S(2)}) collective-permute-start(f32[256,256]{1,0:T(8,128)S(1)} %collective-permute-done.3.refs_0_), channel_id=1, source_target_pairs={{0,2},{2,0},{4,6},{6,4},{8,10},{10,8},{12,14},{14,12},{16,18},{18,... | collective-permute-start | bytes 786440 | tf_op jit(solution)/shard_map/ppermute | solution.py:413
  23.9 8.7 %collective-permute-start.6 = (f32[2,128,256]{2,1,0:T(8,128)S(1)}, f32[2,128,256]{2,1,0:T(8,128)S(1)}, u32[]{:S(2)}, u32[]{:S(2)}) collective-permute-start(f32[2,128,256]{2,1,0:T(8,128)S(1)} %get-tuple-element.28.own_ref), channel_id=1, source_target_pairs={{0,2},{2,4},{4,6},{6,8},{8,10},{10,12},{12,14},{14,16},{16,18},{18... | collective-permute-start | bytes 786440 | tf_op jit(solution)/shard_map/ppermute | solution.py:23
  25.9 9.6 %collective-permute-start.5 = (f32[2,128,256]{2,1,0:T(8,128)S(1)}, f32[2,128,256]{2,1,0:T(8,128)S(1)}, u32[]{:S(2)}, u32[]{:S(2)}) collective-permute-start(f32[2,128,256]{2,1,0:T(8,128)S(1)} %shard_map.70.own_ref), channel_id=1, source_target_pairs={{0,2},{2,4},{4,6},{6,8},{8,10},{10,12},{12,14},{14,16},{16,18},{18... | collective-permute-start | bytes 786440 | tf_op jit(solution)/shard_map/ppermute | solution.py:23

commit v5 on v4

--- a/solution.py
+++ b/solution.py
@@ -183,16 +183,21 @@
 
 
 def load_body(pos_hbm, probe_hbm, object_hbm, pos_out, plane_out, object_out, sem):
-    plane = lax.rem(lax.axis_index("frame"), 2)
+    which = lax.rem(lax.axis_index("frame"), 2)
     half = object_hbm.shape[2] // 2
-    moves = [(pos_hbm, pos_out)]
+    moves = [(probe_hbm.at[0, which], plane_out), (pos_hbm, pos_out)]
     for s in range(2):
         for part in range(2):
             for at in (pl.ds(0, half), pl.ds(half, half)):
                 moves.append((object_hbm.at[s, part, at], object_out.at[s, part, at]))
-    moves.append((probe_hbm.at[0, plane], plane_out))
     for copy in run_copies(moves, sem):
         copy.wait()
+
+
+def turn_body(pos_ref, *refs):
+    half = len(refs) // 2
+    for came, out in zip(refs[:half], refs[half:]):
+        out[...] = turned(came[...], pos_ref[0, 0], lax.rem(pos_ref[0, 1], came.shape[1]))
 
 
 def prepare_body(
@@ -218,17 +223,6 @@
     copies[4].wait()
 
 
-def turn_body(pos_ref, first_ref, *refs):
-    out_ref = refs[-1]
-    size = out_ref.shape[-1]
-    row, col = pos_ref[0, 0], lax.rem(pos_ref[0, 1], size)
-    swap = lax.rem(lax.axis_index("frame"), 2) == 1
-    out_ref[:1] = first_ref[...]
-    for m, (came, given) in enumerate(zip(refs[:-1:2], refs[1:-1:2])):
-        for c, planes in enumerate(((came, given), (given, came))):
-            out_ref[1 + m, c] = turned(jnp.where(swap, planes[1][...], planes[0][...]), row, col)
-
-
 def spread(ref, which, shape):
     return jnp.broadcast_to(ref[0:1, which : which + 1], shape)
 
@@ -258,9 +252,16 @@
     return ref[(*at, 0)], ref[(*at, 1)]
 
 
-def inner_body(pos_ref, object_ref, halo_ref, probe_ref, kr_ref, ki_ref, tab, out_ref, patch):
+def inner_body(pos, pos_ref, object_ref, halo_ref, first_ref, kr_ref, ki_ref, tab, *refs):
+    out_ref, probe_ref, patch = refs[-3:]
     states = out_ref.shape[0]
     patch[0], patch[1] = patch_of(0, object_ref, halo_ref, pos_ref)
+    swap = lax.rem(lax.axis_index("frame"), 2) == 1
+    probe_ref[:1] = first_ref[...]
+    for m, (came, given) in enumerate(zip(refs[:-3:2], refs[1:-3:2])):
+        other = turned(given[...], pos[0, 0], lax.rem(pos[0, 1], given.shape[1]))
+        probe_ref[1 + m, 0] = jnp.where(swap, other, came[...])
+        probe_ref[1 + m, 1] = jnp.where(swap, came[...], other)
 
     def body(group):
         waves = forward([times(pair(probe_ref, m), pair(patch)) for m in group], tab)
@@ -408,21 +409,18 @@
         cost_estimate=pl.CostEstimate(flops=2 * size**3, bytes_accessed=60 * unit, transcendentals=0),
     )(*given[:2], *(in_hbm(x) for x in (propagator, amplitude, tab)))
     frames = lax.axis_size("frame")
+    own = call(turn_body, [grid] * len(planes), [SMEM] + [VMEM] * len(planes), moved=16 * unit)(pos, *planes)
     pairs = []
-    for came in planes:
-        pairs += [came, lax.ppermute(came, "frame", [(i, i ^ 1) for i in range(frames)])]
-    (probes,) = call(
-        turn_body, [(states, 2) + grid], [SMEM] + [VMEM] * (1 + len(pairs)), moved=16 * unit * (states - 1)
-    )(pos, first, *pairs)
-
-    (waves,) = call(
+    for came, kept in zip(planes, own):
+        pairs += [kept, lax.ppermute(came, "frame", [(i, i ^ 1) for i in range(frames)])]
+    waves, probes = call(
         inner_body,
-        [(states, 2) + grid],
-        [VMEM] * 7,
+        [(states, 2) + grid] * 2,
+        [SMEM] + [VMEM] * (7 + len(pairs)),
         [pltpu.VMEM((2,) + grid, F32)],
         flops=2 * flops * states,
-        moved=16 * unit * states,
-    )(pos, held, halo_zero, probes, kr, ki, tab)
+        moved=24 * unit * states,
+    )(pos, pos, held, halo_zero, first, kr, ki, tab, *pairs)
     term_one, chi = call(
         functools.partial(middle_body, rows),
         [(2, rows, size), (states, 2) + grid],

time: 36.5 us -> 36.6 us (level)
  Pallas kernels: 14.5 us -> 15.1 us
  waiting for transfers between devices: 15.1 us -> 14.5 us
    ppermute x6, waiting for transfers between devices: 15.1 us -> 14.5 us  [shifted(): lax.ppermute(value, axis, [(i, (i + by) % count) for i in range(count)])]
    pallas_call x2, Pallas kernels: 3.01 us -> 3.58 us  [the longest x1 2.88 us: gradient_of(): call(inner_body, [(states, 2) + grid] * 2, [SMEM] + [VMEM] * (7 + len(pai...]
  transfers between devices with their start and end apart: 7 -> 7, of which waited for: 5 -> 5; matrix products, arithmetic and copies ran while one was open for 0% -> 0% of each run, Pallas kernels for 30% -> 32%
where the time goes in v5:
time: 36.6 us; the launch traced here: 36.4 us
  Pallas kernels  15.1 us (41%)
  waiting for transfers between devices  14.5 us (40%)
  starting transfers between devices  6.69 us (18%)
    ppermute x6, waiting for transfers between devices, shifted(): lax.ppermute(value, axis, [(i, (i + by) % count) for i in range(count)])  14.5 us
    ppermute x6, starting transfers between devices, shifted(): lax.ppermute(value, axis, [(i, (i + by) % count) for i in range(count)])  5.75 us
    pallas_call x1, Pallas kernels, gradient_of(): pl.pallas_call(prepare_body, out_shape=[jax.ShapeDtypeStruct(grid, F32)]...  3.42 us
    pallas_call x1, Pallas kernels, gradient_of(): call(inner_body, [(states, 2) + grid] * 2, [SMEM] + [VMEM] * (7 + len(pai...  2.88 us
    pallas_call x1, Pallas kernels, gradient_of(): call(functools.partial(middle_body, rows), [(2, rows, size), (states, 2)...  2.52 us
    pallas_call x1, Pallas kernels, gradient_of(): call(functools.partial(last_body, rows), [(2, rows, size)], [VMEM] * 5, [...  1.91 us
    pallas_call x2, Pallas kernels, gather(): pl.pallas_call(functools.partial(gather_body, slice_id, rows), out_shape=...  1.85 us
    pallas_call x1, Pallas kernels, gradient_of(): pl.pallas_call(load_body, out_shape=[jax.ShapeDtypeStruct(positions.shape...  1.68 us
  transfers between devices with their start and end apart: 7, of which 5 were waited for; matrix products, arithmetic and copies ran while one was open for 0% of the time, Pallas kernels for 32%

profile of v5, /device:TPU:0, one launch (start us, length us, event | category | flops | bytes accessed | tf_op | source)
XLA Modules:
  0.0 36.4 jit_solution(14317453385936516846)
XLA Ops:
  0.0 0.5 %collective-permute-start = (s32[1,2]{1,0:T(1,128)}, s32[1,2]{1,0:T(1,128)S(1)}, u32[]{:S(2)}, u32[]{:S(2)}) collective-permute-start(s32[1,2]{1,0:T(1,128)} %pos_hbm.3), channel_id=1, source_target_pairs={{0,2},{2,4},{4,6},{6,8},{8,10},{10,12},{12,14},{14,16},{16,18},{18... | collective-permute-start | bytes 32 | tf_op jit(solution)/shard_map/ppermute | solution.py:23
  0.5 1.7 %shard_map.64 = (s32[1,2]{1,0:T(1,128)S(1)}, f32[256,256]{1,0:T(8,128)S(1)}, f32[2,2,256,512]{3,2,1,0:T(8,128)S(1)}) custom-call(s32[1,2]{1,0:T(1,128)} %pos_hbm.3, f32[1,2,256,256]{3,2,1,0:T(8,128)} %probe_hbm.3, f32[2,2,256,512]{3,2,1,0:T(8,128)} %object_hbm.1), custom_call_target="tpu_custom_call" | custom-call | bytes 2621440 | tf_op jit(solution)/shard_map/pallas_call | solution.py:376
  2.2 2.5 %collective-permute-start.3 = (f32[256,256]{1,0:T(8,128)S(1)}, f32[256,256]{1,0:T(8,128)S(1)}, u32[]{:S(2)}, u32[]{:S(2)}) collective-permute-start(f32[256,256]{1,0:T(8,128)S(1)} %get-tuple-element.27), channel_id=1, source_target_pairs={{0,1},{1,0},{2,3},{3,2},{4,5},{5,4},{6,7},{7,6},{8,9},{9,8},{10,11... | collective-permute-start | bytes 786440 | tf_op jit(solution)/shard_map/ppermute | solution.py:23
  4.7 2.1 %collective-permute-done.before_ref = s32[1,2]{1,0:T(1,128)S(1)} collective-permute-done((s32[1,2]{1,0:T(1,128)}, s32[1,2]{1,0:T(1,128)S(1)}, u32[]{:S(2)}, u32[]{:S(2)}) %collective-permute-start) | collective-permute-done | bytes 40 | tf_op jit(solution)/shard_map/ppermute | solution.py:23
  6.9 0.2 shard_map.65
  7.0 2.1 %collective-permute-start.2 = (f32[2,256,256]{2,1,0:T(8,128)S(1)}, f32[2,256,256]{2,1,0:T(8,128)S(1)}, u32[]{:S(2)}, u32[]{:S(2)}) collective-permute-start(f32[2,256,256]{2,1,0:T(8,128)S(1)} %get-tuple-element.22), channel_id=1, source_target_pairs={{0,30},{2,0},{4,2},{6,4},{8,6},{10,8},{12,10},{14,12},{16,14},{18,... | collective-permute-start | bytes 1572872 | tf_op jit(solution)/shard_map/ppermute | solution.py:23
  9.1 0.5 %collective-permute-start.1 = (f32[2,256,256]{2,1,0:T(8,128)S(1)}, f32[2,256,256]{2,1,0:T(8,128)S(1)}, u32[]{:S(2)}, u32[]{:S(2)}) collective-permute-start(f32[2,256,256]{2,1,0:T(8,128)S(1)} %get-tuple-element.21), channel_id=1, source_target_pairs={{0,30},{2,0},{4,2},{6,4},{8,6},{10,8},{12,10},{14,12},{16,14},{18,... | collective-permute-start | bytes 1572872 | tf_op jit(solution)/shard_map/ppermute | solution.py:23
  9.6 1.1 %collective-permute-done.3.refs_0_ = f32[256,256]{1,0:T(8,128)S(1)} collective-permute-done((f32[256,256]{1,0:T(8,128)S(1)}, f32[256,256]{1,0:T(8,128)S(1)}, u32[]{:S(2)}, u32[]{:S(2)}) %collective-permute-start.3) | collective-permute-done | bytes 262176 | tf_op jit(solution)/shard_map/ppermute | solution.py:23
  10.8 0.9 %collective-permute-start.4 = (f32[256,256]{1,0:T(8,128)S(1)}, f32[256,256]{1,0:T(8,128)S(1)}, u32[]{:S(2)}, u32[]{:S(2)}) collective-permute-start(f32[256,256]{1,0:T(8,128)S(1)} %collective-permute-done.3.refs_0_), channel_id=1, source_target_pairs={{0,2},{2,0},{4,6},{6,4},{8,10},{10,8},{12,14},{14,12},{16,18},{18,... | collective-permute-start | bytes 786440 | tf_op jit(solution)/shard_map/ppermute | solution.py:415
  11.7 3.4 %shard_map.66 = (f32[256,256]{1,0:T(8,128)S(1)}, f32[256,256]{1,0:T(8,128)S(1)}, f32[256,256]{1,0:T(8,128)S(1)}, f32[1,2,256,256]{3,2,1,0:T(8,128)S(1)}, bf16[2,4,256,256]{3,2,1,0:T(8,128)(2,1)S(1)}) custom-call(s32[1,2]{1,0:T(1,128)} %pos_hbm.3, f32[1,2,256,256]{3,2,1,0:T(8,128)} %probe_hbm.3, f32[256,256]{1,0:T(8,128)} %prop_hbm.1, ...), custom_call_target="tpu_custom_call" | custom-call | flops 33554432 | bytes 3932160 | tf_op jit(solution)/shard_map/pallas_call | solution.py:395
  15.1 0.7 %shard_map.67.refs_0_ = f32[256,256]{1,0:T(8,128)S(1)} custom-call(s32[1,2]{1,0:T(1,128)S(1)} %get-tuple-element.19.pos_ref.pos, f32[256,256]{1,0:T(8,128)S(1)} %collective-permute-done.3.refs_0_), custom_call_target="tpu_custom_call" | custom-call | bytes 1048576 | tf_op jit(solution)/shard_map/pallas_call | solution.py:412
  15.8 0.0 collective-permute-done.4.refs_1_
  15.9 0.0 collective-permute-done.2.halo_ref
  15.9 2.9 %shard_map.68 = (f32[2,2,256,256]{3,2,1,0:T(8,128)S(1)}, f32[2,2,256,256]{3,2,1,0:T(8,128)S(1)}) custom-call(s32[1,2]{1,0:T(1,128)S(1)} %get-tuple-element.19.pos_ref.pos, s32[1,2]{1,0:T(1,128)S(1)} %get-tuple-element.19.pos_ref.pos, f32[2,2,256,512]{3,2,1,0:T(8,128)S(1)} %get-tuple-element.20.object_ref, ...), custom_call_target="tpu_custom_call" | custom-call | flops 1610612736 | bytes 3145728 | tf_op jit(solution)/shard_map/pallas_call | solution.py:416
  18.8 2.7 %collective-permute-done.1.halo_ref = f32[2,256,256]{2,1,0:T(8,128)S(1)} collective-permute-done((f32[2,256,256]{2,1,0:T(8,128)S(1)}, f32[2,256,256]{2,1,0:T(8,128)S(1)}, u32[]{:S(2)}, u32[]{:S(2)}) %collective-permute-start.1) | collective-permute-done | bytes 524320 | tf_op jit(solution)/shard_map/ppermute | solution.py:23
  21.4 2.5 %shard_map.69 = (f32[2,128,256]{2,1,0:T(8,128)S(1)}, f32[2,2,256,256]{3,2,1,0:T(8,128)S(1)}) custom-call(s32[1,2]{1,0:T(1,128)S(1)} %get-tuple-element.19.pos_ref.pos, f32[2,2,256,512]{3,2,1,0:T(8,128)S(1)} %get-tuple-element.20.object_ref, f32[2,256,256]{2,1,0:T(8,128)S(1)} %collective-permute-done.1.halo_ref, ...), custom_call_target="tpu_custom_call" | custom-call | flops 1610612736 | bytes 4194304 | tf_op jit(solution)/shard_map/pallas_call | solution.py:424
  24.0 0.1 collective-permute-start.6
  24.0 1.9 %shard_map.70.own_ref = f32[2,128,256]{2,1,0:T(8,128)S(1)} custom-call(f32[2,2,256,256]{3,2,1,0:T(8,128)S(1)} %get-tuple-element.30.chi_ref, f32[2,2,256,256]{3,2,1,0:T(8,128)S(1)} %get-tuple-element.31.probe_ref, f32[256,256]{1,0:T(8,128)S(1)} %get-tuple-element.24.kr_ref, f32[256,256]{1,0:T(8,128)S(1)} %get-tuple-element.25.ki_ref, ...), custom_call_target="tpu_custom_call" | custom-call | flops 1610612736 | bytes 2097152 | tf_op jit(solution)/shard_map/pallas_call | solution.py:433
  25.9 0.1 collective-permute-start.5
  26.0 6.7 %collective-permute-done.6.came_ref = f32[2,128,256]{2,1,0:T(8,128)S(1)} collective-permute-done((f32[2,128,256]{2,1,0:T(8,128)S(1)}, f32[2,128,256]{2,1,0:T(8,128)S(1)}, u32[]{:S(2)}, u32[]{:S(2)}) %collective-permute-start.6) | collective-permute-done | bytes 262176 | tf_op jit(solution)/shard_map/ppermute | solution.py:23
  32.7 0.9 %shard_map.71.refs_0_ = f32[2,2,128,512]{3,2,1,0:T(8,128)} custom-call(s32[1,2]{1,0:T(1,128)S(1)} %get-tuple-element.19.pos_ref.pos, s32[1,2]{1,0:T(1,128)S(1)} %collective-permute-done.before_ref, f32[2,128,256]{2,1,0:T(8,128)S(1)} %get-tuple-element.32.own_ref, f32[2,128,256]{2,1,0:T(8,128)S(1)} %collective-permute-done.6.came_ref), custom_call_target="tpu_custom_call" | custom-call | bytes 1048576 | tf_op jit(solution)/shard_map/pallas_call | solution.py:348
  33.6 1.9 %collective-permute-done.5.came_ref = f32[2,128,256]{2,1,0:T(8,128)S(1)} collective-permute-done((f32[2,128,256]{2,1,0:T(8,128)S(1)}, f32[2,128,256]{2,1,0:T(8,128)S(1)}, u32[]{:S(2)}, u32[]{:S(2)}) %collective-permute-start.5) | collective-permute-done | bytes 262176 | tf_op jit(solution)/shard_map/ppermute | solution.py:23
  35.5 0.9 %shard_map.72 = f32[2,2,128,512]{3,2,1,0:T(8,128)} custom-call(s32[1,2]{1,0:T(1,128)S(1)} %get-tuple-element.19.pos_ref.pos, s32[1,2]{1,0:T(1,128)S(1)} %collective-permute-done.before_ref, f32[2,128,256]{2,1,0:T(8,128)S(1)} %shard_map.70.own_ref, f32[2,128,256]{2,1,0:T(8,128)S(1)} %collective-permute-done.5.came_ref, ...), custom_call_target="tpu_custom_call", output_to_operand_aliasing={{}: (4, {})} | custom-call | bytes 1048576 | tf_op jit(solution)/shard_map/pallas_call | solution.py:348
Async XLA Ops:
  0.0 6.9 %collective-permute-start = (s32[1,2]{1,0:T(1,128)}, s32[1,2]{1,0:T(1,128)S(1)}, u32[]{:S(2)}, u32[]{:S(2)}) collective-permute-start(s32[1,2]{1,0:T(1,128)} %pos_hbm.3), channel_id=1, source_target_pairs={{0,2},{2,4},{4,6},{6,8},{8,10},{10,12},{12,14},{14,16},{16,18},{18... | collective-permute-start | bytes 32 | tf_op jit(solution)/shard_map/ppermute | solution.py:23
  2.2 8.6 %collective-permute-start.3 = (f32[256,256]{1,0:T(8,128)S(1)}, f32[256,256]{1,0:T(8,128)S(1)}, u32[]{:S(2)}, u32[]{:S(2)}) collective-permute-start(f32[256,256]{1,0:T(8,128)S(1)} %get-tuple-element.27), channel_id=1, source_target_pairs={{0,1},{1,0},{2,3},{3,2},{4,5},{5,4},{6,7},{7,6},{8,9},{9,8},{10,11... | collective-permute-start | bytes 786440 | tf_op jit(solution)/shard_map/ppermute | solution.py:23
  7.0 8.8 %collective-permute-start.2 = (f32[2,256,256]{2,1,0:T(8,128)S(1)}, f32[2,256,256]{2,1,0:T(8,128)S(1)}, u32[]{:S(2)}, u32[]{:S(2)}) collective-permute-start(f32[2,256,256]{2,1,0:T(8,128)S(1)} %get-tuple-element.22), channel_id=1, source_target_pairs={{0,30},{2,0},{4,2},{6,4},{8,6},{10,8},{12,10},{14,12},{16,14},{18,... | collective-permute-start | bytes 1572872 | tf_op jit(solution)/shard_map/ppermute | solution.py:23
  9.1 12.3 %collective-permute-start.1 = (f32[2,256,256]{2,1,0:T(8,128)S(1)}, f32[2,256,256]{2,1,0:T(8,128)S(1)}, u32[]{:S(2)}, u32[]{:S(2)}) collective-permute-start(f32[2,256,256]{2,1,0:T(8,128)S(1)} %get-tuple-element.21), channel_id=1, source_target_pairs={{0,30},{2,0},{4,2},{6,4},{8,6},{10,8},{12,10},{14,12},{16,14},{18,... | collective-permute-start | bytes 1572872 | tf_op jit(solution)/shard_map/ppermute | solution.py:23
  10.8 5.1 %collective-permute-start.4 = (f32[256,256]{1,0:T(8,128)S(1)}, f32[256,256]{1,0:T(8,128)S(1)}, u32[]{:S(2)}, u32[]{:S(2)}) collective-permute-start(f32[256,256]{1,0:T(8,128)S(1)} %collective-permute-done.3.refs_0_), channel_id=1, source_target_pairs={{0,2},{2,0},{4,6},{6,4},{8,10},{10,8},{12,14},{14,12},{16,18},{18,... | collective-permute-start | bytes 786440 | tf_op jit(solution)/shard_map/ppermute | solution.py:415
  24.0 8.7 %collective-permute-start.6 = (f32[2,128,256]{2,1,0:T(8,128)S(1)}, f32[2,128,256]{2,1,0:T(8,128)S(1)}, u32[]{:S(2)}, u32[]{:S(2)}) collective-permute-start(f32[2,128,256]{2,1,0:T(8,128)S(1)} %get-tuple-element.32.own_ref), channel_id=1, source_target_pairs={{0,2},{2,4},{4,6},{6,8},{8,10},{10,12},{12,14},{14,16},{16,18},{18... | collective-permute-start | bytes 786440 | tf_op jit(solution)/shard_map/ppermute | solution.py:23
  25.9 9.5 %collective-permute-start.5 = (f32[2,128,256]{2,1,0:T(8,128)S(1)}, f32[2,128,256]{2,1,0:T(8,128)S(1)}, u32[]{:S(2)}, u32[]{:S(2)}) collective-permute-start(f32[2,128,256]{2,1,0:T(8,128)S(1)} %shard_map.70.own_ref), channel_id=1, source_target_pairs={{0,2},{2,4},{4,6},{6,8},{8,10},{10,12},{12,14},{14,16},{16,18},{18... | collective-permute-start | bytes 786440 | tf_op jit(solution)/shard_map/ppermute | solution.py:23

commit v6 on v5

--- a/solution.py
+++ b/solution.py
@@ -194,10 +194,15 @@
         copy.wait()
 
 
+def turn_of(pos_ref, size):
+    return jnp.sum(pos_ref[0:1, 0:1]), lax.rem(jnp.sum(pos_ref[0:1, 1:2]), size)
+
+
 def turn_body(pos_ref, *refs):
     half = len(refs) // 2
+    turn = turn_of(pos_ref, refs[0].shape[1])
     for came, out in zip(refs[:half], refs[half:]):
-        out[...] = turned(came[...], pos_ref[0, 0], lax.rem(pos_ref[0, 1], came.shape[1]))
+        out[...] = turned(came[...], *turn)
 
 
 def prepare_body(
@@ -252,14 +257,14 @@
     return ref[(*at, 0)], ref[(*at, 1)]
 
 
-def inner_body(pos, pos_ref, object_ref, halo_ref, first_ref, kr_ref, ki_ref, tab, *refs):
+def inner_body(pos_ref, object_ref, halo_ref, first_ref, kr_ref, ki_ref, tab, *refs):
     out_ref, probe_ref, patch = refs[-3:]
     states = out_ref.shape[0]
     patch[0], patch[1] = patch_of(0, object_ref, halo_ref, pos_ref)
     swap = lax.rem(lax.axis_index("frame"), 2) == 1
     probe_ref[:1] = first_ref[...]
     for m, (came, given) in enumerate(zip(refs[:-3:2], refs[1:-3:2])):
-        other = turned(given[...], pos[0, 0], lax.rem(pos[0, 1], given.shape[1]))
+        other = turned(given[...], *turn_of(pos_ref, given.shape[1]))
         probe_ref[1 + m, 0] = jnp.where(swap, other, came[...])
         probe_ref[1 + m, 1] = jnp.where(swap, came[...], other)
 
@@ -286,7 +291,7 @@
         power[...] = total
 
     in_groups(states, outward)
-    power[...] = 1.0 - amp_ref[...] / jnp.sqrt(power[...] + 1.0)
+    power[...] = 1.0 - amp_ref[...] * lax.rsqrt(power[...] + 1.0)
     term_ref[...] = jnp.zeros_like(term_ref)
     take = pl.ds(pl.multiple_of(lax.axis_index("state") * rows, rows), rows)
 
@@ -332,14 +337,22 @@
     c = lax.broadcasted_iota(jnp.int32, (rows, size), 1)
     here, there = r >= spread(pos_ref, 0, r.shape), r < spread(before_ref, 0, r.shape)
     here_right, there_right = c < spread(pos_ref, 1, c.shape), c < spread(before_ref, 1, c.shape)
+    chunks = 4 if rows % 32 == 0 else 1
+    step = rows // chunks
     copies = []
-    for part in range(2):
-        mine = jnp.where(here, own_ref[part], 0.0)
-        theirs = jnp.where(there, came_ref[part], 0.0)
-        held[part, :, :size] = jnp.where(here_right, 0.0, mine) + jnp.where(there_right, 0.0, theirs)
-        held[part, :, size:] = jnp.where(here_right, mine, 0.0) + jnp.where(there_right, theirs, 0.0)
-        copies.append(pltpu.make_async_copy(held.at[part], out_ref.at[slice_id, part], sem.at[part]))
-        copies[-1].start()
+    for chunk in range(chunks):
+        at = pl.ds(chunk * step, step)
+        cut = slice(chunk * step, chunk * step + step)
+        for part in range(2):
+            mine = jnp.where(here[cut], own_ref[part, at], 0.0)
+            theirs = jnp.where(there[cut], came_ref[part, at], 0.0)
+            left, right = here_right[cut], there_right[cut]
+            held[part, at, :size] = jnp.where(left, 0.0, mine) + jnp.where(right, 0.0, theirs)
+            held[part, at, size:] = jnp.where(left, mine, 0.0) + jnp.where(right, theirs, 0.0)
+            copies.append(
+                pltpu.make_async_copy(held.at[part, at], out_ref.at[slice_id, part, at], sem.at[len(copies)])
+            )
+            copies[-1].start()
     for copy in copies:
         copy.wait()
 
@@ -350,7 +363,7 @@
         out_shape=jax.ShapeDtypeStruct((2, 2, rows, 2 * size), F32),
         in_specs=[VMEM] * 4 + [pl.BlockSpec(memory_space=pl.ANY)] * len(given),
         out_specs=pl.BlockSpec(memory_space=pl.ANY),
-        scratch_shapes=[pltpu.VMEM((2, rows, 2 * size), F32), pltpu.SemaphoreType.DMA((2,))],
+        scratch_shapes=[pltpu.VMEM((2, rows, 2 * size), F32), pltpu.SemaphoreType.DMA((8,))],
         input_output_aliases={4: 0} if given else {},
         compiler_params=pltpu.CompilerParams(vmem_limit_bytes=LIMIT),
         cost_estimate=pl.CostEstimate(flops=0, bytes_accessed=32 * rows * size, transcendentals=0),
@@ -386,12 +399,12 @@
         compiler_params=pltpu.CompilerParams(vmem_limit_bytes=LIMIT),
         cost_estimate=pl.CostEstimate(flops=0, bytes_accessed=40 * unit, transcendentals=0),
     )(*given)
+    planes = []
+    for by in range(1, states):
+        planes.append(shifted(plane, "state", by))
     picked = call(send_body, [(2,) + grid] * 2, [VMEM, VMEM], moved=16 * unit)(before, held)
     halo_zero = shifted(picked[0], "frame", -1)
     halo_one = shifted(picked[1], "frame", -1)
-    planes = []
-    for by in range(1, states):
-        planes.append(shifted(plane, "state", by))
     kr, ki, amp, first, tab = pl.pallas_call(
         prepare_body,
         out_shape=[jax.ShapeDtypeStruct(grid, F32)] * 3
@@ -409,18 +422,18 @@
         cost_estimate=pl.CostEstimate(flops=2 * size**3, bytes_accessed=60 * unit, transcendentals=0),
     )(*given[:2], *(in_hbm(x) for x in (propagator, amplitude, tab)))
     frames = lax.axis_size("frame")
-    own = call(turn_body, [grid] * len(planes), [SMEM] + [VMEM] * len(planes), moved=16 * unit)(pos, *planes)
+    own = call(turn_body, [grid] * len(planes), [VMEM] * (1 + len(planes)), moved=16 * unit)(pos, *planes)
     pairs = []
     for came, kept in zip(planes, own):
         pairs += [kept, lax.ppermute(came, "frame", [(i, i ^ 1) for i in range(frames)])]
     waves, probes = call(
         inner_body,
         [(states, 2) + grid] * 2,
-        [SMEM] + [VMEM] * (7 + len(pairs)),
+        [VMEM] * (7 + len(pairs)),
         [pltpu.VMEM((2,) + grid, F32)],
         flops=2 * flops * states,
         moved=24 * unit * states,
-    )(pos, pos, held, halo_zero, first, kr, ki, tab, *pairs)
+    )(pos, held, halo_zero, first, kr, ki, tab, *pairs)
     term_one, chi = call(
         functools.partial(middle_body, rows),
         [(2, rows, size), (states, 2) + grid],

time: 36.6 us -> 36.5 us (level)
  Pallas kernels: 15.1 us -> 14.1 us
  waiting for transfers between devices: 14.5 us -> 15.4 us
    pallas_call x2, Pallas kernels: 3.58 us -> 2.62 us  [the longest x1 2.38 us: gradient_of(): call(inner_body, [(states, 2) + grid] * 2, [VMEM] * (7 + len(pairs)), [pl...]
    ppermute x6, waiting for transfers between devices: 14.5 us -> 15.4 us  [shifted(): lax.ppermute(value, axis, [(i, (i + by) % count) for i in range(count)])]
  transfers between devices with their start and end apart: 7 -> 7, of which waited for: 5 -> 6; matrix products, arithmetic and copies ran while one was open for 0% -> 0% of each run, Pallas kernels for 32% -> 30%
where the time goes in v6:
time: 36.5 us; the launch traced here: 36.3 us
  waiting for transfers between devices  15.4 us (42%)
  Pallas kernels  14.1 us (39%)
  starting transfers between devices  6.69 us (18%)
    ppermute x6, waiting for transfers between devices, shifted(): lax.ppermute(value, axis, [(i, (i + by) % count) for i in range(count)])  15.4 us
    ppermute x6, starting transfers between devices, shifted(): lax.ppermute(value, axis, [(i, (i + by) % count) for i in range(count)])  5.75 us
    pallas_call x1, Pallas kernels, gradient_of(): pl.pallas_call(prepare_body, out_shape=[jax.ShapeDtypeStruct(grid, F32)]...  3.42 us
    pallas_call x1, Pallas kernels, gradient_of(): call(functools.partial(middle_body, rows), [(2, rows, size), (states, 2)...  2.44 us
    pallas_call x1, Pallas kernels, gradient_of(): call(inner_body, [(states, 2) + grid] * 2, [VMEM] * (7 + len(pairs)), [pl...  2.38 us
    pallas_call x1, Pallas kernels, gradient_of(): call(functools.partial(last_body, rows), [(2, rows, size)], [VMEM] * 5, [...  1.92 us
    pallas_call x2, Pallas kernels, gather(): pl.pallas_call(functools.partial(gather_body, slice_id, rows), out_shape=...  1.88 us
    pallas_call x1, Pallas kernels, gradient_of(): pl.pallas_call(load_body, out_shape=[jax.ShapeDtypeStruct(positions.shape...  1.68 us
  transfers between devices with their start and end apart: 7, of which 6 were waited for; matrix products, arithmetic and copies ran while one was open for 0% of the time, Pallas kernels for 30%

profile of v6, /device:TPU:0, one launch (start us, length us, event | category | flops | bytes accessed | tf_op | source)
XLA Modules:
  0.0 36.3 jit_solution(15522564662049668304)
XLA Ops:
  0.0 0.5 %collective-permute-start = (s32[1,2]{1,0:T(1,128)}, s32[1,2]{1,0:T(1,128)S(1)}, u32[]{:S(2)}, u32[]{:S(2)}) collective-permute-start(s32[1,2]{1,0:T(1,128)} %pos_hbm.3), channel_id=1, source_target_pairs={{0,2},{2,4},{4,6},{6,8},{8,10},{10,12},{12,14},{14,16},{16,18},{18... | collective-permute-start | bytes 32 | tf_op jit(solution)/shard_map/ppermute | solution.py:23
  0.5 1.7 %shard_map.64 = (s32[1,2]{1,0:T(1,128)S(1)}, f32[256,256]{1,0:T(8,128)S(1)}, f32[2,2,256,512]{3,2,1,0:T(8,128)S(1)}) custom-call(s32[1,2]{1,0:T(1,128)} %pos_hbm.3, f32[1,2,256,256]{3,2,1,0:T(8,128)} %probe_hbm.3, f32[2,2,256,512]{3,2,1,0:T(8,128)} %object_hbm.1), custom_call_target="tpu_custom_call" | custom-call | bytes 2621440 | tf_op jit(solution)/shard_map/pallas_call | solution.py:389
  2.2 2.5 %collective-permute-start.3 = (f32[256,256]{1,0:T(8,128)S(1)}, f32[256,256]{1,0:T(8,128)S(1)}, u32[]{:S(2)}, u32[]{:S(2)}) collective-permute-start(f32[256,256]{1,0:T(8,128)S(1)} %get-tuple-element.27), channel_id=1, source_target_pairs={{0,1},{1,0},{2,3},{3,2},{4,5},{5,4},{6,7},{7,6},{8,9},{9,8},{10,11... | collective-permute-start | bytes 786440 | tf_op jit(solution)/shard_map/ppermute | solution.py:23
  4.7 2.1 %collective-permute-done.before_ref = s32[1,2]{1,0:T(1,128)S(1)} collective-permute-done((s32[1,2]{1,0:T(1,128)}, s32[1,2]{1,0:T(1,128)S(1)}, u32[]{:S(2)}, u32[]{:S(2)}) %collective-permute-start) | collective-permute-done | bytes 40 | tf_op jit(solution)/shard_map/ppermute | solution.py:23
  6.9 0.2 shard_map.65
  7.0 2.1 %collective-permute-start.2 = (f32[2,256,256]{2,1,0:T(8,128)S(1)}, f32[2,256,256]{2,1,0:T(8,128)S(1)}, u32[]{:S(2)}, u32[]{:S(2)}) collective-permute-start(f32[2,256,256]{2,1,0:T(8,128)S(1)} %get-tuple-element.22), channel_id=1, source_target_pairs={{0,30},{2,0},{4,2},{6,4},{8,6},{10,8},{12,10},{14,12},{16,14},{18,... | collective-permute-start | bytes 1572872 | tf_op jit(solution)/shard_map/ppermute | solution.py:23
  9.1 0.5 %collective-permute-start.1 = (f32[2,256,256]{2,1,0:T(8,128)S(1)}, f32[2,256,256]{2,1,0:T(8,128)S(1)}, u32[]{:S(2)}, u32[]{:S(2)}) collective-permute-start(f32[2,256,256]{2,1,0:T(8,128)S(1)} %get-tuple-element.21), channel_id=1, source_target_pairs={{0,30},{2,0},{4,2},{6,4},{8,6},{10,8},{12,10},{14,12},{16,14},{18,... | collective-permute-start | bytes 1572872 | tf_op jit(solution)/shard_map/ppermute | solution.py:23
  9.6 1.1 %collective-permute-done.3.refs_0_ = f32[256,256]{1,0:T(8,128)S(1)} collective-permute-done((f32[256,256]{1,0:T(8,128)S(1)}, f32[256,256]{1,0:T(8,128)S(1)}, u32[]{:S(2)}, u32[]{:S(2)}) %collective-permute-start.3) | collective-permute-done | bytes 262176 | tf_op jit(solution)/shard_map/ppermute | solution.py:23
  10.8 0.9 %collective-permute-start.4 = (f32[256,256]{1,0:T(8,128)S(1)}, f32[256,256]{1,0:T(8,128)S(1)}, u32[]{:S(2)}, u32[]{:S(2)}) collective-permute-start(f32[256,256]{1,0:T(8,128)S(1)} %collective-permute-done.3.refs_0_), channel_id=1, source_target_pairs={{0,2},{2,0},{4,6},{6,4},{8,10},{10,8},{12,14},{14,12},{16,18},{18,... | collective-permute-start | bytes 786440 | tf_op jit(solution)/shard_map/ppermute | solution.py:428
  11.7 3.4 %shard_map.66 = (f32[256,256]{1,0:T(8,128)S(1)}, f32[256,256]{1,0:T(8,128)S(1)}, f32[256,256]{1,0:T(8,128)S(1)}, f32[1,2,256,256]{3,2,1,0:T(8,128)S(1)}, bf16[2,4,256,256]{3,2,1,0:T(8,128)(2,1)S(1)}) custom-call(s32[1,2]{1,0:T(1,128)} %pos_hbm.3, f32[1,2,256,256]{3,2,1,0:T(8,128)} %probe_hbm.3, f32[256,256]{1,0:T(8,128)} %prop_hbm.1, ...), custom_call_target="tpu_custom_call" | custom-call | flops 33554432 | bytes 3932160 | tf_op jit(solution)/shard_map/pallas_call | solution.py:408
  15.1 0.2 shard_map.67.refs_0_
  15.4 0.0 collective-permute-done.4.refs_1_
  15.4 0.4 %collective-permute-done.2.halo_ref = f32[2,256,256]{2,1,0:T(8,128)S(1)} collective-permute-done((f32[2,256,256]{2,1,0:T(8,128)S(1)}, f32[2,256,256]{2,1,0:T(8,128)S(1)}, u32[]{:S(2)}, u32[]{:S(2)}) %collective-permute-start.2) | collective-permute-done | bytes 524320 | tf_op jit(solution)/shard_map/ppermute | solution.py:23
  15.8 2.4 %shard_map.68 = (f32[2,2,256,256]{3,2,1,0:T(8,128)S(1)}, f32[2,2,256,256]{3,2,1,0:T(8,128)S(1)}) custom-call(s32[1,2]{1,0:T(1,128)S(1)} %get-tuple-element.19.pos_ref, f32[2,2,256,512]{3,2,1,0:T(8,128)S(1)} %get-tuple-element.20.object_ref, f32[2,256,256]{2,1,0:T(8,128)S(1)} %collective-permute-done.2.halo_ref, ...), custom_call_target="tpu_custom_call" | custom-call | flops 1610612736 | bytes 3145728 | tf_op jit(solution)/shard_map/pallas_call | solution.py:429
  18.2 3.2 %collective-permute-done.1.halo_ref = f32[2,256,256]{2,1,0:T(8,128)S(1)} collective-permute-done((f32[2,256,256]{2,1,0:T(8,128)S(1)}, f32[2,256,256]{2,1,0:T(8,128)S(1)}, u32[]{:S(2)}, u32[]{:S(2)}) %collective-permute-start.1) | collective-permute-done | bytes 524320 | tf_op jit(solution)/shard_map/ppermute | solution.py:23
  21.4 2.4 %shard_map.69 = (f32[2,128,256]{2,1,0:T(8,128)S(1)}, f32[2,2,256,256]{3,2,1,0:T(8,128)S(1)}) custom-call(s32[1,2]{1,0:T(1,128)S(1)} %get-tuple-element.19.pos_ref, f32[2,2,256,512]{3,2,1,0:T(8,128)S(1)} %get-tuple-element.20.object_ref, f32[2,256,256]{2,1,0:T(8,128)S(1)} %collective-permute-done.1.halo_ref, ...), custom_call_target="tpu_custom_call" | custom-call | flops 1610612736 | bytes 4194304 | tf_op jit(solution)/shard_map/pallas_call | solution.py:437
  23.9 0.1 collective-permute-start.6
  23.9 1.9 %shard_map.70.own_ref = f32[2,128,256]{2,1,0:T(8,128)S(1)} custom-call(f32[2,2,256,256]{3,2,1,0:T(8,128)S(1)} %get-tuple-element.30.chi_ref, f32[2,2,256,256]{3,2,1,0:T(8,128)S(1)} %get-tuple-element.31.probe_ref, f32[256,256]{1,0:T(8,128)S(1)} %get-tuple-element.24.kr_ref, f32[256,256]{1,0:T(8,128)S(1)} %get-tuple-element.25.ki_ref, ...), custom_call_target="tpu_custom_call" | custom-call | flops 1610612736 | bytes 2097152 | tf_op jit(solution)/shard_map/pallas_call | solution.py:446
  25.9 0.1 collective-permute-start.5
  25.9 6.7 %collective-permute-done.6.came_ref = f32[2,128,256]{2,1,0:T(8,128)S(1)} collective-permute-done((f32[2,128,256]{2,1,0:T(8,128)S(1)}, f32[2,128,256]{2,1,0:T(8,128)S(1)}, u32[]{:S(2)}, u32[]{:S(2)}) %collective-permute-start.6) | collective-permute-done | bytes 262176 | tf_op jit(solution)/shard_map/ppermute | solution.py:23
  32.6 0.9 %shard_map.71.refs_0_ = f32[2,2,128,512]{3,2,1,0:T(8,128)} custom-call(s32[1,2]{1,0:T(1,128)S(1)} %get-tuple-element.19.pos_ref, s32[1,2]{1,0:T(1,128)S(1)} %collective-permute-done.before_ref, f32[2,128,256]{2,1,0:T(8,128)S(1)} %get-tuple-element.32.own_ref, f32[2,128,256]{2,1,0:T(8,128)S(1)} %collective-permute-done.6.came_ref), custom_call_target="tpu_custom_call" | custom-call | bytes 1048576 | tf_op jit(solution)/shard_map/pallas_call | solution.py:361
  33.5 1.9 %collective-permute-done.5.came_ref = f32[2,128,256]{2,1,0:T(8,128)S(1)} collective-permute-done((f32[2,128,256]{2,1,0:T(8,128)S(1)}, f32[2,128,256]{2,1,0:T(8,128)S(1)}, u32[]{:S(2)}, u32[]{:S(2)}) %collective-permute-start.5) | collective-permute-done | bytes 262176 | tf_op jit(solution)/shard_map/ppermute | solution.py:23
  35.4 0.9 %shard_map.72 = f32[2,2,128,512]{3,2,1,0:T(8,128)} custom-call(s32[1,2]{1,0:T(1,128)S(1)} %get-tuple-element.19.pos_ref, s32[1,2]{1,0:T(1,128)S(1)} %collective-permute-done.before_ref, f32[2,128,256]{2,1,0:T(8,128)S(1)} %shard_map.70.own_ref, f32[2,128,256]{2,1,0:T(8,128)S(1)} %collective-permute-done.5.came_ref, ...), custom_call_target="tpu_custom_call", output_to_operand_aliasing={{}: (4, {})} | custom-call | bytes 1048576 | tf_op jit(solution)/shard_map/pallas_call | solution.py:361
Async XLA Ops:
  0.0 6.9 %collective-permute-start = (s32[1,2]{1,0:T(1,128)}, s32[1,2]{1,0:T(1,128)S(1)}, u32[]{:S(2)}, u32[]{:S(2)}) collective-permute-start(s32[1,2]{1,0:T(1,128)} %pos_hbm.3), channel_id=1, source_target_pairs={{0,2},{2,4},{4,6},{6,8},{8,10},{10,12},{12,14},{14,16},{16,18},{18... | collective-permute-start | bytes 32 | tf_op jit(solution)/shard_map/ppermute | solution.py:23
  2.2 8.6 %collective-permute-start.3 = (f32[256,256]{1,0:T(8,128)S(1)}, f32[256,256]{1,0:T(8,128)S(1)}, u32[]{:S(2)}, u32[]{:S(2)}) collective-permute-start(f32[256,256]{1,0:T(8,128)S(1)} %get-tuple-element.27), channel_id=1, source_target_pairs={{0,1},{1,0},{2,3},{3,2},{4,5},{5,4},{6,7},{7,6},{8,9},{9,8},{10,11... | collective-permute-start | bytes 786440 | tf_op jit(solution)/shard_map/ppermute | solution.py:23
  7.0 8.8 %collective-permute-start.2 = (f32[2,256,256]{2,1,0:T(8,128)S(1)}, f32[2,256,256]{2,1,0:T(8,128)S(1)}, u32[]{:S(2)}, u32[]{:S(2)}) collective-permute-start(f32[2,256,256]{2,1,0:T(8,128)S(1)} %get-tuple-element.22), channel_id=1, source_target_pairs={{0,30},{2,0},{4,2},{6,4},{8,6},{10,8},{12,10},{14,12},{16,14},{18,... | collective-permute-start | bytes 1572872 | tf_op jit(solution)/shard_map/ppermute | solution.py:23
  9.1 12.3 %collective-permute-start.1 = (f32[2,256,256]{2,1,0:T(8,128)S(1)}, f32[2,256,256]{2,1,0:T(8,128)S(1)}, u32[]{:S(2)}, u32[]{:S(2)}) collective-permute-start(f32[2,256,256]{2,1,0:T(8,128)S(1)} %get-tuple-element.21), channel_id=1, source_target_pairs={{0,30},{2,0},{4,2},{6,4},{8,6},{10,8},{12,10},{14,12},{16,14},{18,... | collective-permute-start | bytes 1572872 | tf_op jit(solution)/shard_map/ppermute | solution.py:23
  10.8 4.6 %collective-permute-start.4 = (f32[256,256]{1,0:T(8,128)S(1)}, f32[256,256]{1,0:T(8,128)S(1)}, u32[]{:S(2)}, u32[]{:S(2)}) collective-permute-start(f32[256,256]{1,0:T(8,128)S(1)} %collective-permute-done.3.refs_0_), channel_id=1, source_target_pairs={{0,2},{2,0},{4,6},{6,4},{8,10},{10,8},{12,14},{14,12},{16,18},{18,... | collective-permute-start | bytes 786440 | tf_op jit(solution)/shard_map/ppermute | solution.py:428
  23.9 8.7 %collective-permute-start.6 = (f32[2,128,256]{2,1,0:T(8,128)S(1)}, f32[2,128,256]{2,1,0:T(8,128)S(1)}, u32[]{:S(2)}, u32[]{:S(2)}) collective-permute-start(f32[2,128,256]{2,1,0:T(8,128)S(1)} %get-tuple-element.32.own_ref), channel_id=1, source_target_pairs={{0,2},{2,4},{4,6},{6,8},{8,10},{10,12},{12,14},{14,16},{16,18},{18... | collective-permute-start | bytes 786440 | tf_op jit(solution)/shard_map/ppermute | solution.py:23
  25.9 9.5 %collective-permute-start.5 = (f32[2,128,256]{2,1,0:T(8,128)S(1)}, f32[2,128,256]{2,1,0:T(8,128)S(1)}, u32[]{:S(2)}, u32[]{:S(2)}) collective-permute-start(f32[2,128,256]{2,1,0:T(8,128)S(1)} %shard_map.70.own_ref), channel_id=1, source_target_pairs={{0,2},{2,4},{4,6},{6,8},{8,10},{10,12},{12,14},{14,16},{16,18},{18... | collective-permute-start | bytes 786440 | tf_op jit(solution)/shard_map/ppermute | solution.py:23

commit v7 on v5

--- a/solution.py
+++ b/solution.py
@@ -156,8 +156,7 @@
     return top, mid, (left - mid.astype(F32)).astype(BF16)
 
 
-def by_parity(value):
-    size = value.shape[0]
+def parity_picks(size):
     h = size // 2
     picks = []
     for along in (0, 1):
@@ -165,6 +164,10 @@
         source = lax.broadcasted_iota(jnp.int32, (size, size), 1 - along)
         wanted = jnp.where(place < h, 2 * place, 2 * (place - h) + 1)
         picks.append(jnp.where(source == wanted, 1.0, 0.0).astype(BF16))
+    return picks
+
+
+def by_parity(value, picks):
     top, mid, low = thirds(value)
     value = (dot(picks[0], top) + dot(picks[0], mid)) + dot(picks[0], low)
     top, mid, low = thirds(value)
@@ -180,6 +183,26 @@
     for copy in copies:
         copy.start()
     return copies
+
+
+def is_odd():
+    return lax.rem(lax.axis_index("frame"), 2) == 1
+
+
+def spread(ref, frame, which, shape):
+    return jnp.broadcast_to(ref[frame : frame + 1, which : which + 1], shape)
+
+
+def turn_of(at_ref, frame, size):
+    row = jnp.sum(at_ref[frame : frame + 1, 0:1])
+    return row, lax.rem(jnp.sum(at_ref[frame : frame + 1, 1:2]), size)
+
+
+def owned(at_ref, frame, shape, start=0):
+    gap = lax.broadcasted_iota(jnp.int32, shape, 0) + start - spread(at_ref, frame, 0, shape)
+    odd = is_odd()
+    low = odd if frame == 0 else jnp.logical_not(odd)
+    return jnp.where(low, gap, -1 - gap) < 0
 
 
 def load_body(pos_hbm, probe_hbm, object_hbm, pos_out, plane_out, object_out, sem):
@@ -194,74 +217,64 @@
         copy.wait()
 
 
-def turn_body(pos_ref, *refs):
-    half = len(refs) // 2
-    for came, out in zip(refs[:half], refs[half:]):
-        out[...] = turned(came[...], pos_ref[0, 0], lax.rem(pos_ref[0, 1], came.shape[1]))
+def send_body(pos_ref, before_ref, object_ref, at_ref, even_ref, zero_ref, one_ref):
+    size = object_ref.shape[-2]
+    odd = is_odd()
+    at_ref[0:1] = jnp.where(odd, before_ref[...], pos_ref[...])
+    at_ref[1:2] = jnp.where(odd, pos_ref[...], before_ref[...])
+    c = lax.broadcasted_iota(jnp.int32, (size, size), 1)
+    even_right, odd_right = c < spread(at_ref, 0, 1, c.shape), c < spread(at_ref, 1, 1, c.shape)
+    for s, out in enumerate((zero_ref, one_ref)):
+        for part in range(2):
+            left, right = object_ref[s, part, :, :size], object_ref[s, part, :, size:]
+            even_ref[s, part] = jnp.where(even_right, right, left)
+            out[part] = jnp.where(odd_right, right, left)
 
 
 def prepare_body(
-    pos_hbm, probe_hbm, prop_hbm, amp_hbm, tab_hbm,
+    at_ref, prev_ref, probe_hbm, prop_hbm, amp_hbm, tab_hbm,
     wave_re, wave_im, amp_out, first_out, tab_out,
-    pos, probe, prop, amp, sem,
+    probe, prop, amp, sem,
 ):
-    copies = run_copies(
-        ((pos_hbm, pos), (probe_hbm, probe), (prop_hbm, prop), (amp_hbm, amp), (tab_hbm, tab_out)), sem
-    )
+    copies = run_copies(((probe_hbm, probe), (prop_hbm, prop), (amp_hbm, amp), (tab_hbm, tab_out)), sem)
+    size = prop.shape[0]
+    picks = parity_picks(size)
     copies[0].wait()
+    for frame in range(2):
+        turn = turn_of(at_ref, frame, size)
+        for c in range(2):
+            first_out[frame, c] = turned(probe[0, c], *turn)
     copies[1].wait()
-    size = prop.shape[0]
-    row, col = pos[0, 0], lax.rem(pos[0, 1], size)
-    for c in range(2):
-        first_out[0, c] = turned(probe[0, c], row, col)
-    copies[2].wait()
-    phase = by_parity(prop[...])
+    phase = by_parity(prop[...], picks)
     wave_re[...] = jnp.cos(phase)
     wave_im[...] = jnp.sin(phase)
+    copies[2].wait()
+    odd = is_odd()
+    amp_out[0] = by_parity(jnp.where(odd, prev_ref[0], amp[0]), picks)
+    amp_out[1] = by_parity(jnp.where(odd, amp[0], prev_ref[0]), picks)
     copies[3].wait()
-    amp_out[...] = by_parity(amp[0])
-    copies[4].wait()
-
-
-def spread(ref, which, shape):
-    return jnp.broadcast_to(ref[0:1, which : which + 1], shape)
-
-
-def wrapped(ref, s, part, col_ref):
-    size = ref.shape[-2]
-    c = lax.broadcasted_iota(jnp.int32, (size, size), 1)
-    return jnp.where(c < spread(col_ref, 1, c.shape), ref[s, part, :, size:], ref[s, part, :, :size])
-
-
-def send_body(before_ref, object_ref, zero_ref, one_ref):
-    for s, out in enumerate((zero_ref, one_ref)):
-        for part in range(2):
-            out[part] = wrapped(object_ref, s, part, before_ref)
-
-
-def patch_of(s, object_ref, halo_ref, pos_ref):
-    size = halo_ref.shape[-1]
-    r = lax.broadcasted_iota(jnp.int32, (size, size), 0)
-    return [
-        jnp.where(r < spread(pos_ref, 0, r.shape), halo_ref[part], wrapped(object_ref, s, part, pos_ref))
-        for part in range(2)
-    ]
+
+
+def patch_of(frame, at_ref, own, came):
+    mine = owned(at_ref, frame, own[0].shape)
+    return [jnp.where(mine, own[part], came[part]) for part in range(2)]
 
 
 def pair(ref, *at):
     return ref[(*at, 0)], ref[(*at, 1)]
 
 
-def inner_body(pos, pos_ref, object_ref, halo_ref, first_ref, kr_ref, ki_ref, tab, *refs):
+def inner_body(frame, at_ref, own_ref, came_ref, first_ref, kr_ref, ki_ref, tab, *refs):
     out_ref, probe_ref, patch = refs[-3:]
     states = out_ref.shape[0]
-    patch[0], patch[1] = patch_of(0, object_ref, halo_ref, pos_ref)
-    swap = lax.rem(lax.axis_index("frame"), 2) == 1
-    probe_ref[:1] = first_ref[...]
-    for m, (came, given) in enumerate(zip(refs[:-3:2], refs[1:-3:2])):
-        other = turned(given[...], pos[0, 0], lax.rem(pos[0, 1], given.shape[1]))
-        probe_ref[1 + m, 0] = jnp.where(swap, other, came[...])
-        probe_ref[1 + m, 1] = jnp.where(swap, came[...], other)
+    own, came = (own_ref.at[0], came_ref.at[0]) if frame == 0 else (own_ref, came_ref)
+    patch[0], patch[1] = patch_of(frame, at_ref, own, came)
+    odd = is_odd()
+    turn = turn_of(at_ref, frame, patch.shape[-1])
+    probe_ref[0] = first_ref[frame]
+    for m, (plane, swapped) in enumerate(zip(refs[:-3:2], refs[1:-3:2])):
+        probe_ref[1 + m, 0] = turned(jnp.where(odd, swapped[...], plane[...]), *turn)
+        probe_ref[1 + m, 1] = turned(jnp.where(odd, plane[...], swapped[...]), *turn)
 
     def body(group):
         waves = forward([times(pair(probe_ref, m), pair(patch)) for m in group], tab)
@@ -272,9 +285,10 @@
     in_groups(states, body)
 
 
-def middle_body(rows, pos_ref, object_ref, halo_ref, inner_ref, amp_ref, tab, term_ref, chi_ref, patch, far, power):
+def middle_body(frame, rows, at_ref, own_ref, came_ref, inner_ref, amp_ref, tab, term_ref, chi_ref, patch, far, power):
     states = inner_ref.shape[0]
-    patch[0], patch[1] = patch_of(1, object_ref, halo_ref, pos_ref)
+    own, came = (own_ref.at[1], came_ref.at[1]) if frame == 0 else (own_ref, came_ref)
+    patch[0], patch[1] = patch_of(frame, at_ref, own, came)
     power[...] = jnp.zeros_like(power)
 
     def outward(group):
@@ -286,7 +300,7 @@
         power[...] = total
 
     in_groups(states, outward)
-    power[...] = 1.0 - amp_ref[...] / jnp.sqrt(power[...] + 1.0)
+    power[...] = 1.0 - amp_ref[frame] * lax.rsqrt(power[...] + 1.0)
     term_ref[...] = jnp.zeros_like(term_ref)
     take = pl.ds(pl.multiple_of(lax.axis_index("state") * rows, rows), rows)
 
@@ -324,37 +338,37 @@
     in_groups(states, body)
 
 
-def gather_body(slice_id, rows, pos_ref, before_ref, own_ref, came_ref, *refs):
-    out_ref, held, sem = refs[-3:]
-    size = own_ref.shape[-1]
+def finish_body(rows, at_ref, one_even, zero_even, one_odd, chi_ref, probe_ref, kr_ref, ki_ref, tab, out_ref, front, term, held, sem):
+    size = front.shape[-1]
     start = lax.axis_index("state") * rows
-    r = lax.broadcasted_iota(jnp.int32, (rows, size), 0) + start
     c = lax.broadcasted_iota(jnp.int32, (rows, size), 1)
-    here, there = r >= spread(pos_ref, 0, r.shape), r < spread(before_ref, 0, r.shape)
-    here_right, there_right = c < spread(pos_ref, 1, c.shape), c < spread(before_ref, 1, c.shape)
-    copies = []
-    for part in range(2):
-        mine = jnp.where(here, own_ref[part], 0.0)
-        theirs = jnp.where(there, came_ref[part], 0.0)
-        held[part, :, :size] = jnp.where(here_right, 0.0, mine) + jnp.where(there_right, 0.0, theirs)
-        held[part, :, size:] = jnp.where(here_right, mine, 0.0) + jnp.where(there_right, theirs, 0.0)
-        copies.append(pltpu.make_async_copy(held.at[part], out_ref.at[slice_id, part], sem.at[part]))
-        copies[-1].start()
+    frames = [(owned(at_ref, k, c.shape, start), c < spread(at_ref, k, 1, c.shape)) for k in range(2)]
+    chunks = 2 if rows % 16 == 0 else 1
+    step = rows // chunks
+
+    def leave(s, terms):
+        copies = []
+        for chunk in range(chunks):
+            at = pl.ds(chunk * step, step)
+            cut = slice(chunk * step, chunk * step + step)
+            for part in range(2):
+                left, right = 0.0, 0.0
+                for (mine, over), given in zip(frames, terms):
+                    value = jnp.where(mine[cut], given[part, at], 0.0)
+                    left += jnp.where(over[cut], 0.0, value)
+                    right += jnp.where(over[cut], value, 0.0)
+                held[s, part, at, :size] = left
+                held[s, part, at, size:] = right
+                place = (s * chunks + chunk) * 2 + part
+                copies.append(pltpu.make_async_copy(held.at[s, part, at], out_ref.at[s, part, at], sem.at[place]))
+                copies[-1].start()
+        return copies
+
+    copies = leave(1, (one_even, one_odd))
+    last_body(rows, chi_ref, probe_ref, kr_ref, ki_ref, tab, term, front)
+    copies += leave(0, (zero_even, term))
     for copy in copies:
         copy.wait()
-
-
-def gather(slice_id, rows, size, pos, before, own, came, *given):
-    return pl.pallas_call(
-        functools.partial(gather_body, slice_id, rows),
-        out_shape=jax.ShapeDtypeStruct((2, 2, rows, 2 * size), F32),
-        in_specs=[VMEM] * 4 + [pl.BlockSpec(memory_space=pl.ANY)] * len(given),
-        out_specs=pl.BlockSpec(memory_space=pl.ANY),
-        scratch_shapes=[pltpu.VMEM((2, rows, 2 * size), F32), pltpu.SemaphoreType.DMA((2,))],
-        input_output_aliases={4: 0} if given else {},
-        compiler_params=pltpu.CompilerParams(vmem_limit_bytes=LIMIT),
-        cost_estimate=pl.CostEstimate(flops=0, bytes_accessed=32 * rows * size, transcendentals=0),
-    )(pos, before, own, came, *given)
 
 
 def on_device(object_slices, probe, amplitude, positions, propagator):
@@ -370,8 +384,12 @@
     grid = (size, size)
     unit = size * size
     flops = 24 * size**3
+    frames = lax.axis_size("frame")
+    across = [(i, (i + 1) % frames if i % 2 else (i - 1) % frames) for i in range(frames)]
+    beside = [(i, i ^ 1) for i in range(frames)]
     tab = tables(size)
     before = shifted(positions, "frame", 1)
+    lent = shifted(amplitude, "frame", 1)
     given = [in_hbm(x) for x in (positions, probe, object_slices)]
     pos, plane, held = pl.pallas_call(
         load_body,
@@ -386,61 +404,86 @@
         compiler_params=pltpu.CompilerParams(vmem_limit_bytes=LIMIT),
         cost_estimate=pl.CostEstimate(flops=0, bytes_accessed=40 * unit, transcendentals=0),
     )(*given)
-    picked = call(send_body, [(2,) + grid] * 2, [VMEM, VMEM], moved=16 * unit)(before, held)
-    halo_zero = shifted(picked[0], "frame", -1)
-    halo_one = shifted(picked[1], "frame", -1)
     planes = []
     for by in range(1, states):
         planes.append(shifted(plane, "state", by))
-    kr, ki, amp, first, tab = pl.pallas_call(
+    at, even, zero, one = pl.pallas_call(
+        send_body,
+        out_shape=[jax.ShapeDtypeStruct((2, 2), jnp.int32)]
+        + [jax.ShapeDtypeStruct(shape, F32) for shape in ((2, 2) + grid, (2,) + grid, (2,) + grid)],
+        in_specs=[VMEM] * 3,
+        out_specs=[VMEM] * 4,
+        compiler_params=pltpu.CompilerParams(vmem_limit_bytes=LIMIT),
+        cost_estimate=pl.CostEstimate(flops=0, bytes_accessed=64 * unit, transcendentals=0),
+    )(pos, before, held)
+    came_zero = lax.ppermute(zero, "frame", across)
+    came_one = lax.ppermute(one, "frame", across)
+    came_even = lax.ppermute(even, "frame", beside)
+    kr, ki, amps, first, tab = pl.pallas_call(
         prepare_body,
-        out_shape=[jax.ShapeDtypeStruct(grid, F32)] * 3
-        + [jax.ShapeDtypeStruct(x.shape, x.dtype) for x in (probe, tab)],
-        in_specs=[HBM] * 5,
+        out_shape=[jax.ShapeDtypeStruct(shape, F32) for shape in (grid, grid, (2,) + grid, (2, 2) + grid)]
+        + [jax.ShapeDtypeStruct(tab.shape, tab.dtype)],
+        in_specs=[VMEM] * 2 + [HBM] * 4,
         out_specs=[VMEM] * 5,
         scratch_shapes=[
-            pltpu.SMEM(positions.shape, jnp.int32),
             pltpu.VMEM(probe.shape, F32),
             pltpu.VMEM(grid, F32),
             pltpu.VMEM(amplitude.shape, F32),
-            pltpu.SemaphoreType.DMA((5,)),
+            pltpu.SemaphoreType.DMA((4,)),
         ],
         compiler_params=pltpu.CompilerParams(vmem_limit_bytes=LIMIT),
         cost_estimate=pl.CostEstimate(flops=2 * size**3, bytes_accessed=60 * unit, transcendentals=0),
-    )(*given[:2], *(in_hbm(x) for x in (propagator, amplitude, tab)))
-    frames = lax.axis_size("frame")
-    own = call(turn_body, [grid] * len(planes), [SMEM] + [VMEM] * len(planes), moved=16 * unit)(pos, *planes)
+    )(at, lent, given[1], *(in_hbm(x) for x in (propagator, amplitude, tab)))
     pairs = []
-    for came, kept in zip(planes, own):
-        pairs += [kept, lax.ppermute(came, "frame", [(i, i ^ 1) for i in range(frames)])]
-    waves, probes = call(
-        inner_body,
-        [(states, 2) + grid] * 2,
-        [SMEM] + [VMEM] * (7 + len(pairs)),
-        [pltpu.VMEM((2,) + grid, F32)],
-        flops=2 * flops * states,
-        moved=24 * unit * states,
-    )(pos, pos, held, halo_zero, first, kr, ki, tab, *pairs)
-    term_one, chi = call(
-        functools.partial(middle_body, rows),
-        [(2, rows, size), (states, 2) + grid],
-        [VMEM] * 6,
-        [pltpu.VMEM((2,) + grid, F32), pltpu.VMEM((states, 2) + grid, F32), pltpu.VMEM(grid, F32)],
-        flops=2 * flops * states,
-        moved=32 * unit * states,
-    )(pos, held, halo_one, waves, amp, tab)
-    came_one = shifted(term_one, "frame", 1)
-    (term_zero,) = call(
+    for plane in planes:
+        pairs += [plane, lax.ppermute(plane, "frame", beside)]
+
+    def inner(frame, own, came):
+        return call(
+            functools.partial(inner_body, frame),
+            [(states, 2) + grid] * 2,
+            [VMEM] * (7 + len(pairs)),
+            [pltpu.VMEM((2,) + grid, F32)],
+            flops=2 * flops * states,
+            moved=24 * unit * states,
+        )(at, own, came, first, kr, ki, tab, *pairs)
+
+    def middle(frame, own, came, waves):
+        return call(
+            functools.partial(middle_body, frame, rows),
+            [(2, rows, size), (states, 2) + grid],
+            [VMEM] * 6,
+            [pltpu.VMEM((2,) + grid, F32), pltpu.VMEM((states, 2) + grid, F32), pltpu.VMEM(grid, F32)],
+            flops=2 * flops * states,
+            moved=32 * unit * states,
+        )(at, own, came, waves, amps, tab)
+
+    even_waves, even_probes = inner(0, even, came_even)
+    waves, probes = inner(1, zero, came_zero)
+    one_even, chi = middle(0, even, came_even, even_waves)
+    (zero_even,) = call(
         functools.partial(last_body, rows),
         [(2, rows, size)],
         [VMEM] * 5,
         [pltpu.VMEM((states, 2) + grid, F32)],
         flops=2 * flops * states,
         moved=16 * unit * states,
-    )(chi, probes, kr, ki, tab)
-    came_zero = shifted(term_zero, "frame", 1)
-    gradient = gather(1, rows, size, pos, before, term_one, came_one)
-    return gather(0, rows, size, pos, before, term_zero, came_zero, gradient)
+    )(chi, even_probes, kr, ki, tab)
+    one_odd, chi = middle(1, one, came_one, waves)
+    return pl.pallas_call(
+        functools.partial(finish_body, rows),
+        out_shape=jax.ShapeDtypeStruct((2, 2, rows, 2 * size), F32),
+        in_specs=[VMEM] * 9,
+        out_specs=pl.BlockSpec(memory_space=pl.ANY),
+        scratch_shapes=[
+            pltpu.VMEM((states, 2) + grid, F32),
+            pltpu.VMEM((2, rows, size), F32),
+            pltpu.VMEM((2, 2, rows, 2 * size), F32),
+            pltpu.SemaphoreType.DMA((8,)),
+        ],
+        compiler_params=pltpu.CompilerParams(vmem_limit_bytes=LIMIT),
+        cost_estimate=pl.CostEstimate(flops=2 * flops * states, bytes_accessed=32 * unit * states, transcendentals=0),
+    )(at, one_even, zero_even, one_odd, chi, probes, kr, ki, tab)
 
 
 def solution(mesh):

time: 36.6 us -> 53.9 us (1.47)
  the two profiles are of different devices: /device:TPU:0 before, /device:TPU:1 now
where the time goes in v7:
time: 53.9 us; the launch traced here: 53.7 us
  waiting for transfers between devices  23.3 us (43%)
  Pallas kernels  20.9 us (39%)
  starting transfers between devices  9.42 us (17%)
    ppermute x3, waiting for transfers between devices, shifted(): lax.ppermute(value, axis, [(i, (i + by) % count) for i in range(count)])  23.3 us
    pallas_call x2, Pallas kernels, middle(): call(functools.partial(middle_body, frame, rows), [(2, rows, size), (stat...  4.94 us
    pallas_call x2, Pallas kernels, inner(): call(functools.partial(inner_body, frame), [(states, 2) + grid] * 2, [VME...  4.9 us
    ppermute x3, starting transfers between devices, shifted(): lax.ppermute(value, axis, [(i, (i + by) % count) for i in range(count)])  4.31 us
    pallas_call x1, Pallas kernels, gradient_of(): pl.pallas_call(prepare_body, out_shape=[jax.ShapeDtypeStruct(shape, F32)...  4.13 us
    pallas_call x1, Pallas kernels, gradient_of(): pl.pallas_call(functools.partial(finish_body, rows), out_shape=jax.ShapeD...  2.96 us
    ppermute x1, starting transfers between devices, gradient_of(): came_even = lax.ppermute(even, 'frame', beside)  2.62 us
    pallas_call x1, Pallas kernels, gradient_of(): call(functools.partial(last_body, rows), [(2, rows, size)], [VMEM] * 5, [...  1.96 us
  transfers between devices with their start and end apart: 7, of which 2 were waited for; matrix products, arithmetic and copies ran while one was open for 0% of the time, Pallas kernels for 20%

profile of v7, /device:TPU:1, one launch (start us, length us, event | category | flops | bytes accessed | tf_op | source)
XLA Modules:
  0.0 53.7 jit_solution(2614746798200033061)
XLA Ops:
  0.0 0.0 copy-start
  0.0 2.6 %collective-permute-start = (s32[1,2]{1,0:T(1,128)}, s32[1,2]{1,0:T(1,128)S(1)}, u32[]{:S(2)}, u32[]{:S(2)}) collective-permute-start(s32[1,2]{1,0:T(1,128)} %pos_hbm.1), channel_id=1, source_target_pairs={{0,2},{2,4},{4,6},{6,8},{8,10},{10,12},{12,14},{14,16},{16,18},{18... | collective-permute-start | bytes 32 | tf_op jit(solution)/shard_map/ppermute | solution.py:23
  2.6 1.7 %shard_map.64 = (s32[1,2]{1,0:T(1,128)S(1)}, f32[256,256]{1,0:T(8,128)S(1)}, f32[2,2,256,512]{3,2,1,0:T(8,128)S(1)}) custom-call(s32[1,2]{1,0:T(1,128)} %pos_hbm.1, f32[1,2,256,256]{3,2,1,0:T(8,128)} %probe_hbm.3, f32[2,2,256,512]{3,2,1,0:T(8,128)} %object_hbm.1), custom_call_target="tpu_custom_call" | custom-call | bytes 2621440 | tf_op jit(solution)/shard_map/pallas_call | solution.py:394
  4.3 0.0 collective-permute-done.before_ref
  4.3 0.3 shard_map.65
  4.7 2.6 %collective-permute-start.1 = (f32[2,2,256,256]{3,2,1,0:T(8,128)S(1)}, f32[2,2,256,256]{3,2,1,0:T(8,128)S(1)}, u32[]{:S(2)}, u32[]{:S(2)}) collective-permute-start(f32[2,2,256,256]{3,2,1,0:T(8,128)S(1)} %get-tuple-element.28.own_ref), channel_id=1, source_target_pairs={{0,2},{2,0},{4,6},{6,4},{8,10},{10,8},{12,14},{14,12},{16,18},{18,... | collective-permute-start | bytes 3145736 | tf_op jit(solution)/shard_map/ppermute | solution.py:421
  7.3 1.7 %collective-permute-start.3 = (f32[256,256]{1,0:T(8,128)S(1)}, f32[256,256]{1,0:T(8,128)S(1)}, u32[]{:S(2)}, u32[]{:S(2)}) collective-permute-start(f32[256,256]{1,0:T(8,128)S(1)} %get-tuple-element.33), channel_id=1, source_target_pairs={{0,1},{1,0},{2,3},{3,2},{4,5},{5,4},{6,7},{7,6},{8,9},{9,8},{10,11... | collective-permute-start | bytes 786440 | tf_op jit(solution)/shard_map/ppermute | solution.py:23
  8.9 0.0 collective-permute-start.6
  9.0 1.7 %collective-permute-start.5 = (f32[2,256,256]{2,1,0:T(8,128)S(1)}, f32[2,256,256]{2,1,0:T(8,128)S(1)}, u32[]{:S(2)}, u32[]{:S(2)}) collective-permute-start(f32[2,256,256]{2,1,0:T(8,128)S(1)} %get-tuple-element.39.own_ref), channel_id=1, source_target_pairs={{0,30},{2,4},{4,2},{6,8},{8,6},{10,12},{12,10},{14,16},{16,14},{18... | collective-permute-start | bytes 1572872 | tf_op jit(solution)/shard_map/ppermute | solution.py:420
  10.7 0.0 copy-done
  10.7 0.0 collective-permute-start.2
  10.7 4.7 %collective-permute-done.3.refs_0_ = f32[256,256]{1,0:T(8,128)S(1)} collective-permute-done((f32[256,256]{1,0:T(8,128)S(1)}, f32[256,256]{1,0:T(8,128)S(1)}, u32[]{:S(2)}, u32[]{:S(2)}) %collective-permute-start.3) | collective-permute-done | bytes 262176 | tf_op jit(solution)/shard_map/ppermute | solution.py:23
  15.5 0.7 %collective-permute-start.4 = (f32[256,256]{1,0:T(8,128)S(1)}, f32[256,256]{1,0:T(8,128)S(1)}, u32[]{:S(2)}, u32[]{:S(2)}) collective-permute-start(f32[256,256]{1,0:T(8,128)S(1)} %collective-permute-done.3.refs_0_), channel_id=1, source_target_pairs={{0,2},{2,0},{4,6},{6,4},{8,10},{10,8},{12,14},{14,12},{16,18},{18,... | collective-permute-start | bytes 786440 | tf_op jit(solution)/shard_map/ppermute | solution.py:439
  16.2 18.5 %collective-permute-done.2.prev_ref = f32[1,256,256]{2,1,0:T(8,128)S(1)} collective-permute-done((f32[1,256,256]{2,1,0:T(8,128)S(1)}, f32[1,256,256]{2,1,0:T(8,128)S(1)}, u32[]{:S(2)}, u32[]{:S(2)}) %collective-permute-start.2) | collective-permute-done | bytes 262176 | tf_op jit(solution)/shard_map/ppermute | solution.py:23
  34.7 4.1 %shard_map.66 = (f32[256,256]{1,0:T(8,128)S(1)}, f32[256,256]{1,0:T(8,128)S(1)}, f32[2,256,256]{2,1,0:T(8,128)S(1)}, f32[2,2,256,256]{3,2,1,0:T(8,128)S(1)}, bf16[2,4,256,256]{3,2,1,0:T(8,128)(2,1)S(1)}) custom-call(s32[2,2]{1,0:T(2,128)S(1)} %get-tuple-element.27.at_ref, f32[1,256,256]{2,1,0:T(8,128)S(1)} %collective-permute-done.2.prev_ref, ...), custom_call_target="tpu_custom_call" | custom-call | flops 33554432 | bytes 3932160 | tf_op jit(solution)/shard_map/pallas_call | solution.py:422
  38.9 0.0 collective-permute-done.4.refs_1_
  38.9 0.0 collective-permute-done.6.came_ref
  38.9 2.5 %shard_map.70 = (f32[2,2,256,256]{3,2,1,0:T(8,128)S(1)}, f32[2,2,256,256]{3,2,1,0:T(8,128)S(1)}) custom-call(s32[2,2]{1,0:T(2,128)S(1)} %get-tuple-element.27.at_ref, f32[2,256,256]{2,1,0:T(8,128)S(1)} %get-tuple-element.40.own_ref, f32[2,256,256]{2,1,0:T(8,128)S(1)} %collective-permute-done.6.came_ref, f32[2,2,256,256]{3,2,1,0:T(8,128)S(1)} %get-tuple-element.29.first_ref, ...), custom_call_target="tpu_custom_call" | custom-call | flops 1610612736 | bytes 3145728 | tf_op jit(solution)/shard_map/pallas_call | solution.py:442
  41.4 0.0 collective-permute-done.5.came_ref
  41.4 2.5 %shard_map.71 = (f32[2,128,256]{2,1,0:T(8,128)S(1)}, f32[2,2,256,256]{3,2,1,0:T(8,128)S(1)}) custom-call(s32[2,2]{1,0:T(2,128)S(1)} %get-tuple-element.27.at_ref, f32[2,256,256]{2,1,0:T(8,128)S(1)} %get-tuple-element.39.own_ref, f32[2,256,256]{2,1,0:T(8,128)S(1)} %collective-permute-done.5.came_ref, f32[2,2,256,256]{3,2,1,0:T(8,128)S(1)} %get-tuple-element.41.inner_ref, ...), custom_call_target="tpu_custom_call" | custom-call | flops 1610612736 | bytes 4194304 | tf_op jit(solution)/shard_map/pallas_call | solution.py:452
  43.9 0.0 collective-permute-done.1.came_ref
  43.9 2.4 %shard_map.67 = (f32[2,2,256,256]{3,2,1,0:T(8,128)S(1)}, f32[2,2,256,256]{3,2,1,0:T(8,128)S(1)}) custom-call(s32[2,2]{1,0:T(2,128)S(1)} %get-tuple-element.27.at_ref, f32[2,2,256,256]{3,2,1,0:T(8,128)S(1)} %get-tuple-element.28.own_ref, f32[2,2,256,256]{3,2,1,0:T(8,128)S(1)} %collective-permute-done.1.came_ref, ...), custom_call_target="tpu_custom_call" | custom-call | flops 1610612736 | bytes 3145728 | tf_op jit(solution)/shard_map/pallas_call | solution.py:442
  46.3 2.5 %shard_map.68 = (f32[2,128,256]{2,1,0:T(8,128)S(1)}, f32[2,2,256,256]{3,2,1,0:T(8,128)S(1)}) custom-call(s32[2,2]{1,0:T(2,128)S(1)} %get-tuple-element.27.at_ref, f32[2,2,256,256]{3,2,1,0:T(8,128)S(1)} %get-tuple-element.28.own_ref, f32[2,2,256,256]{3,2,1,0:T(8,128)S(1)} %collective-permute-done.1.came_ref, ...), custom_call_target="tpu_custom_call" | custom-call | flops 1610612736 | bytes 4194304 | tf_op jit(solution)/shard_map/pallas_call | solution.py:452
  48.8 2.0 %shard_map.69.zero_even = f32[2,128,256]{2,1,0:T(8,128)S(1)} custom-call(f32[2,2,256,256]{3,2,1,0:T(8,128)S(1)} %get-tuple-element.37.chi_ref, f32[2,2,256,256]{3,2,1,0:T(8,128)S(1)} %get-tuple-element.38.probe_ref, f32[256,256]{1,0:T(8,128)S(1)} %get-tuple-element.30.kr_ref, f32[256,256]{1,0:T(8,128)S(1)} %get-tuple-element.31.ki_ref, ...), custom_call_target="tpu_custom_call" | custom-call | flops 1610612736 | bytes 2097152 | tf_op jit(solution)/shard_map/pallas_call | solution.py:464
  50.8 3.0 %shard_map.72 = f32[2,2,128,512]{3,2,1,0:T(8,128)} custom-call(s32[2,2]{1,0:T(2,128)S(1)} %get-tuple-element.27.at_ref, f32[2,128,256]{2,1,0:T(8,128)S(1)} %get-tuple-element.36.one_even, f32[2,128,256]{2,1,0:T(8,128)S(1)} %shard_map.69.zero_even, f32[2,128,256]{2,1,0:T(8,128)S(1)} %get-tuple-element.42.one_odd, ...), custom_call_target="tpu_custom_call" | custom-call | flops 1610612736 | bytes 4194304 | tf_op jit(solution)/shard_map/pallas_call | solution.py:473
Async XLA Ops:
  0.0 10.7 %copy-start = (f32[1,256,256]{2,1,0:T(8,128)S(1)}, f32[1,256,256]{2,1,0:T(8,128)}, u32[]{:S(2)}) copy-start(f32[1,256,256]{2,1,0:T(8,128)} %amp_hbm.1) | copy-start | bytes 786436
  0.0 4.3 %collective-permute-start = (s32[1,2]{1,0:T(1,128)}, s32[1,2]{1,0:T(1,128)S(1)}, u32[]{:S(2)}, u32[]{:S(2)}) collective-permute-start(s32[1,2]{1,0:T(1,128)} %pos_hbm.1), channel_id=1, source_target_pairs={{0,2},{2,4},{4,6},{6,8},{8,10},{10,12},{12,14},{14,16},{16,18},{18... | collective-permute-start | bytes 32 | tf_op jit(solution)/shard_map/ppermute | solution.py:23
  4.7 39.2 %collective-permute-start.1 = (f32[2,2,256,256]{3,2,1,0:T(8,128)S(1)}, f32[2,2,256,256]{3,2,1,0:T(8,128)S(1)}, u32[]{:S(2)}, u32[]{:S(2)}) collective-permute-start(f32[2,2,256,256]{3,2,1,0:T(8,128)S(1)} %get-tuple-element.28.own_ref), channel_id=1, source_target_pairs={{0,2},{2,0},{4,6},{6,4},{8,10},{10,8},{12,14},{14,12},{16,18},{18,... | collective-permute-start | bytes 3145736 | tf_op jit(solution)/shard_map/ppermute | solution.py:421
  7.3 8.2 %collective-permute-start.3 = (f32[256,256]{1,0:T(8,128)S(1)}, f32[256,256]{1,0:T(8,128)S(1)}, u32[]{:S(2)}, u32[]{:S(2)}) collective-permute-start(f32[256,256]{1,0:T(8,128)S(1)} %get-tuple-element.33), channel_id=1, source_target_pairs={{0,1},{1,0},{2,3},{3,2},{4,5},{5,4},{6,7},{7,6},{8,9},{9,8},{10,11... | collective-permute-start | bytes 786440 | tf_op jit(solution)/shard_map/ppermute | solution.py:23
  8.9 29.9 %collective-permute-start.6 = (f32[2,256,256]{2,1,0:T(8,128)S(1)}, f32[2,256,256]{2,1,0:T(8,128)S(1)}, u32[]{:S(2)}, u32[]{:S(2)}) collective-permute-start(f32[2,256,256]{2,1,0:T(8,128)S(1)} %get-tuple-element.40.own_ref), channel_id=1, source_target_pairs={{0,30},{2,4},{4,2},{6,8},{8,6},{10,12},{12,10},{14,16},{16,14},{18... | collective-permute-start | bytes 1572872 | tf_op jit(solution)/shard_map/ppermute | solution.py:419
  9.0 32.4 %collective-permute-start.5 = (f32[2,256,256]{2,1,0:T(8,128)S(1)}, f32[2,256,256]{2,1,0:T(8,128)S(1)}, u32[]{:S(2)}, u32[]{:S(2)}) collective-permute-start(f32[2,256,256]{2,1,0:T(8,128)S(1)} %get-tuple-element.39.own_ref), channel_id=1, source_target_pairs={{0,30},{2,4},{4,2},{6,8},{8,6},{10,12},{12,10},{14,16},{16,14},{18... | collective-permute-start | bytes 1572872 | tf_op jit(solution)/shard_map/ppermute | solution.py:420
  10.7 24.0 %collective-permute-start.2 = (f32[1,256,256]{2,1,0:T(8,128)S(1)}, f32[1,256,256]{2,1,0:T(8,128)S(1)}, u32[]{:S(2)}, u32[]{:S(2)}) collective-permute-start(f32[1,256,256]{2,1,0:T(8,128)S(1)} %copy-done), channel_id=1, source_target_pairs={{0,2},{2,4},{4,6},{6,8},{8,10},{10,12},{12,14},{14,16},{16,18},{18... | collective-permute-start | bytes 786440 | tf_op jit(solution)/shard_map/ppermute | solution.py:23
  15.5 23.4 %collective-permute-start.4 = (f32[256,256]{1,0:T(8,128)S(1)}, f32[256,256]{1,0:T(8,128)S(1)}, u32[]{:S(2)}, u32[]{:S(2)}) collective-permute-start(f32[256,256]{1,0:T(8,128)S(1)} %collective-permute-done.3.refs_0_), channel_id=1, source_target_pairs={{0,2},{2,0},{4,6},{6,4},{8,10},{10,8},{12,14},{14,12},{16,18},{18,... | collective-permute-start | bytes 786440 | tf_op jit(solution)/shard_map/ppermute | solution.py:439

commit v8 on v6

--- a/solution.py
+++ b/solution.py
@@ -194,77 +194,84 @@
         copy.wait()
 
 
-def turn_of(pos_ref, size):
-    return jnp.sum(pos_ref[0:1, 0:1]), lax.rem(jnp.sum(pos_ref[0:1, 1:2]), size)
-
-
-def turn_body(pos_ref, *refs):
+def flipped(paired):
+    return lax.axis_index("state") == 1 if paired else False
+
+
+def turn_of(at_ref, size):
+    return jnp.sum(at_ref[0:1, 0:1]), lax.rem(jnp.sum(at_ref[0:1, 1:2]), size)
+
+
+def turn_body(at_ref, *refs):
     half = len(refs) // 2
-    turn = turn_of(pos_ref, refs[0].shape[1])
+    turn = turn_of(at_ref, refs[0].shape[1])
     for came, out in zip(refs[:half], refs[half:]):
         out[...] = turned(came[...], *turn)
 
 
 def prepare_body(
-    pos_hbm, probe_hbm, prop_hbm, amp_hbm, tab_hbm,
+    paired, at_ref, lent_ref, probe_hbm, prop_hbm, amp_hbm, tab_hbm,
     wave_re, wave_im, amp_out, first_out, tab_out,
-    pos, probe, prop, amp, sem,
+    probe, prop, amp, sem,
 ):
-    copies = run_copies(
-        ((pos_hbm, pos), (probe_hbm, probe), (prop_hbm, prop), (amp_hbm, amp), (tab_hbm, tab_out)), sem
-    )
+    copies = run_copies(((probe_hbm, probe), (prop_hbm, prop), (amp_hbm, amp), (tab_hbm, tab_out)), sem)
+    size = prop.shape[0]
     copies[0].wait()
+    turn = turn_of(at_ref, size)
+    for c in range(2):
+        first_out[0, c] = turned(probe[0, c], *turn)
     copies[1].wait()
-    size = prop.shape[0]
-    row, col = pos[0, 0], lax.rem(pos[0, 1], size)
-    for c in range(2):
-        first_out[0, c] = turned(probe[0, c], row, col)
-    copies[2].wait()
     phase = by_parity(prop[...])
     wave_re[...] = jnp.cos(phase)
     wave_im[...] = jnp.sin(phase)
+    copies[2].wait()
+    amp_out[...] = by_parity(jnp.where(flipped(paired), lent_ref[0], amp[0]))
     copies[3].wait()
-    amp_out[...] = by_parity(amp[0])
-    copies[4].wait()
-
-
-def spread(ref, which, shape):
-    return jnp.broadcast_to(ref[0:1, which : which + 1], shape)
-
-
-def wrapped(ref, s, part, col_ref):
+
+
+def spread(ref, frame, which, shape):
+    return jnp.broadcast_to(ref[frame : frame + 1, which : which + 1], shape)
+
+
+def covered(paired, at_ref, frame, shape, start=0):
+    gap = lax.broadcasted_iota(jnp.int32, shape, 0) + start - spread(at_ref, frame, 0, shape)
+    gap = gap if frame else -1 - gap
+    return jnp.where(flipped(paired), -1 - gap, gap) < 0
+
+
+def wrapped(ref, s, part, at_ref, frame):
     size = ref.shape[-2]
     c = lax.broadcasted_iota(jnp.int32, (size, size), 1)
-    return jnp.where(c < spread(col_ref, 1, c.shape), ref[s, part, :, size:], ref[s, part, :, :size])
-
-
-def send_body(before_ref, object_ref, zero_ref, one_ref):
+    return jnp.where(c < spread(at_ref, frame, 1, c.shape), ref[s, part, :, size:], ref[s, part, :, :size])
+
+
+def send_body(paired, pos_ref, before_ref, object_ref, at_ref, zero_ref, one_ref):
+    flip = flipped(paired)
+    at_ref[0:1] = jnp.where(flip, before_ref[...], pos_ref[...])
+    at_ref[1:2] = jnp.where(flip, pos_ref[...], before_ref[...])
     for s, out in enumerate((zero_ref, one_ref)):
         for part in range(2):
-            out[part] = wrapped(object_ref, s, part, before_ref)
-
-
-def patch_of(s, object_ref, halo_ref, pos_ref):
+            out[part] = wrapped(object_ref, s, part, at_ref, 1)
+
+
+def patch_of(paired, s, object_ref, halo_ref, at_ref):
     size = halo_ref.shape[-1]
-    r = lax.broadcasted_iota(jnp.int32, (size, size), 0)
-    return [
-        jnp.where(r < spread(pos_ref, 0, r.shape), halo_ref[part], wrapped(object_ref, s, part, pos_ref))
-        for part in range(2)
-    ]
+    mine = covered(paired, at_ref, 0, (size, size))
+    return [jnp.where(mine, wrapped(object_ref, s, part, at_ref, 0), halo_ref[part]) for part in range(2)]
 
 
 def pair(ref, *at):
     return ref[(*at, 0)], ref[(*at, 1)]
 
 
-def inner_body(pos_ref, object_ref, halo_ref, first_ref, kr_ref, ki_ref, tab, *refs):
+def inner_body(paired, at_ref, object_ref, halo_ref, first_ref, kr_ref, ki_ref, tab, *refs):
     out_ref, probe_ref, patch = refs[-3:]
     states = out_ref.shape[0]
-    patch[0], patch[1] = patch_of(0, object_ref, halo_ref, pos_ref)
+    patch[0], patch[1] = patch_of(paired, 0, object_ref, halo_ref, at_ref)
     swap = lax.rem(lax.axis_index("frame"), 2) == 1
     probe_ref[:1] = first_ref[...]
     for m, (came, given) in enumerate(zip(refs[:-3:2], refs[1:-3:2])):
-        other = turned(given[...], *turn_of(pos_ref, given.shape[1]))
+        other = turned(given[...], *turn_of(at_ref, given.shape[1]))
         probe_ref[1 + m, 0] = jnp.where(swap, other, came[...])
         probe_ref[1 + m, 1] = jnp.where(swap, came[...], other)
 
@@ -277,9 +284,18 @@
     in_groups(states, body)
 
 
-def middle_body(rows, pos_ref, object_ref, halo_ref, inner_ref, amp_ref, tab, term_ref, chi_ref, patch, far, power):
+def blocks_of(rows, paired):
+    starts = [lax.axis_index("state")]
+    if paired:
+        starts.append(lax.rem(lax.axis_index("frame"), 2))
+    return [pl.ds(pl.multiple_of(start * rows, rows), rows) for start in starts]
+
+
+def middle_body(paired, rows, at_ref, object_ref, halo_ref, inner_ref, amp_ref, tab, *refs):
+    chi_ref, patch, far, power = refs[-4:]
+    terms = refs[:-4]
     states = inner_ref.shape[0]
-    patch[0], patch[1] = patch_of(1, object_ref, halo_ref, pos_ref)
+    patch[0], patch[1] = patch_of(paired, 1, object_ref, halo_ref, at_ref)
     power[...] = jnp.zeros_like(power)
 
     def outward(group):
@@ -292,27 +308,35 @@
 
     in_groups(states, outward)
     power[...] = 1.0 - amp_ref[...] * lax.rsqrt(power[...] + 1.0)
-    term_ref[...] = jnp.zeros_like(term_ref)
-    take = pl.ds(pl.multiple_of(lax.axis_index("state") * rows, rows), rows)
+    for term_ref in terms:
+        term_ref[...] = jnp.zeros_like(term_ref)
 
     def homeward(group):
         waves = inverse([(power[...] * far[m, 0], power[...] * far[m, 1]) for m in group], tab)
         for m, wave in zip(group, waves):
             far[m, 0], far[m, 1] = wave
             chi_ref[m, 0], chi_ref[m, 1] = times_conj(pair(patch), wave)
-        for m in group:
-            part = times_conj(
-                (inner_ref[m, 0, take], inner_ref[m, 1, take]), (far[m, 0, take], far[m, 1, take])
-            )
-            term_ref[0] += part[0]
-            term_ref[1] += part[1]
+        for term_ref, take in zip(terms, blocks_of(rows, paired)):
+            for m in group:
+                part = times_conj(
+                    (inner_ref[m, 0, take], inner_ref[m, 1, take]), (far[m, 0, take], far[m, 1, take])
+                )
+                term_ref[0] += part[0]
+                term_ref[1] += part[1]
 
     in_groups(states, homeward)
 
 
-def last_body(rows, chi_ref, probe_ref, kr_ref, ki_ref, tab, term_ref, front):
+def front_term(m, take, front, probe_ref, tab, term_ref):
+    wave = columns_inverse(front[m, 0, take], front[m, 1, take], tab)
+    part = times_conj((probe_ref[m, 0, take], probe_ref[m, 1, take]), wave)
+    term_ref[0] += part[0]
+    term_ref[1] += part[1]
+
+
+def last_body(paired, rows, chi_ref, probe_ref, kr_ref, ki_ref, tab, term_ref, front):
     states = chi_ref.shape[0]
-    take = pl.ds(pl.multiple_of(lax.axis_index("state") * rows, rows), rows)
+    take = blocks_of(rows, paired)[-1]
     term_ref[...] = jnp.zeros_like(term_ref)
 
     def body(group):
@@ -321,22 +345,29 @@
         for m, wave in zip(group, waves):
             front[m, 0], front[m, 1] = wave
         for m in group:
-            wave = columns_inverse(front[m, 0, take], front[m, 1, take], tab)
-            part = times_conj((probe_ref[m, 0, take], probe_ref[m, 1, take]), wave)
-            term_ref[0] += part[0]
-            term_ref[1] += part[1]
+            front_term(m, take, front, probe_ref, tab, term_ref)
 
     in_groups(states, body)
 
 
-def gather_body(slice_id, rows, pos_ref, before_ref, own_ref, came_ref, *refs):
+def keep_body(rows, front_ref, probe_ref, tab, term_ref):
+    take = blocks_of(rows, True)[0]
+    term_ref[...] = jnp.zeros_like(term_ref)
+
+    def body(group):
+        for m in group:
+            front_term(m, take, front_ref, probe_ref, tab, term_ref)
+
+    in_groups(front_ref.shape[0], body)
+
+
+def gather_body(slice_id, paired, rows, at_ref, own_ref, came_ref, *refs):
     out_ref, held, sem = refs[-3:]
     size = own_ref.shape[-1]
     start = lax.axis_index("state") * rows
-    r = lax.broadcasted_iota(jnp.int32, (rows, size), 0) + start
     c = lax.broadcasted_iota(jnp.int32, (rows, size), 1)
-    here, there = r >= spread(pos_ref, 0, r.shape), r < spread(before_ref, 0, r.shape)
-    here_right, there_right = c < spread(pos_ref, 1, c.shape), c < spread(before_ref, 1, c.shape)
+    here, there = (covered(paired, at_ref, frame, c.shape, start) for frame in range(2))
+    here_right, there_right = (c < spread(at_ref, frame, 1, c.shape) for frame in range(2))
     chunks = 4 if rows % 32 == 0 else 1
     step = rows // chunks
     copies = []
@@ -357,17 +388,17 @@
         copy.wait()
 
 
-def gather(slice_id, rows, size, pos, before, own, came, *given):
+def gather(slice_id, paired, rows, size, at, own, came, *given):
     return pl.pallas_call(
-        functools.partial(gather_body, slice_id, rows),
+        functools.partial(gather_body, slice_id, paired, rows),
         out_shape=jax.ShapeDtypeStruct((2, 2, rows, 2 * size), F32),
-        in_specs=[VMEM] * 4 + [pl.BlockSpec(memory_space=pl.ANY)] * len(given),
+        in_specs=[VMEM] * 3 + [pl.BlockSpec(memory_space=pl.ANY)] * len(given),
         out_specs=pl.BlockSpec(memory_space=pl.ANY),
         scratch_shapes=[pltpu.VMEM((2, rows, 2 * size), F32), pltpu.SemaphoreType.DMA((8,))],
-        input_output_aliases={4: 0} if given else {},
+        input_output_aliases={3: 0} if given else {},
         compiler_params=pltpu.CompilerParams(vmem_limit_bytes=LIMIT),
         cost_estimate=pl.CostEstimate(flops=0, bytes_accessed=32 * rows * size, transcendentals=0),
-    )(pos, before, own, came, *given)
+    )(at, own, came, *given)
 
 
 def on_device(object_slices, probe, amplitude, positions, propagator):
@@ -379,12 +410,29 @@
     return gradient_of(object_slices, probe, amplitude, positions, propagator, states, size, rows)
 
 
+def routes(frames, paired):
+    if not paired:
+        up = [(i, (i + 1) % frames) for i in range(frames)]
+        return "frame", [(j, i) for i, j in up], None, up
+    halo, lend, give = [], [], []
+    for f in range(frames):
+        behind, ahead = (f - 1) % frames, (f + 1) % frames
+        halo += [(2 * f, 2 * behind), (2 * f + 1, 2 * ahead + 1)]
+        lend += [(2 * f + 1, 2 * ahead + 1)]
+        give += [(2 * f, 2 * f + 1), (2 * f + 1, 2 * f - 1)] if f % 2 else [(2 * f, 2 * f + 2), (2 * f + 1, 2 * f)]
+    return ("frame", "state"), halo, lend, give
+
+
 def gradient_of(object_slices, probe, amplitude, positions, propagator, states, size, rows):
+    paired = states == 2
     grid = (size, size)
     unit = size * size
     flops = 24 * size**3
+    frames = lax.axis_size("frame")
+    axes, halo_route, lend_route, give_route = routes(frames, paired)
     tab = tables(size)
     before = shifted(positions, "frame", 1)
+    lent = lax.ppermute(amplitude, axes, lend_route) if paired else amplitude
     given = [in_hbm(x) for x in (positions, probe, object_slices)]
     pos, plane, held = pl.pallas_call(
         load_body,
@@ -402,58 +450,70 @@
     planes = []
     for by in range(1, states):
         planes.append(shifted(plane, "state", by))
-    picked = call(send_body, [(2,) + grid] * 2, [VMEM, VMEM], moved=16 * unit)(before, held)
-    halo_zero = shifted(picked[0], "frame", -1)
-    halo_one = shifted(picked[1], "frame", -1)
+    at, zero, one = pl.pallas_call(
+        functools.partial(send_body, paired),
+        out_shape=[jax.ShapeDtypeStruct((2, 2), jnp.int32)] + [jax.ShapeDtypeStruct((2,) + grid, F32)] * 2,
+        in_specs=[VMEM] * 3,
+        out_specs=[VMEM] * 3,
+        compiler_params=pltpu.CompilerParams(vmem_limit_bytes=LIMIT),
+        cost_estimate=pl.CostEstimate(flops=0, bytes_accessed=64 * unit, transcendentals=0),
+    )(pos, before, held)
+    halo_zero = lax.ppermute(zero, axes, halo_route)
+    halo_one = lax.ppermute(one, axes, halo_route)
     kr, ki, amp, first, tab = pl.pallas_call(
-        prepare_body,
+        functools.partial(prepare_body, paired),
         out_shape=[jax.ShapeDtypeStruct(grid, F32)] * 3
         + [jax.ShapeDtypeStruct(x.shape, x.dtype) for x in (probe, tab)],
-        in_specs=[HBM] * 5,
+        in_specs=[VMEM] * 2 + [HBM] * 4,
         out_specs=[VMEM] * 5,
         scratch_shapes=[
-            pltpu.SMEM(positions.shape, jnp.int32),
             pltpu.VMEM(probe.shape, F32),
             pltpu.VMEM(grid, F32),
             pltpu.VMEM(amplitude.shape, F32),
-            pltpu.SemaphoreType.DMA((5,)),
+            pltpu.SemaphoreType.DMA((4,)),
         ],
         compiler_params=pltpu.CompilerParams(vmem_limit_bytes=LIMIT),
         cost_estimate=pl.CostEstimate(flops=2 * size**3, bytes_accessed=60 * unit, transcendentals=0),
-    )(*given[:2], *(in_hbm(x) for x in (propagator, amplitude, tab)))
-    frames = lax.axis_size("frame")
-    own = call(turn_body, [grid] * len(planes), [VMEM] * (1 + len(planes)), moved=16 * unit)(pos, *planes)
+    )(at, lent, given[1], *(in_hbm(x) for x in (propagator, amplitude, tab)))
+    own = call(turn_body, [grid] * len(planes), [VMEM] * (1 + len(planes)), moved=16 * unit)(at, *planes)
     pairs = []
     for came, kept in zip(planes, own):
         pairs += [kept, lax.ppermute(came, "frame", [(i, i ^ 1) for i in range(frames)])]
     waves, probes = call(
-        inner_body,
+        functools.partial(inner_body, paired),
         [(states, 2) + grid] * 2,
         [VMEM] * (7 + len(pairs)),
         [pltpu.VMEM((2,) + grid, F32)],
         flops=2 * flops * states,
         moved=24 * unit * states,
-    )(pos, held, halo_zero, first, kr, ki, tab, *pairs)
-    term_one, chi = call(
-        functools.partial(middle_body, rows),
-        [(2, rows, size), (states, 2) + grid],
+    )(at, held, halo_zero, first, kr, ki, tab, *pairs)
+    *terms, chi = call(
+        functools.partial(middle_body, paired, rows),
+        [(2, rows, size)] * (2 if paired else 1) + [(states, 2) + grid],
         [VMEM] * 6,
         [pltpu.VMEM((2,) + grid, F32), pltpu.VMEM((states, 2) + grid, F32), pltpu.VMEM(grid, F32)],
         flops=2 * flops * states,
         moved=32 * unit * states,
-    )(pos, held, halo_one, waves, amp, tab)
-    came_one = shifted(term_one, "frame", 1)
-    (term_zero,) = call(
-        functools.partial(last_body, rows),
-        [(2, rows, size)],
+    )(at, held, halo_one, waves, amp, tab)
+    came_one = lax.ppermute(terms[-1], axes, give_route)
+    term_zero, front = call(
+        functools.partial(last_body, paired, rows),
+        [(2, rows, size), (states, 2) + grid],
         [VMEM] * 5,
-        [pltpu.VMEM((states, 2) + grid, F32)],
         flops=2 * flops * states,
         moved=16 * unit * states,
     )(chi, probes, kr, ki, tab)
-    came_zero = shifted(term_zero, "frame", 1)
-    gradient = gather(1, rows, size, pos, before, term_one, came_one)
-    return gather(0, rows, size, pos, before, term_zero, came_zero, gradient)
+    came_zero = lax.ppermute(term_zero, axes, give_route)
+    if paired:
+        (term_zero,) = call(
+            functools.partial(keep_body, rows),
+            [(2, rows, size)],
+            [VMEM] * 3,
+            flops=flops * states // 8,
+            moved=16 * unit,
+        )(front, probes, tab)
+    gradient = gather(1, paired, rows, size, at, terms[0], came_one)
+    return gather(0, paired, rows, size, at, term_zero, came_zero, gradient)
 
 
 def solution(mesh):

time: 36.5 us -> 45.6 us (1.25)
  starting transfers between devices: 6.69 us -> 14 us
  waiting for transfers between devices: 15.4 us -> 16.5 us
  Pallas kernels: 14.1 us -> 14.8 us
    ppermute x0 -> x5, waiting for transfers between devices: none -> 13.9 us  [the longest x1 8.54 us: gradient_of(): came_one = lax.ppermute(terms[-1], axes, give_route)]
    ppermute x6 -> x2, waiting for transfers between devices: 15.4 us -> 2.54 us  [shifted(): lax.ppermute(value, axis, [(i, (i + by) % count) for i in range(count)])]
    ppermute x0 -> x5, starting transfers between devices: none -> 10.1 us  [the longest x1 6.73 us: gradient_of(): came_zero = lax.ppermute(term_zero, axes, give_route)]
    ppermute x6 -> x2, starting transfers between devices: 5.75 us -> 3.08 us  [shifted(): lax.ppermute(value, axis, [(i, (i + by) % count) for i in range(count)])]
    pallas_call x7 -> x8, Pallas kernels: 12.2 us -> 12.8 us  [the longest x1 3.52 us: gradient_of(): pl.pallas_call(functools.partial(prepare_body, paired), out_shape=[jax.Sh...]
  transfers between devices with their start and end apart: 7 -> 8, of which waited for: 6 -> 6; matrix products, arithmetic and copies ran while one was open for 0% -> 0% of each run, Pallas kernels for 30% -> 25%
where the time goes in v8:
time: 45.6 us; the launch traced here: 45.4 us
  waiting for transfers between devices  16.5 us (36%)
  Pallas kernels  14.8 us (32%)
  starting transfers between devices  14 us (31%)
    ppermute x1, waiting for transfers between devices, gradient_of(): came_one = lax.ppermute(terms[-1], axes, give_route)  8.54 us
    ppermute x1, starting transfers between devices, gradient_of(): came_zero = lax.ppermute(term_zero, axes, give_route)  6.73 us
    pallas_call x1, Pallas kernels, gradient_of(): pl.pallas_call(functools.partial(prepare_body, paired), out_shape=[jax.Sh...  3.52 us
    ppermute x1, waiting for transfers between devices, gradient_of(): halo_one = lax.ppermute(one, axes, halo_route)  3.25 us
    ppermute x2, starting transfers between devices, shifted(): lax.ppermute(value, axis, [(i, (i + by) % count) for i in range(count)])  3.08 us
    ppermute x2, waiting for transfers between devices, shifted(): lax.ppermute(value, axis, [(i, (i + by) % count) for i in range(count)])  2.54 us
    pallas_call x1, Pallas kernels, gradient_of(): call(functools.partial(middle_body, paired, rows), [(2, rows, size)] * (2...  2.51 us
    pallas_call x1, Pallas kernels, gradient_of(): call(functools.partial(inner_body, paired), [(states, 2) + grid] * 2, [VM...  2.36 us
  transfers between devices with their start and end apart: 8, of which 6 were waited for; matrix products, arithmetic and copies ran while one was open for 0% of the time, Pallas kernels for 25%

profile of v8, /device:TPU:0, one launch (start us, length us, event | category | flops | bytes accessed | tf_op | source)
XLA Modules:
  0.0 45.4 jit_solution(6953565365046709903)
XLA Ops:
  0.0 0.0 copy-start
  0.0 0.5 %collective-permute-start = (s32[1,2]{1,0:T(1,128)}, s32[1,2]{1,0:T(1,128)S(1)}, u32[]{:S(2)}, u32[]{:S(2)}) collective-permute-start(s32[1,2]{1,0:T(1,128)} %pos_hbm.1), channel_id=1, source_target_pairs={{0,2},{2,4},{4,6},{6,8},{8,10},{10,12},{12,14},{14,16},{16,18},{18... | collective-permute-start | bytes 32 | tf_op jit(solution)/shard_map/ppermute | solution.py:23
  0.5 1.7 %shard_map.64 = (s32[1,2]{1,0:T(1,128)S(1)}, f32[256,256]{1,0:T(8,128)S(1)}, f32[2,2,256,512]{3,2,1,0:T(8,128)S(1)}) custom-call(s32[1,2]{1,0:T(1,128)} %pos_hbm.1, f32[1,2,256,256]{3,2,1,0:T(8,128)} %probe_hbm.3, f32[2,2,256,512]{3,2,1,0:T(8,128)} %object_hbm.1), custom_call_target="tpu_custom_call" | custom-call | bytes 2621440 | tf_op jit(solution)/shard_map/pallas_call | solution.py:437
  2.2 2.6 %collective-permute-start.4 = (f32[256,256]{1,0:T(8,128)S(1)}, f32[256,256]{1,0:T(8,128)S(1)}, u32[]{:S(2)}, u32[]{:S(2)}) collective-permute-start(f32[256,256]{1,0:T(8,128)S(1)} %get-tuple-element.32), channel_id=1, source_target_pairs={{0,1},{1,0},{2,3},{3,2},{4,5},{5,4},{6,7},{7,6},{8,9},{9,8},{10,11... | collective-permute-start | bytes 786440 | tf_op jit(solution)/shard_map/ppermute | solution.py:23
  4.8 2.1 %collective-permute-done.before_ref = s32[1,2]{1,0:T(1,128)S(1)} collective-permute-done((s32[1,2]{1,0:T(1,128)}, s32[1,2]{1,0:T(1,128)S(1)}, u32[]{:S(2)}, u32[]{:S(2)}) %collective-permute-start) | collective-permute-done | bytes 40 | tf_op jit(solution)/shard_map/ppermute | solution.py:23
  6.9 0.2 shard_map.65
  7.1 2.1 %collective-permute-start.2 = (f32[2,256,256]{2,1,0:T(8,128)S(1)}, f32[2,256,256]{2,1,0:T(8,128)S(1)}, u32[]{:S(2)}, u32[]{:S(2)}) collective-permute-start(f32[2,256,256]{2,1,0:T(8,128)S(1)} %get-tuple-element.27), channel_id=1, source_target_pairs={{0,30},{1,3},{2,0},{3,5},{4,2},{5,7},{6,4},{7,9},{8,6},{9,11},{10,... | collective-permute-start | bytes 1572872 | tf_op jit(solution)/shard_map/ppermute | solution.py:461
  9.2 0.6 %collective-permute-start.1 = (f32[2,256,256]{2,1,0:T(8,128)S(1)}, f32[2,256,256]{2,1,0:T(8,128)S(1)}, u32[]{:S(2)}, u32[]{:S(2)}) collective-permute-start(f32[2,256,256]{2,1,0:T(8,128)S(1)} %get-tuple-element.26), channel_id=1, source_target_pairs={{0,30},{1,3},{2,0},{3,5},{4,2},{5,7},{6,4},{7,9},{8,6},{9,11},{10,... | collective-permute-start | bytes 1572872 | tf_op jit(solution)/shard_map/ppermute | solution.py:462
  9.7 0.0 copy-done
  9.7 0.7 %collective-permute-start.3 = (f32[1,256,256]{2,1,0:T(8,128)S(1)}, f32[1,256,256]{2,1,0:T(8,128)S(1)}, u32[]{:S(2)}, u32[]{:S(2)}) collective-permute-start(f32[1,256,256]{2,1,0:T(8,128)S(1)} %copy-done), channel_id=1, source_target_pairs={{1,3},{3,5},{5,7},{7,9},{9,11},{11,13},{13,15},{15,17},{17,19},{19... | collective-permute-start | bytes 786440 | tf_op jit(solution)/shard_map/ppermute | solution.py:435
  10.4 0.5 %collective-permute-done.4.refs_0_ = f32[256,256]{1,0:T(8,128)S(1)} collective-permute-done((f32[256,256]{1,0:T(8,128)S(1)}, f32[256,256]{1,0:T(8,128)S(1)}, u32[]{:S(2)}, u32[]{:S(2)}) %collective-permute-start.4) | collective-permute-done | bytes 262176 | tf_op jit(solution)/shard_map/ppermute | solution.py:23
  10.9 0.9 %collective-permute-start.5 = (f32[256,256]{1,0:T(8,128)S(1)}, f32[256,256]{1,0:T(8,128)S(1)}, u32[]{:S(2)}, u32[]{:S(2)}) collective-permute-start(f32[256,256]{1,0:T(8,128)S(1)} %collective-permute-done.4.refs_0_), channel_id=1, source_target_pairs={{0,2},{2,0},{4,6},{6,4},{8,10},{10,8},{12,14},{14,12},{16,18},{18,... | collective-permute-start | bytes 786440 | tf_op jit(solution)/shard_map/ppermute | solution.py:481
  11.8 0.2 shard_map.67.refs_0_
  12.0 0.0 collective-permute-done.3.lent_ref
  12.0 3.5 %shard_map.66 = (f32[256,256]{1,0:T(8,128)S(1)}, f32[256,256]{1,0:T(8,128)S(1)}, f32[256,256]{1,0:T(8,128)S(1)}, f32[1,2,256,256]{3,2,1,0:T(8,128)S(1)}, bf16[2,4,256,256]{3,2,1,0:T(8,128)(2,1)S(1)}) custom-call(s32[2,2]{1,0:T(2,128)S(1)} %get-tuple-element.25.at_ref, f32[1,256,256]{2,1,0:T(8,128)S(1)} %collective-permute-done.3.lent_ref, ...), custom_call_target="tpu_custom_call" | custom-call | flops 33554432 | bytes 3932160 | tf_op jit(solution)/shard_map/pallas_call | solution.py:463
  15.5 0.0 collective-permute-done.5.refs_1_
  15.6 0.3 collective-permute-done.2.halo_ref
  15.9 2.4 %shard_map.68 = (f32[2,2,256,256]{3,2,1,0:T(8,128)S(1)}, f32[2,2,256,256]{3,2,1,0:T(8,128)S(1)}) custom-call(s32[2,2]{1,0:T(2,128)S(1)} %get-tuple-element.25.at_ref, f32[2,2,256,512]{3,2,1,0:T(8,128)S(1)} %get-tuple-element.24.object_ref, f32[2,256,256]{2,1,0:T(8,128)S(1)} %collective-permute-done.2.halo_ref, ...), custom_call_target="tpu_custom_call" | custom-call | flops 1610612736 | bytes 3145728 | tf_op jit(solution)/shard_map/pallas_call | solution.py:482
  18.2 3.3 %collective-permute-done.1.halo_ref = f32[2,256,256]{2,1,0:T(8,128)S(1)} collective-permute-done((f32[2,256,256]{2,1,0:T(8,128)S(1)}, f32[2,256,256]{2,1,0:T(8,128)S(1)}, u32[]{:S(2)}, u32[]{:S(2)}) %collective-permute-start.1) | collective-permute-done | bytes 524320 | tf_op jit(solution)/shard_map/ppermute | solution.py:462
  21.5 2.5 %shard_map.69 = (f32[2,128,256]{2,1,0:T(8,128)S(1)}, f32[2,128,256]{2,1,0:T(8,128)S(1)}, f32[2,2,256,256]{3,2,1,0:T(8,128)S(1)}) custom-call(s32[2,2]{1,0:T(2,128)S(1)} %get-tuple-element.25.at_ref, f32[2,2,256,512]{3,2,1,0:T(8,128)S(1)} %get-tuple-element.24.object_ref, f32[2,256,256]{2,1,0:T(8,128)S(1)} %collective-permute-done.1.halo_ref, ...), custom_call_target="tpu_custom_call" | custom-call | flops 1610612736 | bytes 4194304 | tf_op jit(solution)/shard_map/pallas_call | solution.py:490
  24.0 0.0 collective-permute-start.7
  24.0 1.9 %shard_map.70 = (f32[2,128,256]{2,1,0:T(8,128)S(1)}, f32[2,2,256,256]{3,2,1,0:T(8,128)S(1)}) custom-call(f32[2,2,256,256]{3,2,1,0:T(8,128)S(1)} %get-tuple-element.35.chi_ref, f32[2,2,256,256]{3,2,1,0:T(8,128)S(1)} %get-tuple-element.36.probe_ref, f32[256,256]{1,0:T(8,128)S(1)} %get-tuple-element.29.kr_ref, f32[256,256]{1,0:T(8,128)S(1)} %get-tuple-element.30.ki_ref, ...), custom_call_target="tpu_custom_call" | custom-call | flops 1610612736 | bytes 2097152 | tf_op jit(solution)/shard_map/pallas_call | solution.py:499
  25.9 6.7 %collective-permute-start.6 = (f32[2,128,256]{2,1,0:T(8,128)S(1)}, f32[2,128,256]{2,1,0:T(8,128)S(1)}, u32[]{:S(2)}, u32[]{:S(2)}) collective-permute-start(f32[2,128,256]{2,1,0:T(8,128)S(1)} %get-tuple-element.38), channel_id=1, source_target_pairs={{0,2},{1,0},{2,3},{3,1},{4,6},{5,4},{6,7},{7,5},{8,10},{9,8},{10,1... | collective-permute-start | bytes 786440 | tf_op jit(solution)/shard_map/ppermute | solution.py:506
  32.7 0.4 shard_map.71.own_ref
  33.1 8.5 %collective-permute-done.7.came_ref = f32[2,128,256]{2,1,0:T(8,128)S(1)} collective-permute-done((f32[2,128,256]{2,1,0:T(8,128)S(1)}, f32[2,128,256]{2,1,0:T(8,128)S(1)}, u32[]{:S(2)}, u32[]{:S(2)}) %collective-permute-start.7) | collective-permute-done | bytes 262176 | tf_op jit(solution)/shard_map/ppermute | solution.py:498
  41.6 1.0 %shard_map.72.refs_0_ = f32[2,2,128,512]{3,2,1,0:T(8,128)} custom-call(s32[2,2]{1,0:T(2,128)S(1)} %get-tuple-element.25.at_ref, f32[2,128,256]{2,1,0:T(8,128)S(1)} %get-tuple-element.39.own_ref, f32[2,128,256]{2,1,0:T(8,128)S(1)} %collective-permute-done.7.came_ref), custom_call_target="tpu_custom_call" | custom-call | bytes 1048576 | tf_op jit(solution)/shard_map/pallas_call | solution.py:392
  42.6 1.8 %collective-permute-done.6.came_ref = f32[2,128,256]{2,1,0:T(8,128)S(1)} collective-permute-done((f32[2,128,256]{2,1,0:T(8,128)S(1)}, f32[2,128,256]{2,1,0:T(8,128)S(1)}, u32[]{:S(2)}, u32[]{:S(2)}) %collective-permute-start.6) | collective-permute-done | bytes 262176 | tf_op jit(solution)/shard_map/ppermute | solution.py:506
  44.4 1.0 %shard_map.73 = f32[2,2,128,512]{3,2,1,0:T(8,128)} custom-call(s32[2,2]{1,0:T(2,128)S(1)} %get-tuple-element.25.at_ref, f32[2,128,256]{2,1,0:T(8,128)S(1)} %shard_map.71.own_ref, f32[2,128,256]{2,1,0:T(8,128)S(1)} %collective-permute-done.6.came_ref, f32[2,2,128,512]{3,2,1,0:T(8,128)} %shard_map.72.refs_0_), custom_call_target="tpu_custom_call", output_to_operand_aliasing={{}: (3, {})} | custom-call | bytes 1048576 | tf_op jit(solution)/shard_map/pallas_call | solution.py:392
Async XLA Ops:
  0.0 9.7 %copy-start = (f32[1,256,256]{2,1,0:T(8,128)S(1)}, f32[1,256,256]{2,1,0:T(8,128)}, u32[]{:S(2)}) copy-start(f32[1,256,256]{2,1,0:T(8,128)} %amp_hbm.1) | copy-start | bytes 786436
  0.0 6.9 %collective-permute-start = (s32[1,2]{1,0:T(1,128)}, s32[1,2]{1,0:T(1,128)S(1)}, u32[]{:S(2)}, u32[]{:S(2)}) collective-permute-start(s32[1,2]{1,0:T(1,128)} %pos_hbm.1), channel_id=1, source_target_pairs={{0,2},{2,4},{4,6},{6,8},{8,10},{10,12},{12,14},{14,16},{16,18},{18... | collective-permute-start | bytes 32 | tf_op jit(solution)/shard_map/ppermute | solution.py:23
  2.2 8.7 %collective-permute-start.4 = (f32[256,256]{1,0:T(8,128)S(1)}, f32[256,256]{1,0:T(8,128)S(1)}, u32[]{:S(2)}, u32[]{:S(2)}) collective-permute-start(f32[256,256]{1,0:T(8,128)S(1)} %get-tuple-element.32), channel_id=1, source_target_pairs={{0,1},{1,0},{2,3},{3,2},{4,5},{5,4},{6,7},{7,6},{8,9},{9,8},{10,11... | collective-permute-start | bytes 786440 | tf_op jit(solution)/shard_map/ppermute | solution.py:23
  7.1 8.8 %collective-permute-start.2 = (f32[2,256,256]{2,1,0:T(8,128)S(1)}, f32[2,256,256]{2,1,0:T(8,128)S(1)}, u32[]{:S(2)}, u32[]{:S(2)}) collective-permute-start(f32[2,256,256]{2,1,0:T(8,128)S(1)} %get-tuple-element.27), channel_id=1, source_target_pairs={{0,30},{1,3},{2,0},{3,5},{4,2},{5,7},{6,4},{7,9},{8,6},{9,11},{10,... | collective-permute-start | bytes 1572872 | tf_op jit(solution)/shard_map/ppermute | solution.py:461
  9.2 12.3 %collective-permute-start.1 = (f32[2,256,256]{2,1,0:T(8,128)S(1)}, f32[2,256,256]{2,1,0:T(8,128)S(1)}, u32[]{:S(2)}, u32[]{:S(2)}) collective-permute-start(f32[2,256,256]{2,1,0:T(8,128)S(1)} %get-tuple-element.26), channel_id=1, source_target_pairs={{0,30},{1,3},{2,0},{3,5},{4,2},{5,7},{6,4},{7,9},{8,6},{9,11},{10,... | collective-permute-start | bytes 1572872 | tf_op jit(solution)/shard_map/ppermute | solution.py:462
  9.7 2.3 %collective-permute-start.3 = (f32[1,256,256]{2,1,0:T(8,128)S(1)}, f32[1,256,256]{2,1,0:T(8,128)S(1)}, u32[]{:S(2)}, u32[]{:S(2)}) collective-permute-start(f32[1,256,256]{2,1,0:T(8,128)S(1)} %copy-done), channel_id=1, source_target_pairs={{1,3},{3,5},{5,7},{7,9},{9,11},{11,13},{13,15},{15,17},{17,19},{19... | collective-permute-start | bytes 786440 | tf_op jit(solution)/shard_map/ppermute | solution.py:435
  10.9 4.7 %collective-permute-start.5 = (f32[256,256]{1,0:T(8,128)S(1)}, f32[256,256]{1,0:T(8,128)S(1)}, u32[]{:S(2)}, u32[]{:S(2)}) collective-permute-start(f32[256,256]{1,0:T(8,128)S(1)} %collective-permute-done.4.refs_0_), channel_id=1, source_target_pairs={{0,2},{2,0},{4,6},{6,4},{8,10},{10,8},{12,14},{14,12},{16,18},{18,... | collective-permute-start | bytes 786440 | tf_op jit(solution)/shard_map/ppermute | solution.py:481
  24.0 17.6 %collective-permute-start.7 = (f32[2,128,256]{2,1,0:T(8,128)S(1)}, f32[2,128,256]{2,1,0:T(8,128)S(1)}, u32[]{:S(2)}, u32[]{:S(2)}) collective-permute-start(f32[2,128,256]{2,1,0:T(8,128)S(1)} %get-tuple-element.40), channel_id=1, source_target_pairs={{0,2},{1,0},{2,3},{3,1},{4,6},{5,4},{6,7},{7,5},{8,10},{9,8},{10,1... | collective-permute-start | bytes 786440 | tf_op jit(solution)/shard_map/ppermute | solution.py:498
  25.9 18.5 %collective-permute-start.6 = (f32[2,128,256]{2,1,0:T(8,128)S(1)}, f32[2,128,256]{2,1,0:T(8,128)S(1)}, u32[]{:S(2)}, u32[]{:S(2)}) collective-permute-start(f32[2,128,256]{2,1,0:T(8,128)S(1)} %get-tuple-element.38), channel_id=1, source_target_pairs={{0,2},{1,0},{2,3},{3,1},{4,6},{5,4},{6,7},{7,5},{8,10},{9,8},{10,1... | collective-permute-start | bytes 786440 | tf_op jit(solution)/shard_map/ppermute | solution.py:506

commit v9 on v8

--- a/solution.py
+++ b/solution.py
@@ -210,11 +210,14 @@
 
 
 def prepare_body(
-    paired, at_ref, lent_ref, probe_hbm, prop_hbm, amp_hbm, tab_hbm,
-    wave_re, wave_im, amp_out, first_out, tab_out,
-    probe, prop, amp, sem,
+    paired, pos_ref, before_ref, over_ref, probe_hbm, prop_hbm, tab_hbm,
+    at_ref, wave_re, wave_im, first_out, tab_out,
+    probe, prop, sem,
 ):
-    copies = run_copies(((probe_hbm, probe), (prop_hbm, prop), (amp_hbm, amp), (tab_hbm, tab_out)), sem)
+    copies = run_copies(((probe_hbm, probe), (prop_hbm, prop), (tab_hbm, tab_out)), sem)
+    flip = flipped(paired)
+    at_ref[0:1] = jnp.where(flip, over_ref[...], pos_ref[...])
+    at_ref[1:2] = jnp.where(flip, pos_ref[...], before_ref[...])
     size = prop.shape[0]
     copies[0].wait()
     turn = turn_of(at_ref, size)
@@ -225,8 +228,10 @@
     wave_re[...] = jnp.cos(phase)
     wave_im[...] = jnp.sin(phase)
     copies[2].wait()
-    amp_out[...] = by_parity(jnp.where(flipped(paired), lent_ref[0], amp[0]))
-    copies[3].wait()
+
+
+def measure_body(paired, amp_ref, lent_ref, out_ref):
+    out_ref[...] = by_parity(jnp.where(flipped(paired), lent_ref[0], amp_ref[0]))
 
 
 def spread(ref, frame, which, shape):
@@ -245,13 +250,11 @@
     return jnp.where(c < spread(at_ref, frame, 1, c.shape), ref[s, part, :, size:], ref[s, part, :, :size])
 
 
-def send_body(paired, pos_ref, before_ref, object_ref, at_ref, zero_ref, one_ref):
-    flip = flipped(paired)
-    at_ref[0:1] = jnp.where(flip, before_ref[...], pos_ref[...])
-    at_ref[1:2] = jnp.where(flip, pos_ref[...], before_ref[...])
+def send_body(paired, pos_ref, before_ref, object_ref, zero_ref, one_ref, to_ref):
+    to_ref[...] = jnp.where(flipped(paired), pos_ref[...], before_ref[...])
     for s, out in enumerate((zero_ref, one_ref)):
         for part in range(2):
-            out[part] = wrapped(object_ref, s, part, at_ref, 1)
+            out[part] = wrapped(object_ref, s, part, to_ref, 0)
 
 
 def patch_of(paired, s, object_ref, halo_ref, at_ref):
@@ -418,7 +421,7 @@
     for f in range(frames):
         behind, ahead = (f - 1) % frames, (f + 1) % frames
         halo += [(2 * f, 2 * behind), (2 * f + 1, 2 * ahead + 1)]
-        lend += [(2 * f + 1, 2 * ahead + 1)]
+        lend += [(2 * f, 2 * ahead + 1)]
         give += [(2 * f, 2 * f + 1), (2 * f + 1, 2 * f - 1)] if f % 2 else [(2 * f, 2 * f + 2), (2 * f + 1, 2 * f)]
     return ("frame", "state"), halo, lend, give
 
@@ -431,8 +434,9 @@
     frames = lax.axis_size("frame")
     axes, halo_route, lend_route, give_route = routes(frames, paired)
     tab = tables(size)
-    before = shifted(positions, "frame", 1)
-    lent = lax.ppermute(amplitude, axes, lend_route) if paired else amplitude
+    up = [(i, (i + 1) % frames) for i in range(frames)]
+    before = lax.ppermute(positions, axes, [(2 * i, 2 * j) for i, j in up] if paired else up)
+    over = lax.ppermute(positions, axes, [(2 * i + 1, 2 * j + 1) for i, j in up]) if paired else before
     given = [in_hbm(x) for x in (positions, probe, object_slices)]
     pos, plane, held = pl.pallas_call(
         load_body,
@@ -450,35 +454,34 @@
     planes = []
     for by in range(1, states):
         planes.append(shifted(plane, "state", by))
-    at, zero, one = pl.pallas_call(
+    zero, one = call(
         functools.partial(send_body, paired),
-        out_shape=[jax.ShapeDtypeStruct((2, 2), jnp.int32)] + [jax.ShapeDtypeStruct((2,) + grid, F32)] * 2,
-        in_specs=[VMEM] * 3,
-        out_specs=[VMEM] * 3,
-        compiler_params=pltpu.CompilerParams(vmem_limit_bytes=LIMIT),
-        cost_estimate=pl.CostEstimate(flops=0, bytes_accessed=64 * unit, transcendentals=0),
+        [(2,) + grid] * 2,
+        [VMEM] * 3,
+        [pltpu.VMEM(positions.shape, jnp.int32)],
+        moved=64 * unit,
     )(pos, before, held)
     halo_zero = lax.ppermute(zero, axes, halo_route)
     halo_one = lax.ppermute(one, axes, halo_route)
-    kr, ki, amp, first, tab = pl.pallas_call(
+    lent = lax.ppermute(amplitude, axes, lend_route) if paired else amplitude
+    at, kr, ki, first, tab = pl.pallas_call(
         functools.partial(prepare_body, paired),
-        out_shape=[jax.ShapeDtypeStruct(grid, F32)] * 3
+        out_shape=[jax.ShapeDtypeStruct((2, 2), jnp.int32)]
+        + [jax.ShapeDtypeStruct(grid, F32)] * 2
         + [jax.ShapeDtypeStruct(x.shape, x.dtype) for x in (probe, tab)],
-        in_specs=[VMEM] * 2 + [HBM] * 4,
+        in_specs=[VMEM] * 3 + [HBM] * 3,
         out_specs=[VMEM] * 5,
-        scratch_shapes=[
-            pltpu.VMEM(probe.shape, F32),
-            pltpu.VMEM(grid, F32),
-            pltpu.VMEM(amplitude.shape, F32),
-            pltpu.SemaphoreType.DMA((4,)),
-        ],
+        scratch_shapes=[pltpu.VMEM(probe.shape, F32), pltpu.VMEM(grid, F32), pltpu.SemaphoreType.DMA((3,))],
         compiler_params=pltpu.CompilerParams(vmem_limit_bytes=LIMIT),
         cost_estimate=pl.CostEstimate(flops=2 * size**3, bytes_accessed=60 * unit, transcendentals=0),
-    )(at, lent, given[1], *(in_hbm(x) for x in (propagator, amplitude, tab)))
+    )(pos, before, over, given[1], in_hbm(propagator), in_hbm(tab))
     own = call(turn_body, [grid] * len(planes), [VMEM] * (1 + len(planes)), moved=16 * unit)(at, *planes)
     pairs = []
     for came, kept in zip(planes, own):
         pairs += [kept, lax.ppermute(came, "frame", [(i, i ^ 1) for i in range(frames)])]
+    (amp,) = call(functools.partial(measure_body, paired), [grid], [VMEM] * 2, flops=size**3, moved=12 * unit)(
+        amplitude, lent
+    )
     waves, probes = call(
         functools.partial(inner_body, paired),
         [(states, 2) + grid] * 2,

time: 45.6 us -> 43.7 us (0.958)
  waiting for transfers between devices: 16.5 us -> 12.1 us
  starting transfers between devices: 14 us -> 16.5 us
    ppermute x1, waiting for transfers between devices: 8.54 us -> 5.17 us  [gradient_of(): came_one = lax.ppermute(terms[-1], axes, give_route)]
    ppermute x0 -> x2, waiting for transfers between devices: none -> 3.36 us  [the longest x1 3.35 us: gradient_of(): lax.ppermute(positions, axes, [(2 * i, 2 * j) for i, j in up] if paired e...]
    ppermute x0 -> x2, starting transfers between devices: none -> 3.17 us  [the longest x1 2.52 us: gradient_of(): lax.ppermute(positions, axes, [(2 * i, 2 * j) for i, j in up] if paired e...]
    ppermute x1, waiting for transfers between devices: 3.25 us -> 0.64 us  [gradient_of(): halo_one = lax.ppermute(one, axes, halo_route)]
    ppermute x2 -> x1, waiting for transfers between devices: 2.54 us -> 0.01 us  [shifted(): lax.ppermute(value, axis, [(i, (i + by) % count) for i in range(count)])]
    ppermute x2 -> x1, starting transfers between devices: 3.08 us -> 1.29 us  [shifted(): lax.ppermute(value, axis, [(i, (i + by) % count) for i in range(count)])]
    ppermute x1, starting transfers between devices: 2.08 us -> 0.49 us  [gradient_of(): halo_zero = lax.ppermute(zero, axes, halo_route)]
    ppermute x1, starting transfers between devices: 0.56 us -> 1.97 us  [gradient_of(): halo_one = lax.ppermute(one, axes, halo_route)]
  transfers between devices with their start and end apart: 8 -> 9, of which waited for: 6 -> 5; matrix products, arithmetic and copies ran while one was open for 0% -> 0% of each run, Pallas kernels for 25% -> 26%
where the time goes in v9:
time: 43.7 us; the launch traced here: 43.5 us
  starting transfers between devices  16.5 us (38%)
  Pallas kernels  14.7 us (34%)
  waiting for transfers between devices  12.1 us (28%)
    ppermute x1, starting transfers between devices, gradient_of(): came_zero = lax.ppermute(term_zero, axes, give_route)  7.81 us
    ppermute x1, waiting for transfers between devices, gradient_of(): came_one = lax.ppermute(terms[-1], axes, give_route)  5.17 us
    ppermute x1, waiting for transfers between devices, gradient_of(): lax.ppermute(positions, axes, [(2 * i, 2 * j) for i, j in up] if paired e...  3.35 us
    pallas_call x1, Pallas kernels, gradient_of(): pl.pallas_call(functools.partial(prepare_body, paired), out_shape=[jax.Sh...  2.86 us
    pallas_call x1, Pallas kernels, gradient_of(): call(functools.partial(middle_body, paired, rows), [(2, rows, size)] * (2...  2.53 us
    ppermute x1, starting transfers between devices, gradient_of(): lax.ppermute(positions, axes, [(2 * i, 2 * j) for i, j in up] if paired e...  2.52 us
    pallas_call x1, Pallas kernels, gradient_of(): call(functools.partial(inner_body, paired), [(states, 2) + grid] * 2, [VM...  2.36 us
    ppermute x1, starting transfers between devices, gradient_of(): halo_one = lax.ppermute(one, axes, halo_route)  1.97 us
  transfers between devices with their start and end apart: 9, of which 5 were waited for; matrix products, arithmetic and copies ran while one was open for 0% of the time, Pallas kernels for 26%

profile of v9, /device:TPU:0, one launch (start us, length us, event | category | flops | bytes accessed | tf_op | source)
XLA Modules:
  0.0 43.5 jit_solution(18232817142218556606)
XLA Ops:
  0.0 0.0 copy-start.1
  0.0 2.5 %collective-permute-start = (s32[1,2]{1,0:T(1,128)}, s32[1,2]{1,0:T(1,128)S(1)}, u32[]{:S(2)}, u32[]{:S(2)}) collective-permute-start(s32[1,2]{1,0:T(1,128)} %pos_hbm.1), channel_id=1, source_target_pairs={{0,2},{2,4},{4,6},{6,8},{8,10},{10,12},{12,14},{14,16},{16,18},{18... | collective-permute-start | bytes 32 | tf_op jit(solution)/shard_map/ppermute | solution.py:438
  2.5 1.7 %shard_map.64 = (s32[1,2]{1,0:T(1,128)S(1)}, f32[256,256]{1,0:T(8,128)S(1)}, f32[2,2,256,512]{3,2,1,0:T(8,128)S(1)}) custom-call(s32[1,2]{1,0:T(1,128)} %pos_hbm.1, f32[1,2,256,256]{3,2,1,0:T(8,128)} %probe_hbm.3, f32[2,2,256,512]{3,2,1,0:T(8,128)} %object_hbm.1), custom_call_target="tpu_custom_call" | custom-call | bytes 2621440 | tf_op jit(solution)/shard_map/pallas_call | solution.py:441
  4.2 1.3 %collective-permute-start.4 = (f32[256,256]{1,0:T(8,128)S(1)}, f32[256,256]{1,0:T(8,128)S(1)}, u32[]{:S(2)}, u32[]{:S(2)}) collective-permute-start(f32[256,256]{1,0:T(8,128)S(1)} %get-tuple-element.31), channel_id=1, source_target_pairs={{0,1},{1,0},{2,3},{3,2},{4,5},{5,4},{6,7},{7,6},{8,9},{9,8},{10,11... | collective-permute-start | bytes 786440 | tf_op jit(solution)/shard_map/ppermute | solution.py:23
  5.5 3.4 %collective-permute-done.before_ref = s32[1,2]{1,0:T(1,128)S(1)} collective-permute-done((s32[1,2]{1,0:T(1,128)}, s32[1,2]{1,0:T(1,128)S(1)}, u32[]{:S(2)}, u32[]{:S(2)}) %collective-permute-start) | collective-permute-done | bytes 40 | tf_op jit(solution)/shard_map/ppermute | solution.py:438
  8.9 0.2 shard_map.66
  9.1 0.5 %collective-permute-start.3 = (f32[2,256,256]{2,1,0:T(8,128)S(1)}, f32[2,256,256]{2,1,0:T(8,128)S(1)}, u32[]{:S(2)}, u32[]{:S(2)}) collective-permute-start(f32[2,256,256]{2,1,0:T(8,128)S(1)} %get-tuple-element.26), channel_id=1, source_target_pairs={{0,30},{1,3},{2,0},{3,5},{4,2},{5,7},{6,4},{7,9},{8,6},{9,11},{10,... | collective-permute-start | bytes 1572872 | tf_op jit(solution)/shard_map/ppermute | solution.py:464
  9.6 2.0 %collective-permute-start.2 = (f32[2,256,256]{2,1,0:T(8,128)S(1)}, f32[2,256,256]{2,1,0:T(8,128)S(1)}, u32[]{:S(2)}, u32[]{:S(2)}) collective-permute-start(f32[2,256,256]{2,1,0:T(8,128)S(1)} %get-tuple-element.25), channel_id=1, source_target_pairs={{0,30},{1,3},{2,0},{3,5},{4,2},{5,7},{6,4},{7,9},{8,6},{9,11},{10,... | collective-permute-start | bytes 1572872 | tf_op jit(solution)/shard_map/ppermute | solution.py:465
  11.5 0.0 copy-done
  11.5 1.3 %collective-permute-start.6 = (f32[1,256,256]{2,1,0:T(8,128)S(1)}, f32[1,256,256]{2,1,0:T(8,128)S(1)}, u32[]{:S(2)}, u32[]{:S(2)}) collective-permute-start(f32[1,256,256]{2,1,0:T(8,128)S(1)} %copy-done), channel_id=1, source_target_pairs={{0,3},{2,5},{4,7},{6,9},{8,11},{10,13},{12,15},{14,17},{16,19},{18... | collective-permute-start | bytes 786440 | tf_op jit(solution)/shard_map/ppermute | solution.py:466
  12.8 0.0 collective-permute-done.4.refs_0_
  12.8 0.5 %collective-permute-start.5 = (f32[256,256]{1,0:T(8,128)S(1)}, f32[256,256]{1,0:T(8,128)S(1)}, u32[]{:S(2)}, u32[]{:S(2)}) collective-permute-start(f32[256,256]{1,0:T(8,128)S(1)} %collective-permute-done.4.refs_0_), channel_id=1, source_target_pairs={{0,2},{2,0},{4,6},{6,4},{8,10},{10,8},{12,14},{14,12},{16,18},{18,... | collective-permute-start | bytes 786440 | tf_op jit(solution)/shard_map/ppermute | solution.py:481
  13.3 0.0 copy-done.1
  13.3 0.7 %collective-permute-start.1 = (s32[1,2]{1,0:T(1,128)S(1)}, s32[1,2]{1,0:T(1,128)S(1)}, u32[]{:S(2)}, u32[]{:S(2)}) collective-permute-start(s32[1,2]{1,0:T(1,128)S(1)} %copy-done.1), channel_id=1, source_target_pairs={{1,3},{3,5},{5,7},{7,9},{9,11},{11,13},{13,15},{15,17},{17,19},{19... | collective-permute-start | bytes 32 | tf_op jit(solution)/shard_map/ppermute | solution.py:439
  14.0 0.0 collective-permute-done.1.over_ref
  14.0 2.9 %shard_map.65 = (s32[2,2]{1,0:T(2,128)S(1)}, f32[256,256]{1,0:T(8,128)S(1)}, f32[256,256]{1,0:T(8,128)S(1)}, f32[1,2,256,256]{3,2,1,0:T(8,128)S(1)}, bf16[2,4,256,256]{3,2,1,0:T(8,128)(2,1)S(1)}) custom-call(s32[1,2]{1,0:T(1,128)S(1)} %get-tuple-element.22.pos_ref, s32[1,2]{1,0:T(1,128)S(1)} %collective-permute-done.before_ref, ...), custom_call_target="tpu_custom_call" | custom-call | flops 33554432 | bytes 3932160 | tf_op jit(solution)/shard_map/pallas_call | solution.py:467
  16.8 0.2 shard_map.67.refs_0_
  17.1 1.1 %collective-permute-done.6.lent_ref = f32[1,256,256]{2,1,0:T(8,128)S(1)} collective-permute-done((f32[1,256,256]{2,1,0:T(8,128)S(1)}, f32[1,256,256]{2,1,0:T(8,128)S(1)}, u32[]{:S(2)}, u32[]{:S(2)}) %collective-permute-start.6) | collective-permute-done | bytes 262176 | tf_op jit(solution)/shard_map/ppermute | solution.py:466
  18.2 0.6 %shard_map.69.amp_ref = f32[256,256]{1,0:T(8,128)S(1)} custom-call(f32[1,256,256]{2,1,0:T(8,128)S(1)} %copy-done, f32[1,256,256]{2,1,0:T(8,128)S(1)} %collective-permute-done.6.lent_ref), custom_call_target="tpu_custom_call" | custom-call | flops 16777216 | bytes 786432 | tf_op jit(solution)/shard_map/pallas_call | solution.py:482
  18.8 0.0 collective-permute-done.5.refs_1_
  18.9 0.0 collective-permute-done.3.halo_ref
  18.9 2.4 %shard_map.68 = (f32[2,2,256,256]{3,2,1,0:T(8,128)S(1)}, f32[2,2,256,256]{3,2,1,0:T(8,128)S(1)}) custom-call(s32[2,2]{1,0:T(2,128)S(1)} %get-tuple-element.23.at_ref, f32[2,2,256,512]{3,2,1,0:T(8,128)S(1)} %get-tuple-element.24.object_ref, f32[2,256,256]{2,1,0:T(8,128)S(1)} %collective-permute-done.3.halo_ref, ...), custom_call_target="tpu_custom_call" | custom-call | flops 1610612736 | bytes 3145728 | tf_op jit(solution)/shard_map/pallas_call | solution.py:485
  21.2 0.6 %collective-permute-done.2.halo_ref = f32[2,256,256]{2,1,0:T(8,128)S(1)} collective-permute-done((f32[2,256,256]{2,1,0:T(8,128)S(1)}, f32[2,256,256]{2,1,0:T(8,128)S(1)}, u32[]{:S(2)}, u32[]{:S(2)}) %collective-permute-start.2) | collective-permute-done | bytes 524320 | tf_op jit(solution)/shard_map/ppermute | solution.py:465
  21.9 2.5 %shard_map.70 = (f32[2,128,256]{2,1,0:T(8,128)S(1)}, f32[2,128,256]{2,1,0:T(8,128)S(1)}, f32[2,2,256,256]{3,2,1,0:T(8,128)S(1)}) custom-call(s32[2,2]{1,0:T(2,128)S(1)} %get-tuple-element.23.at_ref, f32[2,2,256,512]{3,2,1,0:T(8,128)S(1)} %get-tuple-element.24.object_ref, f32[2,256,256]{2,1,0:T(8,128)S(1)} %collective-permute-done.2.halo_ref, ...), custom_call_target="tpu_custom_call" | custom-call | flops 1610612736 | bytes 4194304 | tf_op jit(solution)/shard_map/pallas_call | solution.py:493
  24.4 0.0 collective-permute-start.8
  24.4 1.9 %shard_map.71 = (f32[2,128,256]{2,1,0:T(8,128)S(1)}, f32[2,2,256,256]{3,2,1,0:T(8,128)S(1)}) custom-call(f32[2,2,256,256]{3,2,1,0:T(8,128)S(1)} %get-tuple-element.33.chi_ref, f32[2,2,256,256]{3,2,1,0:T(8,128)S(1)} %get-tuple-element.34.probe_ref, f32[256,256]{1,0:T(8,128)S(1)} %get-tuple-element.28.kr_ref, f32[256,256]{1,0:T(8,128)S(1)} %get-tuple-element.29.ki_ref, ...), custom_call_target="tpu_custom_call" | custom-call | flops 1610612736 | bytes 2097152 | tf_op jit(solution)/shard_map/pallas_call | solution.py:502
  26.3 7.8 %collective-permute-start.7 = (f32[2,128,256]{2,1,0:T(8,128)S(1)}, f32[2,128,256]{2,1,0:T(8,128)S(1)}, u32[]{:S(2)}, u32[]{:S(2)}) collective-permute-start(f32[2,128,256]{2,1,0:T(8,128)S(1)} %get-tuple-element.36), channel_id=1, source_target_pairs={{0,2},{1,0},{2,3},{3,1},{4,6},{5,4},{6,7},{7,5},{8,10},{9,8},{10,1... | collective-permute-start | bytes 786440 | tf_op jit(solution)/shard_map/ppermute | solution.py:509
  34.1 0.4 shard_map.72.own_ref
  34.6 5.2 %collective-permute-done.8.came_ref = f32[2,128,256]{2,1,0:T(8,128)S(1)} collective-permute-done((f32[2,128,256]{2,1,0:T(8,128)S(1)}, f32[2,128,256]{2,1,0:T(8,128)S(1)}, u32[]{:S(2)}, u32[]{:S(2)}) %collective-permute-start.8) | collective-permute-done | bytes 262176 | tf_op jit(solution)/shard_map/ppermute | solution.py:501
  39.7 1.0 %shard_map.73.refs_0_ = f32[2,2,128,512]{3,2,1,0:T(8,128)} custom-call(s32[2,2]{1,0:T(2,128)S(1)} %get-tuple-element.23.at_ref, f32[2,128,256]{2,1,0:T(8,128)S(1)} %get-tuple-element.37.own_ref, f32[2,128,256]{2,1,0:T(8,128)S(1)} %collective-permute-done.8.came_ref), custom_call_target="tpu_custom_call" | custom-call | bytes 1048576 | tf_op jit(solution)/shard_map/pallas_call | solution.py:395
  40.7 1.8 %collective-permute-done.7.came_ref = f32[2,128,256]{2,1,0:T(8,128)S(1)} collective-permute-done((f32[2,128,256]{2,1,0:T(8,128)S(1)}, f32[2,128,256]{2,1,0:T(8,128)S(1)}, u32[]{:S(2)}, u32[]{:S(2)}) %collective-permute-start.7) | collective-permute-done | bytes 262176 | tf_op jit(solution)/shard_map/ppermute | solution.py:509
  42.5 1.0 %shard_map.74 = f32[2,2,128,512]{3,2,1,0:T(8,128)} custom-call(s32[2,2]{1,0:T(2,128)S(1)} %get-tuple-element.23.at_ref, f32[2,128,256]{2,1,0:T(8,128)S(1)} %shard_map.72.own_ref, f32[2,128,256]{2,1,0:T(8,128)S(1)} %collective-permute-done.7.came_ref, f32[2,2,128,512]{3,2,1,0:T(8,128)} %shard_map.73.refs_0_), custom_call_target="tpu_custom_call", output_to_operand_aliasing={{}: (3, {})} | custom-call | bytes 1048576 | tf_op jit(solution)/shard_map/pallas_call | solution.py:395
  (1 shorter events, 0.0 us)
Async XLA Ops:
  0.0 13.3 %copy-start.1 = (s32[1,2]{1,0:T(1,128)S(1)}, s32[1,2]{1,0:T(1,128)}, u32[]{:S(2)}) copy-start(s32[1,2]{1,0:T(1,128)} %pos_hbm.1) | copy-start | bytes 28
  0.0 11.5 %copy-start = (f32[1,256,256]{2,1,0:T(8,128)S(1)}, f32[1,256,256]{2,1,0:T(8,128)}, u32[]{:S(2)}) copy-start(f32[1,256,256]{2,1,0:T(8,128)} %amp_ref.1) | copy-start | bytes 786436
  0.0 8.9 %collective-permute-start = (s32[1,2]{1,0:T(1,128)}, s32[1,2]{1,0:T(1,128)S(1)}, u32[]{:S(2)}, u32[]{:S(2)}) collective-permute-start(s32[1,2]{1,0:T(1,128)} %pos_hbm.1), channel_id=1, source_target_pairs={{0,2},{2,4},{4,6},{6,8},{8,10},{10,12},{12,14},{14,16},{16,18},{18... | collective-permute-start | bytes 32 | tf_op jit(solution)/shard_map/ppermute | solution.py:438
  4.2 8.6 %collective-permute-start.4 = (f32[256,256]{1,0:T(8,128)S(1)}, f32[256,256]{1,0:T(8,128)S(1)}, u32[]{:S(2)}, u32[]{:S(2)}) collective-permute-start(f32[256,256]{1,0:T(8,128)S(1)} %get-tuple-element.31), channel_id=1, source_target_pairs={{0,1},{1,0},{2,3},{3,2},{4,5},{5,4},{6,7},{7,6},{8,9},{9,8},{10,11... | collective-permute-start | bytes 786440 | tf_op jit(solution)/shard_map/ppermute | solution.py:23
  9.1 9.8 %collective-permute-start.3 = (f32[2,256,256]{2,1,0:T(8,128)S(1)}, f32[2,256,256]{2,1,0:T(8,128)S(1)}, u32[]{:S(2)}, u32[]{:S(2)}) collective-permute-start(f32[2,256,256]{2,1,0:T(8,128)S(1)} %get-tuple-element.26), channel_id=1, source_target_pairs={{0,30},{1,3},{2,0},{3,5},{4,2},{5,7},{6,4},{7,9},{8,6},{9,11},{10,... | collective-permute-start | bytes 1572872 | tf_op jit(solution)/shard_map/ppermute | solution.py:464
  9.6 12.3 %collective-permute-start.2 = (f32[2,256,256]{2,1,0:T(8,128)S(1)}, f32[2,256,256]{2,1,0:T(8,128)S(1)}, u32[]{:S(2)}, u32[]{:S(2)}) collective-permute-start(f32[2,256,256]{2,1,0:T(8,128)S(1)} %get-tuple-element.25), channel_id=1, source_target_pairs={{0,30},{1,3},{2,0},{3,5},{4,2},{5,7},{6,4},{7,9},{8,6},{9,11},{10,... | collective-permute-start | bytes 1572872 | tf_op jit(solution)/shard_map/ppermute | solution.py:465
  11.5 6.7 %collective-permute-start.6 = (f32[1,256,256]{2,1,0:T(8,128)S(1)}, f32[1,256,256]{2,1,0:T(8,128)S(1)}, u32[]{:S(2)}, u32[]{:S(2)}) collective-permute-start(f32[1,256,256]{2,1,0:T(8,128)S(1)} %copy-done), channel_id=1, source_target_pairs={{0,3},{2,5},{4,7},{6,9},{8,11},{10,13},{12,15},{14,17},{16,19},{18... | collective-permute-start | bytes 786440 | tf_op jit(solution)/shard_map/ppermute | solution.py:466
  12.8 6.0 %collective-permute-start.5 = (f32[256,256]{1,0:T(8,128)S(1)}, f32[256,256]{1,0:T(8,128)S(1)}, u32[]{:S(2)}, u32[]{:S(2)}) collective-permute-start(f32[256,256]{1,0:T(8,128)S(1)} %collective-permute-done.4.refs_0_), channel_id=1, source_target_pairs={{0,2},{2,0},{4,6},{6,4},{8,10},{10,8},{12,14},{14,12},{16,18},{18,... | collective-permute-start | bytes 786440 | tf_op jit(solution)/shard_map/ppermute | solution.py:481
  13.3 0.7 %collective-permute-start.1 = (s32[1,2]{1,0:T(1,128)S(1)}, s32[1,2]{1,0:T(1,128)S(1)}, u32[]{:S(2)}, u32[]{:S(2)}) collective-permute-start(s32[1,2]{1,0:T(1,128)S(1)} %copy-done.1), channel_id=1, source_target_pairs={{1,3},{3,5},{5,7},{7,9},{9,11},{11,13},{13,15},{15,17},{17,19},{19... | collective-permute-start | bytes 32 | tf_op jit(solution)/shard_map/ppermute | solution.py:439
  24.4 15.3 %collective-permute-start.8 = (f32[2,128,256]{2,1,0:T(8,128)S(1)}, f32[2,128,256]{2,1,0:T(8,128)S(1)}, u32[]{:S(2)}, u32[]{:S(2)}) collective-permute-start(f32[2,128,256]{2,1,0:T(8,128)S(1)} %get-tuple-element.38), channel_id=1, source_target_pairs={{0,2},{1,0},{2,3},{3,1},{4,6},{5,4},{6,7},{7,5},{8,10},{9,8},{10,1... | collective-permute-start | bytes 786440 | tf_op jit(solution)/shard_map/ppermute | solution.py:501
  26.3 16.2 %collective-permute-start.7 = (f32[2,128,256]{2,1,0:T(8,128)S(1)}, f32[2,128,256]{2,1,0:T(8,128)S(1)}, u32[]{:S(2)}, u32[]{:S(2)}) collective-permute-start(f32[2,128,256]{2,1,0:T(8,128)S(1)} %get-tuple-element.36), channel_id=1, source_target_pairs={{0,2},{1,0},{2,3},{3,1},{4,6},{5,4},{6,7},{7,5},{8,10},{9,8},{10,1... | collective-permute-start | bytes 786440 | tf_op jit(solution)/shard_map/ppermute | solution.py:509

commit v10 on v6

--- a/solution.py
+++ b/solution.py
@@ -182,14 +182,18 @@
     return copies
 
 
+def quarters(object_hbm, s, out):
+    half = object_hbm.shape[2] // 2
+    return [
+        (object_hbm.at[s, part, at], out.at[part, at])
+        for part in range(2)
+        for at in (pl.ds(0, half), pl.ds(half, half))
+    ]
+
+
 def load_body(pos_hbm, probe_hbm, object_hbm, pos_out, plane_out, object_out, sem):
     which = lax.rem(lax.axis_index("frame"), 2)
-    half = object_hbm.shape[2] // 2
-    moves = [(probe_hbm.at[0, which], plane_out), (pos_hbm, pos_out)]
-    for s in range(2):
-        for part in range(2):
-            for at in (pl.ds(0, half), pl.ds(half, half)):
-                moves.append((object_hbm.at[s, part, at], object_out.at[s, part, at]))
+    moves = [(probe_hbm.at[0, which], plane_out), (pos_hbm, pos_out)] + quarters(object_hbm, 0, object_out)
     for copy in run_copies(moves, sem):
         copy.wait()
 
@@ -232,23 +236,29 @@
     return jnp.broadcast_to(ref[0:1, which : which + 1], shape)
 
 
-def wrapped(ref, s, part, col_ref):
+def wrapped(ref, part, col_ref):
     size = ref.shape[-2]
     c = lax.broadcasted_iota(jnp.int32, (size, size), 1)
-    return jnp.where(c < spread(col_ref, 1, c.shape), ref[s, part, :, size:], ref[s, part, :, :size])
-
-
-def send_body(before_ref, object_ref, zero_ref, one_ref):
-    for s, out in enumerate((zero_ref, one_ref)):
-        for part in range(2):
-            out[part] = wrapped(object_ref, s, part, before_ref)
-
-
-def patch_of(s, object_ref, halo_ref, pos_ref):
+    return jnp.where(c < spread(col_ref, 1, c.shape), ref[part, :, size:], ref[part, :, :size])
+
+
+def send_body(before_ref, object_ref, out_ref):
+    for part in range(2):
+        out_ref[part] = wrapped(object_ref, part, before_ref)
+
+
+def load_send_body(before_ref, object_hbm, object_out, out_ref, sem):
+    copies = run_copies(quarters(object_hbm, 1, object_out), sem)
+    for copy in copies:
+        copy.wait()
+    send_body(before_ref, object_out, out_ref)
+
+
+def patch_of(object_ref, halo_ref, pos_ref):
     size = halo_ref.shape[-1]
     r = lax.broadcasted_iota(jnp.int32, (size, size), 0)
     return [
-        jnp.where(r < spread(pos_ref, 0, r.shape), halo_ref[part], wrapped(object_ref, s, part, pos_ref))
+        jnp.where(r < spread(pos_ref, 0, r.shape), halo_ref[part], wrapped(object_ref, part, pos_ref))
         for part in range(2)
     ]
 
@@ -260,7 +270,7 @@
 def inner_body(pos_ref, object_ref, halo_ref, first_ref, kr_ref, ki_ref, tab, *refs):
     out_ref, probe_ref, patch = refs[-3:]
     states = out_ref.shape[0]
-    patch[0], patch[1] = patch_of(0, object_ref, halo_ref, pos_ref)
+    patch[0], patch[1] = patch_of(object_ref, halo_ref, pos_ref)
     swap = lax.rem(lax.axis_index("frame"), 2) == 1
     probe_ref[:1] = first_ref[...]
     for m, (came, given) in enumerate(zip(refs[:-3:2], refs[1:-3:2])):
@@ -277,9 +287,9 @@
     in_groups(states, body)
 
 
-def middle_body(rows, pos_ref, object_ref, halo_ref, inner_ref, amp_ref, tab, term_ref, chi_ref, patch, far, power):
+def middle_body(rows, pos_ref, object_ref, halo_ref, inner_ref, amp_ref, tab, term_ref, half_ref, patch, far, power):
     states = inner_ref.shape[0]
-    patch[0], patch[1] = patch_of(1, object_ref, halo_ref, pos_ref)
+    patch[0], patch[1] = patch_of(object_ref, halo_ref, pos_ref)
     power[...] = jnp.zeros_like(power)
 
     def outward(group):
@@ -296,27 +306,26 @@
     take = pl.ds(pl.multiple_of(lax.axis_index("state") * rows, rows), rows)
 
     def homeward(group):
-        waves = inverse([(power[...] * far[m, 0], power[...] * far[m, 1]) for m in group], tab)
+        waves = [rows_inverse(power[...] * far[m, 0], power[...] * far[m, 1], tab) for m in group]
         for m, wave in zip(group, waves):
-            far[m, 0], far[m, 1] = wave
-            chi_ref[m, 0], chi_ref[m, 1] = times_conj(pair(patch), wave)
+            half_ref[m, 0], half_ref[m, 1] = wave
         for m in group:
-            part = times_conj(
-                (inner_ref[m, 0, take], inner_ref[m, 1, take]), (far[m, 0, take], far[m, 1, take])
-            )
+            wave = columns_inverse(half_ref[m, 0, take], half_ref[m, 1, take], tab)
+            part = times_conj((inner_ref[m, 0, take], inner_ref[m, 1, take]), wave)
             term_ref[0] += part[0]
             term_ref[1] += part[1]
 
     in_groups(states, homeward)
 
 
-def last_body(rows, chi_ref, probe_ref, kr_ref, ki_ref, tab, term_ref, front):
-    states = chi_ref.shape[0]
+def last_body(rows, half_ref, patch, probe_ref, kr_ref, ki_ref, tab, term_ref, front):
+    states = half_ref.shape[0]
     take = pl.ds(pl.multiple_of(lax.axis_index("state") * rows, rows), rows)
     term_ref[...] = jnp.zeros_like(term_ref)
 
     def body(group):
-        waves = forward([pair(chi_ref, m) for m in group], tab)
+        waves = [columns_inverse(*pair(half_ref, m), tab) for m in group]
+        waves = forward([times_conj(pair(patch), wave) for wave in waves], tab)
         waves = [rows_inverse(*times_conj((kr_ref[...], ki_ref[...]), wave), tab) for wave in waves]
         for m, wave in zip(group, waves):
             front[m, 0], front[m, 1] = wave
@@ -386,25 +395,32 @@
     tab = tables(size)
     before = shifted(positions, "frame", 1)
     given = [in_hbm(x) for x in (positions, probe, object_slices)]
-    pos, plane, held = pl.pallas_call(
+    pos, plane, held_zero = pl.pallas_call(
         load_body,
         out_shape=[
             jax.ShapeDtypeStruct(positions.shape, jnp.int32),
             jax.ShapeDtypeStruct(grid, F32),
-            jax.ShapeDtypeStruct(object_slices.shape, F32),
+            jax.ShapeDtypeStruct(object_slices.shape[1:], F32),
         ],
         in_specs=[HBM] * 3,
         out_specs=[VMEM] * 3,
-        scratch_shapes=[pltpu.SemaphoreType.DMA((10,))],
+        scratch_shapes=[pltpu.SemaphoreType.DMA((6,))],
         compiler_params=pltpu.CompilerParams(vmem_limit_bytes=LIMIT),
-        cost_estimate=pl.CostEstimate(flops=0, bytes_accessed=40 * unit, transcendentals=0),
+        cost_estimate=pl.CostEstimate(flops=0, bytes_accessed=24 * unit, transcendentals=0),
     )(*given)
     planes = []
     for by in range(1, states):
         planes.append(shifted(plane, "state", by))
-    picked = call(send_body, [(2,) + grid] * 2, [VMEM, VMEM], moved=16 * unit)(before, held)
-    halo_zero = shifted(picked[0], "frame", -1)
-    halo_one = shifted(picked[1], "frame", -1)
+    (picked,) = call(send_body, [(2,) + grid], [VMEM, VMEM], moved=24 * unit)(before, held_zero)
+    halo_zero = shifted(picked, "frame", -1)
+    held_one, picked = call(
+        load_send_body,
+        [object_slices.shape[1:], (2,) + grid],
+        [VMEM, HBM],
+        [pltpu.SemaphoreType.DMA((4,))],
+        moved=40 * unit,
+    )(before, given[2])
+    halo_one = shifted(picked, "frame", -1)
     kr, ki, amp, first, tab = pl.pallas_call(
         prepare_body,
         out_shape=[jax.ShapeDtypeStruct(grid, F32)] * 3
@@ -433,24 +449,24 @@
         [pltpu.VMEM((2,) + grid, F32)],
         flops=2 * flops * states,
         moved=24 * unit * states,
-    )(pos, held, halo_zero, first, kr, ki, tab, *pairs)
-    term_one, chi = call(
+    )(pos, held_zero, halo_zero, first, kr, ki, tab, *pairs)
+    term_one, half, patch = call(
         functools.partial(middle_body, rows),
-        [(2, rows, size), (states, 2) + grid],
+        [(2, rows, size), (states, 2) + grid, (2,) + grid],
         [VMEM] * 6,
-        [pltpu.VMEM((2,) + grid, F32), pltpu.VMEM((states, 2) + grid, F32), pltpu.VMEM(grid, F32)],
+        [pltpu.VMEM((states, 2) + grid, F32), pltpu.VMEM(grid, F32)],
         flops=2 * flops * states,
         moved=32 * unit * states,
-    )(pos, held, halo_one, waves, amp, tab)
+    )(pos, held_one, halo_one, waves, amp, tab)
     came_one = shifted(term_one, "frame", 1)
     (term_zero,) = call(
         functools.partial(last_body, rows),
         [(2, rows, size)],
-        [VMEM] * 5,
+        [VMEM] * 6,
         [pltpu.VMEM((states, 2) + grid, F32)],
         flops=2 * flops * states,
         moved=16 * unit * states,
-    )(chi, probes, kr, ki, tab)
+    )(half, patch, probes, kr, ki, tab)
     came_zero = shifted(term_zero, "frame", 1)
     gradient = gather(1, rows, size, pos, before, term_one, came_one)
     return gather(0, rows, size, pos, before, term_zero, came_zero, gradient)

time: 36.5 us -> 35.8 us (0.981)
  waiting for transfers between devices: 15.4 us -> 14.1 us
  Pallas kernels: 14.1 us -> 15.2 us
  starting transfers between devices: 6.69 us -> 6.19 us
    pallas_call x2 -> x3, Pallas kernels: 2.08 us -> 3.86 us  [the longest x1 2.41 us: gradient_of(): call(functools.partial(last_body, rows), [(2, rows, size)], [VMEM] * 6, [...]
    ppermute x6, waiting for transfers between devices: 15.4 us -> 14.1 us  [shifted(): lax.ppermute(value, axis, [(i, (i + by) % count) for i in range(count)])]
    ppermute x1, starting transfers between devices: 0.95 us -> 0.51 us  [gradient_of(): lax.ppermute(came, 'frame', [(i, i ^ 1) for i in range(frames)])]
  transfers between devices with their start and end apart: 7 -> 7, of which waited for: 6 -> 5; matrix products, arithmetic and copies ran while one was open for 0% -> 0% of each run, Pallas kernels for 30% -> 34%
where the time goes in v10:
time: 35.8 us; the launch traced here: 35.6 us
  Pallas kernels  15.2 us (42%)
  waiting for transfers between devices  14.1 us (39%)
  starting transfers between devices  6.19 us (17%)
    ppermute x6, waiting for transfers between devices, shifted(): lax.ppermute(value, axis, [(i, (i + by) % count) for i in range(count)])  14.1 us
    ppermute x6, starting transfers between devices, shifted(): lax.ppermute(value, axis, [(i, (i + by) % count) for i in range(count)])  5.67 us
    pallas_call x1, Pallas kernels, gradient_of(): pl.pallas_call(prepare_body, out_shape=[jax.ShapeDtypeStruct(grid, F32)]...  3.42 us
    pallas_call x1, Pallas kernels, gradient_of(): call(functools.partial(last_body, rows), [(2, rows, size)], [VMEM] * 6, [...  2.41 us
    pallas_call x1, Pallas kernels, gradient_of(): call(inner_body, [(states, 2) + grid] * 2, [VMEM] * (7 + len(pairs)), [pl...  2.35 us
    pallas_call x1, Pallas kernels, gradient_of(): call(functools.partial(middle_body, rows), [(2, rows, size), (states, 2)...  2.12 us
    pallas_call x2, Pallas kernels, gather(): pl.pallas_call(functools.partial(gather_body, slice_id, rows), out_shape=...  1.88 us
    pallas_call x1, Pallas kernels, gradient_of(): call(load_send_body, [object_slices.shape[1:], (2,) + grid], [VMEM, HBM],...  1.33 us
  transfers between devices with their start and end apart: 7, of which 5 were waited for; matrix products, arithmetic and copies ran while one was open for 0% of the time, Pallas kernels for 34%

profile of v10, /device:TPU:0, one launch (start us, length us, event | category | flops | bytes accessed | tf_op | source)
XLA Modules:
  0.0 35.6 jit_solution(1086359024862935699)
XLA Ops:
  0.0 0.5 %collective-permute-start = (s32[1,2]{1,0:T(1,128)}, s32[1,2]{1,0:T(1,128)S(1)}, u32[]{:S(2)}, u32[]{:S(2)}) collective-permute-start(s32[1,2]{1,0:T(1,128)} %pos_hbm.3), channel_id=1, source_target_pairs={{0,2},{2,4},{4,6},{6,8},{8,10},{10,12},{12,14},{14,16},{16,18},{18... | collective-permute-start | bytes 32 | tf_op jit(solution)/shard_map/ppermute | solution.py:23
  0.5 1.3 %shard_map.64 = (s32[1,2]{1,0:T(1,128)S(1)}, f32[256,256]{1,0:T(8,128)S(1)}, f32[2,256,512]{2,1,0:T(8,128)S(1)}) custom-call(s32[1,2]{1,0:T(1,128)} %pos_hbm.3, f32[1,2,256,256]{3,2,1,0:T(8,128)} %probe_hbm.3, f32[2,2,256,512]{3,2,1,0:T(8,128)} %object_hbm.3), custom_call_target="tpu_custom_call" | custom-call | bytes 1572864 | tf_op jit(solution)/shard_map/pallas_call | solution.py:398
  1.8 2.5 %collective-permute-start.3 = (f32[256,256]{1,0:T(8,128)S(1)}, f32[256,256]{1,0:T(8,128)S(1)}, u32[]{:S(2)}, u32[]{:S(2)}) collective-permute-start(f32[256,256]{1,0:T(8,128)S(1)} %get-tuple-element.28), channel_id=1, source_target_pairs={{0,1},{1,0},{2,3},{3,2},{4,5},{5,4},{6,7},{7,6},{8,9},{9,8},{10,11... | collective-permute-start | bytes 786440 | tf_op jit(solution)/shard_map/ppermute | solution.py:23
  4.4 2.5 %collective-permute-done.before_ref = s32[1,2]{1,0:T(1,128)S(1)} collective-permute-done((s32[1,2]{1,0:T(1,128)}, s32[1,2]{1,0:T(1,128)S(1)}, u32[]{:S(2)}, u32[]{:S(2)}) %collective-permute-start) | collective-permute-done | bytes 40 | tf_op jit(solution)/shard_map/ppermute | solution.py:23
  6.9 0.1 shard_map.66
  7.0 1.7 %collective-permute-start.2 = (f32[2,256,256]{2,1,0:T(8,128)S(1)}, f32[2,256,256]{2,1,0:T(8,128)S(1)}, u32[]{:S(2)}, u32[]{:S(2)}) collective-permute-start(f32[2,256,256]{2,1,0:T(8,128)S(1)} %shard_map.66), channel_id=1, source_target_pairs={{0,30},{2,0},{4,2},{6,4},{8,6},{10,8},{12,10},{14,12},{16,14},{18,... | collective-permute-start | bytes 1572872 | tf_op jit(solution)/shard_map/ppermute | solution.py:23
  8.7 1.3 %shard_map.65 = (f32[2,256,512]{2,1,0:T(8,128)S(1)}, f32[2,256,256]{2,1,0:T(8,128)S(1)}) custom-call(s32[1,2]{1,0:T(1,128)S(1)} %collective-permute-done.before_ref, f32[2,2,256,512]{3,2,1,0:T(8,128)} %object_hbm.3), custom_call_target="tpu_custom_call" | custom-call | bytes 2621440 | tf_op jit(solution)/shard_map/pallas_call | solution.py:416
  10.1 0.8 %collective-permute-start.1 = (f32[2,256,256]{2,1,0:T(8,128)S(1)}, f32[2,256,256]{2,1,0:T(8,128)S(1)}, u32[]{:S(2)}, u32[]{:S(2)}) collective-permute-start(f32[2,256,256]{2,1,0:T(8,128)S(1)} %get-tuple-element.22), channel_id=1, source_target_pairs={{0,30},{2,0},{4,2},{6,4},{8,6},{10,8},{12,10},{14,12},{16,14},{18,... | collective-permute-start | bytes 1572872 | tf_op jit(solution)/shard_map/ppermute | solution.py:23
  10.8 0.0 collective-permute-done.3.refs_0_
  10.8 0.5 %collective-permute-start.4 = (f32[256,256]{1,0:T(8,128)S(1)}, f32[256,256]{1,0:T(8,128)S(1)}, u32[]{:S(2)}, u32[]{:S(2)}) collective-permute-start(f32[256,256]{1,0:T(8,128)S(1)} %collective-permute-done.3.refs_0_), channel_id=1, source_target_pairs={{0,2},{2,0},{4,6},{6,4},{8,10},{10,8},{12,14},{14,12},{16,18},{18,... | collective-permute-start | bytes 786440 | tf_op jit(solution)/shard_map/ppermute | solution.py:444
  11.4 3.4 %shard_map.67 = (f32[256,256]{1,0:T(8,128)S(1)}, f32[256,256]{1,0:T(8,128)S(1)}, f32[256,256]{1,0:T(8,128)S(1)}, f32[1,2,256,256]{3,2,1,0:T(8,128)S(1)}, bf16[2,4,256,256]{3,2,1,0:T(8,128)(2,1)S(1)}) custom-call(s32[1,2]{1,0:T(1,128)} %pos_hbm.3, f32[1,2,256,256]{3,2,1,0:T(8,128)} %probe_hbm.3, f32[256,256]{1,0:T(8,128)} %prop_hbm.1, ...), custom_call_target="tpu_custom_call" | custom-call | flops 33554432 | bytes 3932160 | tf_op jit(solution)/shard_map/pallas_call | solution.py:424
  14.8 0.2 shard_map.68.refs_0_
  15.0 0.0 collective-permute-done.4.refs_1_
  15.0 0.4 %collective-permute-done.2.halo_ref = f32[2,256,256]{2,1,0:T(8,128)S(1)} collective-permute-done((f32[2,256,256]{2,1,0:T(8,128)S(1)}, f32[2,256,256]{2,1,0:T(8,128)S(1)}, u32[]{:S(2)}, u32[]{:S(2)}) %collective-permute-start.2) | collective-permute-done | bytes 524320 | tf_op jit(solution)/shard_map/ppermute | solution.py:23
  15.4 2.4 %shard_map.69 = (f32[2,2,256,256]{3,2,1,0:T(8,128)S(1)}, f32[2,2,256,256]{3,2,1,0:T(8,128)S(1)}) custom-call(s32[1,2]{1,0:T(1,128)S(1)} %get-tuple-element.20.pos_ref, f32[2,256,512]{2,1,0:T(8,128)S(1)} %get-tuple-element.23.object_ref, f32[2,256,256]{2,1,0:T(8,128)S(1)} %collective-permute-done.2.halo_ref, ...), custom_call_target="tpu_custom_call" | custom-call | flops 1610612736 | bytes 3145728 | tf_op jit(solution)/shard_map/pallas_call | solution.py:445
  17.8 3.3 %collective-permute-done.1.halo_ref = f32[2,256,256]{2,1,0:T(8,128)S(1)} collective-permute-done((f32[2,256,256]{2,1,0:T(8,128)S(1)}, f32[2,256,256]{2,1,0:T(8,128)S(1)}, u32[]{:S(2)}, u32[]{:S(2)}) %collective-permute-start.1) | collective-permute-done | bytes 524320 | tf_op jit(solution)/shard_map/ppermute | solution.py:23
  21.0 2.1 %shard_map.70 = (f32[2,128,256]{2,1,0:T(8,128)S(1)}, f32[2,2,256,256]{3,2,1,0:T(8,128)S(1)}, f32[2,256,256]{2,1,0:T(8,128)S(1)}) custom-call(s32[1,2]{1,0:T(1,128)S(1)} %get-tuple-element.20.pos_ref, f32[2,256,512]{2,1,0:T(8,128)S(1)} %get-tuple-element.21.object_ref, f32[2,256,256]{2,1,0:T(8,128)S(1)} %collective-permute-done.1.halo_ref, ...), custom_call_target="tpu_custom_call" | custom-call | flops 1610612736 | bytes 4194304 | tf_op jit(solution)/shard_map/pallas_call | solution.py:453
  23.2 0.1 collective-permute-start.6
  23.2 2.4 %shard_map.71.own_ref = f32[2,128,256]{2,1,0:T(8,128)S(1)} custom-call(f32[2,2,256,256]{3,2,1,0:T(8,128)S(1)} %get-tuple-element.31.half_ref, f32[2,256,256]{2,1,0:T(8,128)S(1)} %get-tuple-element.32.patch, f32[2,2,256,256]{3,2,1,0:T(8,128)S(1)} %get-tuple-element.33.probe_ref, f32[256,256]{1,0:T(8,128)S(1)} %get-tuple-element.25.kr_ref, ...), custom_call_target="tpu_custom_call" | custom-call | flops 1610612736 | bytes 2097152 | tf_op jit(solution)/shard_map/pallas_call | solution.py:462
  25.6 0.1 collective-permute-start.5
  25.7 6.2 %collective-permute-done.6.came_ref = f32[2,128,256]{2,1,0:T(8,128)S(1)} collective-permute-done((f32[2,128,256]{2,1,0:T(8,128)S(1)}, f32[2,128,256]{2,1,0:T(8,128)S(1)}, u32[]{:S(2)}, u32[]{:S(2)}) %collective-permute-start.6) | collective-permute-done | bytes 262176 | tf_op jit(solution)/shard_map/ppermute | solution.py:23
  31.9 0.9 %shard_map.72.refs_0_ = f32[2,2,128,512]{3,2,1,0:T(8,128)} custom-call(s32[1,2]{1,0:T(1,128)S(1)} %get-tuple-element.20.pos_ref, s32[1,2]{1,0:T(1,128)S(1)} %collective-permute-done.before_ref, f32[2,128,256]{2,1,0:T(8,128)S(1)} %get-tuple-element.34.own_ref, f32[2,128,256]{2,1,0:T(8,128)S(1)} %collective-permute-done.6.came_ref), custom_call_target="tpu_custom_call" | custom-call | bytes 1048576 | tf_op jit(solution)/shard_map/pallas_call | solution.py:370
  32.8 1.9 %collective-permute-done.5.came_ref = f32[2,128,256]{2,1,0:T(8,128)S(1)} collective-permute-done((f32[2,128,256]{2,1,0:T(8,128)S(1)}, f32[2,128,256]{2,1,0:T(8,128)S(1)}, u32[]{:S(2)}, u32[]{:S(2)}) %collective-permute-start.5) | collective-permute-done | bytes 262176 | tf_op jit(solution)/shard_map/ppermute | solution.py:23
  34.7 0.9 %shard_map.73 = f32[2,2,128,512]{3,2,1,0:T(8,128)} custom-call(s32[1,2]{1,0:T(1,128)S(1)} %get-tuple-element.20.pos_ref, s32[1,2]{1,0:T(1,128)S(1)} %collective-permute-done.before_ref, f32[2,128,256]{2,1,0:T(8,128)S(1)} %shard_map.71.own_ref, f32[2,128,256]{2,1,0:T(8,128)S(1)} %collective-permute-done.5.came_ref, ...), custom_call_target="tpu_custom_call", output_to_operand_aliasing={{}: (4, {})} | custom-call | bytes 1048576 | tf_op jit(solution)/shard_map/pallas_call | solution.py:370
Async XLA Ops:
  0.0 6.9 %collective-permute-start = (s32[1,2]{1,0:T(1,128)}, s32[1,2]{1,0:T(1,128)S(1)}, u32[]{:S(2)}, u32[]{:S(2)}) collective-permute-start(s32[1,2]{1,0:T(1,128)} %pos_hbm.3), channel_id=1, source_target_pairs={{0,2},{2,4},{4,6},{6,8},{8,10},{10,12},{12,14},{14,16},{16,18},{18... | collective-permute-start | bytes 32 | tf_op jit(solution)/shard_map/ppermute | solution.py:23
  1.8 9.0 %collective-permute-start.3 = (f32[256,256]{1,0:T(8,128)S(1)}, f32[256,256]{1,0:T(8,128)S(1)}, u32[]{:S(2)}, u32[]{:S(2)}) collective-permute-start(f32[256,256]{1,0:T(8,128)S(1)} %get-tuple-element.28), channel_id=1, source_target_pairs={{0,1},{1,0},{2,3},{3,2},{4,5},{5,4},{6,7},{7,6},{8,9},{9,8},{10,11... | collective-permute-start | bytes 786440 | tf_op jit(solution)/shard_map/ppermute | solution.py:23
  7.0 8.4 %collective-permute-start.2 = (f32[2,256,256]{2,1,0:T(8,128)S(1)}, f32[2,256,256]{2,1,0:T(8,128)S(1)}, u32[]{:S(2)}, u32[]{:S(2)}) collective-permute-start(f32[2,256,256]{2,1,0:T(8,128)S(1)} %shard_map.66), channel_id=1, source_target_pairs={{0,30},{2,0},{4,2},{6,4},{8,6},{10,8},{12,10},{14,12},{16,14},{18,... | collective-permute-start | bytes 1572872 | tf_op jit(solution)/shard_map/ppermute | solution.py:23
  10.1 11.0 %collective-permute-start.1 = (f32[2,256,256]{2,1,0:T(8,128)S(1)}, f32[2,256,256]{2,1,0:T(8,128)S(1)}, u32[]{:S(2)}, u32[]{:S(2)}) collective-permute-start(f32[2,256,256]{2,1,0:T(8,128)S(1)} %get-tuple-element.22), channel_id=1, source_target_pairs={{0,30},{2,0},{4,2},{6,4},{8,6},{10,8},{12,10},{14,12},{16,14},{18,... | collective-permute-start | bytes 1572872 | tf_op jit(solution)/shard_map/ppermute | solution.py:23
  10.8 4.2 %collective-permute-start.4 = (f32[256,256]{1,0:T(8,128)S(1)}, f32[256,256]{1,0:T(8,128)S(1)}, u32[]{:S(2)}, u32[]{:S(2)}) collective-permute-start(f32[256,256]{1,0:T(8,128)S(1)} %collective-permute-done.3.refs_0_), channel_id=1, source_target_pairs={{0,2},{2,0},{4,6},{6,4},{8,10},{10,8},{12,14},{14,12},{16,18},{18,... | collective-permute-start | bytes 786440 | tf_op jit(solution)/shard_map/ppermute | solution.py:444
  23.2 8.7 %collective-permute-start.6 = (f32[2,128,256]{2,1,0:T(8,128)S(1)}, f32[2,128,256]{2,1,0:T(8,128)S(1)}, u32[]{:S(2)}, u32[]{:S(2)}) collective-permute-start(f32[2,128,256]{2,1,0:T(8,128)S(1)} %get-tuple-element.34.own_ref), channel_id=1, source_target_pairs={{0,2},{2,4},{4,6},{6,8},{8,10},{10,12},{12,14},{14,16},{16,18},{18... | collective-permute-start | bytes 786440 | tf_op jit(solution)/shard_map/ppermute | solution.py:23
  25.6 9.0 %collective-permute-start.5 = (f32[2,128,256]{2,1,0:T(8,128)S(1)}, f32[2,128,256]{2,1,0:T(8,128)S(1)}, u32[]{:S(2)}, u32[]{:S(2)}) collective-permute-start(f32[2,128,256]{2,1,0:T(8,128)S(1)} %shard_map.71.own_ref), channel_id=1, source_target_pairs={{0,2},{2,4},{4,6},{6,8},{8,10},{10,12},{12,14},{14,16},{16,18},{18... | collective-permute-start | bytes 786440 | tf_op jit(solution)/shard_map/ppermute | solution.py:23

commit v11 on v10

--- a/solution.py
+++ b/solution.py
@@ -267,24 +267,32 @@
     return ref[(*at, 0)], ref[(*at, 1)]
 
 
-def inner_body(pos_ref, object_ref, halo_ref, first_ref, kr_ref, ki_ref, tab, *refs):
-    out_ref, probe_ref, patch = refs[-3:]
-    states = out_ref.shape[0]
+def propagate(probes, patch, kr_ref, ki_ref, tab):
+    waves = forward([times(probe, pair(patch)) for probe in probes], tab)
+    return inverse([times((kr_ref[...], ki_ref[...]), wave) for wave in waves], tab)
+
+
+def own_body(pos_ref, object_ref, halo_ref, first_ref, kr_ref, ki_ref, tab, out_ref, patch):
     patch[0], patch[1] = patch_of(object_ref, halo_ref, pos_ref)
+    (out_ref[0, 0], out_ref[0, 1]), = propagate([pair(first_ref, 0)], patch, kr_ref, ki_ref, tab)
+
+
+def inner_body(pos_ref, patch, mine_ref, first_ref, kr_ref, ki_ref, tab, *refs):
+    out_ref, probe_ref = refs[-2:]
     swap = lax.rem(lax.axis_index("frame"), 2) == 1
-    probe_ref[:1] = first_ref[...]
-    for m, (came, given) in enumerate(zip(refs[:-3:2], refs[1:-3:2])):
+    for m, (came, given) in enumerate(zip(refs[:-2:2], refs[1:-2:2])):
         other = turned(given[...], *turn_of(pos_ref, given.shape[1]))
         probe_ref[1 + m, 0] = jnp.where(swap, other, came[...])
         probe_ref[1 + m, 1] = jnp.where(swap, came[...], other)
+    probe_ref[:1] = first_ref[...]
+    out_ref[:1] = mine_ref[...]
 
     def body(group):
-        waves = forward([times(pair(probe_ref, m), pair(patch)) for m in group], tab)
-        waves = inverse([times((kr_ref[...], ki_ref[...]), wave) for wave in waves], tab)
+        waves = propagate([pair(probe_ref, 1 + m) for m in group], patch, kr_ref, ki_ref, tab)
         for m, wave in zip(group, waves):
-            out_ref[m, 0], out_ref[m, 1] = wave
-
-    in_groups(states, body)
+            out_ref[1 + m, 0], out_ref[1 + m, 1] = wave
+
+    in_groups(out_ref.shape[0] - 1, body)
 
 
 def middle_body(rows, pos_ref, object_ref, halo_ref, inner_ref, amp_ref, tab, term_ref, half_ref, patch, far, power):
@@ -442,14 +450,20 @@
     pairs = []
     for came, kept in zip(planes, own):
         pairs += [kept, lax.ppermute(came, "frame", [(i, i ^ 1) for i in range(frames)])]
+    mine, first_patch = call(
+        own_body,
+        [(1, 2) + grid, (2,) + grid],
+        [VMEM] * 7,
+        flops=2 * flops,
+        moved=24 * unit,
+    )(pos, held_zero, halo_zero, first, kr, ki, tab)
     waves, probes = call(
         inner_body,
         [(states, 2) + grid] * 2,
         [VMEM] * (7 + len(pairs)),
-        [pltpu.VMEM((2,) + grid, F32)],
-        flops=2 * flops * states,
+        flops=2 * flops * (states - 1),
         moved=24 * unit * states,
-    )(pos, held_zero, halo_zero, first, kr, ki, tab, *pairs)
+    )(pos, first_patch, mine, first, kr, ki, tab, *pairs)
     term_one, half, patch = call(
         functools.partial(middle_body, rows),
         [(2, rows, size), (states, 2) + grid, (2,) + grid],

time: 35.8 us -> 37.9 us (1.059)
  waiting for transfers between devices: 14.1 us -> 16.4 us
  starting transfers between devices: 6.19 us -> 4.86 us
  Pallas kernels: 15.2 us -> 16.3 us
    ppermute x6, waiting for transfers between devices: 14.1 us -> 16.4 us  [shifted(): lax.ppermute(value, axis, [(i, (i + by) % count) for i in range(count)])]
    pallas_call x1 -> x2, Pallas kernels: 2.35 us -> 3.41 us  [the longest x1 1.8 us: gradient_of(): call(inner_body, [(states, 2) + grid] * 2, [VMEM] * (7 + len(pairs)), flo...]
    ppermute x6, starting transfers between devices: 5.67 us -> 4.86 us  [shifted(): lax.ppermute(value, axis, [(i, (i + by) % count) for i in range(count)])]
    ppermute x1, starting transfers between devices: 0.51 us -> 0.01 us  [gradient_of(): lax.ppermute(came, 'frame', [(i, i ^ 1) for i in range(frames)])]
  transfers between devices with their start and end apart: 7 -> 7, of which waited for: 5 -> 4; matrix products, arithmetic and copies ran while one was open for 0% -> 0% of each run, Pallas kernels for 34% -> 35%
where the time goes in v11:
time: 37.9 us; the launch traced here: 37.7 us
  waiting for transfers between devices  16.4 us (43%)
  Pallas kernels  16.3 us (43%)
  starting transfers between devices  4.86 us (13%)
    ppermute x6, waiting for transfers between devices, shifted(): lax.ppermute(value, axis, [(i, (i + by) % count) for i in range(count)])  16.4 us
    ppermute x6, starting transfers between devices, shifted(): lax.ppermute(value, axis, [(i, (i + by) % count) for i in range(count)])  4.86 us
    pallas_call x1, Pallas kernels, gradient_of(): pl.pallas_call(prepare_body, out_shape=[jax.ShapeDtypeStruct(grid, F32)]...  3.43 us
    pallas_call x1, Pallas kernels, gradient_of(): call(functools.partial(last_body, rows), [(2, rows, size)], [VMEM] * 6, [...  2.41 us
    pallas_call x1, Pallas kernels, gradient_of(): call(functools.partial(middle_body, rows), [(2, rows, size), (states, 2)...  2.13 us
    pallas_call x2, Pallas kernels, gather(): pl.pallas_call(functools.partial(gather_body, slice_id, rows), out_shape=...  1.88 us
    pallas_call x1, Pallas kernels, gradient_of(): call(inner_body, [(states, 2) + grid] * 2, [VMEM] * (7 + len(pairs)), flo...  1.8 us
    pallas_call x1, Pallas kernels, gradient_of(): call(own_body, [(1, 2) + grid, (2,) + grid], [VMEM] * 7, flops=2 * flops,...  1.6 us
  transfers between devices with their start and end apart: 7, of which 4 were waited for; matrix products, arithmetic and copies ran while one was open for 0% of the time, Pallas kernels for 35%

profile of v11, /device:TPU:0, one launch (start us, length us, event | category | flops | bytes accessed | tf_op | source)
XLA Modules:
  0.0 37.7 jit_solution(5683394398294267550)
XLA Ops:
  0.0 0.5 %collective-permute-start = (s32[1,2]{1,0:T(1,128)}, s32[1,2]{1,0:T(1,128)S(1)}, u32[]{:S(2)}, u32[]{:S(2)}) collective-permute-start(s32[1,2]{1,0:T(1,128)} %pos_hbm.3), channel_id=1, source_target_pairs={{0,2},{2,4},{4,6},{6,8},{8,10},{10,12},{12,14},{14,16},{16,18},{18... | collective-permute-start | bytes 32 | tf_op jit(solution)/shard_map/ppermute | solution.py:23
  0.5 1.3 %shard_map.64 = (s32[1,2]{1,0:T(1,128)S(1)}, f32[256,256]{1,0:T(8,128)S(1)}, f32[2,256,512]{2,1,0:T(8,128)S(1)}) custom-call(s32[1,2]{1,0:T(1,128)} %pos_hbm.3, f32[1,2,256,256]{3,2,1,0:T(8,128)} %probe_hbm.3, f32[2,2,256,512]{3,2,1,0:T(8,128)} %object_hbm.3), custom_call_target="tpu_custom_call" | custom-call | bytes 1572864 | tf_op jit(solution)/shard_map/pallas_call | solution.py:406
  1.8 5.0 %collective-permute-done.before_ref = s32[1,2]{1,0:T(1,128)S(1)} collective-permute-done((s32[1,2]{1,0:T(1,128)}, s32[1,2]{1,0:T(1,128)S(1)}, u32[]{:S(2)}, u32[]{:S(2)}) %collective-permute-start) | collective-permute-done | bytes 40 | tf_op jit(solution)/shard_map/ppermute | solution.py:23
  6.9 0.1 shard_map.66
  7.0 0.1 collective-permute-start.2
  7.1 1.9 %collective-permute-start.3 = (f32[256,256]{1,0:T(8,128)S(1)}, f32[256,256]{1,0:T(8,128)S(1)}, u32[]{:S(2)}, u32[]{:S(2)}) collective-permute-start(f32[256,256]{1,0:T(8,128)S(1)} %get-tuple-element.32), channel_id=1, source_target_pairs={{0,1},{1,0},{2,3},{3,2},{4,5},{5,4},{6,7},{7,6},{8,9},{9,8},{10,11... | collective-permute-start | bytes 786440 | tf_op jit(solution)/shard_map/ppermute | solution.py:23
  9.0 1.3 %shard_map.65 = (f32[2,256,512]{2,1,0:T(8,128)S(1)}, f32[2,256,256]{2,1,0:T(8,128)S(1)}) custom-call(s32[1,2]{1,0:T(1,128)S(1)} %collective-permute-done.before_ref, f32[2,2,256,512]{3,2,1,0:T(8,128)} %object_hbm.3), custom_call_target="tpu_custom_call" | custom-call | bytes 2621440 | tf_op jit(solution)/shard_map/pallas_call | solution.py:424
  10.4 1.7 %collective-permute-start.1 = (f32[2,256,256]{2,1,0:T(8,128)S(1)}, f32[2,256,256]{2,1,0:T(8,128)S(1)}, u32[]{:S(2)}, u32[]{:S(2)}) collective-permute-start(f32[2,256,256]{2,1,0:T(8,128)S(1)} %get-tuple-element.24), channel_id=1, source_target_pairs={{0,30},{2,0},{4,2},{6,4},{8,6},{10,8},{12,10},{14,12},{16,14},{18,... | collective-permute-start | bytes 1572872 | tf_op jit(solution)/shard_map/ppermute | solution.py:23
  12.1 3.9 %collective-permute-done.3.refs_0_ = f32[256,256]{1,0:T(8,128)S(1)} collective-permute-done((f32[256,256]{1,0:T(8,128)S(1)}, f32[256,256]{1,0:T(8,128)S(1)}, u32[]{:S(2)}, u32[]{:S(2)}) %collective-permute-start.3) | collective-permute-done | bytes 262176 | tf_op jit(solution)/shard_map/ppermute | solution.py:23
  15.9 0.0 collective-permute-start.4
  15.9 3.4 %shard_map.67 = (f32[256,256]{1,0:T(8,128)S(1)}, f32[256,256]{1,0:T(8,128)S(1)}, f32[256,256]{1,0:T(8,128)S(1)}, f32[1,2,256,256]{3,2,1,0:T(8,128)S(1)}, bf16[2,4,256,256]{3,2,1,0:T(8,128)(2,1)S(1)}) custom-call(s32[1,2]{1,0:T(1,128)} %pos_hbm.3, f32[1,2,256,256]{3,2,1,0:T(8,128)} %probe_hbm.3, f32[256,256]{1,0:T(8,128)} %prop_hbm.1, ...), custom_call_target="tpu_custom_call" | custom-call | flops 33554432 | bytes 3932160 | tf_op jit(solution)/shard_map/pallas_call | solution.py:432
  19.4 0.2 shard_map.69.refs_0_
  19.6 0.0 collective-permute-done.2.halo_ref
  19.6 1.6 %shard_map.68 = (f32[1,2,256,256]{3,2,1,0:T(8,128)S(1)}, f32[2,256,256]{2,1,0:T(8,128)S(1)}) custom-call(s32[1,2]{1,0:T(1,128)S(1)} %get-tuple-element.22.pos_ref, f32[2,256,512]{2,1,0:T(8,128)S(1)} %get-tuple-element.25.object_ref, f32[2,256,256]{2,1,0:T(8,128)S(1)} %collective-permute-done.2.halo_ref, f32[1,2,256,256]{3,2,1,0:T(8,128)S(1)} %get-tuple-element.26.first_ref, ...), custom_call_target="tpu_custom_call" | custom-call | flops 805306368 | bytes 1572864 | tf_op jit(solution)/shard_map/pallas_call | solution.py:453
  21.2 0.0 collective-permute-done.4.refs_1_
  21.3 1.8 %shard_map.70 = (f32[2,2,256,256]{3,2,1,0:T(8,128)S(1)}, f32[2,2,256,256]{3,2,1,0:T(8,128)S(1)}) custom-call(s32[1,2]{1,0:T(1,128)S(1)} %get-tuple-element.22.pos_ref, f32[2,256,256]{2,1,0:T(8,128)S(1)} %get-tuple-element.30.patch, f32[1,2,256,256]{3,2,1,0:T(8,128)S(1)} %get-tuple-element.31.mine_ref, f32[1,2,256,256]{3,2,1,0:T(8,128)S(1)} %get-tuple-element.26.first_ref, ...), custom_call_target="tpu_custom_call" | custom-call | flops 805306368 | bytes 3145728 | tf_op jit(solution)/shard_map/pallas_call | solution.py:460
  23.1 0.0 collective-permute-done.1.halo_ref
  23.1 2.1 %shard_map.71 = (f32[2,128,256]{2,1,0:T(8,128)S(1)}, f32[2,2,256,256]{3,2,1,0:T(8,128)S(1)}, f32[2,256,256]{2,1,0:T(8,128)S(1)}) custom-call(s32[1,2]{1,0:T(1,128)S(1)} %get-tuple-element.22.pos_ref, f32[2,256,512]{2,1,0:T(8,128)S(1)} %get-tuple-element.23.object_ref, f32[2,256,256]{2,1,0:T(8,128)S(1)} %collective-permute-done.1.halo_ref, ...), custom_call_target="tpu_custom_call" | custom-call | flops 1610612736 | bytes 4194304 | tf_op jit(solution)/shard_map/pallas_call | solution.py:467
  25.2 0.6 %collective-permute-start.6 = (f32[2,128,256]{2,1,0:T(8,128)S(1)}, f32[2,128,256]{2,1,0:T(8,128)S(1)}, u32[]{:S(2)}, u32[]{:S(2)}) collective-permute-start(f32[2,128,256]{2,1,0:T(8,128)S(1)} %get-tuple-element.38.own_ref), channel_id=1, source_target_pairs={{0,2},{2,4},{4,6},{6,8},{8,10},{10,12},{12,14},{14,16},{16,18},{18... | collective-permute-start | bytes 786440 | tf_op jit(solution)/shard_map/ppermute | solution.py:23
  25.8 2.4 %shard_map.72.own_ref = f32[2,128,256]{2,1,0:T(8,128)S(1)} custom-call(f32[2,2,256,256]{3,2,1,0:T(8,128)S(1)} %get-tuple-element.35.half_ref, f32[2,256,256]{2,1,0:T(8,128)S(1)} %get-tuple-element.36.patch, f32[2,2,256,256]{3,2,1,0:T(8,128)S(1)} %get-tuple-element.37.probe_ref, f32[256,256]{1,0:T(8,128)S(1)} %get-tuple-element.27.kr_ref, ...), custom_call_target="tpu_custom_call" | custom-call | flops 1610612736 | bytes 2097152 | tf_op jit(solution)/shard_map/pallas_call | solution.py:476
  28.2 0.1 collective-permute-start.5
  28.3 5.5 %collective-permute-done.6.came_ref = f32[2,128,256]{2,1,0:T(8,128)S(1)} collective-permute-done((f32[2,128,256]{2,1,0:T(8,128)S(1)}, f32[2,128,256]{2,1,0:T(8,128)S(1)}, u32[]{:S(2)}, u32[]{:S(2)}) %collective-permute-start.6) | collective-permute-done | bytes 262176 | tf_op jit(solution)/shard_map/ppermute | solution.py:23
  33.8 0.9 %shard_map.73.refs_0_ = f32[2,2,128,512]{3,2,1,0:T(8,128)} custom-call(s32[1,2]{1,0:T(1,128)S(1)} %get-tuple-element.22.pos_ref, s32[1,2]{1,0:T(1,128)S(1)} %collective-permute-done.before_ref, f32[2,128,256]{2,1,0:T(8,128)S(1)} %get-tuple-element.38.own_ref, f32[2,128,256]{2,1,0:T(8,128)S(1)} %collective-permute-done.6.came_ref), custom_call_target="tpu_custom_call" | custom-call | bytes 1048576 | tf_op jit(solution)/shard_map/pallas_call | solution.py:378
  34.7 2.0 %collective-permute-done.5.came_ref = f32[2,128,256]{2,1,0:T(8,128)S(1)} collective-permute-done((f32[2,128,256]{2,1,0:T(8,128)S(1)}, f32[2,128,256]{2,1,0:T(8,128)S(1)}, u32[]{:S(2)}, u32[]{:S(2)}) %collective-permute-start.5) | collective-permute-done | bytes 262176 | tf_op jit(solution)/shard_map/ppermute | solution.py:23
  36.7 0.9 %shard_map.74 = f32[2,2,128,512]{3,2,1,0:T(8,128)} custom-call(s32[1,2]{1,0:T(1,128)S(1)} %get-tuple-element.22.pos_ref, s32[1,2]{1,0:T(1,128)S(1)} %collective-permute-done.before_ref, f32[2,128,256]{2,1,0:T(8,128)S(1)} %shard_map.72.own_ref, f32[2,128,256]{2,1,0:T(8,128)S(1)} %collective-permute-done.5.came_ref, ...), custom_call_target="tpu_custom_call", output_to_operand_aliasing={{}: (4, {})} | custom-call | bytes 1048576 | tf_op jit(solution)/shard_map/pallas_call | solution.py:378
Async XLA Ops:
  0.0 6.9 %collective-permute-start = (s32[1,2]{1,0:T(1,128)}, s32[1,2]{1,0:T(1,128)S(1)}, u32[]{:S(2)}, u32[]{:S(2)}) collective-permute-start(s32[1,2]{1,0:T(1,128)} %pos_hbm.3), channel_id=1, source_target_pairs={{0,2},{2,4},{4,6},{6,8},{8,10},{10,12},{12,14},{14,16},{16,18},{18... | collective-permute-start | bytes 32 | tf_op jit(solution)/shard_map/ppermute | solution.py:23
  7.0 12.6 %collective-permute-start.2 = (f32[2,256,256]{2,1,0:T(8,128)S(1)}, f32[2,256,256]{2,1,0:T(8,128)S(1)}, u32[]{:S(2)}, u32[]{:S(2)}) collective-permute-start(f32[2,256,256]{2,1,0:T(8,128)S(1)} %shard_map.66), channel_id=1, source_target_pairs={{0,30},{2,0},{4,2},{6,4},{8,6},{10,8},{12,10},{14,12},{16,14},{18,... | collective-permute-start | bytes 1572872 | tf_op jit(solution)/shard_map/ppermute | solution.py:23
  7.1 8.8 %collective-permute-start.3 = (f32[256,256]{1,0:T(8,128)S(1)}, f32[256,256]{1,0:T(8,128)S(1)}, u32[]{:S(2)}, u32[]{:S(2)}) collective-permute-start(f32[256,256]{1,0:T(8,128)S(1)} %get-tuple-element.32), channel_id=1, source_target_pairs={{0,1},{1,0},{2,3},{3,2},{4,5},{5,4},{6,7},{7,6},{8,9},{9,8},{10,11... | collective-permute-start | bytes 786440 | tf_op jit(solution)/shard_map/ppermute | solution.py:23
  10.4 12.7 %collective-permute-start.1 = (f32[2,256,256]{2,1,0:T(8,128)S(1)}, f32[2,256,256]{2,1,0:T(8,128)S(1)}, u32[]{:S(2)}, u32[]{:S(2)}) collective-permute-start(f32[2,256,256]{2,1,0:T(8,128)S(1)} %get-tuple-element.24), channel_id=1, source_target_pairs={{0,30},{2,0},{4,2},{6,4},{8,6},{10,8},{12,10},{14,12},{16,14},{18,... | collective-permute-start | bytes 1572872 | tf_op jit(solution)/shard_map/ppermute | solution.py:23
  15.9 5.3 %collective-permute-start.4 = (f32[256,256]{1,0:T(8,128)S(1)}, f32[256,256]{1,0:T(8,128)S(1)}, u32[]{:S(2)}, u32[]{:S(2)}) collective-permute-start(f32[256,256]{1,0:T(8,128)S(1)} %collective-permute-done.3.refs_0_), channel_id=1, source_target_pairs={{0,2},{2,0},{4,6},{6,4},{8,10},{10,8},{12,14},{14,12},{16,18},{18,... | collective-permute-start | bytes 786440 | tf_op jit(solution)/shard_map/ppermute | solution.py:452
  25.2 8.5 %collective-permute-start.6 = (f32[2,128,256]{2,1,0:T(8,128)S(1)}, f32[2,128,256]{2,1,0:T(8,128)S(1)}, u32[]{:S(2)}, u32[]{:S(2)}) collective-permute-start(f32[2,128,256]{2,1,0:T(8,128)S(1)} %get-tuple-element.38.own_ref), channel_id=1, source_target_pairs={{0,2},{2,4},{4,6},{6,8},{8,10},{10,12},{12,14},{14,16},{16,18},{18... | collective-permute-start | bytes 786440 | tf_op jit(solution)/shard_map/ppermute | solution.py:23
  28.2 8.5 %collective-permute-start.5 = (f32[2,128,256]{2,1,0:T(8,128)S(1)}, f32[2,128,256]{2,1,0:T(8,128)S(1)}, u32[]{:S(2)}, u32[]{:S(2)}) collective-permute-start(f32[2,128,256]{2,1,0:T(8,128)S(1)} %shard_map.72.own_ref), channel_id=1, source_target_pairs={{0,2},{2,4},{4,6},{6,8},{8,10},{10,12},{12,14},{14,16},{16,18},{18... | collective-permute-start | bytes 786440 | tf_op jit(solution)/shard_map/ppermute | solution.py:23

commit v12 on v11

--- a/solution.py
+++ b/solution.py
@@ -202,34 +202,30 @@
     return jnp.sum(pos_ref[0:1, 0:1]), lax.rem(jnp.sum(pos_ref[0:1, 1:2]), size)
 
 
-def turn_body(pos_ref, *refs):
+def turn_body(before_ref, *refs):
     half = len(refs) // 2
-    turn = turn_of(pos_ref, refs[0].shape[1])
+    turn = turn_of(before_ref, refs[0].shape[1])
     for came, out in zip(refs[:half], refs[half:]):
         out[...] = turned(came[...], *turn)
 
 
 def prepare_body(
-    pos_hbm, probe_hbm, prop_hbm, amp_hbm, tab_hbm,
+    before_ref, lent_ref, probe_hbm, prop_hbm, tab_hbm,
     wave_re, wave_im, amp_out, first_out, tab_out,
-    pos, probe, prop, amp, sem,
+    probe, prop, sem,
 ):
-    copies = run_copies(
-        ((pos_hbm, pos), (probe_hbm, probe), (prop_hbm, prop), (amp_hbm, amp), (tab_hbm, tab_out)), sem
-    )
+    copies = run_copies(((probe_hbm, probe), (prop_hbm, prop), (tab_hbm, tab_out)), sem)
+    size = prop.shape[0]
+    amp_out[...] = by_parity(lent_ref[0])
     copies[0].wait()
+    turn = turn_of(before_ref, size)
+    for c in range(2):
+        first_out[0, c] = turned(probe[0, c], *turn)
     copies[1].wait()
-    size = prop.shape[0]
-    row, col = pos[0, 0], lax.rem(pos[0, 1], size)
-    for c in range(2):
-        first_out[0, c] = turned(probe[0, c], row, col)
-    copies[2].wait()
     phase = by_parity(prop[...])
     wave_re[...] = jnp.cos(phase)
     wave_im[...] = jnp.sin(phase)
-    copies[3].wait()
-    amp_out[...] = by_parity(amp[0])
-    copies[4].wait()
+    copies[2].wait()
 
 
 def spread(ref, which, shape):
@@ -242,23 +238,23 @@
     return jnp.where(c < spread(col_ref, 1, c.shape), ref[part, :, size:], ref[part, :, :size])
 
 
-def send_body(before_ref, object_ref, out_ref):
+def send_body(pos_ref, object_ref, out_ref):
     for part in range(2):
-        out_ref[part] = wrapped(object_ref, part, before_ref)
-
-
-def load_send_body(before_ref, object_hbm, object_out, out_ref, sem):
+        out_ref[part] = wrapped(object_ref, part, pos_ref)
+
+
+def load_send_body(pos_ref, object_hbm, object_out, out_ref, sem):
     copies = run_copies(quarters(object_hbm, 1, object_out), sem)
     for copy in copies:
         copy.wait()
-    send_body(before_ref, object_out, out_ref)
-
-
-def patch_of(object_ref, halo_ref, pos_ref):
+    send_body(pos_ref, object_out, out_ref)
+
+
+def patch_of(object_ref, halo_ref, before_ref):
     size = halo_ref.shape[-1]
     r = lax.broadcasted_iota(jnp.int32, (size, size), 0)
     return [
-        jnp.where(r < spread(pos_ref, 0, r.shape), halo_ref[part], wrapped(object_ref, part, pos_ref))
+        jnp.where(r < spread(before_ref, 0, r.shape), wrapped(object_ref, part, before_ref), halo_ref[part])
         for part in range(2)
     ]
 
@@ -272,16 +268,16 @@
     return inverse([times((kr_ref[...], ki_ref[...]), wave) for wave in waves], tab)
 
 
-def own_body(pos_ref, object_ref, halo_ref, first_ref, kr_ref, ki_ref, tab, out_ref, patch):
-    patch[0], patch[1] = patch_of(object_ref, halo_ref, pos_ref)
+def own_body(before_ref, object_ref, halo_ref, first_ref, kr_ref, ki_ref, tab, out_ref, patch):
+    patch[0], patch[1] = patch_of(object_ref, halo_ref, before_ref)
     (out_ref[0, 0], out_ref[0, 1]), = propagate([pair(first_ref, 0)], patch, kr_ref, ki_ref, tab)
 
 
-def inner_body(pos_ref, patch, mine_ref, first_ref, kr_ref, ki_ref, tab, *refs):
+def inner_body(before_ref, patch, mine_ref, first_ref, kr_ref, ki_ref, tab, *refs):
     out_ref, probe_ref = refs[-2:]
     swap = lax.rem(lax.axis_index("frame"), 2) == 1
     for m, (came, given) in enumerate(zip(refs[:-2:2], refs[1:-2:2])):
-        other = turned(given[...], *turn_of(pos_ref, given.shape[1]))
+        other = turned(given[...], *turn_of(before_ref, given.shape[1]))
         probe_ref[1 + m, 0] = jnp.where(swap, other, came[...])
         probe_ref[1 + m, 1] = jnp.where(swap, came[...], other)
     probe_ref[:1] = first_ref[...]
@@ -295,9 +291,9 @@
     in_groups(out_ref.shape[0] - 1, body)
 
 
-def middle_body(rows, pos_ref, object_ref, halo_ref, inner_ref, amp_ref, tab, term_ref, half_ref, patch, far, power):
+def middle_body(rows, before_ref, object_ref, halo_ref, inner_ref, amp_ref, tab, term_ref, half_ref, patch, far, power):
     states = inner_ref.shape[0]
-    patch[0], patch[1] = patch_of(object_ref, halo_ref, pos_ref)
+    patch[0], patch[1] = patch_of(object_ref, halo_ref, before_ref)
     power[...] = jnp.zeros_like(power)
 
     def outward(group):
@@ -352,8 +348,8 @@
     start = lax.axis_index("state") * rows
     r = lax.broadcasted_iota(jnp.int32, (rows, size), 0) + start
     c = lax.broadcasted_iota(jnp.int32, (rows, size), 1)
-    here, there = r >= spread(pos_ref, 0, r.shape), r < spread(before_ref, 0, r.shape)
-    here_right, there_right = c < spread(pos_ref, 1, c.shape), c < spread(before_ref, 1, c.shape)
+    here, there = r < spread(before_ref, 0, r.shape), r >= spread(pos_ref, 0, r.shape)
+    here_right, there_right = c < spread(before_ref, 1, c.shape), c < spread(pos_ref, 1, c.shape)
     chunks = 4 if rows % 32 == 0 else 1
     step = rows // chunks
     copies = []
@@ -402,6 +398,7 @@
     flops = 24 * size**3
     tab = tables(size)
     before = shifted(positions, "frame", 1)
+    lent = shifted(amplitude, "frame", 1)
     given = [in_hbm(x) for x in (positions, probe, object_slices)]
     pos, plane, held_zero = pl.pallas_call(
         load_body,
@@ -419,34 +416,28 @@
     planes = []
     for by in range(1, states):
         planes.append(shifted(plane, "state", by))
-    (picked,) = call(send_body, [(2,) + grid], [VMEM, VMEM], moved=24 * unit)(before, held_zero)
-    halo_zero = shifted(picked, "frame", -1)
+    (picked,) = call(send_body, [(2,) + grid], [VMEM, VMEM], moved=24 * unit)(pos, held_zero)
+    halo_zero = shifted(picked, "frame", 1)
     held_one, picked = call(
         load_send_body,
         [object_slices.shape[1:], (2,) + grid],
         [VMEM, HBM],
         [pltpu.SemaphoreType.DMA((4,))],
         moved=40 * unit,
-    )(before, given[2])
-    halo_one = shifted(picked, "frame", -1)
+    )(pos, given[2])
+    halo_one = shifted(picked, "frame", 1)
     kr, ki, amp, first, tab = pl.pallas_call(
         prepare_body,
         out_shape=[jax.ShapeDtypeStruct(grid, F32)] * 3
         + [jax.ShapeDtypeStruct(x.shape, x.dtype) for x in (probe, tab)],
-        in_specs=[HBM] * 5,
+        in_specs=[VMEM] * 2 + [HBM] * 3,
         out_specs=[VMEM] * 5,
-        scratch_shapes=[
-            pltpu.SMEM(positions.shape, jnp.int32),
-            pltpu.VMEM(probe.shape, F32),
-            pltpu.VMEM(grid, F32),
-            pltpu.VMEM(amplitude.shape, F32),
-            pltpu.SemaphoreType.DMA((5,)),
-        ],
+        scratch_shapes=[pltpu.VMEM(probe.shape, F32), pltpu.VMEM(grid, F32), pltpu.SemaphoreType.DMA((3,))],
         compiler_params=pltpu.CompilerParams(vmem_limit_bytes=LIMIT),
         cost_estimate=pl.CostEstimate(flops=2 * size**3, bytes_accessed=60 * unit, transcendentals=0),
-    )(*given[:2], *(in_hbm(x) for x in (propagator, amplitude, tab)))
+    )(before, lent, given[1], *(in_hbm(x) for x in (propagator, tab)))
     frames = lax.axis_size("frame")
-    own = call(turn_body, [grid] * len(planes), [VMEM] * (1 + len(planes)), moved=16 * unit)(pos, *planes)
+    own = call(turn_body, [grid] * len(planes), [VMEM] * (1 + len(planes)), moved=16 * unit)(before, *planes)
     pairs = []
     for came, kept in zip(planes, own):
         pairs += [kept, lax.ppermute(came, "frame", [(i, i ^ 1) for i in range(frames)])]
@@ -456,14 +447,14 @@
         [VMEM] * 7,
         flops=2 * flops,
         moved=24 * unit,
-    )(pos, held_zero, halo_zero, first, kr, ki, tab)
+    )(before, held_zero, halo_zero, first, kr, ki, tab)
     waves, probes = call(
         inner_body,
         [(states, 2) + grid] * 2,
         [VMEM] * (7 + len(pairs)),
         flops=2 * flops * (states - 1),
         moved=24 * unit * states,
-    )(pos, first_patch, mine, first, kr, ki, tab, *pairs)
+    )(before, first_patch, mine, first, kr, ki, tab, *pairs)
     term_one, half, patch = call(
         functools.partial(middle_body, rows),
         [(2, rows, size), (states, 2) + grid, (2,) + grid],
@@ -471,8 +462,8 @@
         [pltpu.VMEM((states, 2) + grid, F32), pltpu.VMEM(grid, F32)],
         flops=2 * flops * states,
         moved=32 * unit * states,
-    )(pos, held_one, halo_one, waves, amp, tab)
-    came_one = shifted(term_one, "frame", 1)
+    )(before, held_one, halo_one, waves, amp, tab)
+    came_one = shifted(term_one, "frame", -1)
     (term_zero,) = call(
         functools.partial(last_body, rows),
         [(2, rows, size)],
@@ -481,7 +472,7 @@
         flops=2 * flops * states,
         moved=16 * unit * states,
     )(half, patch, probes, kr, ki, tab)
-    came_zero = shifted(term_zero, "frame", 1)
+    came_zero = shifted(term_zero, "frame", -1)
     gradient = gather(1, rows, size, pos, before, term_one, came_one)
     return gather(0, rows, size, pos, before, term_zero, came_zero, gradient)
 

time: 37.9 us -> 41.2 us (1.087)
  starting transfers between devices: 4.86 us -> 8.46 us
    ppermute x6 -> x7, starting transfers between devices: 4.86 us -> 7.3 us  [shifted(): lax.ppermute(value, axis, [(i, (i + by) % count) for i in range(count)])]
    ppermute x1, starting transfers between devices: 0.01 us -> 1.16 us  [gradient_of(): lax.ppermute(came, 'frame', [(i, i ^ 1) for i in range(frames)])]
    ppermute x6 -> x7, waiting for transfers between devices: 16.4 us -> 16.6 us  [shifted(): lax.ppermute(value, axis, [(i, (i + by) % count) for i in range(count)])]
  transfers between devices with their start and end apart: 7 -> 8, of which waited for: 4 -> 3; matrix products, arithmetic and copies ran while one was open for 0% -> 0% of each run, Pallas kernels for 35% -> 28%
where the time goes in v12:
time: 41.2 us; the launch traced here: 41.1 us
  waiting for transfers between devices  16.6 us (40%)
  Pallas kernels  15.9 us (39%)
  starting transfers between devices  8.46 us (21%)
    ppermute x7, waiting for transfers between devices, shifted(): lax.ppermute(value, axis, [(i, (i + by) % count) for i in range(count)])  16.6 us
    ppermute x7, starting transfers between devices, shifted(): lax.ppermute(value, axis, [(i, (i + by) % count) for i in range(count)])  7.3 us
    pallas_call x1, Pallas kernels, gradient_of(): pl.pallas_call(prepare_body, out_shape=[jax.ShapeDtypeStruct(grid, F32)]...  3.04 us
    pallas_call x1, Pallas kernels, gradient_of(): call(functools.partial(last_body, rows), [(2, rows, size)], [VMEM] * 6, [...  2.41 us
    pallas_call x1, Pallas kernels, gradient_of(): call(functools.partial(middle_body, rows), [(2, rows, size), (states, 2)...  2.13 us
    pallas_call x2, Pallas kernels, gather(): pl.pallas_call(functools.partial(gather_body, slice_id, rows), out_shape=...  1.88 us
    pallas_call x1, Pallas kernels, gradient_of(): call(inner_body, [(states, 2) + grid] * 2, [VMEM] * (7 + len(pairs)), flo...  1.81 us
    pallas_call x1, Pallas kernels, gradient_of(): call(own_body, [(1, 2) + grid, (2,) + grid], [VMEM] * 7, flops=2 * flops,...  1.6 us
  transfers between devices with their start and end apart: 8, of which 3 were waited for; matrix products, arithmetic and copies ran while one was open for 0% of the time, Pallas kernels for 28%

profile of v12, /device:TPU:0, one launch (start us, length us, event | category | flops | bytes accessed | tf_op | source)
XLA Modules:
  0.0 41.1 jit_solution(10417909750533013362)
XLA Ops:
  0.0 1.3 %shard_map.64 = (s32[1,2]{1,0:T(1,128)S(1)}, f32[256,256]{1,0:T(8,128)S(1)}, f32[2,256,512]{2,1,0:T(8,128)S(1)}) custom-call(s32[1,2]{1,0:T(1,128)} %pos_hbm.1, f32[1,2,256,256]{3,2,1,0:T(8,128)} %probe_hbm.3, f32[2,2,256,512]{3,2,1,0:T(8,128)} %object_hbm.3), custom_call_target="tpu_custom_call" | custom-call | bytes 1572864 | tf_op jit(solution)/shard_map/pallas_call | solution.py:403
  1.3 0.0 copy-start.1
  1.4 0.0 copy-start
  1.4 0.1 shard_map.66
  1.5 0.5 %collective-permute-start.2 = (f32[2,256,256]{2,1,0:T(8,128)S(1)}, f32[2,256,256]{2,1,0:T(8,128)S(1)}, u32[]{:S(2)}, u32[]{:S(2)}) collective-permute-start(f32[2,256,256]{2,1,0:T(8,128)S(1)} %shard_map.66), channel_id=1, source_target_pairs={{0,2},{2,4},{4,6},{6,8},{8,10},{10,12},{12,14},{14,16},{16,18},{18... | collective-permute-start | bytes 1572872 | tf_op jit(solution)/shard_map/ppermute | solution.py:23
  2.0 2.6 %collective-permute-start.4 = (f32[256,256]{1,0:T(8,128)S(1)}, f32[256,256]{1,0:T(8,128)S(1)}, u32[]{:S(2)}, u32[]{:S(2)}) collective-permute-start(f32[256,256]{1,0:T(8,128)S(1)} %get-tuple-element.32), channel_id=1, source_target_pairs={{0,1},{1,0},{2,3},{3,2},{4,5},{5,4},{6,7},{7,6},{8,9},{9,8},{10,11... | collective-permute-start | bytes 786440 | tf_op jit(solution)/shard_map/ppermute | solution.py:23
  4.6 1.3 %shard_map.65 = (f32[2,256,512]{2,1,0:T(8,128)S(1)}, f32[2,256,256]{2,1,0:T(8,128)S(1)}) custom-call(s32[1,2]{1,0:T(1,128)S(1)} %get-tuple-element.22.pos_ref, f32[2,2,256,512]{3,2,1,0:T(8,128)} %object_hbm.3), custom_call_target="tpu_custom_call" | custom-call | bytes 2621440 | tf_op jit(solution)/shard_map/pallas_call | solution.py:421
  5.9 1.3 %collective-permute-start.1 = (f32[2,256,256]{2,1,0:T(8,128)S(1)}, f32[2,256,256]{2,1,0:T(8,128)S(1)}, u32[]{:S(2)}, u32[]{:S(2)}) collective-permute-start(f32[2,256,256]{2,1,0:T(8,128)S(1)} %get-tuple-element.24), channel_id=1, source_target_pairs={{0,2},{2,4},{4,6},{6,8},{8,10},{10,12},{12,14},{14,16},{16,18},{18... | collective-permute-start | bytes 1572872 | tf_op jit(solution)/shard_map/ppermute | solution.py:23
  7.3 0.0 copy-done.1
  7.3 0.4 collective-permute-start.3
  7.6 3.1 %collective-permute-done.4.refs_0_ = f32[256,256]{1,0:T(8,128)S(1)} collective-permute-done((f32[256,256]{1,0:T(8,128)S(1)}, f32[256,256]{1,0:T(8,128)S(1)}, u32[]{:S(2)}, u32[]{:S(2)}) %collective-permute-start.4) | collective-permute-done | bytes 262176 | tf_op jit(solution)/shard_map/ppermute | solution.py:23
  10.7 1.2 %collective-permute-start.5 = (f32[256,256]{1,0:T(8,128)S(1)}, f32[256,256]{1,0:T(8,128)S(1)}, u32[]{:S(2)}, u32[]{:S(2)}) collective-permute-start(f32[256,256]{1,0:T(8,128)S(1)} %collective-permute-done.4.refs_0_), channel_id=1, source_target_pairs={{0,2},{2,0},{4,6},{6,4},{8,10},{10,8},{12,14},{14,12},{16,18},{18,... | collective-permute-start | bytes 786440 | tf_op jit(solution)/shard_map/ppermute | solution.py:443
  11.9 0.0 copy-done
  11.9 0.0 collective-permute-start
  11.9 10.5 %collective-permute-done.before_ref = s32[1,2]{1,0:T(1,128)S(1)} collective-permute-done((s32[1,2]{1,0:T(1,128)S(1)}, s32[1,2]{1,0:T(1,128)S(1)}, u32[]{:S(2)}, u32[]{:S(2)}) %collective-permute-start) | collective-permute-done | bytes 40 | tf_op jit(solution)/shard_map/ppermute | solution.py:23
  22.4 0.2 shard_map.69.refs_0_
  22.6 0.0 collective-permute-done.3.lent_ref
  22.6 3.0 %shard_map.67 = (f32[256,256]{1,0:T(8,128)S(1)}, f32[256,256]{1,0:T(8,128)S(1)}, f32[256,256]{1,0:T(8,128)S(1)}, f32[1,2,256,256]{3,2,1,0:T(8,128)S(1)}, bf16[2,4,256,256]{3,2,1,0:T(8,128)(2,1)S(1)}) custom-call(s32[1,2]{1,0:T(1,128)S(1)} %collective-permute-done.before_ref, f32[1,256,256]{2,1,0:T(8,128)S(1)} %collective-permute-done.3.lent_ref, ...), custom_call_target="tpu_custom_call" | custom-call | flops 33554432 | bytes 3932160 | tf_op jit(solution)/shard_map/pallas_call | solution.py:429
  25.7 0.0 collective-permute-done.2.halo_ref
  25.7 1.6 %shard_map.68 = (f32[1,2,256,256]{3,2,1,0:T(8,128)S(1)}, f32[2,256,256]{2,1,0:T(8,128)S(1)}) custom-call(s32[1,2]{1,0:T(1,128)S(1)} %collective-permute-done.before_ref, f32[2,256,512]{2,1,0:T(8,128)S(1)} %get-tuple-element.25.object_ref, f32[2,256,256]{2,1,0:T(8,128)S(1)} %collective-permute-done.2.halo_ref, ...), custom_call_target="tpu_custom_call" | custom-call | flops 805306368 | bytes 1572864 | tf_op jit(solution)/shard_map/pallas_call | solution.py:444
  27.3 0.0 collective-permute-done.5.refs_1_
  27.3 1.8 %shard_map.70 = (f32[2,2,256,256]{3,2,1,0:T(8,128)S(1)}, f32[2,2,256,256]{3,2,1,0:T(8,128)S(1)}) custom-call(s32[1,2]{1,0:T(1,128)S(1)} %collective-permute-done.before_ref, f32[2,256,256]{2,1,0:T(8,128)S(1)} %get-tuple-element.30.patch, f32[1,2,256,256]{3,2,1,0:T(8,128)S(1)} %get-tuple-element.31.mine_ref, ...), custom_call_target="tpu_custom_call" | custom-call | flops 805306368 | bytes 3145728 | tf_op jit(solution)/shard_map/pallas_call | solution.py:451
  29.1 0.0 collective-permute-done.1.halo_ref
  29.2 2.1 %shard_map.71 = (f32[2,128,256]{2,1,0:T(8,128)S(1)}, f32[2,2,256,256]{3,2,1,0:T(8,128)S(1)}, f32[2,256,256]{2,1,0:T(8,128)S(1)}) custom-call(s32[1,2]{1,0:T(1,128)S(1)} %collective-permute-done.before_ref, f32[2,256,512]{2,1,0:T(8,128)S(1)} %get-tuple-element.23.object_ref, f32[2,256,256]{2,1,0:T(8,128)S(1)} %collective-permute-done.1.halo_ref, ...), custom_call_target="tpu_custom_call" | custom-call | flops 1610612736 | bytes 4194304 | tf_op jit(solution)/shard_map/pallas_call | solution.py:458
  31.3 0.1 collective-permute-start.7
  31.4 2.4 %shard_map.72.own_ref = f32[2,128,256]{2,1,0:T(8,128)S(1)} custom-call(f32[2,2,256,256]{3,2,1,0:T(8,128)S(1)} %get-tuple-element.35.half_ref, f32[2,256,256]{2,1,0:T(8,128)S(1)} %get-tuple-element.36.patch, f32[2,2,256,256]{3,2,1,0:T(8,128)S(1)} %get-tuple-element.37.probe_ref, f32[256,256]{1,0:T(8,128)S(1)} %get-tuple-element.27.kr_ref, ...), custom_call_target="tpu_custom_call" | custom-call | flops 1610612736 | bytes 2097152 | tf_op jit(solution)/shard_map/pallas_call | solution.py:467
  33.8 2.5 %collective-permute-start.6 = (f32[2,128,256]{2,1,0:T(8,128)S(1)}, f32[2,128,256]{2,1,0:T(8,128)S(1)}, u32[]{:S(2)}, u32[]{:S(2)}) collective-permute-start(f32[2,128,256]{2,1,0:T(8,128)S(1)} %shard_map.72.own_ref), channel_id=1, source_target_pairs={{0,30},{2,0},{4,2},{6,4},{8,6},{10,8},{12,10},{14,12},{16,14},{18,... | collective-permute-start | bytes 786440 | tf_op jit(solution)/shard_map/ppermute | solution.py:23
  36.2 0.0 collective-permute-done.7.came_ref
  36.2 0.9 %shard_map.73.refs_0_ = f32[2,2,128,512]{3,2,1,0:T(8,128)} custom-call(s32[1,2]{1,0:T(1,128)S(1)} %get-tuple-element.22.pos_ref, s32[1,2]{1,0:T(1,128)S(1)} %collective-permute-done.before_ref, f32[2,128,256]{2,1,0:T(8,128)S(1)} %get-tuple-element.38.own_ref, f32[2,128,256]{2,1,0:T(8,128)S(1)} %collective-permute-done.7.came_ref), custom_call_target="tpu_custom_call" | custom-call | bytes 1048576 | tf_op jit(solution)/shard_map/pallas_call | solution.py:374
  37.2 2.9 %collective-permute-done.6.came_ref = f32[2,128,256]{2,1,0:T(8,128)S(1)} collective-permute-done((f32[2,128,256]{2,1,0:T(8,128)S(1)}, f32[2,128,256]{2,1,0:T(8,128)S(1)}, u32[]{:S(2)}, u32[]{:S(2)}) %collective-permute-start.6) | collective-permute-done | bytes 262176 | tf_op jit(solution)/shard_map/ppermute | solution.py:23
  40.1 0.9 %shard_map.74 = f32[2,2,128,512]{3,2,1,0:T(8,128)} custom-call(s32[1,2]{1,0:T(1,128)S(1)} %get-tuple-element.22.pos_ref, s32[1,2]{1,0:T(1,128)S(1)} %collective-permute-done.before_ref, f32[2,128,256]{2,1,0:T(8,128)S(1)} %shard_map.72.own_ref, f32[2,128,256]{2,1,0:T(8,128)S(1)} %collective-permute-done.6.came_ref, ...), custom_call_target="tpu_custom_call", output_to_operand_aliasing={{}: (4, {})} | custom-call | bytes 1048576 | tf_op jit(solution)/shard_map/pallas_call | solution.py:374
Async XLA Ops:
  1.3 5.9 %copy-start.1 = (f32[1,256,256]{2,1,0:T(8,128)S(1)}, f32[1,256,256]{2,1,0:T(8,128)}, u32[]{:S(2)}) copy-start(f32[1,256,256]{2,1,0:T(8,128)} %param.8) | copy-start | bytes 786436
  1.4 10.5 %copy-start = (s32[1,2]{1,0:T(1,128)S(1)}, s32[1,2]{1,0:T(1,128)}, u32[]{:S(2)}) copy-start(s32[1,2]{1,0:T(1,128)} %pos_hbm.1) | copy-start | bytes 28
  1.5 24.2 %collective-permute-start.2 = (f32[2,256,256]{2,1,0:T(8,128)S(1)}, f32[2,256,256]{2,1,0:T(8,128)S(1)}, u32[]{:S(2)}, u32[]{:S(2)}) collective-permute-start(f32[2,256,256]{2,1,0:T(8,128)S(1)} %shard_map.66), channel_id=1, source_target_pairs={{0,2},{2,4},{4,6},{6,8},{8,10},{10,12},{12,14},{14,16},{16,18},{18... | collective-permute-start | bytes 1572872 | tf_op jit(solution)/shard_map/ppermute | solution.py:23
  2.0 8.7 %collective-permute-start.4 = (f32[256,256]{1,0:T(8,128)S(1)}, f32[256,256]{1,0:T(8,128)S(1)}, u32[]{:S(2)}, u32[]{:S(2)}) collective-permute-start(f32[256,256]{1,0:T(8,128)S(1)} %get-tuple-element.32), channel_id=1, source_target_pairs={{0,1},{1,0},{2,3},{3,2},{4,5},{5,4},{6,7},{7,6},{8,9},{9,8},{10,11... | collective-permute-start | bytes 786440 | tf_op jit(solution)/shard_map/ppermute | solution.py:23
  5.9 23.2 %collective-permute-start.1 = (f32[2,256,256]{2,1,0:T(8,128)S(1)}, f32[2,256,256]{2,1,0:T(8,128)S(1)}, u32[]{:S(2)}, u32[]{:S(2)}) collective-permute-start(f32[2,256,256]{2,1,0:T(8,128)S(1)} %get-tuple-element.24), channel_id=1, source_target_pairs={{0,2},{2,4},{4,6},{6,8},{8,10},{10,12},{12,14},{14,16},{16,18},{18... | collective-permute-start | bytes 1572872 | tf_op jit(solution)/shard_map/ppermute | solution.py:23
  7.3 15.4 %collective-permute-start.3 = (f32[1,256,256]{2,1,0:T(8,128)S(1)}, f32[1,256,256]{2,1,0:T(8,128)S(1)}, u32[]{:S(2)}, u32[]{:S(2)}) collective-permute-start(f32[1,256,256]{2,1,0:T(8,128)S(1)} %copy-done.1), channel_id=1, source_target_pairs={{0,2},{2,4},{4,6},{6,8},{8,10},{10,12},{12,14},{14,16},{16,18},{18... | collective-permute-start | bytes 786440 | tf_op jit(solution)/shard_map/ppermute | solution.py:23
  10.7 16.6 %collective-permute-start.5 = (f32[256,256]{1,0:T(8,128)S(1)}, f32[256,256]{1,0:T(8,128)S(1)}, u32[]{:S(2)}, u32[]{:S(2)}) collective-permute-start(f32[256,256]{1,0:T(8,128)S(1)} %collective-permute-done.4.refs_0_), channel_id=1, source_target_pairs={{0,2},{2,0},{4,6},{6,4},{8,10},{10,8},{12,14},{14,12},{16,18},{18,... | collective-permute-start | bytes 786440 | tf_op jit(solution)/shard_map/ppermute | solution.py:443
  11.9 10.5 %collective-permute-start = (s32[1,2]{1,0:T(1,128)S(1)}, s32[1,2]{1,0:T(1,128)S(1)}, u32[]{:S(2)}, u32[]{:S(2)}) collective-permute-start(s32[1,2]{1,0:T(1,128)S(1)} %copy-done), channel_id=1, source_target_pairs={{0,2},{2,4},{4,6},{6,8},{8,10},{10,12},{12,14},{14,16},{16,18},{18... | collective-permute-start | bytes 32 | tf_op jit(solution)/shard_map/ppermute | solution.py:23
  31.3 4.9 %collective-permute-start.7 = (f32[2,128,256]{2,1,0:T(8,128)S(1)}, f32[2,128,256]{2,1,0:T(8,128)S(1)}, u32[]{:S(2)}, u32[]{:S(2)}) collective-permute-start(f32[2,128,256]{2,1,0:T(8,128)S(1)} %get-tuple-element.38.own_ref), channel_id=1, source_target_pairs={{0,30},{2,0},{4,2},{6,4},{8,6},{10,8},{12,10},{14,12},{16,14},{18,... | collective-permute-start | bytes 786440 | tf_op jit(solution)/shard_map/ppermute | solution.py:23
  33.8 6.3 %collective-permute-start.6 = (f32[2,128,256]{2,1,0:T(8,128)S(1)}, f32[2,128,256]{2,1,0:T(8,128)S(1)}, u32[]{:S(2)}, u32[]{:S(2)}) collective-permute-start(f32[2,128,256]{2,1,0:T(8,128)S(1)} %shard_map.72.own_ref), channel_id=1, source_target_pairs={{0,30},{2,0},{4,2},{6,4},{8,6},{10,8},{12,10},{14,12},{16,14},{18,... | collective-permute-start | bytes 786440 | tf_op jit(solution)/shard_map/ppermute | solution.py:23

commit v13 on v12

--- a/solution.py
+++ b/solution.py
@@ -342,8 +342,9 @@
     in_groups(states, body)
 
 
-def gather_body(slice_id, rows, pos_ref, before_ref, own_ref, came_ref, *refs):
+def gather_body(slice_id, rows, pos_ref, before_ref, own_ref, came_ref, other_ref, *refs):
     out_ref, held, sem = refs[-3:]
+    odd = lax.rem(lax.axis_index("frame"), 2) == 1
     size = own_ref.shape[-1]
     start = lax.axis_index("state") * rows
     r = lax.broadcasted_iota(jnp.int32, (rows, size), 0) + start
@@ -358,7 +359,10 @@
         cut = slice(chunk * step, chunk * step + step)
         for part in range(2):
             mine = jnp.where(here[cut], own_ref[part, at], 0.0)
-            theirs = jnp.where(there[cut], came_ref[part, at], 0.0)
+            came = came_ref[part, at]
+            if slice_id:
+                came = jnp.where(odd, came, other_ref[part, at])
+            theirs = jnp.where(there[cut], came, 0.0)
             left, right = here_right[cut], there_right[cut]
             held[part, at, :size] = jnp.where(left, 0.0, mine) + jnp.where(right, 0.0, theirs)
             held[part, at, size:] = jnp.where(left, mine, 0.0) + jnp.where(right, theirs, 0.0)
@@ -370,17 +374,17 @@
         copy.wait()
 
 
-def gather(slice_id, rows, size, pos, before, own, came, *given):
+def gather(slice_id, rows, size, pos, before, own, came, other, *given):
     return pl.pallas_call(
         functools.partial(gather_body, slice_id, rows),
         out_shape=jax.ShapeDtypeStruct((2, 2, rows, 2 * size), F32),
-        in_specs=[VMEM] * 4 + [pl.BlockSpec(memory_space=pl.ANY)] * len(given),
+        in_specs=[VMEM] * 5 + [pl.BlockSpec(memory_space=pl.ANY)] * len(given),
         out_specs=pl.BlockSpec(memory_space=pl.ANY),
         scratch_shapes=[pltpu.VMEM((2, rows, 2 * size), F32), pltpu.SemaphoreType.DMA((8,))],
-        input_output_aliases={4: 0} if given else {},
+        input_output_aliases={5: 0} if given else {},
         compiler_params=pltpu.CompilerParams(vmem_limit_bytes=LIMIT),
         cost_estimate=pl.CostEstimate(flops=0, bytes_accessed=32 * rows * size, transcendentals=0),
-    )(pos, before, own, came, *given)
+    )(pos, before, own, came, other, *given)
 
 
 def on_device(object_slices, probe, amplitude, positions, propagator):
@@ -463,7 +467,7 @@
         flops=2 * flops * states,
         moved=32 * unit * states,
     )(before, held_one, halo_one, waves, amp, tab)
-    came_one = shifted(term_one, "frame", -1)
+    came_one = lax.ppermute(term_one, "frame", [(i, (i - 1) % frames) for i in range(0, frames, 2)])
     (term_zero,) = call(
         functools.partial(last_body, rows),
         [(2, rows, size)],
@@ -473,8 +477,9 @@
         moved=16 * unit * states,
     )(half, patch, probes, kr, ki, tab)
     came_zero = shifted(term_zero, "frame", -1)
-    gradient = gather(1, rows, size, pos, before, term_one, came_one)
-    return gather(0, rows, size, pos, before, term_zero, came_zero, gradient)
+    came_beside = lax.ppermute(term_one, "frame", [(i, i - 1) for i in range(1, frames, 2)])
+    gradient = gather(1, rows, size, pos, before, term_one, came_one, came_beside)
+    return gather(0, rows, size, pos, before, term_zero, came_zero, pos, gradient)
 
 
 def solution(mesh):

time: 41.2 us -> 44.5 us (1.080)
  starting transfers between devices: 8.46 us -> 11.6 us
    ppermute x0 -> x2, starting transfers between devices: none -> 2.6 us  [the longest x1 1.31 us: gradient_of(): lax.ppermute(term_one, 'frame', [(i, (i - 1) % frames) for i in range(0,...]
    ppermute x7 -> x6, starting transfers between devices: 7.3 us -> 7.89 us  [shifted(): lax.ppermute(value, axis, [(i, (i + by) % count) for i in range(count)])]
    ppermute x7 -> x6, waiting for transfers between devices: 16.6 us -> 16.5 us  [shifted(): lax.ppermute(value, axis, [(i, (i + by) % count) for i in range(count)])]
  transfers between devices with their start and end apart: 8 -> 9, of which waited for: 3 -> 3; matrix products, arithmetic and copies ran while one was open for 0% -> 0% of each run, Pallas kernels for 28% -> 26%
where the time goes in v13:
time: 44.5 us; the launch traced here: 44.2 us
  waiting for transfers between devices  16.6 us (37%)
  Pallas kernels  15.9 us (36%)
  starting transfers between devices  11.6 us (26%)
    ppermute x6, waiting for transfers between devices, shifted(): lax.ppermute(value, axis, [(i, (i + by) % count) for i in range(count)])  16.5 us
    ppermute x6, starting transfers between devices, shifted(): lax.ppermute(value, axis, [(i, (i + by) % count) for i in range(count)])  7.89 us
    pallas_call x1, Pallas kernels, gradient_of(): pl.pallas_call(prepare_body, out_shape=[jax.ShapeDtypeStruct(grid, F32)]...  3.04 us
    pallas_call x1, Pallas kernels, gradient_of(): call(functools.partial(last_body, rows), [(2, rows, size)], [VMEM] * 6, [...  2.41 us
    pallas_call x1, Pallas kernels, gradient_of(): call(functools.partial(middle_body, rows), [(2, rows, size), (states, 2)...  2.13 us
    pallas_call x2, Pallas kernels, gather(): pl.pallas_call(functools.partial(gather_body, slice_id, rows), out_shape=...  1.88 us
    pallas_call x1, Pallas kernels, gradient_of(): call(inner_body, [(states, 2) + grid] * 2, [VMEM] * (7 + len(pairs)), flo...  1.81 us
    pallas_call x1, Pallas kernels, gradient_of(): call(own_body, [(1, 2) + grid, (2,) + grid], [VMEM] * 7, flops=2 * flops,...  1.6 us
  transfers between devices with their start and end apart: 9, of which 3 were waited for; matrix products, arithmetic and copies ran while one was open for 0% of the time, Pallas kernels for 26%

profile of v13, /device:TPU:0, one launch (start us, length us, event | category | flops | bytes accessed | tf_op | source)
XLA Modules:
  0.0 44.2 jit_solution(6259553801707028783)
XLA Ops:
  0.0 1.3 %shard_map.64 = (s32[1,2]{1,0:T(1,128)S(1)}, f32[256,256]{1,0:T(8,128)S(1)}, f32[2,256,512]{2,1,0:T(8,128)S(1)}) custom-call(s32[1,2]{1,0:T(1,128)} %pos_hbm.1, f32[1,2,256,256]{3,2,1,0:T(8,128)} %probe_hbm.3, f32[2,2,256,512]{3,2,1,0:T(8,128)} %object_hbm.3), custom_call_target="tpu_custom_call" | custom-call | bytes 1572864 | tf_op jit(solution)/shard_map/pallas_call | solution.py:407
  1.3 0.0 copy-start.1
  1.4 0.0 copy-start
  1.4 0.1 shard_map.66
  1.5 0.5 %collective-permute-start.2 = (f32[2,256,256]{2,1,0:T(8,128)S(1)}, f32[2,256,256]{2,1,0:T(8,128)S(1)}, u32[]{:S(2)}, u32[]{:S(2)}) collective-permute-start(f32[2,256,256]{2,1,0:T(8,128)S(1)} %shard_map.66), channel_id=1, source_target_pairs={{0,2},{2,4},{4,6},{6,8},{8,10},{10,12},{12,14},{14,16},{16,18},{18... | collective-permute-start | bytes 1572872 | tf_op jit(solution)/shard_map/ppermute | solution.py:23
  2.0 2.6 %collective-permute-start.4 = (f32[256,256]{1,0:T(8,128)S(1)}, f32[256,256]{1,0:T(8,128)S(1)}, u32[]{:S(2)}, u32[]{:S(2)}) collective-permute-start(f32[256,256]{1,0:T(8,128)S(1)} %get-tuple-element.32), channel_id=1, source_target_pairs={{0,1},{1,0},{2,3},{3,2},{4,5},{5,4},{6,7},{7,6},{8,9},{9,8},{10,11... | collective-permute-start | bytes 786440 | tf_op jit(solution)/shard_map/ppermute | solution.py:23
  4.6 1.3 %shard_map.65 = (f32[2,256,512]{2,1,0:T(8,128)S(1)}, f32[2,256,256]{2,1,0:T(8,128)S(1)}) custom-call(s32[1,2]{1,0:T(1,128)S(1)} %get-tuple-element.22.pos_ref.other_ref, f32[2,2,256,512]{3,2,1,0:T(8,128)} %object_hbm.3), custom_call_target="tpu_custom_call" | custom-call | bytes 2621440 | tf_op jit(solution)/shard_map/pallas_call | solution.py:425
  5.9 1.3 %collective-permute-start.1 = (f32[2,256,256]{2,1,0:T(8,128)S(1)}, f32[2,256,256]{2,1,0:T(8,128)S(1)}, u32[]{:S(2)}, u32[]{:S(2)}) collective-permute-start(f32[2,256,256]{2,1,0:T(8,128)S(1)} %get-tuple-element.24), channel_id=1, source_target_pairs={{0,2},{2,4},{4,6},{6,8},{8,10},{10,12},{12,14},{14,16},{16,18},{18... | collective-permute-start | bytes 1572872 | tf_op jit(solution)/shard_map/ppermute | solution.py:23
  7.3 0.0 copy-done.1
  7.3 0.4 collective-permute-start.3
  7.6 3.1 %collective-permute-done.4.refs_0_ = f32[256,256]{1,0:T(8,128)S(1)} collective-permute-done((f32[256,256]{1,0:T(8,128)S(1)}, f32[256,256]{1,0:T(8,128)S(1)}, u32[]{:S(2)}, u32[]{:S(2)}) %collective-permute-start.4) | collective-permute-done | bytes 262176 | tf_op jit(solution)/shard_map/ppermute | solution.py:23
  10.7 1.2 %collective-permute-start.5 = (f32[256,256]{1,0:T(8,128)S(1)}, f32[256,256]{1,0:T(8,128)S(1)}, u32[]{:S(2)}, u32[]{:S(2)}) collective-permute-start(f32[256,256]{1,0:T(8,128)S(1)} %collective-permute-done.4.refs_0_), channel_id=1, source_target_pairs={{0,2},{2,0},{4,6},{6,4},{8,10},{10,8},{12,14},{14,12},{16,18},{18,... | collective-permute-start | bytes 786440 | tf_op jit(solution)/shard_map/ppermute | solution.py:447
  11.9 0.0 collective-permute-start
  11.9 10.5 %collective-permute-done.before_ref = s32[1,2]{1,0:T(1,128)S(1)} collective-permute-done((s32[1,2]{1,0:T(1,128)S(1)}, s32[1,2]{1,0:T(1,128)S(1)}, u32[]{:S(2)}, u32[]{:S(2)}) %collective-permute-start) | collective-permute-done | bytes 40 | tf_op jit(solution)/shard_map/ppermute | solution.py:23
  22.4 0.2 shard_map.69.refs_0_
  22.6 0.0 collective-permute-done.3.lent_ref
  22.6 3.0 %shard_map.67 = (f32[256,256]{1,0:T(8,128)S(1)}, f32[256,256]{1,0:T(8,128)S(1)}, f32[256,256]{1,0:T(8,128)S(1)}, f32[1,2,256,256]{3,2,1,0:T(8,128)S(1)}, bf16[2,4,256,256]{3,2,1,0:T(8,128)(2,1)S(1)}) custom-call(s32[1,2]{1,0:T(1,128)S(1)} %collective-permute-done.before_ref, f32[1,256,256]{2,1,0:T(8,128)S(1)} %collective-permute-done.3.lent_ref, ...), custom_call_target="tpu_custom_call" | custom-call | flops 33554432 | bytes 3932160 | tf_op jit(solution)/shard_map/pallas_call | solution.py:433
  25.7 0.0 collective-permute-done.2.halo_ref
  25.7 1.6 %shard_map.68 = (f32[1,2,256,256]{3,2,1,0:T(8,128)S(1)}, f32[2,256,256]{2,1,0:T(8,128)S(1)}) custom-call(s32[1,2]{1,0:T(1,128)S(1)} %collective-permute-done.before_ref, f32[2,256,512]{2,1,0:T(8,128)S(1)} %get-tuple-element.25.object_ref, f32[2,256,256]{2,1,0:T(8,128)S(1)} %collective-permute-done.2.halo_ref, ...), custom_call_target="tpu_custom_call" | custom-call | flops 805306368 | bytes 1572864 | tf_op jit(solution)/shard_map/pallas_call | solution.py:448
  27.3 0.0 collective-permute-done.5.refs_1_
  27.3 1.8 %shard_map.70 = (f32[2,2,256,256]{3,2,1,0:T(8,128)S(1)}, f32[2,2,256,256]{3,2,1,0:T(8,128)S(1)}) custom-call(s32[1,2]{1,0:T(1,128)S(1)} %collective-permute-done.before_ref, f32[2,256,256]{2,1,0:T(8,128)S(1)} %get-tuple-element.30.patch, f32[1,2,256,256]{3,2,1,0:T(8,128)S(1)} %get-tuple-element.31.mine_ref, ...), custom_call_target="tpu_custom_call" | custom-call | flops 805306368 | bytes 3145728 | tf_op jit(solution)/shard_map/pallas_call | solution.py:455
  29.1 0.0 collective-permute-done.1.halo_ref
  29.2 2.1 %shard_map.71 = (f32[2,128,256]{2,1,0:T(8,128)S(1)}, f32[2,2,256,256]{3,2,1,0:T(8,128)S(1)}, f32[2,256,256]{2,1,0:T(8,128)S(1)}) custom-call(s32[1,2]{1,0:T(1,128)S(1)} %collective-permute-done.before_ref, f32[2,256,512]{2,1,0:T(8,128)S(1)} %get-tuple-element.23.object_ref, f32[2,256,256]{2,1,0:T(8,128)S(1)} %collective-permute-done.1.halo_ref, ...), custom_call_target="tpu_custom_call" | custom-call | flops 1610612736 | bytes 4194304 | tf_op jit(solution)/shard_map/pallas_call | solution.py:462
  31.3 1.3 %collective-permute-start.7 = (f32[2,128,256]{2,1,0:T(8,128)S(1)}, f32[2,128,256]{2,1,0:T(8,128)S(1)}, u32[]{:S(2)}, u32[]{:S(2)}) collective-permute-start(f32[2,128,256]{2,1,0:T(8,128)S(1)} %get-tuple-element.38.own_ref), channel_id=1, source_target_pairs={{0,30},{4,2},{8,6},{12,10},{16,14},{20,18},{24,22},{28,26},{1,31},... | collective-permute-start | bytes 786440 | tf_op jit(solution)/shard_map/ppermute | solution.py:470
  32.6 1.3 %collective-permute-start.8 = (f32[2,128,256]{2,1,0:T(8,128)S(1)}, f32[2,128,256]{2,1,0:T(8,128)S(1)}, u32[]{:S(2)}, u32[]{:S(2)}) collective-permute-start(f32[2,128,256]{2,1,0:T(8,128)S(1)} %get-tuple-element.38.own_ref), channel_id=1, source_target_pairs={{2,0},{6,4},{10,8},{14,12},{18,16},{22,20},{26,24},{30,28},{3,1},{... | collective-permute-start | bytes 786440 | tf_op jit(solution)/shard_map/ppermute | solution.py:480
  33.9 2.4 %shard_map.72.own_ref = f32[2,128,256]{2,1,0:T(8,128)S(1)} custom-call(f32[2,2,256,256]{3,2,1,0:T(8,128)S(1)} %get-tuple-element.35.half_ref, f32[2,256,256]{2,1,0:T(8,128)S(1)} %get-tuple-element.36.patch, f32[2,2,256,256]{3,2,1,0:T(8,128)S(1)} %get-tuple-element.37.probe_ref, f32[256,256]{1,0:T(8,128)S(1)} %get-tuple-element.27.kr_ref, ...), custom_call_target="tpu_custom_call" | custom-call | flops 1610612736 | bytes 2097152 | tf_op jit(solution)/shard_map/pallas_call | solution.py:471
  36.3 3.1 %collective-permute-start.6 = (f32[2,128,256]{2,1,0:T(8,128)S(1)}, f32[2,128,256]{2,1,0:T(8,128)S(1)}, u32[]{:S(2)}, u32[]{:S(2)}) collective-permute-start(f32[2,128,256]{2,1,0:T(8,128)S(1)} %shard_map.72.own_ref), channel_id=1, source_target_pairs={{0,30},{2,0},{4,2},{6,4},{8,6},{10,8},{12,10},{14,12},{16,14},{18,... | collective-permute-start | bytes 786440 | tf_op jit(solution)/shard_map/ppermute | solution.py:23
  39.4 0.0 collective-permute-done.7.came_ref
  39.4 0.0 collective-permute-done.8.other_ref
  39.4 0.9 %shard_map.73.refs_0_ = f32[2,2,128,512]{3,2,1,0:T(8,128)} custom-call(s32[1,2]{1,0:T(1,128)S(1)} %get-tuple-element.22.pos_ref.other_ref, s32[1,2]{1,0:T(1,128)S(1)} %collective-permute-done.before_ref, f32[2,128,256]{2,1,0:T(8,128)S(1)} %get-tuple-element.38.own_ref, f32[2,128,256]{2,1,0:T(8,128)S(1)} %collective-permute-done.7.came_ref, ...), custom_call_target="tpu_custom_call" | custom-call | bytes 1048576 | tf_op jit(solution)/shard_map/pallas_call | solution.py:378
  40.4 2.9 %collective-permute-done.6.came_ref = f32[2,128,256]{2,1,0:T(8,128)S(1)} collective-permute-done((f32[2,128,256]{2,1,0:T(8,128)S(1)}, f32[2,128,256]{2,1,0:T(8,128)S(1)}, u32[]{:S(2)}, u32[]{:S(2)}) %collective-permute-start.6) | collective-permute-done | bytes 262176 | tf_op jit(solution)/shard_map/ppermute | solution.py:23
  43.3 0.9 %shard_map.74 = f32[2,2,128,512]{3,2,1,0:T(8,128)} custom-call(s32[1,2]{1,0:T(1,128)S(1)} %get-tuple-element.22.pos_ref.other_ref, s32[1,2]{1,0:T(1,128)S(1)} %collective-permute-done.before_ref, f32[2,128,256]{2,1,0:T(8,128)S(1)} %shard_map.72.own_ref, f32[2,128,256]{2,1,0:T(8,128)S(1)} %collective-permute-done.6.came_ref, ...), custom_call_target="tpu_custom_call", output_to_operand_aliasing={{}: (5, {})} | custom-call | bytes 1048576 | tf_op jit(solution)/shard_map/pallas_call | solution.py:378
  (1 shorter events, 0.0 us)
Async XLA Ops:
  1.3 5.9 %copy-start.1 = (f32[1,256,256]{2,1,0:T(8,128)S(1)}, f32[1,256,256]{2,1,0:T(8,128)}, u32[]{:S(2)}) copy-start(f32[1,256,256]{2,1,0:T(8,128)} %param.8) | copy-start | bytes 786436
  1.4 10.5 %copy-start = (s32[1,2]{1,0:T(1,128)S(1)}, s32[1,2]{1,0:T(1,128)}, u32[]{:S(2)}) copy-start(s32[1,2]{1,0:T(1,128)} %pos_hbm.1) | copy-start | bytes 28
  1.5 24.2 %collective-permute-start.2 = (f32[2,256,256]{2,1,0:T(8,128)S(1)}, f32[2,256,256]{2,1,0:T(8,128)S(1)}, u32[]{:S(2)}, u32[]{:S(2)}) collective-permute-start(f32[2,256,256]{2,1,0:T(8,128)S(1)} %shard_map.66), channel_id=1, source_target_pairs={{0,2},{2,4},{4,6},{6,8},{8,10},{10,12},{12,14},{14,16},{16,18},{18... | collective-permute-start | bytes 1572872 | tf_op jit(solution)/shard_map/ppermute | solution.py:23
  2.0 8.7 %collective-permute-start.4 = (f32[256,256]{1,0:T(8,128)S(1)}, f32[256,256]{1,0:T(8,128)S(1)}, u32[]{:S(2)}, u32[]{:S(2)}) collective-permute-start(f32[256,256]{1,0:T(8,128)S(1)} %get-tuple-element.32), channel_id=1, source_target_pairs={{0,1},{1,0},{2,3},{3,2},{4,5},{5,4},{6,7},{7,6},{8,9},{9,8},{10,11... | collective-permute-start | bytes 786440 | tf_op jit(solution)/shard_map/ppermute | solution.py:23
  5.9 23.2 %collective-permute-start.1 = (f32[2,256,256]{2,1,0:T(8,128)S(1)}, f32[2,256,256]{2,1,0:T(8,128)S(1)}, u32[]{:S(2)}, u32[]{:S(2)}) collective-permute-start(f32[2,256,256]{2,1,0:T(8,128)S(1)} %get-tuple-element.24), channel_id=1, source_target_pairs={{0,2},{2,4},{4,6},{6,8},{8,10},{10,12},{12,14},{14,16},{16,18},{18... | collective-permute-start | bytes 1572872 | tf_op jit(solution)/shard_map/ppermute | solution.py:23
  7.3 15.4 %collective-permute-start.3 = (f32[1,256,256]{2,1,0:T(8,128)S(1)}, f32[1,256,256]{2,1,0:T(8,128)S(1)}, u32[]{:S(2)}, u32[]{:S(2)}) collective-permute-start(f32[1,256,256]{2,1,0:T(8,128)S(1)} %copy-done.1), channel_id=1, source_target_pairs={{0,2},{2,4},{4,6},{6,8},{8,10},{10,12},{12,14},{14,16},{16,18},{18... | collective-permute-start | bytes 786440 | tf_op jit(solution)/shard_map/ppermute | solution.py:23
  10.7 16.6 %collective-permute-start.5 = (f32[256,256]{1,0:T(8,128)S(1)}, f32[256,256]{1,0:T(8,128)S(1)}, u32[]{:S(2)}, u32[]{:S(2)}) collective-permute-start(f32[256,256]{1,0:T(8,128)S(1)} %collective-permute-done.4.refs_0_), channel_id=1, source_target_pairs={{0,2},{2,0},{4,6},{6,4},{8,10},{10,8},{12,14},{14,12},{16,18},{18,... | collective-permute-start | bytes 786440 | tf_op jit(solution)/shard_map/ppermute | solution.py:447
  11.9 10.5 %collective-permute-start = (s32[1,2]{1,0:T(1,128)S(1)}, s32[1,2]{1,0:T(1,128)S(1)}, u32[]{:S(2)}, u32[]{:S(2)}) collective-permute-start(s32[1,2]{1,0:T(1,128)S(1)} %copy-done), channel_id=1, source_target_pairs={{0,2},{2,4},{4,6},{6,8},{8,10},{10,12},{12,14},{14,16},{16,18},{18... | collective-permute-start | bytes 32 | tf_op jit(solution)/shard_map/ppermute | solution.py:23
  31.3 8.1 %collective-permute-start.7 = (f32[2,128,256]{2,1,0:T(8,128)S(1)}, f32[2,128,256]{2,1,0:T(8,128)S(1)}, u32[]{:S(2)}, u32[]{:S(2)}) collective-permute-start(f32[2,128,256]{2,1,0:T(8,128)S(1)} %get-tuple-element.38.own_ref), channel_id=1, source_target_pairs={{0,30},{4,2},{8,6},{12,10},{16,14},{20,18},{24,22},{28,26},{1,31},... | collective-permute-start | bytes 786440 | tf_op jit(solution)/shard_map/ppermute | solution.py:470
  32.6 6.8 %collective-permute-start.8 = (f32[2,128,256]{2,1,0:T(8,128)S(1)}, f32[2,128,256]{2,1,0:T(8,128)S(1)}, u32[]{:S(2)}, u32[]{:S(2)}) collective-permute-start(f32[2,128,256]{2,1,0:T(8,128)S(1)} %get-tuple-element.38.own_ref), channel_id=1, source_target_pairs={{2,0},{6,4},{10,8},{14,12},{18,16},{22,20},{26,24},{30,28},{3,1},{... | collective-permute-start | bytes 786440 | tf_op jit(solution)/shard_map/ppermute | solution.py:480
  36.3 7.0 %collective-permute-start.6 = (f32[2,128,256]{2,1,0:T(8,128)S(1)}, f32[2,128,256]{2,1,0:T(8,128)S(1)}, u32[]{:S(2)}, u32[]{:S(2)}) collective-permute-start(f32[2,128,256]{2,1,0:T(8,128)S(1)} %shard_map.72.own_ref), channel_id=1, source_target_pairs={{0,30},{2,0},{4,2},{6,4},{8,6},{10,8},{12,10},{14,12},{16,14},{18,... | collective-permute-start | bytes 786440 | tf_op jit(solution)/shard_map/ppermute | solution.py:23

commit v14 on v12

--- a/solution.py
+++ b/solution.py
@@ -210,22 +210,23 @@
 
 
 def prepare_body(
-    before_ref, lent_ref, probe_hbm, prop_hbm, tab_hbm,
+    before_ref, probe_hbm, prop_hbm, amp_hbm, tab_hbm,
     wave_re, wave_im, amp_out, first_out, tab_out,
-    probe, prop, sem,
+    probe, prop, amp, sem,
 ):
-    copies = run_copies(((probe_hbm, probe), (prop_hbm, prop), (tab_hbm, tab_out)), sem)
+    copies = run_copies(((amp_hbm, amp), (probe_hbm, probe), (prop_hbm, prop), (tab_hbm, tab_out)), sem)
     size = prop.shape[0]
-    amp_out[...] = by_parity(lent_ref[0])
     copies[0].wait()
+    amp_out[...] = by_parity(amp[0])
+    copies[1].wait()
     turn = turn_of(before_ref, size)
     for c in range(2):
         first_out[0, c] = turned(probe[0, c], *turn)
-    copies[1].wait()
+    copies[2].wait()
     phase = by_parity(prop[...])
     wave_re[...] = jnp.cos(phase)
     wave_im[...] = jnp.sin(phase)
-    copies[2].wait()
+    copies[3].wait()
 
 
 def spread(ref, which, shape):
@@ -291,8 +292,7 @@
     in_groups(out_ref.shape[0] - 1, body)
 
 
-def middle_body(rows, before_ref, object_ref, halo_ref, inner_ref, amp_ref, tab, term_ref, half_ref, patch, far, power):
-    states = inner_ref.shape[0]
+def outward_body(before_ref, object_ref, halo_ref, inner_ref, tab, far, power, patch):
     patch[0], patch[1] = patch_of(object_ref, halo_ref, before_ref)
     power[...] = jnp.zeros_like(power)
 
@@ -304,13 +304,16 @@
             total += wave[0] * wave[0] + wave[1] * wave[1]
         power[...] = total
 
-    in_groups(states, outward)
-    power[...] = 1.0 - amp_ref[...] * lax.rsqrt(power[...] + 1.0)
+    in_groups(inner_ref.shape[0], outward)
+
+
+def middle_body(rows, far, power, inner_ref, amp_ref, tab, term_ref, half_ref, factor):
+    factor[...] = 1.0 - amp_ref[...] * lax.rsqrt(power[...] + 1.0)
     term_ref[...] = jnp.zeros_like(term_ref)
     take = pl.ds(pl.multiple_of(lax.axis_index("state") * rows, rows), rows)
 
     def homeward(group):
-        waves = [rows_inverse(power[...] * far[m, 0], power[...] * far[m, 1], tab) for m in group]
+        waves = [rows_inverse(factor[...] * far[m, 0], factor[...] * far[m, 1], tab) for m in group]
         for m, wave in zip(group, waves):
             half_ref[m, 0], half_ref[m, 1] = wave
         for m in group:
@@ -319,7 +322,7 @@
             term_ref[0] += part[0]
             term_ref[1] += part[1]
 
-    in_groups(states, homeward)
+    in_groups(inner_ref.shape[0], homeward)
 
 
 def last_body(rows, half_ref, patch, probe_ref, kr_ref, ki_ref, tab, term_ref, front):
@@ -398,7 +401,6 @@
     flops = 24 * size**3
     tab = tables(size)
     before = shifted(positions, "frame", 1)
-    lent = shifted(amplitude, "frame", 1)
     given = [in_hbm(x) for x in (positions, probe, object_slices)]
     pos, plane, held_zero = pl.pallas_call(
         load_body,
@@ -430,12 +432,18 @@
         prepare_body,
         out_shape=[jax.ShapeDtypeStruct(grid, F32)] * 3
         + [jax.ShapeDtypeStruct(x.shape, x.dtype) for x in (probe, tab)],
-        in_specs=[VMEM] * 2 + [HBM] * 3,
+        in_specs=[VMEM] + [HBM] * 4,
         out_specs=[VMEM] * 5,
-        scratch_shapes=[pltpu.VMEM(probe.shape, F32), pltpu.VMEM(grid, F32), pltpu.SemaphoreType.DMA((3,))],
+        scratch_shapes=[
+            pltpu.VMEM(probe.shape, F32),
+            pltpu.VMEM(grid, F32),
+            pltpu.VMEM(amplitude.shape, F32),
+            pltpu.SemaphoreType.DMA((4,)),
+        ],
         compiler_params=pltpu.CompilerParams(vmem_limit_bytes=LIMIT),
         cost_estimate=pl.CostEstimate(flops=2 * size**3, bytes_accessed=60 * unit, transcendentals=0),
-    )(before, lent, given[1], *(in_hbm(x) for x in (propagator, tab)))
+    )(before, given[1], *(in_hbm(x) for x in (propagator, amplitude, tab)))
+    amp = shifted(amp, "frame", 1)
     frames = lax.axis_size("frame")
     own = call(turn_body, [grid] * len(planes), [VMEM] * (1 + len(planes)), moved=16 * unit)(before, *planes)
     pairs = []
@@ -455,14 +463,21 @@
         flops=2 * flops * (states - 1),
         moved=24 * unit * states,
     )(before, first_patch, mine, first, kr, ki, tab, *pairs)
-    term_one, half, patch = call(
+    far, power, patch = call(
+        outward_body,
+        [(states, 2) + grid, grid, (2,) + grid],
+        [VMEM] * 5,
+        flops=flops * states,
+        moved=32 * unit * states,
+    )(before, held_one, halo_one, waves, tab)
+    term_one, half = call(
         functools.partial(middle_body, rows),
-        [(2, rows, size), (states, 2) + grid, (2,) + grid],
-        [VMEM] * 6,
-        [pltpu.VMEM((states, 2) + grid, F32), pltpu.VMEM(grid, F32)],
-        flops=2 * flops * states,
+        [(2, rows, size), (states, 2) + grid],
+        [VMEM] * 5,
+        [pltpu.VMEM(grid, F32)],
+        flops=flops * states,
         moved=32 * unit * states,
-    )(before, held_one, halo_one, waves, amp, tab)
+    )(far, power, waves, amp, tab)
     came_one = shifted(term_one, "frame", -1)
     (term_zero,) = call(
         functools.partial(last_body, rows),

time: 41.2 us -> 42 us (1.019)
  the two profiles are of different devices: /device:TPU:0 before, /device:TPU:1 now
where the time goes in v14:
time: 42 us; the launch traced here: 41.9 us
  Pallas kernels  16.3 us (39%)
  starting transfers between devices  14.7 us (35%)
  waiting for transfers between devices  10.7 us (25%)
    ppermute x7, starting transfers between devices, shifted(): lax.ppermute(value, axis, [(i, (i + by) % count) for i in range(count)])  14.7 us
    ppermute x7, waiting for transfers between devices, shifted(): lax.ppermute(value, axis, [(i, (i + by) % count) for i in range(count)])  10.7 us
    pallas_call x1, Pallas kernels, gradient_of(): pl.pallas_call(prepare_body, out_shape=[jax.ShapeDtypeStruct(grid, F32)]...  3.54 us
    pallas_call x1, Pallas kernels, gradient_of(): call(functools.partial(last_body, rows), [(2, rows, size)], [VMEM] * 6, [...  2.4 us
    pallas_call x2, Pallas kernels, gather(): pl.pallas_call(functools.partial(gather_body, slice_id, rows), out_shape=...  1.88 us
    pallas_call x1, Pallas kernels, gradient_of(): call(inner_body, [(states, 2) + grid] * 2, [VMEM] * (7 + len(pairs)), flo...  1.81 us
    pallas_call x1, Pallas kernels, gradient_of(): call(own_body, [(1, 2) + grid, (2,) + grid], [VMEM] * 7, flops=2 * flops,...  1.6 us
    pallas_call x1, Pallas kernels, gradient_of(): call(load_send_body, [object_slices.shape[1:], (2,) + grid], [VMEM, HBM],...  1.33 us
  transfers between devices with their start and end apart: 8, of which 3 were waited for; matrix products, arithmetic and copies ran while one was open for 0% of the time, Pallas kernels for 31%

profile of v14, /device:TPU:1, one launch (start us, length us, event | category | flops | bytes accessed | tf_op | source)
XLA Modules:
  0.0 41.9 jit_solution(18100913267420781000)
XLA Ops:
  0.0 1.3 %shard_map.64 = (s32[1,2]{1,0:T(1,128)S(1)}, f32[256,256]{1,0:T(8,128)S(1)}, f32[2,256,512]{2,1,0:T(8,128)S(1)}) custom-call(s32[1,2]{1,0:T(1,128)} %pos_hbm.1, f32[1,2,256,256]{3,2,1,0:T(8,128)} %probe_hbm.3, f32[2,2,256,512]{3,2,1,0:T(8,128)} %object_hbm.3), custom_call_target="tpu_custom_call" | custom-call | bytes 1572864 | tf_op jit(solution)/shard_map/pallas_call | solution.py:405
  1.3 0.0 copy-start
  1.4 0.1 shard_map.66
  1.5 2.7 %collective-permute-start.2 = (f32[2,256,256]{2,1,0:T(8,128)S(1)}, f32[2,256,256]{2,1,0:T(8,128)S(1)}, u32[]{:S(2)}, u32[]{:S(2)}) collective-permute-start(f32[2,256,256]{2,1,0:T(8,128)S(1)} %shard_map.66), channel_id=1, source_target_pairs={{0,2},{2,4},{4,6},{6,8},{8,10},{10,12},{12,14},{14,16},{16,18},{18... | collective-permute-start | bytes 1572872 | tf_op jit(solution)/shard_map/ppermute | solution.py:23
  4.1 1.2 %collective-permute-start.3 = (f32[256,256]{1,0:T(8,128)S(1)}, f32[256,256]{1,0:T(8,128)S(1)}, u32[]{:S(2)}, u32[]{:S(2)}) collective-permute-start(f32[256,256]{1,0:T(8,128)S(1)} %get-tuple-element.34), channel_id=1, source_target_pairs={{0,1},{1,0},{2,3},{3,2},{4,5},{5,4},{6,7},{7,6},{8,9},{9,8},{10,11... | collective-permute-start | bytes 786440 | tf_op jit(solution)/shard_map/ppermute | solution.py:23
  5.4 1.3 %shard_map.65 = (f32[2,256,512]{2,1,0:T(8,128)S(1)}, f32[2,256,256]{2,1,0:T(8,128)S(1)}) custom-call(s32[1,2]{1,0:T(1,128)S(1)} %get-tuple-element.24.pos_ref, f32[2,2,256,512]{3,2,1,0:T(8,128)} %object_hbm.3), custom_call_target="tpu_custom_call" | custom-call | bytes 2621440 | tf_op jit(solution)/shard_map/pallas_call | solution.py:423
  6.7 0.4 collective-permute-start.1
  7.1 4.2 %collective-permute-done.3.refs_0_ = f32[256,256]{1,0:T(8,128)S(1)} collective-permute-done((f32[256,256]{1,0:T(8,128)S(1)}, f32[256,256]{1,0:T(8,128)S(1)}, u32[]{:S(2)}, u32[]{:S(2)}) %collective-permute-start.3) | collective-permute-done | bytes 262176 | tf_op jit(solution)/shard_map/ppermute | solution.py:23
  11.4 0.0 collective-permute-start.4
  11.4 0.0 copy-done
  11.4 2.2 %collective-permute-start = (s32[1,2]{1,0:T(1,128)S(1)}, s32[1,2]{1,0:T(1,128)S(1)}, u32[]{:S(2)}, u32[]{:S(2)}) collective-permute-start(s32[1,2]{1,0:T(1,128)S(1)} %copy-done), channel_id=1, source_target_pairs={{0,2},{2,4},{4,6},{6,8},{8,10},{10,12},{12,14},{14,16},{16,18},{18... | collective-permute-start | bytes 32 | tf_op jit(solution)/shard_map/ppermute | solution.py:23
  13.5 2.4 %collective-permute-done.before_ref = s32[1,2]{1,0:T(1,128)S(1)} collective-permute-done((s32[1,2]{1,0:T(1,128)S(1)}, s32[1,2]{1,0:T(1,128)S(1)}, u32[]{:S(2)}, u32[]{:S(2)}) %collective-permute-start) | collective-permute-done | bytes 40 | tf_op jit(solution)/shard_map/ppermute | solution.py:23
  15.9 3.5 %shard_map.67 = (f32[256,256]{1,0:T(8,128)S(1)}, f32[256,256]{1,0:T(8,128)S(1)}, f32[256,256]{1,0:T(8,128)S(1)}, f32[1,2,256,256]{3,2,1,0:T(8,128)S(1)}, bf16[2,4,256,256]{3,2,1,0:T(8,128)(2,1)S(1)}) custom-call(s32[1,2]{1,0:T(1,128)S(1)} %collective-permute-done.before_ref, f32[1,2,256,256]{3,2,1,0:T(8,128)} %probe_hbm.3, f32[256,256]{1,0:T(8,128)} %prop_hbm.1, ...), custom_call_target="tpu_custom_call" | custom-call | flops 33554432 | bytes 3932160 | tf_op jit(solution)/shard_map/pallas_call | solution.py:431
  19.5 2.6 %collective-permute-start.5 = (f32[256,256]{1,0:T(8,128)S(1)}, f32[256,256]{1,0:T(8,128)S(1)}, u32[]{:S(2)}, u32[]{:S(2)}) collective-permute-start(f32[256,256]{1,0:T(8,128)S(1)} %get-tuple-element.38), channel_id=1, source_target_pairs={{0,2},{2,4},{4,6},{6,8},{8,10},{10,12},{12,14},{14,16},{16,18},{18... | collective-permute-start | bytes 786440 | tf_op jit(solution)/shard_map/ppermute | solution.py:23
  22.1 0.2 shard_map.69.refs_0_
  22.3 0.0 collective-permute-done.2.halo_ref
  22.3 1.6 %shard_map.68 = (f32[1,2,256,256]{3,2,1,0:T(8,128)S(1)}, f32[2,256,256]{2,1,0:T(8,128)S(1)}) custom-call(s32[1,2]{1,0:T(1,128)S(1)} %collective-permute-done.before_ref, f32[2,256,512]{2,1,0:T(8,128)S(1)} %get-tuple-element.27.object_ref, f32[2,256,256]{2,1,0:T(8,128)S(1)} %collective-permute-done.2.halo_ref, ...), custom_call_target="tpu_custom_call" | custom-call | flops 805306368 | bytes 1572864 | tf_op jit(solution)/shard_map/pallas_call | solution.py:452
  23.9 0.0 collective-permute-done.4.refs_1_
  23.9 1.8 %shard_map.70 = (f32[2,2,256,256]{3,2,1,0:T(8,128)S(1)}, f32[2,2,256,256]{3,2,1,0:T(8,128)S(1)}) custom-call(s32[1,2]{1,0:T(1,128)S(1)} %collective-permute-done.before_ref, f32[2,256,256]{2,1,0:T(8,128)S(1)} %get-tuple-element.32.patch, f32[1,2,256,256]{3,2,1,0:T(8,128)S(1)} %get-tuple-element.33.mine_ref, ...), custom_call_target="tpu_custom_call" | custom-call | flops 805306368 | bytes 3145728 | tf_op jit(solution)/shard_map/pallas_call | solution.py:459
  25.7 0.0 collective-permute-done.1.halo_ref
  25.8 1.2 %shard_map.71 = (f32[2,2,256,256]{3,2,1,0:T(8,128)S(1)}, f32[256,256]{1,0:T(8,128)S(1)}, f32[2,256,256]{2,1,0:T(8,128)S(1)}) custom-call(s32[1,2]{1,0:T(1,128)S(1)} %collective-permute-done.before_ref, f32[2,256,512]{2,1,0:T(8,128)S(1)} %get-tuple-element.25.object_ref, f32[2,256,256]{2,1,0:T(8,128)S(1)} %collective-permute-done.1.halo_ref, ...), custom_call_target="tpu_custom_call" | custom-call | flops 805306368 | bytes 4194304 | tf_op jit(solution)/shard_map/pallas_call | solution.py:466
  26.9 0.0 collective-permute-done.5.amp_ref
  27.0 0.9 %shard_map.72 = (f32[2,128,256]{2,1,0:T(8,128)S(1)}, f32[2,2,256,256]{3,2,1,0:T(8,128)S(1)}) custom-call(f32[2,2,256,256]{3,2,1,0:T(8,128)S(1)} %get-tuple-element.36.far, f32[256,256]{1,0:T(8,128)S(1)} %get-tuple-element.37.power, f32[2,2,256,256]{3,2,1,0:T(8,128)S(1)} %get-tuple-element.35.inner_ref, f32[256,256]{1,0:T(8,128)S(1)} %collective-permute-done.5.amp_ref, ...), custom_call_target="tpu_custom_call" | custom-call | flops 805306368 | bytes 4194304 | tf_op jit(solution)/shard_map/pallas_call | solution.py:473
  27.9 4.8 %collective-permute-start.7 = (f32[2,128,256]{2,1,0:T(8,128)S(1)}, f32[2,128,256]{2,1,0:T(8,128)S(1)}, u32[]{:S(2)}, u32[]{:S(2)}) collective-permute-start(f32[2,128,256]{2,1,0:T(8,128)S(1)} %get-tuple-element.42.own_ref), channel_id=1, source_target_pairs={{0,30},{2,0},{4,2},{6,4},{8,6},{10,8},{12,10},{14,12},{16,14},{18,... | collective-permute-start | bytes 786440 | tf_op jit(solution)/shard_map/ppermute | solution.py:23
  32.7 2.4 %shard_map.73.own_ref = f32[2,128,256]{2,1,0:T(8,128)S(1)} custom-call(f32[2,2,256,256]{3,2,1,0:T(8,128)S(1)} %get-tuple-element.39.half_ref, f32[2,256,256]{2,1,0:T(8,128)S(1)} %get-tuple-element.40.patch, f32[2,2,256,256]{3,2,1,0:T(8,128)S(1)} %get-tuple-element.41.probe_ref, f32[256,256]{1,0:T(8,128)S(1)} %get-tuple-element.29.kr_ref, ...), custom_call_target="tpu_custom_call" | custom-call | flops 1610612736 | bytes 2097152 | tf_op jit(solution)/shard_map/pallas_call | solution.py:482
  35.1 0.9 %collective-permute-start.6 = (f32[2,128,256]{2,1,0:T(8,128)S(1)}, f32[2,128,256]{2,1,0:T(8,128)S(1)}, u32[]{:S(2)}, u32[]{:S(2)}) collective-permute-start(f32[2,128,256]{2,1,0:T(8,128)S(1)} %shard_map.73.own_ref), channel_id=1, source_target_pairs={{0,30},{2,0},{4,2},{6,4},{8,6},{10,8},{12,10},{14,12},{16,14},{18,... | collective-permute-start | bytes 786440 | tf_op jit(solution)/shard_map/ppermute | solution.py:23
  36.0 0.0 collective-permute-done.7.came_ref
  36.0 0.9 %shard_map.74.refs_0_ = f32[2,2,128,512]{3,2,1,0:T(8,128)} custom-call(s32[1,2]{1,0:T(1,128)S(1)} %get-tuple-element.24.pos_ref, s32[1,2]{1,0:T(1,128)S(1)} %collective-permute-done.before_ref, f32[2,128,256]{2,1,0:T(8,128)S(1)} %get-tuple-element.42.own_ref, f32[2,128,256]{2,1,0:T(8,128)S(1)} %collective-permute-done.7.came_ref), custom_call_target="tpu_custom_call" | custom-call | bytes 1048576 | tf_op jit(solution)/shard_map/pallas_call | solution.py:377
  36.9 4.0 %collective-permute-done.6.came_ref = f32[2,128,256]{2,1,0:T(8,128)S(1)} collective-permute-done((f32[2,128,256]{2,1,0:T(8,128)S(1)}, f32[2,128,256]{2,1,0:T(8,128)S(1)}, u32[]{:S(2)}, u32[]{:S(2)}) %collective-permute-start.6) | collective-permute-done | bytes 262176 | tf_op jit(solution)/shard_map/ppermute | solution.py:23
  40.9 0.9 %shard_map.75 = f32[2,2,128,512]{3,2,1,0:T(8,128)} custom-call(s32[1,2]{1,0:T(1,128)S(1)} %get-tuple-element.24.pos_ref, s32[1,2]{1,0:T(1,128)S(1)} %collective-permute-done.before_ref, f32[2,128,256]{2,1,0:T(8,128)S(1)} %shard_map.73.own_ref, f32[2,128,256]{2,1,0:T(8,128)S(1)} %collective-permute-done.6.came_ref, ...), custom_call_target="tpu_custom_call", output_to_operand_aliasing={{}: (4, {})} | custom-call | bytes 1048576 | tf_op jit(solution)/shard_map/pallas_call | solution.py:377
Async XLA Ops:
  1.3 10.0 %copy-start = (s32[1,2]{1,0:T(1,128)S(1)}, s32[1,2]{1,0:T(1,128)}, u32[]{:S(2)}) copy-start(s32[1,2]{1,0:T(1,128)} %pos_hbm.1) | copy-start | bytes 28
  1.5 20.8 %collective-permute-start.2 = (f32[2,256,256]{2,1,0:T(8,128)S(1)}, f32[2,256,256]{2,1,0:T(8,128)S(1)}, u32[]{:S(2)}, u32[]{:S(2)}) collective-permute-start(f32[2,256,256]{2,1,0:T(8,128)S(1)} %shard_map.66), channel_id=1, source_target_pairs={{0,2},{2,4},{4,6},{6,8},{8,10},{10,12},{12,14},{14,16},{16,18},{18... | collective-permute-start | bytes 1572872 | tf_op jit(solution)/shard_map/ppermute | solution.py:23
  4.1 7.2 %collective-permute-start.3 = (f32[256,256]{1,0:T(8,128)S(1)}, f32[256,256]{1,0:T(8,128)S(1)}, u32[]{:S(2)}, u32[]{:S(2)}) collective-permute-start(f32[256,256]{1,0:T(8,128)S(1)} %get-tuple-element.34), channel_id=1, source_target_pairs={{0,1},{1,0},{2,3},{3,2},{4,5},{5,4},{6,7},{7,6},{8,9},{9,8},{10,11... | collective-permute-start | bytes 786440 | tf_op jit(solution)/shard_map/ppermute | solution.py:23
  6.7 19.1 %collective-permute-start.1 = (f32[2,256,256]{2,1,0:T(8,128)S(1)}, f32[2,256,256]{2,1,0:T(8,128)S(1)}, u32[]{:S(2)}, u32[]{:S(2)}) collective-permute-start(f32[2,256,256]{2,1,0:T(8,128)S(1)} %get-tuple-element.26), channel_id=1, source_target_pairs={{0,2},{2,4},{4,6},{6,8},{8,10},{10,12},{12,14},{14,16},{16,18},{18... | collective-permute-start | bytes 1572872 | tf_op jit(solution)/shard_map/ppermute | solution.py:23
  11.4 12.6 %collective-permute-start.4 = (f32[256,256]{1,0:T(8,128)S(1)}, f32[256,256]{1,0:T(8,128)S(1)}, u32[]{:S(2)}, u32[]{:S(2)}) collective-permute-start(f32[256,256]{1,0:T(8,128)S(1)} %collective-permute-done.3.refs_0_), channel_id=1, source_target_pairs={{0,2},{2,0},{4,6},{6,4},{8,10},{10,8},{12,14},{14,12},{16,18},{18,... | collective-permute-start | bytes 786440 | tf_op jit(solution)/shard_map/ppermute | solution.py:451
  11.4 4.6 %collective-permute-start = (s32[1,2]{1,0:T(1,128)S(1)}, s32[1,2]{1,0:T(1,128)S(1)}, u32[]{:S(2)}, u32[]{:S(2)}) collective-permute-start(s32[1,2]{1,0:T(1,128)S(1)} %copy-done), channel_id=1, source_target_pairs={{0,2},{2,4},{4,6},{6,8},{8,10},{10,12},{12,14},{14,16},{16,18},{18... | collective-permute-start | bytes 32 | tf_op jit(solution)/shard_map/ppermute | solution.py:23
  19.5 7.5 %collective-permute-start.5 = (f32[256,256]{1,0:T(8,128)S(1)}, f32[256,256]{1,0:T(8,128)S(1)}, u32[]{:S(2)}, u32[]{:S(2)}) collective-permute-start(f32[256,256]{1,0:T(8,128)S(1)} %get-tuple-element.38), channel_id=1, source_target_pairs={{0,2},{2,4},{4,6},{6,8},{8,10},{10,12},{12,14},{14,16},{16,18},{18... | collective-permute-start | bytes 786440 | tf_op jit(solution)/shard_map/ppermute | solution.py:23
  27.9 8.1 %collective-permute-start.7 = (f32[2,128,256]{2,1,0:T(8,128)S(1)}, f32[2,128,256]{2,1,0:T(8,128)S(1)}, u32[]{:S(2)}, u32[]{:S(2)}) collective-permute-start(f32[2,128,256]{2,1,0:T(8,128)S(1)} %get-tuple-element.42.own_ref), channel_id=1, source_target_pairs={{0,30},{2,0},{4,2},{6,4},{8,6},{10,8},{12,10},{14,12},{16,14},{18,... | collective-permute-start | bytes 786440 | tf_op jit(solution)/shard_map/ppermute | solution.py:23
  35.1 5.8 %collective-permute-start.6 = (f32[2,128,256]{2,1,0:T(8,128)S(1)}, f32[2,128,256]{2,1,0:T(8,128)S(1)}, u32[]{:S(2)}, u32[]{:S(2)}) collective-permute-start(f32[2,128,256]{2,1,0:T(8,128)S(1)} %shard_map.73.own_ref), channel_id=1, source_target_pairs={{0,30},{2,0},{4,2},{6,4},{8,6},{10,8},{12,10},{14,12},{16,14},{18,... | collective-permute-start | bytes 786440 | tf_op jit(solution)/shard_map/ppermute | solution.py:23
